TPU v7x, 128 devices: a whole 4x4x4 slice. The times are simulated.
128 devices in a mesh: row: 8 (over y_hi, x), col: 16 (over z, y_lo, core).
Axes of the slice: x: 4, y: 4 (y_hi: 2, y_lo: 2; y = y_hi * 2 + y_lo), z: 4, core: 2. Of those that a mesh axis runs over, the one named last changes fastest.
Arguments:
- normals: float32 [2048, 16384], P('row', 'col'), may hold values from -6 to 6
- factor: float32 [16384, 16384], P('row', 'col'), as said below
- cell_entity: int32 [16384], P('row'), may hold values from 0 to 1023
- scale: float32 [16384], P('row'), may hold values from 0.25 to 2
- volatility: float32 [16384], P('row'), may hold values from 0.1 to 0.6
- retention: int32 [16384], P('row'), may hold values from 1 to 11
- limit: int32 [16384], P('row'), may hold values from 1 to 15
Outputs:
- entity_loss: float32 [2, 2048, 1024], P(None, 'col', 'row')
Inputs may be any that keep to these rules, and one draw needn't show every extreme that they name: factor is zero above the diagonal and one on it.
All inputs are finite; a program needn't handle non-finite values.
Results may differ from a plain program's by a relative error of at most 0.000078.
Values sent between devices are 32-bit elements; how exact they have to be, the bound alone decides.
No kernel may reach another device: no remote copies, remote signals or barrier semaphores. Data moves between devices by JAX's collectives and lax.ppermute only.
A program may use at most 128 MiB of HBM per device.

v0:
```python
import functools

import jax
import jax.numpy as jnp
import numpy as np
from jax import lax
from jax.experimental import pallas as pl
from jax.experimental.pallas import tpu as pltpu
from jax.sharding import PartitionSpec as P


ENT = 1024
CHUNKS = 2
ROWS = 128 // CHUNKS
DEPTH = (768, 640, 640)
DOFF = (0, 768, 1408)
TILE = 256
COLS = (768, 768, 512)
COFF = (0, 768, 1536)
BOTH = ("row", "col")


def unflat(i):
    row, col = divmod(i, 16)
    return row // 4, row % 4, col // 4, col // 2 % 2, col % 2


def flat(yh, x, z, yl, core):
    return (yh * 4 + x) * 16 + z * 4 + yl * 2 + core


def perm(step):
    return [(i, flat(*step(*unflat(i)))) for i in range(128)]


CORE = perm(lambda yh, x, z, yl, c: (yh, x, z, yl, 1 - c))
ROW_DIMS = (
    perm(lambda yh, x, z, yl, c: (yh, x ^ 1, z, yl, c)),
    perm(lambda yh, x, z, yl, c: (yh, 3 - x, z, yl, c)),
    perm(lambda yh, x, z, yl, c: (1 - yh, x, z, yl, c)),
)
COL_DIMS = (
    perm(lambda yh, x, z, yl, c: (yh, x, z ^ 1, yl, c)),
    perm(lambda yh, x, z, yl, c: (yh, x, 3 - z, yl, c)),
    perm(lambda yh, x, z, yl, c: (yh, x, z, 1 - yl, c)),
)


def gray(v):
    return v ^ (v >> 1)


def ungray(v):
    return (v & 2) | ((v ^ (v >> 1)) & 1)


def tables():
    out = np.zeros((128, 3, 2, 4, 3), np.int32)
    for i in range(128):
        yh, x, z, yl, _ = unflat(i)
        here_r, here_c = gray(x) | yh << 2, gray(z) | yl << 2
        e_of_d = {}
        for e in range(8):
            h = here_r ^ e
            source = (h >> 2) * 4 + ungray(h & 3)
            e_of_d[(gray(source >> 1) | (source & 1) << 2) ^ here_c] = e
        for q in range(3):
            for m in range(8):
                bits = [1 - (m >> 2 & 1), 1 - (m >> 1 & 1), 1 - (m & 1)]
                e = e_of_d[sum(b << (q + s) % 3 for s, b in enumerate(bits))]
                for p in range(3):
                    out[i, q, m // 4, m % 4, p] = sum(
                        (e >> (p + s) % 3 & 1) << s for s in range(3)
                    )
    return out.reshape(128, 72)


def permute(x, pairs):
    return lax.ppermute(x, BOTH, pairs)


def split(x):
    high = lax.reduce_precision(x, 8, 7)
    return high.astype(jnp.bfloat16), (x - high).astype(jnp.bfloat16)


def mm_kernel(qs, tbl, *refs):
    blocks, factors = refs[:12], refs[12:16]
    outs, both = refs[16 : 16 + len(qs)], refs[16 + len(qs)]
    fho, flo, fhp, flp = factors
    m = 4 * ROWS
    t = pl.program_id(0)
    first = 0
    starts = []
    for q in qs:
        starts.append(first)
        first += COLS[q] // TILE

    @pl.when(functools.reduce(jnp.logical_or, [t == v for v in starts]))
    def _():
        for i in range(4):
            for p in range(3):
                v = blocks[i * 3 + p][0]
                h = v.astype(jnp.bfloat16)
                cols = pl.ds(DOFF[p], DEPTH[p])
                both[pl.ds(i * ROWS, ROWS), cols] = h
                both[pl.ds(m + i * ROWS, ROWS), cols] = (v - h.astype(jnp.float32)).astype(jnp.bfloat16)

    dot = functools.partial(
        lax.dot_general,
        dimension_numbers=(((1,), (1,)), ((), ())),
        preferred_element_type=jnp.float32,
    )
    own, far, high = pl.ds(0, 1024), pl.ds(1024, 1024), pl.ds(0, m)
    acc = dot(both[:, own], fho[...]) + dot(both[:, far], fhp[...])
    low = dot(both[high, own], flo[...]) + dot(both[high, far], flp[...])
    acc = (acc[:m] + (acc[m:] + low)).reshape(4, ROWS, TILE)
    for k, q in enumerate(qs):
        if len(qs) == 1:
            outs[k][...] = acc
        else:

            @pl.when((t >= starts[k]) & (t < starts[k] + COLS[q] // TILE))
            def _(k=k):
                outs[k][...] = acc


def mm(tbl, gathered, factors, qs):
    sizes = [COLS[q] // TILE for q in qs]
    starts = [sum(sizes[:k]) for k in range(len(qs))]

    def which(t):
        return sum(((t >= v).astype(jnp.int32) for v in starts[1:]), jnp.int32(0))

    specs = [
        pl.BlockSpec((1, ROWS, DEPTH[p]), lambda t, tb, k=i * 3 + p: (tb[which(t) * 12 + k], 0, 0))
        for i in range(4)
        for p in range(3)
    ]
    specs += [pl.BlockSpec((TILE, 1024), lambda t, tb: (COFF[qs[0]] // TILE + t, 0))] * 4
    return pl.pallas_call(
        functools.partial(mm_kernel, qs),
        out_shape=[jax.ShapeDtypeStruct((4, ROWS, COLS[q]), jnp.float32) for q in qs],
        grid_spec=pltpu.PrefetchScalarGridSpec(
            num_scalar_prefetch=1,
            grid=(sum(sizes),),
            in_specs=specs,
            out_specs=[
                pl.BlockSpec(
                    (4, ROWS, TILE),
                    lambda t, tb, k=k: (0, 0, jnp.clip(t - starts[k], 0, sizes[k] - 1)),
                )
                for k in range(len(qs))
            ],
            scratch_shapes=[pltpu.VMEM((8 * ROWS, 2048), jnp.bfloat16)],
        ),
        cost_estimate=pl.CostEstimate(
            flops=2 * 3 * 4 * ROWS * 2048 * sum(sizes) * TILE,
            bytes_accessed=4 * ROWS * 2048 * 4 + sum(sizes) * TILE * (2048 * 4 + 16 * ROWS),
            transcendentals=0,
        ),
        compiler_params=pltpu.CompilerParams(vmem_limit_bytes=32 * 2**20),
    )(tbl, *(gathered * 4), *factors)


def step(normals, factor, cell_entity, scale, volatility, retention, limit):
    row, col = lax.axis_index("row"), lax.axis_index("col")
    core = col & 1
    tbl = lax.dynamic_index_in_dim(jnp.asarray(tables()), row * 16 + col, 0, False).reshape(6, 12)

    given = permute(lax.dynamic_slice_in_dim(normals, (1 - core) * 128, 128, 0), CORE)
    kept = lax.dynamic_slice_in_dim(normals, core * 128, 128, 0)
    factor, given = lax.optimization_barrier((factor, given))
    far_factor = permute(factor, CORE)
    block = jnp.concatenate([kept, given], axis=1)

    gathered = [
        lax.optimization_barrier(
            [block[None, c * ROWS : (c + 1) * ROWS, DOFF[p] : DOFF[p] + DEPTH[p]] for p in range(3)]
        )
        for c in range(CHUNKS)
    ]
    for s in range(3):
        for c in range(CHUNKS):
            came = lax.optimization_barrier([permute(gathered[c][p], ROW_DIMS[(p + s) % 3]) for p in range(3)])
            gathered[c] = [jnp.concatenate([gathered[c][p], came[p]], axis=0) for p in range(3)]

    fho, flo = split(factor)
    norms = jnp.sum(factor * factor, axis=1)
    fhp, flp = split(far_factor)
    far_norms = jnp.sum(far_factor * far_factor, axis=1)
    factors = (fho, flo, fhp, flp)
    norms = norms + far_norms
    for d in range(3):
        norms = norms + permute(norms, COL_DIMS[d])

    inv = lax.rsqrt(norms)[None, :]
    floor_level = 0.25 * retention.astype(jnp.float32)
    cover = 0.25 * limit.astype(jnp.float32)
    onehot = (cell_entity[:, None] == jnp.arange(ENT, dtype=jnp.int32)[None, :]).astype(jnp.float32)
    every = (0, 1, 2)
    send_tbl, keep_tbl = tbl[0::2].reshape(36), tbl[1::2].reshape(36)
    results = []
    for c in range(CHUNKS):
        sent = mm(send_tbl, gathered[c], factors, every)
        came = lax.optimization_barrier([permute(sent[q], COL_DIMS[q]) for q in range(3)])
        kept = mm(keep_tbl, gathered[c], factors, every)
        second = lax.optimization_barrier([permute(kept[q][:2] + came[q][:2], COL_DIMS[(q + 1) % 3]) for q in range(3)])
        held = [kept[q][2:] + came[q][2:] + second[q] for q in range(3)]
        third = [permute(held[q][0], COL_DIMS[(q + 2) % 3]) for q in range(3)]
        mixed = jnp.concatenate([held[q][1] + third[q] for q in range(3)], axis=1)
        if c:
            mixed, _ = lax.optimization_barrier((mixed, sums))
        ground = scale[None, :] * jnp.exp(volatility[None, :] * (mixed * inv))
        ceded = jnp.minimum(jnp.maximum(ground - floor_level[None, :], 0.0), cover[None, :])
        net = ground - ceded
        sums = jnp.einsum("ksc,ce->kse", jnp.stack([net, ceded]), onehot, precision=lax.Precision.HIGH)
        parts = lax.all_to_all(sums, "row", split_axis=2, concat_axis=0, tiled=True)
        results.append(jnp.sum(parts.reshape(8, 2, ROWS, 128), axis=0))
    return jnp.concatenate(results, axis=1)


def solution(mesh):
    return jax.shard_map(
        step,
        mesh=mesh,
        in_specs=(
            P("row", "col"),
            P("row", "col"),
            P("row"),
            P("row"),
            P("row"),
            P("row"),
            P("row"),
        ),
        out_specs=P(None, "col", "row"),
        check_vma=False,
    )
```

profile of v0, /device:TPU:0, one launch (start us, length us, event | category | flops | bytes accessed | tf_op | source)
XLA Modules:
  0.0 224.7 jit_solution(7873691889557929160)
XLA Ops:
  7.3 2.1 collective-permute-start.2
  9.4 3.2 %collective-permute-start.3 = (f32[1,64,640]{2,1,0:T(8,128)S(1)}, f32[1,64,640]{2,1,0:T(8,128)S(1)}, u32[]{:S(2)}, u32[]{:S(2)}) collective-permute-start(f32[1,64,640]{2,1,0:T(8,128)S(1)} %get-tuple-element.59), channel_id=1, source_target_pairs={{0,64},{1,65},{2,66},{3,67},{4,68},{5,69},{6,70},{7,71},{8,72},{9,... | collective-permute-start | bytes 491528 | tf_op jit(solution)/shard_map/ppermute | solution.py:79
  13.2 4.3 %multiply_reduce_fusion.1 = (f32[2048]{0:T(1024)S(1)}, bf16[2048,1024]{1,0:T(8,128)(2,1)S(1)}, bf16[2048,1024]{1,0:T(8,128)(2,1)S(1)}) fusion(f32[2048,1024]{1,0:T(8,128)} %param.9), kind=kLoop, calls=%fused_computation.8 | loop fusion | flops 12580864 | bytes 16785408 | tf_op jit(solution)/shard_map/reduce_sum | solution.py:189
  21.4 4.4 %collective-permute-done.24 = f32[1,64,640]{2,1,0:T(8,128)S(1)} collective-permute-done((f32[1,64,640]{2,1,0:T(8,128)S(1)}, f32[1,64,640]{2,1,0:T(8,128)S(1)}, u32[]{:S(2)}, u32[]{:S(2)}) %collective-permute-start.24) | collective-permute-done | bytes 163872 | tf_op jit(solution)/shard_map/ppermute | solution.py:79
  28.1 6.5 %collective-permute-done.5 = f32[2,64,640]{2,1,0:T(8,128)S(1)} collective-permute-done((f32[2,64,640]{2,1,0:T(8,128)S(1)}, f32[2,64,640]{2,1,0:T(8,128)S(1)}, u32[]{:S(2)}, u32[]{:S(2)}) %collective-permute-start.5) | collective-permute-done | bytes 327712 | tf_op jit(solution)/shard_map/ppermute | solution.py:79
  41.4 3.1 %collective-permute-done.27 = f32[2,64,640]{2,1,0:T(8,128)S(1)} collective-permute-done((f32[2,64,640]{2,1,0:T(8,128)S(1)}, f32[2,64,640]{2,1,0:T(8,128)S(1)}, u32[]{:S(2)}, u32[]{:S(2)}) %collective-permute-start.27) | collective-permute-done | bytes 327712 | tf_op jit(solution)/shard_map/ppermute | solution.py:79
  44.7 4.9 %collective-permute-done.26 = f32[2,64,768]{2,1,0:T(8,128)S(1)} collective-permute-done((f32[2,64,768]{2,1,0:T(8,128)S(1)}, f32[2,64,768]{2,1,0:T(8,128)S(1)}, u32[]{:S(2)}, u32[]{:S(2)}) %collective-permute-start.26) | collective-permute-done | bytes 393248 | tf_op jit(solution)/shard_map/ppermute | solution.py:79
  49.6 2.7 %collective-permute-start.29 = (f32[4,64,768]{2,1,0:T(8,128)S(1)}, f32[4,64,768]{2,1,0:T(8,128)S(1)}, u32[]{:S(2)}, u32[]{:S(2)}) collective-permute-start(f32[4,64,768]{2,1,0:T(8,128)S(1)} %pad_maximum_fusion.1), channel_id=1, source_target_pairs={{0,64},{1,65},{2,66},{3,67},{4,68},{5,69},{6,70},{7,71},{8,72},{9,... | collective-permute-start | bytes 2359304 | tf_op jit(solution)/shard_map/ppermute | solution.py:79
  52.4 6.6 %collective-permute-done.9 = f32[4,64,640]{2,1,0:T(8,128)S(1)} collective-permute-done((f32[4,64,640]{2,1,0:T(8,128)S(1)}, f32[4,64,640]{2,1,0:T(8,128)S(1)}, u32[]{:S(2)}, u32[]{:S(2)}) %collective-permute-start.9) | collective-permute-done | bytes 655392 | tf_op jit(solution)/shard_map/ppermute | solution.py:79
  59.0 2.5 %collective-permute-start.31 = (f32[4,64,640]{2,1,0:T(8,128)S(1)}, f32[4,64,640]{2,1,0:T(8,128)S(1)}, u32[]{:S(2)}, u32[]{:S(2)}) collective-permute-start(f32[4,64,640]{2,1,0:T(8,128)S(1)} %pad_maximum_fusion.5), channel_id=1, source_target_pairs={{0,48},{1,49},{2,50},{3,51},{4,52},{5,53},{6,54},{7,55},{8,56},{9,... | collective-permute-start | bytes 1966088 | tf_op jit(solution)/shard_map/ppermute | solution.py:79
  62.4 4.0 %collective-permute-done.7 = f32[4,64,768]{2,1,0:T(8,128)S(1)} collective-permute-done((f32[4,64,768]{2,1,0:T(8,128)S(1)}, f32[4,64,768]{2,1,0:T(8,128)S(1)}, u32[]{:S(2)}, u32[]{:S(2)}) %collective-permute-start.7) | collective-permute-done | bytes 786464 | tf_op jit(solution)/shard_map/ppermute | solution.py:79
  66.4 4.4 %collective-permute-done.31 = f32[4,64,640]{2,1,0:T(8,128)S(1)} collective-permute-done((f32[4,64,640]{2,1,0:T(8,128)S(1)}, f32[4,64,640]{2,1,0:T(8,128)S(1)}, u32[]{:S(2)}, u32[]{:S(2)}) %collective-permute-start.31) | collective-permute-done | bytes 655392 | tf_op jit(solution)/shard_map/ppermute | solution.py:79
  72.2 4.7 %collective-permute-done.29 = f32[4,64,768]{2,1,0:T(8,128)S(1)} collective-permute-done((f32[4,64,768]{2,1,0:T(8,128)S(1)}, f32[4,64,768]{2,1,0:T(8,128)S(1)}, u32[]{:S(2)}, u32[]{:S(2)}) %collective-permute-start.29) | collective-permute-done | bytes 786464 | tf_op jit(solution)/shard_map/ppermute | solution.py:79
  77.2 5.6 %multiply_reduce_fusion = (f32[2048]{0:T(1024)S(1)}, bf16[2048,1024]{1,0:T(8,128)(2,1)}, bf16[2048,1024]{1,0:T(8,128)(2,1)S(1)}) fusion(f32[2048,1024]{1,0:T(8,128)} %collective-permute-done.10), kind=kLoop, calls=%fused_computation.7 | loop fusion | flops 12580864 | bytes 16785408 | tf_op jit(solution)/shard_map/reduce_sum | solution.py:191
  84.7 11.5 %shard_map.82 = (f32[4,64,768]{2,1,0:T(8,128)S(1)}, f32[4,64,768]{2,1,0:T(8,128)S(1)}, f32[4,64,512]{2,1,0:T(8,128)S(1)}) custom-call(s32[36]{0:T(128)S(1)} %reshape.301.tbl, f32[8,64,768]{2,1,0:T(8,128)S(1)} %constant_dynamic-update-slice_fusion.refs_0_.refs_3_.refs_6_.refs_9_, ...), custom_call_target="tpu_custom_call" | custom-call | flops 6442450944 | bytes 20971520 | tf_op jit(solution)/shard_map/pallas_call | solution.py:141
  96.3 11.6 %shard_map.83 = (f32[4,64,768]{2,1,0:T(8,128)S(1)}, f32[4,64,768]{2,1,0:T(8,128)S(1)}, f32[4,64,512]{2,1,0:T(8,128)S(1)}) custom-call(s32[36]{0:T(128)S(1)} %reshape.302.tbl, f32[8,64,768]{2,1,0:T(8,128)S(1)} %constant_dynamic-update-slice_fusion.refs_0_.refs_3_.refs_6_.refs_9_, ...), custom_call_target="tpu_custom_call" | custom-call | flops 6442450944 | bytes 20971520 | tf_op jit(solution)/shard_map/pallas_call | solution.py:141
  108.0 4.0 %collective-permute-start.12 = (f32[4,64,768]{2,1,0:T(8,128)S(1)}, f32[4,64,768]{2,1,0:T(8,128)S(1)}, u32[]{:S(2)}, u32[]{:S(2)}) collective-permute-start(f32[4,64,768]{2,1,0:T(8,128)S(1)} %get-tuple-element.72), channel_id=1, source_target_pairs={{0,12},{1,13},{2,14},{3,15},{4,8},{5,9},{6,10},{7,11},{8,4},{9,5},... | collective-permute-start | bytes 2359304 | tf_op jit(solution)/shard_map/ppermute | solution.py:79
  112.5 11.6 %shard_map.84 = (f32[4,64,768]{2,1,0:T(8,128)S(1)}, f32[4,64,768]{2,1,0:T(8,128)S(1)}, f32[4,64,512]{2,1,0:T(8,128)S(1)}) custom-call(s32[36]{0:T(128)S(1)} %reshape.301.tbl, f32[8,64,768]{2,1,0:T(8,128)S(1)} %constant_dynamic-update-slice_fusion.12.refs_0_.refs_3_.refs_6_.refs_9_, ...), custom_call_target="tpu_custom_call" | custom-call | flops 6442450944 | bytes 20971520 | tf_op jit(solution)/shard_map/pallas_call | solution.py:141
  125.8 11.6 %shard_map.85 = (f32[4,64,768]{2,1,0:T(8,128)S(1)}, f32[4,64,768]{2,1,0:T(8,128)S(1)}, f32[4,64,512]{2,1,0:T(8,128)S(1)}) custom-call(s32[36]{0:T(128)S(1)} %reshape.302.tbl, f32[8,64,768]{2,1,0:T(8,128)S(1)} %constant_dynamic-update-slice_fusion.12.refs_0_.refs_3_.refs_6_.refs_9_, ...), custom_call_target="tpu_custom_call" | custom-call | flops 6442450944 | bytes 20971520 | tf_op jit(solution)/shard_map/pallas_call | solution.py:141
  137.4 3.3 %collective-permute-start.33 = (f32[4,64,768]{2,1,0:T(8,128)S(1)}, f32[4,64,768]{2,1,0:T(8,128)S(1)}, u32[]{:S(2)}, u32[]{:S(2)}) collective-permute-start(f32[4,64,768]{2,1,0:T(8,128)S(1)} %get-tuple-element.96), channel_id=1, source_target_pairs={{0,12},{1,13},{2,14},{3,15},{4,8},{5,9},{6,10},{7,11},{8,4},{9,5},... | collective-permute-start | bytes 2359304 | tf_op jit(solution)/shard_map/ppermute | solution.py:79
  144.4 10.4 %collective-permute-done.34 = f32[4,64,512]{2,1,0:T(8,128)S(1)} collective-permute-done((f32[4,64,512]{2,1,0:T(8,128)S(1)}, f32[4,64,512]{2,1,0:T(8,128)S(1)}, u32[]{:S(2)}, u32[]{:S(2)}) %collective-permute-start.34) | collective-permute-done | bytes 524320 | tf_op jit(solution)/shard_map/ppermute | solution.py:79
  154.9 3.8 %collective-permute-done.33 = f32[4,64,768]{2,1,0:T(8,128)S(1)} collective-permute-done((f32[4,64,768]{2,1,0:T(8,128)S(1)}, f32[4,64,768]{2,1,0:T(8,128)S(1)}, u32[]{:S(2)}, u32[]{:S(2)}) %collective-permute-start.33) | collective-permute-done | bytes 786464 | tf_op jit(solution)/shard_map/ppermute | solution.py:79
  160.7 3.2 %collective-permute-start.35 = (f32[2,64,768]{2,1,0:T(8,128)S(1)}, f32[2,64,768]{2,1,0:T(8,128)S(1)}, u32[]{:S(2)}, u32[]{:S(2)}) collective-permute-start(f32[2,64,768]{2,1,0:T(8,128)S(1)} %slice_add_fusion.1), channel_id=1, source_target_pairs={{0,12},{1,13},{2,14},{3,15},{4,8},{5,9},{6,10},{7,11},{8,4},{9,5},... | collective-permute-start | bytes 1179656 | tf_op jit(solution)/shard_map/ppermute | solution.py:79
  167.2 2.7 %collective-permute-start.19 = (f32[64,512]{1,0:T(8,128)S(1)}, f32[64,512]{1,0:T(8,128)S(1)}, u32[]{:S(2)}, u32[]{:S(2)}) collective-permute-start(f32[64,512]{1,0:T(8,128)S(1)} %slice_bitcast_fusion.12), channel_id=1, source_target_pairs={{0,12},{1,13},{2,14},{3,15},{4,8},{5,9},{6,10},{7,11},{8,4},{9,5},... | collective-permute-start | bytes 393224 | tf_op jit(solution)/shard_map/ppermute | solution.py:79
  173.4 2.7 %collective-permute-start.40 = (f32[64,512]{1,0:T(8,128)S(1)}, f32[64,512]{1,0:T(8,128)S(1)}, u32[]{:S(2)}, u32[]{:S(2)}) collective-permute-start(f32[64,512]{1,0:T(8,128)S(1)} %slice_bitcast_fusion.10), channel_id=1, source_target_pairs={{0,12},{1,13},{2,14},{3,15},{4,8},{5,9},{6,10},{7,11},{8,4},{9,5},... | collective-permute-start | bytes 393224 | tf_op jit(solution)/shard_map/ppermute | solution.py:79
  176.1 3.6 %collective-permute-done.40 = f32[64,512]{1,0:T(8,128)S(1)} collective-permute-done((f32[64,512]{1,0:T(8,128)S(1)}, f32[64,512]{1,0:T(8,128)S(1)}, u32[]{:S(2)}, u32[]{:S(2)}) %collective-permute-start.40) | collective-permute-done | bytes 131104 | tf_op jit(solution)/shard_map/ppermute | solution.py:79
  180.4 2.4 %fusion.5 = f32[2,64,1024]{2,1,0:T(8,128)S(1)} fusion(s32[2048]{0:T(1024)S(1)} %copy-done.4, f32[1,64,2048]{2,1,0:T(8,128)S(1)} %get-tuple-element.122, f32[1,64,2048]{2,1,0:T(8,128)S(1)} %get-tuple-element.121), kind=kOutput, calls=%fused_computation.11 | convolution fusion | flops 1612972032 | bytes 1581056 | tf_op jit(solution)/shard_map/ksc,ce->kse/dot_general | solution.py:217
  183.1 2.4 %fusion.3 = f32[2,64,1024]{2,1,0:T(8,128)S(1)} fusion(s32[2048]{0:T(1024)S(1)} %copy-done.4, f32[1,64,2048]{2,1,0:T(8,128)S(1)} %get-tuple-element.120, f32[1,64,2048]{2,1,0:T(8,128)S(1)} %get-tuple-element.119), kind=kOutput, calls=%fused_computation.10 | convolution fusion | flops 1612972032 | bytes 1581056 | tf_op jit(solution)/shard_map/ksc,ce->kse/dot_general | solution.py:217
  188.0 5.9 %all-to-all-start.1 = ((f32[8,1,16384]{2,1,0:T(1,128)}), f32[8,1,16384]{2,1,0:T(1,128)S(1)}, u32[]{:S(2)}, u32[]{:S(2)}) async-start(f32[8,1,16384]{2,1,0:T(1,128)} %reshape.311), calls=%async_computation.1 | async-start | bytes 1048576 | tf_op jit(solution)/shard_map/all_to_all | solution.py:218
  196.4 9.8 %all-to-all-done.1 = f32[8,1,16384]{2,1,0:T(1,128)S(1)} async-done(((f32[8,1,16384]{2,1,0:T(1,128)}), f32[8,1,16384]{2,1,0:T(1,128)S(1)}, u32[]{:S(2)}, u32[]{:S(2)}) %all-to-all-start.1) | async-done | bytes 524320 | tf_op jit(solution)/shard_map/all_to_all | solution.py:218
  206.2 3.8 %all-to-all-start = ((f32[8,1,16384]{2,1,0:T(1,128)}), f32[8,1,16384]{2,1,0:T(1,128)S(1)}, u32[]{:S(2)}, u32[]{:S(2)}) async-start(f32[8,1,16384]{2,1,0:T(1,128)} %reshape.313), calls=%async_computation | async-start | bytes 1048576 | tf_op jit(solution)/shard_map/all_to_all | solution.py:218
  213.1 6.7 %all-to-all-done = f32[8,1,16384]{2,1,0:T(1,128)S(1)} async-done(((f32[8,1,16384]{2,1,0:T(1,128)}), f32[8,1,16384]{2,1,0:T(1,128)S(1)}, u32[]{:S(2)}, u32[]{:S(2)}) %all-to-all-start) | async-done | bytes 524320 | tf_op jit(solution)/shard_map/all_to_all | solution.py:218
  (160 shorter events, 54.1 us)
Async XLA Ops:
  3.3 73.9 %collective-permute-start.10 = (f32[2048,1024]{1,0:T(8,128)}, f32[2048,1024]{1,0:T(8,128)}, u32[]{:S(2)}, u32[]{:S(2)}) collective-permute-start(f32[2048,1024]{1,0:T(8,128)} %param.9), channel_id=1, source_target_pairs={{0,1},{1,0},{2,3},{3,2},{4,5},{5,4},{6,7},{7,6},{8,9},{9,8},{10,11... | collective-permute-start | bytes 25165832 | tf_op jit(solution)/shard_map/ppermute | solution.py:79
  5.6 14.4 %collective-permute-start.1 = (f32[1,64,768]{2,1,0:T(8,128)S(1)}, f32[1,64,768]{2,1,0:T(8,128)S(1)}, u32[]{:S(2)}, u32[]{:S(2)}) collective-permute-start(f32[1,64,768]{2,1,0:T(8,128)S(1)} %get-tuple-element.57), channel_id=1, source_target_pairs={{0,16},{1,17},{2,18},{3,19},{4,20},{5,21},{6,22},{7,23},{8,24},{9,... | collective-permute-start | bytes 589832 | tf_op jit(solution)/shard_map/ppermute | solution.py:79
  7.3 10.3 %collective-permute-start.2 = (f32[1,64,640]{2,1,0:T(8,128)S(1)}, f32[1,64,640]{2,1,0:T(8,128)S(1)}, u32[]{:S(2)}, u32[]{:S(2)}) collective-permute-start(f32[1,64,640]{2,1,0:T(8,128)S(1)} %get-tuple-element.58), channel_id=1, source_target_pairs={{0,48},{1,49},{2,50},{3,51},{4,52},{5,53},{6,54},{7,55},{8,56},{9,... | collective-permute-start | bytes 491528 | tf_op jit(solution)/shard_map/ppermute | solution.py:79
  12.6 13.9 %collective-permute-start.23 = (f32[1,64,768]{2,1,0:T(8,128)S(1)}, f32[1,64,768]{2,1,0:T(8,128)S(1)}, u32[]{:S(2)}, u32[]{:S(2)}) collective-permute-start(f32[1,64,768]{2,1,0:T(8,128)S(1)} %get-tuple-element.82), channel_id=1, source_target_pairs={{0,16},{1,17},{2,18},{3,19},{4,20},{5,21},{6,22},{7,23},{8,24},{9,... | collective-permute-start | bytes 589832 | tf_op jit(solution)/shard_map/ppermute | solution.py:79
  20.0 18.2 %collective-permute-start.4 = (f32[2,64,768]{2,1,0:T(8,128)S(1)}, f32[2,64,768]{2,1,0:T(8,128)S(1)}, u32[]{:S(2)}, u32[]{:S(2)}) collective-permute-start(f32[2,64,768]{2,1,0:T(8,128)S(1)} %pad_maximum_fusion.7), channel_id=1, source_target_pairs={{0,48},{1,49},{2,50},{3,51},{4,52},{5,53},{6,54},{7,55},{8,56},{9,... | collective-permute-start | bytes 1179656 | tf_op jit(solution)/shard_map/ppermute | solution.py:79
  25.8 10.6 %collective-permute-start.6 = (f32[2,64,640]{2,1,0:T(8,128)S(1)}, f32[2,64,640]{2,1,0:T(8,128)S(1)}, u32[]{:S(2)}, u32[]{:S(2)}) collective-permute-start(f32[2,64,640]{2,1,0:T(8,128)S(1)} %pad_maximum_fusion.10), channel_id=1, source_target_pairs={{0,16},{1,17},{2,18},{3,19},{4,20},{5,21},{6,22},{7,23},{8,24},{9,... | collective-permute-start | bytes 983048 | tf_op jit(solution)/shard_map/ppermute | solution.py:79
  26.4 14.2 %collective-permute-start.28 = (f32[2,64,640]{2,1,0:T(8,128)S(1)}, f32[2,64,640]{2,1,0:T(8,128)S(1)}, u32[]{:S(2)}, u32[]{:S(2)}) collective-permute-start(f32[2,64,640]{2,1,0:T(8,128)S(1)} %pad_maximum_fusion.12), channel_id=1, source_target_pairs={{0,16},{1,17},{2,18},{3,19},{4,20},{5,21},{6,22},{7,23},{8,24},{9,... | collective-permute-start | bytes 983048 | tf_op jit(solution)/shard_map/ppermute | solution.py:79
  34.6 9.9 %collective-permute-start.27 = (f32[2,64,640]{2,1,0:T(8,128)S(1)}, f32[2,64,640]{2,1,0:T(8,128)S(1)}, u32[]{:S(2)}, u32[]{:S(2)}) collective-permute-start(f32[2,64,640]{2,1,0:T(8,128)S(1)} %pad_maximum_fusion.11), channel_id=1, source_target_pairs={{0,64},{1,65},{2,66},{3,67},{4,68},{5,69},{6,70},{7,71},{8,72},{9,... | collective-permute-start | bytes 983048 | tf_op jit(solution)/shard_map/ppermute | solution.py:79
  36.4 13.2 %collective-permute-start.26 = (f32[2,64,768]{2,1,0:T(8,128)S(1)}, f32[2,64,768]{2,1,0:T(8,128)S(1)}, u32[]{:S(2)}, u32[]{:S(2)}) collective-permute-start(f32[2,64,768]{2,1,0:T(8,128)S(1)} %pad_maximum_fusion.8), channel_id=1, source_target_pairs={{0,48},{1,49},{2,50},{3,51},{4,52},{5,53},{6,54},{7,55},{8,56},{9,... | collective-permute-start | bytes 1179656 | tf_op jit(solution)/shard_map/ppermute | solution.py:79
  38.3 20.7 %collective-permute-start.9 = (f32[4,64,640]{2,1,0:T(8,128)S(1)}, f32[4,64,640]{2,1,0:T(8,128)S(1)}, u32[]{:S(2)}, u32[]{:S(2)}) collective-permute-start(f32[4,64,640]{2,1,0:T(8,128)S(1)} %pad_maximum_fusion.3), channel_id=1, source_target_pairs={{0,48},{1,49},{2,50},{3,51},{4,52},{5,53},{6,54},{7,55},{8,56},{9,... | collective-permute-start | bytes 1966088 | tf_op jit(solution)/shard_map/ppermute | solution.py:79
  40.7 20.9 %collective-permute-start.8 = (f32[4,64,640]{2,1,0:T(8,128)S(1)}, f32[4,64,640]{2,1,0:T(8,128)S(1)}, u32[]{:S(2)}, u32[]{:S(2)}) collective-permute-start(f32[4,64,640]{2,1,0:T(8,128)S(1)} %pad_maximum_fusion.2), channel_id=1, source_target_pairs={{0,16},{1,17},{2,18},{3,19},{4,20},{5,21},{6,22},{7,23},{8,24},{9,... | collective-permute-start | bytes 1966088 | tf_op jit(solution)/shard_map/ppermute | solution.py:79
  44.5 21.9 %collective-permute-start.7 = (f32[4,64,768]{2,1,0:T(8,128)S(1)}, f32[4,64,768]{2,1,0:T(8,128)S(1)}, u32[]{:S(2)}, u32[]{:S(2)}) collective-permute-start(f32[4,64,768]{2,1,0:T(8,128)S(1)} %pad_maximum_fusion), channel_id=1, source_target_pairs={{0,64},{1,65},{2,66},{3,67},{4,68},{5,69},{6,70},{7,71},{8,72},{9,... | collective-permute-start | bytes 2359304 | tf_op jit(solution)/shard_map/ppermute | solution.py:79
  49.6 27.2 %collective-permute-start.29 = (f32[4,64,768]{2,1,0:T(8,128)S(1)}, f32[4,64,768]{2,1,0:T(8,128)S(1)}, u32[]{:S(2)}, u32[]{:S(2)}) collective-permute-start(f32[4,64,768]{2,1,0:T(8,128)S(1)} %pad_maximum_fusion.1), channel_id=1, source_target_pairs={{0,64},{1,65},{2,66},{3,67},{4,68},{5,69},{6,70},{7,71},{8,72},{9,... | collective-permute-start | bytes 2359304 | tf_op jit(solution)/shard_map/ppermute | solution.py:79
  59.0 11.8 %collective-permute-start.31 = (f32[4,64,640]{2,1,0:T(8,128)S(1)}, f32[4,64,640]{2,1,0:T(8,128)S(1)}, u32[]{:S(2)}, u32[]{:S(2)}) collective-permute-start(f32[4,64,640]{2,1,0:T(8,128)S(1)} %pad_maximum_fusion.5), channel_id=1, source_target_pairs={{0,48},{1,49},{2,50},{3,51},{4,52},{5,53},{6,54},{7,55},{8,56},{9,... | collective-permute-start | bytes 1966088 | tf_op jit(solution)/shard_map/ppermute | solution.py:79
  61.6 10.6 %collective-permute-start.30 = (f32[4,64,640]{2,1,0:T(8,128)S(1)}, f32[4,64,640]{2,1,0:T(8,128)S(1)}, u32[]{:S(2)}, u32[]{:S(2)}) collective-permute-start(f32[4,64,640]{2,1,0:T(8,128)S(1)} %pad_maximum_fusion.4), channel_id=1, source_target_pairs={{0,16},{1,17},{2,18},{3,19},{4,20},{5,21},{6,22},{7,23},{8,24},{9,... | collective-permute-start | bytes 1966088 | tf_op jit(solution)/shard_map/ppermute | solution.py:79
  82.8 29.7 %collective-permute-start.20 = (f32[2048]{0:T(1024)S(1)}, f32[2048]{0:T(1024)S(1)}, u32[]{:S(2)}, u32[]{:S(2)}) collective-permute-start(f32[2048]{0:T(1024)S(1)} %add.113), channel_id=1, source_target_pairs={{0,4},{1,5},{2,6},{3,7},{4,0},{5,1},{6,2},{7,3},{8,12},{9,13},{10,... | collective-permute-start | bytes 24584 | tf_op jit(solution)/shard_map/ppermute | solution.py:79
  107.8 33.4 %collective-permute-start.11 = (f32[4,64,768]{2,1,0:T(8,128)S(1)}, f32[4,64,768]{2,1,0:T(8,128)S(1)}, u32[]{:S(2)}, u32[]{:S(2)}) collective-permute-start(f32[4,64,768]{2,1,0:T(8,128)S(1)} %get-tuple-element.71), channel_id=1, source_target_pairs={{0,4},{1,5},{2,6},{3,7},{4,0},{5,1},{6,2},{7,3},{8,12},{9,13},{10,... | collective-permute-start | bytes 2359304 | tf_op jit(solution)/shard_map/ppermute | solution.py:79
  108.0 33.2 %collective-permute-start.12 = (f32[4,64,768]{2,1,0:T(8,128)S(1)}, f32[4,64,768]{2,1,0:T(8,128)S(1)}, u32[]{:S(2)}, u32[]{:S(2)}) collective-permute-start(f32[4,64,768]{2,1,0:T(8,128)S(1)} %get-tuple-element.72), channel_id=1, source_target_pairs={{0,12},{1,13},{2,14},{3,15},{4,8},{5,9},{6,10},{7,11},{8,4},{9,5},... | collective-permute-start | bytes 2359304 | tf_op jit(solution)/shard_map/ppermute | solution.py:79
  112.1 28.6 %collective-permute-start.13 = (f32[4,64,512]{2,1,0:T(8,128)S(1)}, f32[4,64,512]{2,1,0:T(8,128)S(1)}, u32[]{:S(2)}, u32[]{:S(2)}) collective-permute-start(f32[4,64,512]{2,1,0:T(8,128)S(1)} %get-tuple-element.73), channel_id=1, source_target_pairs={{0,2},{1,3},{2,0},{3,1},{4,6},{5,7},{6,4},{7,5},{8,10},{9,11},{10,... | collective-permute-start | bytes 1572872 | tf_op jit(solution)/shard_map/ppermute | solution.py:79
  112.5 11.6 %collective-permute-start.21 = (f32[2048]{0:T(1024)S(1)}, f32[2048]{0:T(1024)S(1)}, u32[]{:S(2)}, u32[]{:S(2)}) collective-permute-start(f32[2048]{0:T(1024)S(1)} %add.114), channel_id=1, source_target_pairs={{0,12},{1,13},{2,14},{3,15},{4,8},{5,9},{6,10},{7,11},{8,4},{9,5},... | collective-permute-start | bytes 24584 | tf_op jit(solution)/shard_map/ppermute | solution.py:79
  124.1 13.3 %collective-permute-start.22 = (f32[2048]{0:T(1024)S(1)}, f32[2048]{0:T(1024)S(1)}, u32[]{:S(2)}, u32[]{:S(2)}) collective-permute-start(f32[2048]{0:T(1024)S(1)} %add.115), channel_id=1, source_target_pairs={{0,2},{1,3},{2,0},{3,1},{4,6},{5,7},{6,4},{7,5},{8,10},{9,11},{10,... | collective-permute-start | bytes 24584 | tf_op jit(solution)/shard_map/ppermute | solution.py:79
  137.3 17.5 %collective-permute-start.32 = (f32[4,64,768]{2,1,0:T(8,128)S(1)}, f32[4,64,768]{2,1,0:T(8,128)S(1)}, u32[]{:S(2)}, u32[]{:S(2)}) collective-permute-start(f32[4,64,768]{2,1,0:T(8,128)S(1)} %get-tuple-element.95), channel_id=1, source_target_pairs={{0,4},{1,5},{2,6},{3,7},{4,0},{5,1},{6,2},{7,3},{8,12},{9,13},{10,... | collective-permute-start | bytes 2359304 | tf_op jit(solution)/shard_map/ppermute | solution.py:79
  137.4 21.2 %collective-permute-start.33 = (f32[4,64,768]{2,1,0:T(8,128)S(1)}, f32[4,64,768]{2,1,0:T(8,128)S(1)}, u32[]{:S(2)}, u32[]{:S(2)}) collective-permute-start(f32[4,64,768]{2,1,0:T(8,128)S(1)} %get-tuple-element.96), channel_id=1, source_target_pairs={{0,12},{1,13},{2,14},{3,15},{4,8},{5,9},{6,10},{7,11},{8,4},{9,5},... | collective-permute-start | bytes 2359304 | tf_op jit(solution)/shard_map/ppermute | solution.py:79
  140.7 14.1 %collective-permute-start.34 = (f32[4,64,512]{2,1,0:T(8,128)S(1)}, f32[4,64,512]{2,1,0:T(8,128)S(1)}, u32[]{:S(2)}, u32[]{:S(2)}) collective-permute-start(f32[4,64,512]{2,1,0:T(8,128)S(1)} %get-tuple-element.97), channel_id=1, source_target_pairs={{0,2},{1,3},{2,0},{3,1},{4,6},{5,7},{6,4},{7,5},{8,10},{9,11},{10,... | collective-permute-start | bytes 1572872 | tf_op jit(solution)/shard_map/ppermute | solution.py:79
  141.3 19.4 %collective-permute-start.16 = (f32[2,64,512]{2,1,0:T(8,128)S(1)}, f32[2,64,512]{2,1,0:T(8,128)S(1)}, u32[]{:S(2)}, u32[]{:S(2)}) collective-permute-start(f32[2,64,512]{2,1,0:T(8,128)S(1)} %slice_add_fusion.5), channel_id=1, source_target_pairs={{0,4},{1,5},{2,6},{3,7},{4,0},{5,1},{6,2},{7,3},{8,12},{9,13},{10,... | collective-permute-start | bytes 786440 | tf_op jit(solution)/shard_map/ppermute | solution.py:79
  142.7 21.1 %collective-permute-start.15 = (f32[2,64,768]{2,1,0:T(8,128)S(1)}, f32[2,64,768]{2,1,0:T(8,128)S(1)}, u32[]{:S(2)}, u32[]{:S(2)}) collective-permute-start(f32[2,64,768]{2,1,0:T(8,128)S(1)} %slice_add_fusion.2), channel_id=1, source_target_pairs={{0,2},{1,3},{2,0},{3,1},{4,6},{5,7},{6,4},{7,5},{8,10},{9,11},{10,... | collective-permute-start | bytes 1179656 | tf_op jit(solution)/shard_map/ppermute | solution.py:79
  154.8 9.9 %collective-permute-start.14 = (f32[2,64,768]{2,1,0:T(8,128)S(1)}, f32[2,64,768]{2,1,0:T(8,128)S(1)}, u32[]{:S(2)}, u32[]{:S(2)}) collective-permute-start(f32[2,64,768]{2,1,0:T(8,128)S(1)} %slice_add_fusion.3), channel_id=1, source_target_pairs={{0,12},{1,13},{2,14},{3,15},{4,8},{5,9},{6,10},{7,11},{8,4},{9,5},... | collective-permute-start | bytes 1179656 | tf_op jit(solution)/shard_map/ppermute | solution.py:79
  160.7 10.5 %collective-permute-start.35 = (f32[2,64,768]{2,1,0:T(8,128)S(1)}, f32[2,64,768]{2,1,0:T(8,128)S(1)}, u32[]{:S(2)}, u32[]{:S(2)}) collective-permute-start(f32[2,64,768]{2,1,0:T(8,128)S(1)} %slice_add_fusion.1), channel_id=1, source_target_pairs={{0,12},{1,13},{2,14},{3,15},{4,8},{5,9},{6,10},{7,11},{8,4},{9,5},... | collective-permute-start | bytes 1179656 | tf_op jit(solution)/shard_map/ppermute | solution.py:79
  164.8 14.9 %collective-permute-start.17 = (f32[64,768]{1,0:T(8,128)S(1)}, f32[64,768]{1,0:T(8,128)S(1)}, u32[]{:S(2)}, u32[]{:S(2)}) collective-permute-start(f32[64,768]{1,0:T(8,128)S(1)} %slice_bitcast_fusion.6), channel_id=1, source_target_pairs={{0,2},{1,3},{2,0},{3,1},{4,6},{5,7},{6,4},{7,5},{8,10},{9,11},{10,... | collective-permute-start | bytes 589832 | tf_op jit(solution)/shard_map/ppermute | solution.py:79
  165.7 14.1 %collective-permute-start.18 = (f32[64,768]{1,0:T(8,128)S(1)}, f32[64,768]{1,0:T(8,128)S(1)}, u32[]{:S(2)}, u32[]{:S(2)}) collective-permute-start(f32[64,768]{1,0:T(8,128)S(1)} %slice_bitcast_fusion.4), channel_id=1, source_target_pairs={{0,4},{1,5},{2,6},{3,7},{4,0},{5,1},{6,2},{7,3},{8,12},{9,13},{10,... | collective-permute-start | bytes 589832 | tf_op jit(solution)/shard_map/ppermute | solution.py:79
  188.0 18.2 %all-to-all-start.1 = ((f32[8,1,16384]{2,1,0:T(1,128)}), f32[8,1,16384]{2,1,0:T(1,128)S(1)}, u32[]{:S(2)}, u32[]{:S(2)}) async-start(f32[8,1,16384]{2,1,0:T(1,128)} %reshape.311), calls=%async_computation.1 | async-start | bytes 1048576 | tf_op jit(solution)/shard_map/all_to_all | solution.py:218
  206.2 13.6 %all-to-all-start = ((f32[8,1,16384]{2,1,0:T(1,128)}), f32[8,1,16384]{2,1,0:T(1,128)S(1)}, u32[]{:S(2)}, u32[]{:S(2)}) async-start(f32[8,1,16384]{2,1,0:T(1,128)} %reshape.313), calls=%async_computation | async-start | bytes 1048576 | tf_op jit(solution)/shard_map/all_to_all | solution.py:218
  (16 other events, 110.2 us)
where the time goes:
time: 225 us
  waiting for transfers between devices  81.6 us (36%)
  starting transfers between devices  62.5 us (28%)
  Pallas kernels  46.2 us (21%)
  other arithmetic  16.7 us (7%)
  local copies, waits for them, and re-layouts  12.1 us (5%)
  matrix products  4.82 us (2%)
    ppermute x41, waiting for transfers between devices, permute(): return lax.ppermute(x, BOTH, pairs)  65.1 us
    ppermute x41, starting transfers between devices, permute(): return lax.ppermute(x, BOTH, pairs)  52.8 us
    pallas_call x4, Pallas kernels, mm(): pl.pallas_call(functools.partial(mm_kernel, qs), out_shape=[jax.ShapeDtyp...  46.2 us
    all_to_all x2, waiting for transfers between devices, step(): parts = lax.all_to_all(sums, 'row', split_axis=2, concat_axis=0, tiled=True)  16.5 us
    all_to_all x2, starting transfers between devices, step(): parts = lax.all_to_all(sums, 'row', split_axis=2, concat_axis=0, tiled=True)  9.69 us
    unnamed x30, local copies, waits for them, and re-layouts  6.02 us
    reduce_sum x1, other arithmetic, step(): far_norms = jnp.sum(far_factor * far_factor, axis=1)  5.56 us
    dot_general x2, matrix products, step(): jnp.einsum('ksc,ce->kse', jnp.stack([net, ceded]), onehot, precision=lax....  4.82 us
  transfers between devices with their start and end apart: 43, of which 21 were waited for; matrix products, arithmetic and copies ran while one was open for 7% of the time, Pallas kernels for 21%

commit v1 on v0

v1 whole, which is shorter than its diff:
```python
import functools

import jax
import jax.numpy as jnp
import numpy as np
from jax import lax
from jax.experimental import pallas as pl
from jax.experimental.pallas import tpu as pltpu
from jax.sharding import PartitionSpec as P


ENT = 1024
CHUNKS = 2
ROWS = 128 // CHUNKS
DEPTH = (768, 640, 640)
DOFF = (0, 768, 1408)
TILE = 256
COLS = (768, 768, 512)
COFF = (0, 768, 1536)
BOTH = ("row", "col")


def unflat(i):
    row, col = divmod(i, 16)
    return row // 4, row % 4, col // 4, col // 2 % 2, col % 2


def flat(yh, x, z, yl, core):
    return (yh * 4 + x) * 16 + z * 4 + yl * 2 + core


def perm(step):
    return [(i, flat(*step(*unflat(i)))) for i in range(128)]


CORE = perm(lambda yh, x, z, yl, c: (yh, x, z, yl, 1 - c))
ROW_DIMS = (
    perm(lambda yh, x, z, yl, c: (yh, x ^ 1, z, yl, c)),
    perm(lambda yh, x, z, yl, c: (yh, 3 - x, z, yl, c)),
    perm(lambda yh, x, z, yl, c: (1 - yh, x, z, yl, c)),
)
COL_DIMS = (
    perm(lambda yh, x, z, yl, c: (yh, x, z ^ 1, yl, c)),
    perm(lambda yh, x, z, yl, c: (yh, x, 3 - z, yl, c)),
    perm(lambda yh, x, z, yl, c: (yh, x, z, 1 - yl, c)),
)


def gray(v):
    return v ^ (v >> 1)


def ungray(v):
    return (v & 2) | ((v ^ (v >> 1)) & 1)


def place(e, p):
    return sum((e >> (p + s) % 3 & 1) << s for s in range(3))


def tables():
    out = np.zeros((128, 3, 8), np.int32)
    for i in range(128):
        yh, x, z, yl, _ = unflat(i)
        here_r, here_c = gray(x) | yh << 2, gray(z) | yl << 2
        for e in range(8):
            h = here_r ^ e
            source = (h >> 2) * 4 + ungray(h & 3)
            d = (gray(source >> 1) | (source & 1) << 2) ^ here_c
            for q in range(3):
                out[i, q, e] = 7 - sum((d >> (q + s) % 3 & 1) << 2 - s for s in range(3))
    return out.reshape(128, 24)


def permute(x, pairs):
    return lax.ppermute(x, BOTH, pairs)


def split(x):
    high = lax.reduce_precision(x, 8, 7)
    return high.astype(jnp.bfloat16), (x - high).astype(jnp.bfloat16)


STARTS = tuple(c // TILE for c in COFF)
SIZES = tuple(c // TILE for c in COLS)


def mm_kernel(tbl, *refs):
    first, last, (fho, flo, fhp, flp) = refs[:3], refs[3:6], refs[6:10]
    outs, both = refs[10:16], refs[16]
    m = 8 * ROWS
    t = pl.program_id(0)

    @pl.when(t == 0)
    def _():
        for e in range(8):
            for p in range(3):
                at = place(e, p)
                v = (last if at > 3 else first)[p][at & 3]
                h = v.astype(jnp.bfloat16)
                cols = pl.ds(DOFF[p], DEPTH[p])
                both[pl.ds(e * ROWS, ROWS), cols] = h
                both[pl.ds(m + e * ROWS, ROWS), cols] = (v - h.astype(jnp.float32)).astype(jnp.bfloat16)

    dot = functools.partial(
        lax.dot_general,
        dimension_numbers=(((1,), (1,)), ((), ())),
        preferred_element_type=jnp.float32,
    )
    own, far, high = pl.ds(0, 1024), pl.ds(1024, 1024), pl.ds(0, m)
    acc = dot(both[:, own], fho[...]) + dot(both[:, far], fhp[...])
    low = dot(both[high, own], flo[...]) + dot(both[high, far], flp[...])
    acc = acc[:m] + (acc[m:] + low)
    for q in range(3):

        @pl.when((t >= STARTS[q]) & (t < STARTS[q] + SIZES[q]))
        def _(q=q):
            for e in range(8):
                slot = tbl[q * 8 + e]
                v = acc[e * ROWS : (e + 1) * ROWS]

                @pl.when(slot < 4)
                def _():
                    outs[q][slot] = v

                @pl.when(slot > 3)
                def _():
                    outs[3 + q][slot - 4] = v


def mm(tbl, first, last, factors):
    whole = pl.BlockSpec(memory_space=pltpu.VMEM)
    outs = [
        pl.BlockSpec(
            (4, ROWS, TILE), lambda t, tb, q=q: (0, 0, jnp.clip(t - STARTS[q], 0, SIZES[q] - 1))
        )
        for q in range(3)
    ]
    res = pl.pallas_call(
        mm_kernel,
        out_shape=[jax.ShapeDtypeStruct((4, ROWS, COLS[q]), jnp.float32) for q in range(3)] * 2,
        grid_spec=pltpu.PrefetchScalarGridSpec(
            num_scalar_prefetch=1,
            grid=(2048 // TILE,),
            in_specs=[whole] * 6 + [pl.BlockSpec((TILE, 1024), lambda t, tb: (t, 0))] * 4,
            out_specs=outs * 2,
            scratch_shapes=[pltpu.VMEM((16 * ROWS, 2048), jnp.bfloat16)],
        ),
        cost_estimate=pl.CostEstimate(
            flops=2 * 3 * 8 * ROWS * 2048 * 2048,
            bytes_accessed=2 * 8 * ROWS * 2048 * 4 + 4 * 2048 * 2048,
            transcendentals=0,
        ),
        compiler_params=pltpu.CompilerParams(vmem_limit_bytes=28 * 2**20),
    )(tbl, *first, *last, *factors)
    return res[:3], res[3:]


def tail_kernel(*refs):
    pieces, (cells, out, both) = refs[:12], refs[12:]
    for q in range(3):
        cols = pl.ds(COFF[q], COLS[q])
        kept, came, second, third = pieces[q::3]
        mixed = kept[0] + came[0] + second[0] + third[0]
        inv, scale, vol, floor, cover = (cells[pl.ds(k, 1), cols] for k in range(5))
        ground = scale * jnp.exp(vol * (mixed * inv))
        ceded = jnp.minimum(jnp.maximum(ground - floor, 0.0), cover)
        for k, v in enumerate((ground - ceded, ceded)):
            h = v.astype(jnp.bfloat16)
            both[pl.ds(k * ROWS, ROWS), cols] = h
            both[pl.ds((2 + k) * ROWS, ROWS), cols] = (v - h.astype(jnp.float32)).astype(jnp.bfloat16)
    entity = cells[pl.ds(5, 1), :].astype(jnp.int32)
    for g in range(8):
        lines = lax.broadcasted_iota(jnp.int32, (128, 2048), 0) + g * 128
        onehot = jnp.where(lines == entity, 1.0, 0.0).astype(jnp.bfloat16)
        sums = lax.dot_general(
            both[...], onehot, (((1,), (1,)), ((), ())), preferred_element_type=jnp.float32
        )
        out[g] = sums[: 2 * ROWS] + sums[2 * ROWS :]


def tail(kept, came, second, third, cells):
    def block(at):
        return [pl.BlockSpec((1, ROWS, COLS[q]), lambda i: (at, 0, 0)) for q in range(3)]

    return pl.pallas_call(
        tail_kernel,
        out_shape=jax.ShapeDtypeStruct((8, 2 * ROWS, 128), jnp.float32),
        grid=(1,),
        in_specs=block(3) + block(3) + block(1) + block(0) + [pl.BlockSpec((6, 2048), lambda i: (0, 0))],
        out_specs=pl.BlockSpec((8, 2 * ROWS, 128), lambda i: (0, 0, 0)),
        scratch_shapes=[pltpu.VMEM((4 * ROWS, 2048), jnp.bfloat16)],
        cost_estimate=pl.CostEstimate(
            flops=2 * 4 * ROWS * 2048 * ENT, bytes_accessed=5 * ROWS * 2048 * 4, transcendentals=ROWS * 2048
        ),
        compiler_params=pltpu.CompilerParams(vmem_limit_bytes=16 * 2**20),
    )(*kept, *came, *second, *third, cells)


def step(normals, factor, cell_entity, scale, volatility, retention, limit):
    row, col = lax.axis_index("row"), lax.axis_index("col")
    core = col & 1
    tbl = lax.dynamic_index_in_dim(jnp.asarray(tables()), row * 16 + col, 0, False)

    given = permute(lax.dynamic_slice_in_dim(normals, (1 - core) * 128, 128, 0), CORE)
    kept = lax.dynamic_slice_in_dim(normals, core * 128, 128, 0)
    factor, given = lax.optimization_barrier((factor, given))
    far_factor = permute(factor, CORE)
    block = jnp.concatenate([kept, given], axis=1)

    gathered = [
        lax.optimization_barrier(
            [block[None, c * ROWS : (c + 1) * ROWS, DOFF[p] : DOFF[p] + DEPTH[p]] for p in range(3)]
        )
        for c in range(CHUNKS)
    ]
    last = []
    for s in range(3):
        for c in range(CHUNKS):
            came = lax.optimization_barrier([permute(gathered[c][p], ROW_DIMS[(p + s) % 3]) for p in range(3)])
            if s == 2:
                last.append(came)
                continue
            gathered[c] = [jnp.concatenate([gathered[c][p], came[p]], axis=0) for p in range(3)]

    fho, flo = split(factor)
    norms = jnp.sum(factor * factor, axis=1)
    fhp, flp = split(far_factor)
    far_norms = jnp.sum(far_factor * far_factor, axis=1)
    factors = (fho, flo, fhp, flp)
    norms = norms + far_norms
    for d in range(3):
        norms = norms + permute(norms, COL_DIMS[d])

    cells = jnp.stack(
        [
            lax.rsqrt(norms),
            scale,
            volatility,
            0.25 * retention.astype(jnp.float32),
            0.25 * limit.astype(jnp.float32),
            cell_entity.astype(jnp.float32),
        ]
    )
    results = []
    for c in range(CHUNKS):
        sent, kept = mm(tbl, gathered[c], last[c], factors)
        came = lax.optimization_barrier([permute(sent[q], COL_DIMS[q]) for q in range(3)])
        second = lax.optimization_barrier([permute(kept[q][:2] + came[q][:2], COL_DIMS[(q + 1) % 3]) for q in range(3)])
        third = lax.optimization_barrier(
            [permute(kept[q][2:3] + came[q][2:3] + second[q][:1], COL_DIMS[(q + 2) % 3]) for q in range(3)]
        )
        sums = tail(kept, came, second, third, cells)
        parts = lax.all_to_all(sums, "row", split_axis=0, concat_axis=0, tiled=True)
        results.append(jnp.sum(parts, axis=0).reshape(2, ROWS, 128))
    return jnp.concatenate(results, axis=1)


def solution(mesh):
    return jax.shard_map(
        step,
        mesh=mesh,
        in_specs=(
            P("row", "col"),
            P("row", "col"),
            P("row"),
            P("row"),
            P("row"),
            P("row"),
            P("row"),
        ),
        out_specs=P(None, "col", "row"),
        check_vma=False,
    )
```

time: 225 us -> 210 us (0.933)
  waiting for transfers between devices: 81.6 us -> 65.3 us
  other arithmetic: 16.7 us -> 24.5 us
  matrix products: 4.82 us -> 0 us
    ppermute x41, waiting for transfers between devices: 65.1 us -> 55.1 us  [permute(): return lax.ppermute(x, BOTH, pairs)]
    add x9 -> x6, other arithmetic: 0.42 us -> 7.41 us  [step(): kept[q][2:3] + came[q][2:3] + second[q][:1]]
    all_to_all x2, waiting for transfers between devices: 16.5 us -> 10.2 us  [step(): parts = lax.all_to_all(sums, 'row', split_axis=0, concat_axis=0, tiled=True)]
    add x6, other arithmetic: 0.25 us -> 6.21 us  [step(): kept[q][:2] + came[q][:2]]
    dot_general x2 -> x0, matrix products: 4.82 us -> none  [step(): jnp.einsum('ksc,ce->kse', jnp.stack([net, ceded]), onehot, precision=lax....]
    all_to_all x2 -> x0, other arithmetic: 3.77 us -> none  [step(): parts = lax.all_to_all(sums, 'row', split_axis=2, concat_axis=0, tiled=True)]
    all_to_all x2, starting transfers between devices: 9.69 us -> 12.2 us  [step(): parts = lax.all_to_all(sums, 'row', split_axis=0, concat_axis=0, tiled=True)]
    ppermute x41, starting transfers between devices: 52.8 us -> 50.4 us  [permute(): return lax.ppermute(x, BOTH, pairs)]
  transfers between devices with their start and end apart: 43 -> 43, of which waited for: 21 -> 15; matrix products, arithmetic and copies ran while one was open for 7% -> 13% of each run, Pallas kernels for 21% -> 21%
where the time goes in v1:
time: 210 us; the launch traced here: 209 us
  waiting for transfers between devices  65.3 us (31%)
  starting transfers between devices  62.7 us (30%)
  Pallas kernels  44.4 us (21%)
  other arithmetic  24.5 us (12%)
  local copies, waits for them, and re-layouts  12.1 us (6%)
    ppermute x41, waiting for transfers between devices, permute(): return lax.ppermute(x, BOTH, pairs)  55.1 us
    ppermute x41, starting transfers between devices, permute(): return lax.ppermute(x, BOTH, pairs)  50.4 us
    pallas_call x2, Pallas kernels, mm(): pl.pallas_call(mm_kernel, out_shape=[jax.ShapeDtypeStruct((4, ROWS, COLS[...  36.6 us
    all_to_all x2, starting transfers between devices, step(): parts = lax.all_to_all(sums, 'row', split_axis=0, concat_axis=0, tiled=True)  12.2 us
    all_to_all x2, waiting for transfers between devices, step(): parts = lax.all_to_all(sums, 'row', split_axis=0, concat_axis=0, tiled=True)  10.2 us
    unnamed x44, local copies, waits for them, and re-layouts  8.24 us
    pallas_call x2, Pallas kernels, tail(): pl.pallas_call(tail_kernel, out_shape=jax.ShapeDtypeStruct((8, 2 * ROWS,...  7.81 us
    add x6, other arithmetic, step(): kept[q][2:3] + came[q][2:3] + second[q][:1]  7.41 us
  transfers between devices with their start and end apart: 43, of which 15 were waited for; matrix products, arithmetic and copies ran while one was open for 13% of the time, Pallas kernels for 21%

profile of v1, /device:TPU:0, one launch (start us, length us, event | category | flops | bytes accessed | tf_op | source)
XLA Modules:
  0.0 209.4 jit_solution(17186938568941047914)
XLA Ops:
  1.4 1.9 collective-permute-done
  7.6 2.1 %collective-permute-start.2 = (f32[1,64,640]{2,1,0:T(8,128)S(1)}, f32[1,64,640]{2,1,0:T(8,128)S(1)}, u32[]{:S(2)}, u32[]{:S(2)}) collective-permute-start(f32[1,64,640]{2,1,0:T(8,128)S(1)} %get-tuple-element.63), channel_id=1, source_target_pairs={{0,48},{1,49},{2,50},{3,51},{4,52},{5,53},{6,54},{7,55},{8,56},{9,... | collective-permute-start | bytes 491528 | tf_op jit(solution)/shard_map/ppermute | solution.py:76
  9.7 3.2 %collective-permute-start.3 = (f32[1,64,640]{2,1,0:T(8,128)S(1)}, f32[1,64,640]{2,1,0:T(8,128)S(1)}, u32[]{:S(2)}, u32[]{:S(2)}) collective-permute-start(f32[1,64,640]{2,1,0:T(8,128)S(1)} %get-tuple-element.64), channel_id=1, source_target_pairs={{0,64},{1,65},{2,66},{3,67},{4,68},{5,69},{6,70},{7,71},{8,72},{9,... | collective-permute-start | bytes 491528 | tf_op jit(solution)/shard_map/ppermute | solution.py:76
  13.5 4.3 %multiply_reduce_fusion.1 = (f32[2048]{0:T(1024)S(1)}, bf16[2048,1024]{1,0:T(8,128)(2,1)S(1)}, bf16[2048,1024]{1,0:T(8,128)(2,1)S(1)}) fusion(f32[2048,1024]{1,0:T(8,128)} %param.9), kind=kLoop, calls=%fused_computation.7 | loop fusion | flops 12580864 | bytes 16785408 | tf_op jit(solution)/shard_map/reduce_sum | solution.py:227
  21.7 4.4 %collective-permute-done.24 = f32[1,64,640]{2,1,0:T(8,128)S(1)} collective-permute-done((f32[1,64,640]{2,1,0:T(8,128)S(1)}, f32[1,64,640]{2,1,0:T(8,128)S(1)}, u32[]{:S(2)}, u32[]{:S(2)}) %collective-permute-start.24) | collective-permute-done | bytes 163872 | tf_op jit(solution)/shard_map/ppermute | solution.py:76
  28.5 6.5 %collective-permute-done.5 = f32[2,64,640]{2,1,0:T(8,128)S(1)} collective-permute-done((f32[2,64,640]{2,1,0:T(8,128)S(1)}, f32[2,64,640]{2,1,0:T(8,128)S(1)}, u32[]{:S(2)}, u32[]{:S(2)}) %collective-permute-start.5) | collective-permute-done | bytes 327712 | tf_op jit(solution)/shard_map/ppermute | solution.py:76
  35.0 1.8 collective-permute-done.6
  36.7 1.9 collective-permute-start.26
  41.7 3.3 %collective-permute-done.27 = f32[2,64,640]{2,1,0:T(8,128)S(1)} collective-permute-done((f32[2,64,640]{2,1,0:T(8,128)S(1)}, f32[2,64,640]{2,1,0:T(8,128)S(1)}, u32[]{:S(2)}, u32[]{:S(2)}) %collective-permute-start.27) | collective-permute-done | bytes 327712 | tf_op jit(solution)/shard_map/ppermute | solution.py:76
  45.0 5.0 %collective-permute-done.26 = f32[2,64,768]{2,1,0:T(8,128)S(1)} collective-permute-done((f32[2,64,768]{2,1,0:T(8,128)S(1)}, f32[2,64,768]{2,1,0:T(8,128)S(1)}, u32[]{:S(2)}, u32[]{:S(2)}) %collective-permute-start.26) | collective-permute-done | bytes 393248 | tf_op jit(solution)/shard_map/ppermute | solution.py:76
  50.0 2.7 %collective-permute-start.29 = (f32[4,64,768]{2,1,0:T(8,128)S(1)}, f32[4,64,768]{2,1,0:T(8,128)S(1)}, u32[]{:S(2)}, u32[]{:S(2)}) collective-permute-start(f32[4,64,768]{2,1,0:T(8,128)S(1)} %constant_dynamic-update-slice_fusion.9.refs_0_), channel_id=1, source_target_pairs={{0,64},{1,65},{2,66},{3,67},{4,68},{5,69},{6,70},{7,71},{8,72},{9,... | collective-permute-start | bytes 2359304 | tf_op jit(solution)/shard_map/ppermute | solution.py:76
  52.7 6.7 %collective-permute-done.9.refs_5_ = f32[4,64,640]{2,1,0:T(8,128)S(1)} collective-permute-done((f32[4,64,640]{2,1,0:T(8,128)S(1)}, f32[4,64,640]{2,1,0:T(8,128)S(1)}, u32[]{:S(2)}, u32[]{:S(2)}) %collective-permute-start.9) | collective-permute-done | bytes 655392 | tf_op jit(solution)/shard_map/ppermute | solution.py:76
  59.4 2.6 %collective-permute-start.31 = (f32[4,64,640]{2,1,0:T(8,128)S(1)}, f32[4,64,640]{2,1,0:T(8,128)S(1)}, u32[]{:S(2)}, u32[]{:S(2)}) collective-permute-start(f32[4,64,640]{2,1,0:T(8,128)S(1)} %constant_dynamic-update-slice_fusion.15.refs_2_), channel_id=1, source_target_pairs={{0,48},{1,49},{2,50},{3,51},{4,52},{5,53},{6,54},{7,55},{8,56},{9,... | collective-permute-start | bytes 1966088 | tf_op jit(solution)/shard_map/ppermute | solution.py:76
  62.5 4.3 %multiply_reduce_fusion = (f32[2048]{0:T(1024)S(1)}, bf16[2048,1024]{1,0:T(8,128)(2,1)S(1)}, bf16[2048,1024]{1,0:T(8,128)(2,1)S(1)}) fusion(f32[2048,1024]{1,0:T(8,128)} %collective-permute-done.10), kind=kLoop, calls=%fused_computation.6 | loop fusion | flops 12580864 | bytes 16785408 | tf_op jit(solution)/shard_map/reduce_sum | solution.py:229
  66.8 2.0 collective-permute-start.20
  72.5 4.7 %collective-permute-done.29.refs_3_ = f32[4,64,768]{2,1,0:T(8,128)S(1)} collective-permute-done((f32[4,64,768]{2,1,0:T(8,128)S(1)}, f32[4,64,768]{2,1,0:T(8,128)S(1)}, u32[]{:S(2)}, u32[]{:S(2)}) %collective-permute-start.29) | collective-permute-done | bytes 786464 | tf_op jit(solution)/shard_map/ppermute | solution.py:76
  77.3 4.0 %collective-permute-start.21 = (f32[2048]{0:T(1024)S(1)}, f32[2048]{0:T(1024)S(1)}, u32[]{:S(2)}, u32[]{:S(2)}) collective-permute-start(f32[2048]{0:T(1024)S(1)} %add.93), channel_id=1, source_target_pairs={{0,12},{1,13},{2,14},{3,15},{4,8},{5,9},{6,10},{7,11},{8,4},{9,5},... | collective-permute-start | bytes 24584 | tf_op jit(solution)/shard_map/ppermute | solution.py:76
  81.3 18.3 %shard_map.82 = (f32[4,64,768]{2,1,0:T(8,128)}, f32[4,64,768]{2,1,0:T(8,128)}, f32[4,64,512]{2,1,0:T(8,128)}, f32[4,64,768]{2,1,0:T(8,128)S(1)}, f32[4,64,768]{2,1,0:T(8,128)S(1)}, /*index=5*/f32[4,64,512]{2,1,0:T(8,128)S(1)}) custom-call(s32[24]{0:T(128)S(1)} %fusion.3.tbl, f32[4,64,768]{2,1,0:T(8,128)S(1)} %constant_dynamic-update-slice_fusion.refs_0_, ...), custom_call_target="tpu_custom_call" | custom-call | flops 12884901888 | bytes 25165824 | tf_op jit(solution)/shard_map/pallas_call | solution.py:139
  101.4 1.9 collective-permute-start.22
  103.3 18.3 %shard_map.84 = (f32[4,64,768]{2,1,0:T(8,128)}, f32[4,64,768]{2,1,0:T(8,128)}, f32[4,64,512]{2,1,0:T(8,128)S(1)}, f32[4,64,768]{2,1,0:T(8,128)S(1)}, f32[4,64,76...) custom-call(s32[24]{0:T(128)S(1)} %fusion.3.tbl, f32[4,64,768]{2,1,0:T(8,128)S(1)} %constant_dynamic-update-slice_fusion.9.refs_0_, ...), custom_call_target="tpu_custom_call" | custom-call | flops 12884901888 | bytes 25165824 | tf_op jit(solution)/shard_map/pallas_call | solution.py:139
  124.7 2.6 %collective-permute-start.33 = (f32[4,64,768]{2,1,0:T(8,128)}, f32[4,64,768]{2,1,0:T(8,128)}, u32[]{:S(2)}, u32[]{:S(2)}) collective-permute-start(f32[4,64,768]{2,1,0:T(8,128)} %get-tuple-element.106), channel_id=1, source_target_pairs={{0,12},{1,13},{2,14},{3,15},{4,8},{5,9},{6,10},{7,11},{8,4},{9,5},... | collective-permute-start | bytes 2359304 | tf_op jit(solution)/shard_map/ppermute | solution.py:76
  133.4 8.5 %collective-permute-done.34.refs_5_ = f32[4,64,512]{2,1,0:T(8,128)S(1)} collective-permute-done((f32[4,64,512]{2,1,0:T(8,128)}, f32[4,64,512]{2,1,0:T(8,128)S(1)}, u32[]{:S(2)}, u32[]{:S(2)}) %collective-permute-start.34) | collective-permute-done | bytes 524320 | tf_op jit(solution)/shard_map/ppermute | solution.py:76
  141.8 3.3 %collective-permute-done.33.refs_4_ = f32[4,64,768]{2,1,0:T(8,128)} collective-permute-done((f32[4,64,768]{2,1,0:T(8,128)}, f32[4,64,768]{2,1,0:T(8,128)}, u32[]{:S(2)}, u32[]{:S(2)}) %collective-permute-start.33) | collective-permute-done | bytes 786464 | tf_op jit(solution)/shard_map/ppermute | solution.py:76
  148.7 3.6 %collective-permute-start.35 = (f32[2,64,768]{2,1,0:T(8,128)S(1)}, f32[2,64,768]{2,1,0:T(8,128)S(1)}, u32[]{:S(2)}, u32[]{:S(2)}) collective-permute-start(f32[2,64,768]{2,1,0:T(8,128)S(1)} %slice_add_fusion.1), channel_id=1, source_target_pairs={{0,12},{1,13},{2,14},{3,15},{4,8},{5,9},{6,10},{7,11},{8,4},{9,5},... | collective-permute-start | bytes 1179656 | tf_op jit(solution)/shard_map/ppermute | solution.py:76
  153.4 2.5 %collective-permute-start.19 = (f32[1,64,512]{2,1,0:T(8,128)S(1)}, f32[1,64,512]{2,1,0:T(8,128)S(1)}, u32[]{:S(2)}, u32[]{:S(2)}) collective-permute-start(f32[1,64,512]{2,1,0:T(8,128)S(1)} %slice_add_fusion.11), channel_id=1, source_target_pairs={{0,12},{1,13},{2,14},{3,15},{4,8},{5,9},{6,10},{7,11},{8,4},{9,5},... | collective-permute-start | bytes 393224 | tf_op jit(solution)/shard_map/ppermute | solution.py:76
  158.9 1.8 slice_add_fusion.6
  165.5 3.4 %shard_map.83 = f32[8,128,128]{2,1,0:T(8,128)S(1)} custom-call(f32[4,64,768]{2,1,0:T(8,128)S(1)} %get-tuple-element.75.refs_0_, f32[4,64,768]{2,1,0:T(8,128)S(1)} %get-tuple-element.76.refs_1_, f32[4,64,512]{2,1,0:T(8,128)S(1)} %copy-done.2, f32[4,64,768]{2,1,0:T(8,128)} %collective-permute-done.11.refs_3_, f32[4,64,768]{2,1,0:T(8,128)} %collective-permute-done.12.refs_4_, ...), custom_call_target="tpu_custom_call" | custom-call | flops 1073741824 | bytes 2621440 | tf_op jit(solution)/shard_map/pallas_call | solution.py:186
  169.7 5.0 %all-to-all-start = ((f32[8,128,128]{2,1,0:T(8,128)}), f32[8,128,128]{2,1,0:T(8,128)S(1)}, u32[]{:S(2)}, u32[]{:S(2)}) async-start(f32[8,128,128]{2,1,0:T(8,128)} %copy-done), calls=%async_computation | async-start | bytes 1048576 | tf_op jit(solution)/shard_map/all_to_all | solution.py:254
  177.0 5.1 %collective-permute-done.40.refs_11_ = f32[1,64,512]{2,1,0:T(8,128)S(1)} collective-permute-done((f32[1,64,512]{2,1,0:T(8,128)S(1)}, f32[1,64,512]{2,1,0:T(8,128)S(1)}, u32[]{:S(2)}, u32[]{:S(2)}) %collective-permute-start.40) | collective-permute-done | bytes 131104 | tf_op jit(solution)/shard_map/ppermute | solution.py:76
  187.0 4.4 %shard_map.85 = f32[8,128,128]{2,1,0:T(8,128)} custom-call(f32[4,64,768]{2,1,0:T(8,128)S(1)} %get-tuple-element.102.refs_0_, f32[4,64,768]{2,1,0:T(8,128)S(1)} %get-tuple-element.103.refs_1_, f32[4,64,512]{2,1,0:T(8,128)S(1)} %copy-done.4, f32[4,64,768]{2,1,0:T(8,128)} %collective-permute-done.32.refs_3_, f32[4,64,768]{2,1,0:T(8,128)} %collective-permute-done.33.refs_4_, ...), custom_call_target="tpu_custom_call" | custom-call | flops 1073741824 | bytes 2621440 | tf_op jit(solution)/shard_map/pallas_call | solution.py:186
  191.3 7.2 %all-to-all-start.1 = ((f32[8,128,128]{2,1,0:T(8,128)}), f32[8,128,128]{2,1,0:T(8,128)S(1)}, u32[]{:S(2)}, u32[]{:S(2)}) async-start(f32[8,128,128]{2,1,0:T(8,128)} %shard_map.85), calls=%async_computation.1 | async-start | bytes 1048576 | tf_op jit(solution)/shard_map/all_to_all | solution.py:254
  198.6 10.2 %all-to-all-done.1 = f32[8,128,128]{2,1,0:T(8,128)S(1)} async-done(((f32[8,128,128]{2,1,0:T(8,128)}), f32[8,128,128]{2,1,0:T(8,128)S(1)}, u32[]{:S(2)}, u32[]{:S(2)}) %all-to-all-start.1) | async-done | bytes 524320 | tf_op jit(solution)/shard_map/all_to_all | solution.py:254
  (143 shorter events, 51.7 us)
Async XLA Ops:
  3.3 58.7 %collective-permute-start.10 = (f32[2048,1024]{1,0:T(8,128)}, f32[2048,1024]{1,0:T(8,128)}, u32[]{:S(2)}, u32[]{:S(2)}) collective-permute-start(f32[2048,1024]{1,0:T(8,128)} %param.9), channel_id=1, source_target_pairs={{0,1},{1,0},{2,3},{3,2},{4,5},{5,4},{6,7},{7,6},{8,9},{9,8},{10,11... | collective-permute-start | bytes 25165832 | tf_op jit(solution)/shard_map/ppermute | solution.py:76
  5.9 14.4 %collective-permute-start.1 = (f32[1,64,768]{2,1,0:T(8,128)S(1)}, f32[1,64,768]{2,1,0:T(8,128)S(1)}, u32[]{:S(2)}, u32[]{:S(2)}) collective-permute-start(f32[1,64,768]{2,1,0:T(8,128)S(1)} %get-tuple-element.62), channel_id=1, source_target_pairs={{0,16},{1,17},{2,18},{3,19},{4,20},{5,21},{6,22},{7,23},{8,24},{9,... | collective-permute-start | bytes 589832 | tf_op jit(solution)/shard_map/ppermute | solution.py:76
  12.9 13.9 %collective-permute-start.23 = (f32[1,64,768]{2,1,0:T(8,128)S(1)}, f32[1,64,768]{2,1,0:T(8,128)S(1)}, u32[]{:S(2)}, u32[]{:S(2)}) collective-permute-start(f32[1,64,768]{2,1,0:T(8,128)S(1)} %get-tuple-element.90), channel_id=1, source_target_pairs={{0,16},{1,17},{2,18},{3,19},{4,20},{5,21},{6,22},{7,23},{8,24},{9,... | collective-permute-start | bytes 589832 | tf_op jit(solution)/shard_map/ppermute | solution.py:76
  20.4 18.3 %collective-permute-start.4 = (f32[2,64,768]{2,1,0:T(8,128)S(1)}, f32[2,64,768]{2,1,0:T(8,128)S(1)}, u32[]{:S(2)}, u32[]{:S(2)}) collective-permute-start(f32[2,64,768]{2,1,0:T(8,128)S(1)} %pad_maximum_fusion), channel_id=1, source_target_pairs={{0,48},{1,49},{2,50},{3,51},{4,52},{5,53},{6,54},{7,55},{8,56},{9,... | collective-permute-start | bytes 1179656 | tf_op jit(solution)/shard_map/ppermute | solution.py:76
  26.1 10.6 %collective-permute-start.6 = (f32[2,64,640]{2,1,0:T(8,128)S(1)}, f32[2,64,640]{2,1,0:T(8,128)S(1)}, u32[]{:S(2)}, u32[]{:S(2)}) collective-permute-start(f32[2,64,640]{2,1,0:T(8,128)S(1)} %pad_maximum_fusion.3), channel_id=1, source_target_pairs={{0,16},{1,17},{2,18},{3,19},{4,20},{5,21},{6,22},{7,23},{8,24},{9,... | collective-permute-start | bytes 983048 | tf_op jit(solution)/shard_map/ppermute | solution.py:76
  26.8 14.3 %collective-permute-start.28 = (f32[2,64,640]{2,1,0:T(8,128)S(1)}, f32[2,64,640]{2,1,0:T(8,128)S(1)}, u32[]{:S(2)}, u32[]{:S(2)}) collective-permute-start(f32[2,64,640]{2,1,0:T(8,128)S(1)} %pad_maximum_fusion.5), channel_id=1, source_target_pairs={{0,16},{1,17},{2,18},{3,19},{4,20},{5,21},{6,22},{7,23},{8,24},{9,... | collective-permute-start | bytes 983048 | tf_op jit(solution)/shard_map/ppermute | solution.py:76
  36.7 13.2 %collective-permute-start.26 = (f32[2,64,768]{2,1,0:T(8,128)S(1)}, f32[2,64,768]{2,1,0:T(8,128)S(1)}, u32[]{:S(2)}, u32[]{:S(2)}) collective-permute-start(f32[2,64,768]{2,1,0:T(8,128)S(1)} %pad_maximum_fusion.1), channel_id=1, source_target_pairs={{0,48},{1,49},{2,50},{3,51},{4,52},{5,53},{6,54},{7,55},{8,56},{9,... | collective-permute-start | bytes 1179656 | tf_op jit(solution)/shard_map/ppermute | solution.py:76
  38.6 20.7 %collective-permute-start.9 = (f32[4,64,640]{2,1,0:T(8,128)S(1)}, f32[4,64,640]{2,1,0:T(8,128)S(1)}, u32[]{:S(2)}, u32[]{:S(2)}) collective-permute-start(f32[4,64,640]{2,1,0:T(8,128)S(1)} %constant_dynamic-update-slice_fusion.6.refs_2_), channel_id=1, source_target_pairs={{0,48},{1,49},{2,50},{3,51},{4,52},{5,53},{6,54},{7,55},{8,56},{9,... | collective-permute-start | bytes 1966088 | tf_op jit(solution)/shard_map/ppermute | solution.py:76
  41.0 25.8 %collective-permute-start.8 = (f32[4,64,640]{2,1,0:T(8,128)S(1)}, f32[4,64,640]{2,1,0:T(8,128)S(1)}, u32[]{:S(2)}, u32[]{:S(2)}) collective-permute-start(f32[4,64,640]{2,1,0:T(8,128)S(1)} %constant_dynamic-update-slice_fusion.3.refs_1_), channel_id=1, source_target_pairs={{0,16},{1,17},{2,18},{3,19},{4,20},{5,21},{6,22},{7,23},{8,24},{9,... | collective-permute-start | bytes 1966088 | tf_op jit(solution)/shard_map/ppermute | solution.py:76
  45.0 24.6 %collective-permute-start.7 = (f32[4,64,768]{2,1,0:T(8,128)S(1)}, f32[4,64,768]{2,1,0:T(8,128)S(1)}, u32[]{:S(2)}, u32[]{:S(2)}) collective-permute-start(f32[4,64,768]{2,1,0:T(8,128)S(1)} %constant_dynamic-update-slice_fusion.refs_0_), channel_id=1, source_target_pairs={{0,64},{1,65},{2,66},{3,67},{4,68},{5,69},{6,70},{7,71},{8,72},{9,... | collective-permute-start | bytes 2359304 | tf_op jit(solution)/shard_map/ppermute | solution.py:76
  50.0 27.3 %collective-permute-start.29 = (f32[4,64,768]{2,1,0:T(8,128)S(1)}, f32[4,64,768]{2,1,0:T(8,128)S(1)}, u32[]{:S(2)}, u32[]{:S(2)}) collective-permute-start(f32[4,64,768]{2,1,0:T(8,128)S(1)} %constant_dynamic-update-slice_fusion.9.refs_0_), channel_id=1, source_target_pairs={{0,64},{1,65},{2,66},{3,67},{4,68},{5,69},{6,70},{7,71},{8,72},{9,... | collective-permute-start | bytes 2359304 | tf_op jit(solution)/shard_map/ppermute | solution.py:76
  59.4 11.8 %collective-permute-start.31 = (f32[4,64,640]{2,1,0:T(8,128)S(1)}, f32[4,64,640]{2,1,0:T(8,128)S(1)}, u32[]{:S(2)}, u32[]{:S(2)}) collective-permute-start(f32[4,64,640]{2,1,0:T(8,128)S(1)} %constant_dynamic-update-slice_fusion.15.refs_2_), channel_id=1, source_target_pairs={{0,48},{1,49},{2,50},{3,51},{4,52},{5,53},{6,54},{7,55},{8,56},{9,... | collective-permute-start | bytes 1966088 | tf_op jit(solution)/shard_map/ppermute | solution.py:76
  61.9 10.6 %collective-permute-start.30 = (f32[4,64,640]{2,1,0:T(8,128)S(1)}, f32[4,64,640]{2,1,0:T(8,128)S(1)}, u32[]{:S(2)}, u32[]{:S(2)}) collective-permute-start(f32[4,64,640]{2,1,0:T(8,128)S(1)} %constant_dynamic-update-slice_fusion.12.refs_1_), channel_id=1, source_target_pairs={{0,16},{1,17},{2,18},{3,19},{4,20},{5,21},{6,22},{7,23},{8,24},{9,... | collective-permute-start | bytes 1966088 | tf_op jit(solution)/shard_map/ppermute | solution.py:76
  66.8 10.4 %collective-permute-start.20 = (f32[2048]{0:T(1024)S(1)}, f32[2048]{0:T(1024)S(1)}, u32[]{:S(2)}, u32[]{:S(2)}) collective-permute-start(f32[2048]{0:T(1024)S(1)} %add.92), channel_id=1, source_target_pairs={{0,4},{1,5},{2,6},{3,7},{4,0},{5,1},{6,2},{7,3},{8,12},{9,13},{10,... | collective-permute-start | bytes 24584 | tf_op jit(solution)/shard_map/ppermute | solution.py:76
  77.3 24.1 %collective-permute-start.21 = (f32[2048]{0:T(1024)S(1)}, f32[2048]{0:T(1024)S(1)}, u32[]{:S(2)}, u32[]{:S(2)}) collective-permute-start(f32[2048]{0:T(1024)S(1)} %add.93), channel_id=1, source_target_pairs={{0,12},{1,13},{2,14},{3,15},{4,8},{5,9},{6,10},{7,11},{8,4},{9,5},... | collective-permute-start | bytes 24584 | tf_op jit(solution)/shard_map/ppermute | solution.py:76
  100.4 28.0 %collective-permute-start.11 = (f32[4,64,768]{2,1,0:T(8,128)}, f32[4,64,768]{2,1,0:T(8,128)}, u32[]{:S(2)}, u32[]{:S(2)}) collective-permute-start(f32[4,64,768]{2,1,0:T(8,128)} %get-tuple-element.78), channel_id=1, source_target_pairs={{0,4},{1,5},{2,6},{3,7},{4,0},{5,1},{6,2},{7,3},{8,12},{9,13},{10,... | collective-permute-start | bytes 2359304 | tf_op jit(solution)/shard_map/ppermute | solution.py:76
  100.5 28.0 %collective-permute-start.12 = (f32[4,64,768]{2,1,0:T(8,128)}, f32[4,64,768]{2,1,0:T(8,128)}, u32[]{:S(2)}, u32[]{:S(2)}) collective-permute-start(f32[4,64,768]{2,1,0:T(8,128)} %get-tuple-element.79), channel_id=1, source_target_pairs={{0,12},{1,13},{2,14},{3,15},{4,8},{5,9},{6,10},{7,11},{8,4},{9,5},... | collective-permute-start | bytes 2359304 | tf_op jit(solution)/shard_map/ppermute | solution.py:76
  101.0 27.1 %collective-permute-start.13 = (f32[4,64,512]{2,1,0:T(8,128)}, f32[4,64,512]{2,1,0:T(8,128)}, u32[]{:S(2)}, u32[]{:S(2)}) collective-permute-start(f32[4,64,512]{2,1,0:T(8,128)} %get-tuple-element.80), channel_id=1, source_target_pairs={{0,2},{1,3},{2,0},{3,1},{4,6},{5,7},{6,4},{7,5},{8,10},{9,11},{10,... | collective-permute-start | bytes 1572872 | tf_op jit(solution)/shard_map/ppermute | solution.py:76
  101.4 23.2 %collective-permute-start.22 = (f32[2048]{0:T(1024)S(1)}, f32[2048]{0:T(1024)S(1)}, u32[]{:S(2)}, u32[]{:S(2)}) collective-permute-start(f32[2048]{0:T(1024)S(1)} %add.94), channel_id=1, source_target_pairs={{0,2},{1,3},{2,0},{3,1},{4,6},{5,7},{6,4},{7,5},{8,10},{9,11},{10,... | collective-permute-start | bytes 24584 | tf_op jit(solution)/shard_map/ppermute | solution.py:76
  123.1 18.7 %collective-permute-start.32 = (f32[4,64,768]{2,1,0:T(8,128)}, f32[4,64,768]{2,1,0:T(8,128)}, u32[]{:S(2)}, u32[]{:S(2)}) collective-permute-start(f32[4,64,768]{2,1,0:T(8,128)} %get-tuple-element.105), channel_id=1, source_target_pairs={{0,4},{1,5},{2,6},{3,7},{4,0},{5,1},{6,2},{7,3},{8,12},{9,13},{10,... | collective-permute-start | bytes 2359304 | tf_op jit(solution)/shard_map/ppermute | solution.py:76
  124.7 20.5 %collective-permute-start.33 = (f32[4,64,768]{2,1,0:T(8,128)}, f32[4,64,768]{2,1,0:T(8,128)}, u32[]{:S(2)}, u32[]{:S(2)}) collective-permute-start(f32[4,64,768]{2,1,0:T(8,128)} %get-tuple-element.106), channel_id=1, source_target_pairs={{0,12},{1,13},{2,14},{3,15},{4,8},{5,9},{6,10},{7,11},{8,4},{9,5},... | collective-permute-start | bytes 2359304 | tf_op jit(solution)/shard_map/ppermute | solution.py:76
  128.0 13.8 %collective-permute-start.34 = (f32[4,64,512]{2,1,0:T(8,128)}, f32[4,64,512]{2,1,0:T(8,128)S(1)}, u32[]{:S(2)}, u32[]{:S(2)}) collective-permute-start(f32[4,64,512]{2,1,0:T(8,128)} %copy-done.13), channel_id=1, source_target_pairs={{0,2},{1,3},{2,0},{3,1},{4,6},{5,7},{6,4},{7,5},{8,10},{9,11},{10,... | collective-permute-start | bytes 1572872 | tf_op jit(solution)/shard_map/ppermute | solution.py:76
  129.5 19.2 %collective-permute-start.16 = (f32[2,64,512]{2,1,0:T(8,128)S(1)}, f32[2,64,512]{2,1,0:T(8,128)S(1)}, u32[]{:S(2)}, u32[]{:S(2)}) collective-permute-start(f32[2,64,512]{2,1,0:T(8,128)S(1)} %slice_add_fusion.5), channel_id=1, source_target_pairs={{0,4},{1,5},{2,6},{3,7},{4,0},{5,1},{6,2},{7,3},{8,12},{9,13},{10,... | collective-permute-start | bytes 786440 | tf_op jit(solution)/shard_map/ppermute | solution.py:76
  130.6 21.7 %collective-permute-start.15 = (f32[2,64,768]{2,1,0:T(8,128)S(1)}, f32[2,64,768]{2,1,0:T(8,128)S(1)}, u32[]{:S(2)}, u32[]{:S(2)}) collective-permute-start(f32[2,64,768]{2,1,0:T(8,128)S(1)} %slice_add_fusion.2), channel_id=1, source_target_pairs={{0,2},{1,3},{2,0},{3,1},{4,6},{5,7},{6,4},{7,5},{8,10},{9,11},{10,... | collective-permute-start | bytes 1179656 | tf_op jit(solution)/shard_map/ppermute | solution.py:76
  141.8 10.5 %collective-permute-start.14 = (f32[2,64,768]{2,1,0:T(8,128)S(1)}, f32[2,64,768]{2,1,0:T(8,128)S(1)}, u32[]{:S(2)}, u32[]{:S(2)}) collective-permute-start(f32[2,64,768]{2,1,0:T(8,128)S(1)} %slice_add_fusion.3), channel_id=1, source_target_pairs={{0,12},{1,13},{2,14},{3,15},{4,8},{5,9},{6,10},{7,11},{8,4},{9,5},... | collective-permute-start | bytes 1179656 | tf_op jit(solution)/shard_map/ppermute | solution.py:76
  146.2 11.7 %collective-permute-start.37 = (f32[2,64,512]{2,1,0:T(8,128)S(1)}, f32[2,64,512]{2,1,0:T(8,128)S(1)}, u32[]{:S(2)}, u32[]{:S(2)}) collective-permute-start(f32[2,64,512]{2,1,0:T(8,128)S(1)} %slice_add_fusion.4), channel_id=1, source_target_pairs={{0,4},{1,5},{2,6},{3,7},{4,0},{5,1},{6,2},{7,3},{8,12},{9,13},{10,... | collective-permute-start | bytes 786440 | tf_op jit(solution)/shard_map/ppermute | solution.py:76
  147.6 11.3 %collective-permute-start.36 = (f32[2,64,768]{2,1,0:T(8,128)S(1)}, f32[2,64,768]{2,1,0:T(8,128)S(1)}, u32[]{:S(2)}, u32[]{:S(2)}) collective-permute-start(f32[2,64,768]{2,1,0:T(8,128)S(1)} %slice_add_fusion), channel_id=1, source_target_pairs={{0,2},{1,3},{2,0},{3,1},{4,6},{5,7},{6,4},{7,5},{8,10},{9,11},{10,... | collective-permute-start | bytes 1179656 | tf_op jit(solution)/shard_map/ppermute | solution.py:76
  153.4 12.1 %collective-permute-start.19 = (f32[1,64,512]{2,1,0:T(8,128)S(1)}, f32[1,64,512]{2,1,0:T(8,128)S(1)}, u32[]{:S(2)}, u32[]{:S(2)}) collective-permute-start(f32[1,64,512]{2,1,0:T(8,128)S(1)} %slice_add_fusion.11), channel_id=1, source_target_pairs={{0,12},{1,13},{2,14},{3,15},{4,8},{5,9},{6,10},{7,11},{8,4},{9,5},... | collective-permute-start | bytes 393224 | tf_op jit(solution)/shard_map/ppermute | solution.py:76
  160.7 21.4 %collective-permute-start.39 = (f32[1,64,768]{2,1,0:T(8,128)}, f32[1,64,768]{2,1,0:T(8,128)}, u32[]{:S(2)}, u32[]{:S(2)}) collective-permute-start(f32[1,64,768]{2,1,0:T(8,128)} %slice_add_fusion.6), channel_id=1, source_target_pairs={{0,4},{1,5},{2,6},{3,7},{4,0},{5,1},{6,2},{7,3},{8,12},{9,13},{10,... | collective-permute-start | bytes 589832 | tf_op jit(solution)/shard_map/ppermute | solution.py:76
  163.8 18.3 %collective-permute-start.38 = (f32[1,64,768]{2,1,0:T(8,128)}, f32[1,64,768]{2,1,0:T(8,128)}, u32[]{:S(2)}, u32[]{:S(2)}) collective-permute-start(f32[1,64,768]{2,1,0:T(8,128)} %slice_add_fusion.7), channel_id=1, source_target_pairs={{0,2},{1,3},{2,0},{3,1},{4,6},{5,7},{6,4},{7,5},{8,10},{9,11},{10,... | collective-permute-start | bytes 589832 | tf_op jit(solution)/shard_map/ppermute | solution.py:76
  169.7 21.6 %all-to-all-start = ((f32[8,128,128]{2,1,0:T(8,128)}), f32[8,128,128]{2,1,0:T(8,128)S(1)}, u32[]{:S(2)}, u32[]{:S(2)}) async-start(f32[8,128,128]{2,1,0:T(8,128)} %copy-done), calls=%async_computation | async-start | bytes 1048576 | tf_op jit(solution)/shard_map/all_to_all | solution.py:254
  191.3 17.4 %all-to-all-start.1 = ((f32[8,128,128]{2,1,0:T(8,128)}), f32[8,128,128]{2,1,0:T(8,128)S(1)}, u32[]{:S(2)}, u32[]{:S(2)}) async-start(f32[8,128,128]{2,1,0:T(8,128)} %shard_map.85), calls=%async_computation.1 | async-start | bytes 1048576 | tf_op jit(solution)/shard_map/all_to_all | solution.py:254
  (28 other events, 277.8 us)

commit v2 on v1

v2 whole, which is shorter than its diff:
```python
import functools

import jax
import jax.numpy as jnp
import numpy as np
from jax import lax
from jax.experimental import pallas as pl
from jax.experimental.pallas import tpu as pltpu
from jax.sharding import PartitionSpec as P


ENT = 1024
CHUNKS = 2
ROWS = 128 // CHUNKS
DEPTH = (768, 640, 640)
DOFF = (0, 768, 1408)
TILE = 256
COLS = (768, 768, 512)
COFF = (0, 768, 1536)
BOTH = ("row", "col")


def unflat(i):
    row, col = divmod(i, 16)
    return row // 4, row % 4, col // 4, col // 2 % 2, col % 2


def flat(yh, x, z, yl, core):
    return (yh * 4 + x) * 16 + z * 4 + yl * 2 + core


def perm(step):
    return [(i, flat(*step(*unflat(i)))) for i in range(128)]


CORE = perm(lambda yh, x, z, yl, c: (yh, x, z, yl, 1 - c))
ROW_DIMS = (
    perm(lambda yh, x, z, yl, c: (yh, x ^ 1, z, yl, c)),
    perm(lambda yh, x, z, yl, c: (yh, 3 - x, z, yl, c)),
    perm(lambda yh, x, z, yl, c: (1 - yh, x, z, yl, c)),
)
COL_DIMS = (
    perm(lambda yh, x, z, yl, c: (yh, x, z ^ 1, yl, c)),
    perm(lambda yh, x, z, yl, c: (yh, x, 3 - z, yl, c)),
    perm(lambda yh, x, z, yl, c: (yh, x, z, 1 - yl, c)),
)
ROW_XOR = [[(i, i ^ (k * 16)) for i in range(128)] for k in range(8)]


def gray(v):
    return v ^ (v >> 1)


def ungray(v):
    return (v & 2) | ((v ^ (v >> 1)) & 1)


def place(e, p):
    return sum((e >> (p + s) % 3 & 1) << s for s in range(3))


def tables():
    out = np.zeros((128, 3, 8), np.int32)
    for i in range(128):
        yh, x, z, yl, _ = unflat(i)
        here_r, here_c = gray(x) | yh << 2, gray(z) | yl << 2
        for e in range(8):
            h = here_r ^ e
            source = (h >> 2) * 4 + ungray(h & 3)
            d = (gray(source >> 1) | (source & 1) << 2) ^ here_c
            for q in range(3):
                out[i, q, 7 - sum((d >> (q + s) % 3 & 1) << 2 - s for s in range(3))] = e
    return out.reshape(128, 24)


def permute(x, pairs):
    return lax.ppermute(x, BOTH, pairs)


def split(x):
    high = lax.reduce_precision(x, 8, 7)
    return high.astype(jnp.bfloat16), (x - high).astype(jnp.bfloat16)


STARTS = tuple(c // TILE for c in COFF)
SIZES = tuple(c // TILE for c in COLS)


def mm_kernel(half, tbl, *refs):
    if half == 0:
        first, last, refs = refs[:3], refs[3:6], refs[6:]
    else:
        parts, refs = refs[0], refs[1:]
    (fho, flo, fhp, flp), outs, refs = refs[:4], refs[4:7], refs[7:]
    m = 4 * ROWS
    t = pl.program_id(0)
    if half == 0:
        parts, lhs = refs

        @pl.when(t == 0)
        def _():
            for e in range(8):
                for p in range(3):
                    at = place(e, p)
                    v = (last if at > 3 else first)[p][at & 3]
                    h = v.astype(jnp.bfloat16)
                    cols = pl.ds(DOFF[p], DEPTH[p])
                    parts[0, e, :, cols] = h
                    parts[1, e, :, cols] = (v - h.astype(jnp.float32)).astype(jnp.bfloat16)

    else:
        (lhs,) = refs
    for q in range(3):

        @pl.when(t == STARTS[q])
        def _(q=q):
            for i in range(4):
                e = tbl[q * 8 + half * 4 + i]
                for k in range(2):
                    lhs[pl.ds(k * m + i * ROWS, ROWS), :] = parts[k, e]

    dot = functools.partial(
        lax.dot_general,
        dimension_numbers=(((1,), (1,)), ((), ())),
        preferred_element_type=jnp.float32,
    )
    own, far, high = pl.ds(0, 1024), pl.ds(1024, 1024), pl.ds(0, m)
    rows = pl.ds(pl.multiple_of(t * TILE, TILE), TILE)
    acc = dot(lhs[:, own], fho[rows, :]) + dot(lhs[:, far], fhp[rows, :])
    low = dot(lhs[high, own], flo[rows, :]) + dot(lhs[high, far], flp[rows, :])
    acc = (acc[:m] + (acc[m:] + low)).reshape(4, ROWS, TILE)
    for q in range(3):

        @pl.when((t >= STARTS[q]) & (t < STARTS[q] + SIZES[q]))
        def _(q=q):
            outs[q][...] = acc


def mm(half, tbl, pieces, factors):
    whole = pl.BlockSpec(memory_space=pltpu.VMEM)
    outs = [
        pl.BlockSpec(
            (4, ROWS, TILE), lambda t, tb, q=q: (0, 0, jnp.clip(t - STARTS[q], 0, SIZES[q] - 1))
        )
        for q in range(3)
    ]
    shapes = [jax.ShapeDtypeStruct((4, ROWS, COLS[q]), jnp.float32) for q in range(3)]
    if half == 0:
        outs.append(whole)
        shapes.append(jax.ShapeDtypeStruct((2, 8, ROWS, 2048), jnp.bfloat16))
    res = pl.pallas_call(
        functools.partial(mm_kernel, half),
        out_shape=shapes,
        grid_spec=pltpu.PrefetchScalarGridSpec(
            num_scalar_prefetch=1,
            grid=(2048 // TILE,),
            in_specs=[whole] * (len(pieces) + 4),
            out_specs=outs,
            scratch_shapes=[pltpu.VMEM((8 * ROWS, 2048), jnp.bfloat16)],
        ),
        cost_estimate=pl.CostEstimate(
            flops=2 * 3 * 4 * ROWS * 2048 * 2048,
            bytes_accessed=2 * 4 * ROWS * 2048 * 4 + 4 * 2048 * 2048,
            transcendentals=0,
        ),
        compiler_params=pltpu.CompilerParams(vmem_limit_bytes=8 * 2**20),
    )(tbl, *pieces, *factors)
    return res[:3], res[3:]


def tail_kernel(row, *refs):
    pieces, cells, outs, both = refs[:6], refs[6], refs[7:15], refs[15]
    for q in range(3):
        cols = pl.ds(COFF[q], COLS[q])
        mixed = pieces[q][0] + pieces[3 + q][0]
        inv, scale, vol, floor, cover = (cells[pl.ds(k, 1), cols] for k in range(5))
        ground = scale * jnp.exp(vol * (mixed * inv))
        ceded = jnp.minimum(jnp.maximum(ground - floor, 0.0), cover)
        for k, v in enumerate((ground - ceded, ceded)):
            h = v.astype(jnp.bfloat16)
            both[pl.ds(k * ROWS, ROWS), cols] = h
            both[pl.ds((2 + k) * ROWS, ROWS), cols] = (v - h.astype(jnp.float32)).astype(jnp.bfloat16)
    entity = cells[pl.ds(5, 1), :].astype(jnp.int32)
    for k in range(8):
        lines = lax.broadcasted_iota(jnp.int32, (128, 2048), 0) + (row[0] ^ k) * 128
        onehot = jnp.where(lines == entity, 1.0, 0.0).astype(jnp.bfloat16)
        sums = lax.dot_general(
            both[...], onehot, (((1,), (1,)), ((), ())), preferred_element_type=jnp.float32
        )
        outs[k][...] = sums[: 2 * ROWS] + sums[2 * ROWS :]


def tail(row, held, third, cells):
    def at(shape):
        return pl.BlockSpec(shape, lambda i, r: (0,) * len(shape))

    return pl.pallas_call(
        tail_kernel,
        out_shape=[jax.ShapeDtypeStruct((2 * ROWS, 128), jnp.float32)] * 8,
        grid_spec=pltpu.PrefetchScalarGridSpec(
            num_scalar_prefetch=1,
            grid=(1,),
            in_specs=[at((1, ROWS, COLS[q])) for q in range(3)] * 2 + [at((6, 2048))],
            out_specs=[at((2 * ROWS, 128))] * 8,
            scratch_shapes=[pltpu.VMEM((4 * ROWS, 2048), jnp.bfloat16)],
        ),
        cost_estimate=pl.CostEstimate(
            flops=2 * 4 * ROWS * 2048 * ENT, bytes_accessed=5 * ROWS * 2048 * 4, transcendentals=ROWS * 2048
        ),
        compiler_params=pltpu.CompilerParams(vmem_limit_bytes=16 * 2**20),
    )(row.reshape(1), *held, *third, cells)


def step(normals, factor, cell_entity, scale, volatility, retention, limit):
    row, col = lax.axis_index("row"), lax.axis_index("col")
    core = col & 1
    tbl = lax.dynamic_index_in_dim(jnp.asarray(tables()), row * 16 + col, 0, False)

    given = permute(lax.dynamic_slice_in_dim(normals, (1 - core) * 128, 128, 0), CORE)
    kept = lax.dynamic_slice_in_dim(normals, core * 128, 128, 0)
    factor, given = lax.optimization_barrier((factor, given))
    far_factor = permute(factor, CORE)
    block = jnp.concatenate([kept[:, DEPTH[0] :], given], axis=1)
    gathered = [
        [
            kept[None, c * ROWS : (c + 1) * ROWS, : DEPTH[0]],
            block[None, c * ROWS : (c + 1) * ROWS, : DEPTH[1]],
            block[None, c * ROWS : (c + 1) * ROWS, DEPTH[1] :],
        ]
        for c in range(CHUNKS)
    ]
    last = []
    for s in range(3):
        for c in range(CHUNKS):
            came = lax.optimization_barrier([permute(gathered[c][p], ROW_DIMS[(p + s) % 3]) for p in range(3)])
            if s == 2:
                last.append(came)
                continue
            gathered[c] = [jnp.concatenate([gathered[c][p], came[p]], axis=0) for p in range(3)]

    fho, flo = split(factor)
    norms = jnp.sum(factor * factor, axis=1)
    fhp, flp = split(far_factor)
    far_norms = jnp.sum(far_factor * far_factor, axis=1)
    factors = (fho, flo, fhp, flp)
    norms = norms + far_norms
    for d in range(3):
        norms = norms + permute(norms, COL_DIMS[d])

    cells = jnp.stack(
        [
            lax.rsqrt(norms),
            scale,
            volatility,
            0.25 * retention.astype(jnp.float32),
            0.25 * limit.astype(jnp.float32),
            cell_entity.astype(jnp.float32),
        ]
    )
    results = []
    for c in range(CHUNKS):
        sent, parts = mm(0, tbl, (*gathered[c], *last[c]), factors)
        came = lax.optimization_barrier([permute(sent[q], COL_DIMS[q]) for q in range(3)])
        kept, _ = mm(1, tbl, parts, factors)
        second = lax.optimization_barrier([permute(kept[q][:2] + came[q][:2], COL_DIMS[(q + 1) % 3]) for q in range(3)])
        third = lax.optimization_barrier(
            [permute(kept[q][2:3] + came[q][2:3] + second[q][:1], COL_DIMS[(q + 2) % 3]) for q in range(3)]
        )
        held = [kept[q][3:] + came[q][3:] + second[q][1:] for q in range(3)]
        sums = tail(row, held, third, cells)
        total = sums[0]
        for k in range(1, 8):
            total = total + permute(sums[k], ROW_XOR[k])
        results.append(total.reshape(2, ROWS, 128))
    return jnp.concatenate(results, axis=1)


def solution(mesh):
    return jax.shard_map(
        step,
        mesh=mesh,
        in_specs=(
            P("row", "col"),
            P("row", "col"),
            P("row"),
            P("row"),
            P("row"),
            P("row"),
            P("row"),
        ),
        out_specs=P(None, "col", "row"),
        check_vma=False,
    )
```

time: 210 us -> 213 us (1.014)
  starting transfers between devices: 62.7 us -> 80.1 us
  other arithmetic: 24.5 us -> 8.55 us
  waiting for transfers between devices: 65.3 us -> 74.9 us
  local copies, waits for them, and re-layouts: 12.1 us -> 3.87 us
    ppermute x41 -> x55, starting transfers between devices: 50.4 us -> 80.1 us  [permute(): return lax.ppermute(x, BOTH, pairs)]
    ppermute x41 -> x55, waiting for transfers between devices: 55.1 us -> 74.9 us  [permute(): return lax.ppermute(x, BOTH, pairs)]
    all_to_all x2 -> x0, starting transfers between devices: 12.2 us -> none  [step(): parts = lax.all_to_all(sums, 'row', split_axis=0, concat_axis=0, tiled=True)]
    all_to_all x2 -> x0, waiting for transfers between devices: 10.2 us -> none  [step(): parts = lax.all_to_all(sums, 'row', split_axis=0, concat_axis=0, tiled=True)]
    unnamed x44 -> x10, local copies, waits for them, and re-layouts: 8.24 us -> 0.03 us
    add x6, other arithmetic: 7.41 us -> 0.46 us  [step(): kept[q][2:3] + came[q][2:3] + second[q][:1]]
    add x6, other arithmetic: 6.21 us -> 0.3 us  [step(): kept[q][:2] + came[q][:2]]
    reduce_sum x1, other arithmetic: 4.27 us -> 1.59 us  [step(): norms = jnp.sum(factor * factor, axis=1)]
  transfers between devices with their start and end apart: 43 -> 55, of which waited for: 15 -> 21; matrix products, arithmetic and copies ran while one was open for 13% -> 3% of each run, Pallas kernels for 21% -> 21%
where the time goes in v2:
time: 213 us
  starting transfers between devices  80.1 us (38%)
  waiting for transfers between devices  74.9 us (35%)
  Pallas kernels  45.4 us (21%)
  other arithmetic  8.55 us (4%)
  local copies, waits for them, and re-layouts  3.87 us (2%)
    ppermute x55, starting transfers between devices, permute(): return lax.ppermute(x, BOTH, pairs)  80.1 us
    ppermute x55, waiting for transfers between devices, permute(): return lax.ppermute(x, BOTH, pairs)  74.9 us
    pallas_call x4, Pallas kernels, mm(): pl.pallas_call(functools.partial(mm_kernel, half), out_shape=shapes, grid...  40.8 us
    pallas_call x2, Pallas kernels, tail(): pl.pallas_call(tail_kernel, out_shape=[jax.ShapeDtypeStruct((2 * ROWS, 12...  4.67 us
  transfers between devices with their start and end apart: 55, of which 21 were waited for; matrix products, arithmetic and copies ran while one was open for 3% of the time, Pallas kernels for 21%

profile of v2, /device:TPU:0, one launch (start us, length us, event | category | flops | bytes accessed | tf_op | source)
XLA Modules:
  0.0 213.3 jit_solution(4876002432029415652)
XLA Ops:
  7.4 2.9 %collective-permute-start.2 = (f32[1,64,640]{2,1,0:T(8,128)S(1)}, f32[1,64,640]{2,1,0:T(8,128)S(1)}, u32[]{:S(2)}, u32[]{:S(2)}) collective-permute-start(f32[1,64,640]{2,1,0:T(8,128)S(1)} %get-tuple-element.161), channel_id=1, source_target_pairs={{0,48},{1,49},{2,50},{3,51},{4,52},{5,53},{6,54},{7,55},{8,56},{9,... | collective-permute-start | bytes 491528 | tf_op jit(solution)/shard_map/ppermute | solution.py:77
  10.3 3.2 %collective-permute-start.3 = (f32[1,64,640]{2,1,0:T(8,128)S(1)}, f32[1,64,640]{2,1,0:T(8,128)S(1)}, u32[]{:S(2)}, u32[]{:S(2)}) collective-permute-start(f32[1,64,640]{2,1,0:T(8,128)S(1)} %get-tuple-element.163), channel_id=1, source_target_pairs={{0,64},{1,65},{2,66},{3,67},{4,68},{5,69},{6,70},{7,71},{8,72},{9,... | collective-permute-start | bytes 491528 | tf_op jit(solution)/shard_map/ppermute | solution.py:77
  15.0 3.2 %collective-permute-start.32 = (f32[1,64,640]{2,1,0:T(8,128)S(1)}, f32[1,64,640]{2,1,0:T(8,128)S(1)}, u32[]{:S(2)}, u32[]{:S(2)}) collective-permute-start(f32[1,64,640]{2,1,0:T(8,128)S(1)} %get-tuple-element.164), channel_id=1, source_target_pairs={{0,64},{1,65},{2,66},{3,67},{4,68},{5,69},{6,70},{7,71},{8,72},{9,... | collective-permute-start | bytes 491528 | tf_op jit(solution)/shard_map/ppermute | solution.py:77
  18.3 2.5 %collective-permute-start.4 = (f32[2,64,768]{2,1,0:T(8,128)S(1)}, f32[2,64,768]{2,1,0:T(8,128)S(1)}, u32[]{:S(2)}, u32[]{:S(2)}) collective-permute-start(f32[2,64,768]{2,1,0:T(8,128)S(1)} %pad_maximum_fusion.6), channel_id=1, source_target_pairs={{0,48},{1,49},{2,50},{3,51},{4,52},{5,53},{6,54},{7,55},{8,56},{9,... | collective-permute-start | bytes 1179656 | tf_op jit(solution)/shard_map/ppermute | solution.py:77
  23.6 6.8 %collective-permute-done.5 = f32[2,64,640]{2,1,0:T(8,128)S(1)} collective-permute-done((f32[2,64,640]{2,1,0:T(8,128)S(1)}, f32[2,64,640]{2,1,0:T(8,128)S(1)}, u32[]{:S(2)}, u32[]{:S(2)}) %collective-permute-start.5) | collective-permute-done | bytes 327712 | tf_op jit(solution)/shard_map/ppermute | solution.py:77
  32.1 2.7 %collective-permute-start.33 = (f32[2,64,768]{2,1,0:T(8,128)S(1)}, f32[2,64,768]{2,1,0:T(8,128)S(1)}, u32[]{:S(2)}, u32[]{:S(2)}) collective-permute-start(f32[2,64,768]{2,1,0:T(8,128)S(1)} %pad_maximum_fusion.7), channel_id=1, source_target_pairs={{0,48},{1,49},{2,50},{3,51},{4,52},{5,53},{6,54},{7,55},{8,56},{9,... | collective-permute-start | bytes 1179656 | tf_op jit(solution)/shard_map/ppermute | solution.py:77
  37.3 4.4 %collective-permute-start.9 = (f32[4,64,640]{2,1,0:T(8,128)S(1)}, f32[4,64,640]{2,1,0:T(8,128)S(1)}, u32[]{:S(2)}, u32[]{:S(2)}) collective-permute-start(f32[4,64,640]{2,1,0:T(8,128)S(1)} %pad_maximum_fusion.3.refs_2_), channel_id=1, source_target_pairs={{0,48},{1,49},{2,50},{3,51},{4,52},{5,53},{6,54},{7,55},{8,56},{9,... | collective-permute-start | bytes 1966088 | tf_op jit(solution)/shard_map/ppermute | solution.py:77
  42.6 2.6 %collective-permute-done.33 = f32[2,64,768]{2,1,0:T(8,128)S(1)} collective-permute-done((f32[2,64,768]{2,1,0:T(8,128)S(1)}, f32[2,64,768]{2,1,0:T(8,128)S(1)}, u32[]{:S(2)}, u32[]{:S(2)}) %collective-permute-start.33) | collective-permute-done | bytes 393248 | tf_op jit(solution)/shard_map/ppermute | solution.py:77
  45.3 2.6 %collective-permute-start.36 = (f32[4,64,768]{2,1,0:T(8,128)S(1)}, f32[4,64,768]{2,1,0:T(8,128)S(1)}, u32[]{:S(2)}, u32[]{:S(2)}) collective-permute-start(f32[4,64,768]{2,1,0:T(8,128)S(1)} %pad_maximum_fusion.1.refs_0_), channel_id=1, source_target_pairs={{0,64},{1,65},{2,66},{3,67},{4,68},{5,69},{6,70},{7,71},{8,72},{9,... | collective-permute-start | bytes 2359304 | tf_op jit(solution)/shard_map/ppermute | solution.py:77
  50.2 2.8 %collective-permute-start.38 = (f32[4,64,640]{2,1,0:T(8,128)S(1)}, f32[4,64,640]{2,1,0:T(8,128)S(1)}, u32[]{:S(2)}, u32[]{:S(2)}) collective-permute-start(f32[4,64,640]{2,1,0:T(8,128)S(1)} %pad_maximum_fusion.5.refs_2_), channel_id=1, source_target_pairs={{0,48},{1,49},{2,50},{3,51},{4,52},{5,53},{6,54},{7,55},{8,56},{9,... | collective-permute-start | bytes 1966088 | tf_op jit(solution)/shard_map/ppermute | solution.py:77
  53.0 6.3 %collective-permute-done.9.refs_5_ = f32[4,64,640]{2,1,0:T(8,128)S(1)} collective-permute-done((f32[4,64,640]{2,1,0:T(8,128)S(1)}, f32[4,64,640]{2,1,0:T(8,128)S(1)}, u32[]{:S(2)}, u32[]{:S(2)}) %collective-permute-start.9) | collective-permute-done | bytes 655392 | tf_op jit(solution)/shard_map/ppermute | solution.py:77
  63.8 7.0 %collective-permute-done.38.refs_5_ = f32[4,64,640]{2,1,0:T(8,128)S(1)} collective-permute-done((f32[4,64,640]{2,1,0:T(8,128)S(1)}, f32[4,64,640]{2,1,0:T(8,128)S(1)}, u32[]{:S(2)}, u32[]{:S(2)}) %collective-permute-start.38) | collective-permute-done | bytes 655392 | tf_op jit(solution)/shard_map/ppermute | solution.py:77
  70.9 3.3 %collective-permute-done.36.refs_3_ = f32[4,64,768]{2,1,0:T(8,128)S(1)} collective-permute-done((f32[4,64,768]{2,1,0:T(8,128)S(1)}, f32[4,64,768]{2,1,0:T(8,128)S(1)}, u32[]{:S(2)}, u32[]{:S(2)}) %collective-permute-start.36) | collective-permute-done | bytes 786464 | tf_op jit(solution)/shard_map/ppermute | solution.py:77
  74.2 4.3 %multiply_reduce_fusion = (f32[2048]{0:T(1024)S(1)}, bf16[2048,1024]{1,0:T(8,128)(2,1)S(1)}, bf16[2048,1024]{1,0:T(8,128)(2,1)S(1)}) fusion(f32[2048,1024]{1,0:T(8,128)} %collective-permute-done.10), kind=kLoop, calls=%fused_computation.6 | loop fusion | flops 12580864 | bytes 16785408 | tf_op jit(solution)/shard_map/reduce_sum | solution.py:244
  80.5 10.6 %shard_map.82 = (f32[4,64,768]{2,1,0:T(8,128)S(1)}, f32[4,64,768]{2,1,0:T(8,128)S(1)}, f32[4,64,512]{2,1,0:T(8,128)S(1)}, bf16[2,8,64,2048]{3,2,1,0:T(8,128)(2,1)S(1)}) custom-call(s32[24]{0:T(128)S(1)} %fusion.3.tbl, f32[4,64,768]{2,1,0:T(8,128)S(1)} %pad_maximum_fusion.refs_0_, f32[4,64,640]{2,1,0:T(8,128)S(1)} %pad_maximum_fusion.2.refs_1_, ...), custom_call_target="tpu_custom_call" | custom-call | flops 6442450944 | bytes 20971520 | tf_op jit(solution)/shard_map/pallas_call | solution.py:151
  91.1 9.8 %shard_map.83 = (f32[4,64,768]{2,1,0:T(8,128)S(1)}, f32[4,64,768]{2,1,0:T(8,128)S(1)}, f32[4,64,512]{2,1,0:T(8,128)S(1)}) custom-call(s32[24]{0:T(128)S(1)} %fusion.3.tbl, bf16[2,8,64,2048]{3,2,1,0:T(8,128)(2,1)S(1)} %get-tuple-element.84.refs_0_, bf16[2048,1024]{1,0:T(8,128)(2,1)S(1)} %get-tuple-element.146.refs_6_.refs_1_, ...), custom_call_target="tpu_custom_call" | custom-call | flops 6442450944 | bytes 20971520 | tf_op jit(solution)/shard_map/pallas_call | solution.py:151
  101.1 4.0 %collective-permute-start.12 = (f32[4,64,768]{2,1,0:T(8,128)S(1)}, f32[4,64,768]{2,1,0:T(8,128)S(1)}, u32[]{:S(2)}, u32[]{:S(2)}) collective-permute-start(f32[4,64,768]{2,1,0:T(8,128)S(1)} %get-tuple-element.87), channel_id=1, source_target_pairs={{0,12},{1,13},{2,14},{3,15},{4,8},{5,9},{6,10},{7,11},{8,4},{9,5},... | collective-permute-start | bytes 2359304 | tf_op jit(solution)/shard_map/ppermute | solution.py:77
  105.5 10.6 %shard_map.85 = (f32[4,64,768]{2,1,0:T(8,128)S(1)}, f32[4,64,768]{2,1,0:T(8,128)S(1)}, f32[4,64,512]{2,1,0:T(8,128)S(1)}, bf16[2,8,64,2048]{3,2,1,0:T(8,128)(2,1)S(1)}) custom-call(s32[24]{0:T(128)S(1)} %fusion.3.tbl, f32[4,64,768]{2,1,0:T(8,128)S(1)} %pad_maximum_fusion.1.refs_0_, f32[4,64,640]{2,1,0:T(8,128)S(1)} %pad_maximum_fusion.4.refs_1_, ...), custom_call_target="tpu_custom_call" | custom-call | flops 6442450944 | bytes 20971520 | tf_op jit(solution)/shard_map/pallas_call | solution.py:151
  116.1 3.6 %collective-permute-done.21 = f32[2048]{0:T(1024)S(1)} collective-permute-done((f32[2048]{0:T(1024)S(1)}, f32[2048]{0:T(1024)S(1)}, u32[]{:S(2)}, u32[]{:S(2)}) %collective-permute-start.21) | collective-permute-done | bytes 8224 | tf_op jit(solution)/shard_map/ppermute | solution.py:77
  119.8 3.2 %collective-permute-start.40 = (f32[4,64,768]{2,1,0:T(8,128)S(1)}, f32[4,64,768]{2,1,0:T(8,128)S(1)}, u32[]{:S(2)}, u32[]{:S(2)}) collective-permute-start(f32[4,64,768]{2,1,0:T(8,128)S(1)} %get-tuple-element.120), channel_id=1, source_target_pairs={{0,12},{1,13},{2,14},{3,15},{4,8},{5,9},{6,10},{7,11},{8,4},{9,5},... | collective-permute-start | bytes 2359304 | tf_op jit(solution)/shard_map/ppermute | solution.py:77
  123.0 9.8 %shard_map.86 = (f32[4,64,768]{2,1,0:T(8,128)S(1)}, f32[4,64,768]{2,1,0:T(8,128)S(1)}, f32[4,64,512]{2,1,0:T(8,128)S(1)}) custom-call(s32[24]{0:T(128)S(1)} %fusion.3.tbl, bf16[2,8,64,2048]{3,2,1,0:T(8,128)(2,1)S(1)} %get-tuple-element.117.refs_0_, bf16[2048,1024]{1,0:T(8,128)(2,1)S(1)} %get-tuple-element.146.refs_6_.refs_1_, ...), custom_call_target="tpu_custom_call" | custom-call | flops 6442450944 | bytes 20971520 | tf_op jit(solution)/shard_map/pallas_call | solution.py:151
  135.2 12.5 %collective-permute-done.41 = f32[4,64,512]{2,1,0:T(8,128)S(1)} collective-permute-done((f32[4,64,512]{2,1,0:T(8,128)S(1)}, f32[4,64,512]{2,1,0:T(8,128)S(1)}, u32[]{:S(2)}, u32[]{:S(2)}) %collective-permute-start.41) | collective-permute-done | bytes 524320 | tf_op jit(solution)/shard_map/ppermute | solution.py:77
  150.1 8.8 %collective-permute-done.15 = f32[2,64,768]{2,1,0:T(8,128)S(1)} collective-permute-done((f32[2,64,768]{2,1,0:T(8,128)S(1)}, f32[2,64,768]{2,1,0:T(8,128)S(1)}, u32[]{:S(2)}, u32[]{:S(2)}) %collective-permute-start.15) | collective-permute-done | bytes 393248 | tf_op jit(solution)/shard_map/ppermute | solution.py:77
  159.0 3.3 %collective-permute-start.19 = (f32[1,64,512]{2,1,0:T(8,128)S(1)}, f32[1,64,512]{2,1,0:T(8,128)S(1)}, u32[]{:S(2)}, u32[]{:S(2)}) collective-permute-start(f32[1,64,512]{2,1,0:T(8,128)S(1)} %get-tuple-element.155), channel_id=1, source_target_pairs={{0,12},{1,13},{2,14},{3,15},{4,8},{5,9},{6,10},{7,11},{8,4},{9,5},... | collective-permute-start | bytes 393224 | tf_op jit(solution)/shard_map/ppermute | solution.py:77
  163.9 4.0 %collective-permute-done.42 = f32[2,64,768]{2,1,0:T(8,128)S(1)} collective-permute-done((f32[2,64,768]{2,1,0:T(8,128)S(1)}, f32[2,64,768]{2,1,0:T(8,128)S(1)}, u32[]{:S(2)}, u32[]{:S(2)}) %collective-permute-start.42) | collective-permute-done | bytes 393248 | tf_op jit(solution)/shard_map/ppermute | solution.py:77
  176.9 3.5 %collective-permute-start.26 = (f32[128,128]{1,0:T(8,128)S(1)}, f32[128,128]{1,0:T(8,128)S(1)}, u32[]{:S(2)}, u32[]{:S(2)}) collective-permute-start(f32[128,128]{1,0:T(8,128)S(1)} %get-tuple-element.104), channel_id=1, source_target_pairs={{0,64},{1,65},{2,66},{3,67},{4,68},{5,69},{6,70},{7,71},{8,72},{9,... | collective-permute-start | bytes 196616 | tf_op jit(solution)/shard_map/ppermute | solution.py:77
  182.8 7.1 %collective-permute-start.28 = (f32[128,128]{1,0:T(8,128)S(1)}, f32[128,128]{1,0:T(8,128)S(1)}, u32[]{:S(2)}, u32[]{:S(2)}) collective-permute-start(f32[128,128]{1,0:T(8,128)S(1)} %get-tuple-element.106), channel_id=1, source_target_pairs={{0,96},{1,97},{2,98},{3,99},{4,100},{5,101},{6,102},{7,103},{8,104... | collective-permute-start | bytes 196616 | tf_op jit(solution)/shard_map/ppermute | solution.py:77
  190.0 4.3 %collective-permute-start.49 = (f32[128,128]{1,0:T(8,128)S(1)}, f32[128,128]{1,0:T(8,128)S(1)}, u32[]{:S(2)}, u32[]{:S(2)}) collective-permute-start(f32[128,128]{1,0:T(8,128)S(1)} %get-tuple-element.135), channel_id=1, source_target_pairs={{0,32},{1,33},{2,34},{3,35},{4,36},{5,37},{6,38},{7,39},{8,40},{9,... | collective-permute-start | bytes 196616 | tf_op jit(solution)/shard_map/ppermute | solution.py:77
  194.7 3.0 %collective-permute-start.51 = (f32[128,128]{1,0:T(8,128)S(1)}, f32[128,128]{1,0:T(8,128)S(1)}, u32[]{:S(2)}, u32[]{:S(2)}) collective-permute-start(f32[128,128]{1,0:T(8,128)S(1)} %get-tuple-element.137), channel_id=1, source_target_pairs={{0,64},{1,65},{2,66},{3,67},{4,68},{5,69},{6,70},{7,71},{8,72},{9,... | collective-permute-start | bytes 196616 | tf_op jit(solution)/shard_map/ppermute | solution.py:77
  197.8 6.9 %collective-permute-start.53 = (f32[128,128]{1,0:T(8,128)S(1)}, f32[128,128]{1,0:T(8,128)S(1)}, u32[]{:S(2)}, u32[]{:S(2)}) collective-permute-start(f32[128,128]{1,0:T(8,128)S(1)} %get-tuple-element.139), channel_id=1, source_target_pairs={{0,96},{1,97},{2,98},{3,99},{4,100},{5,101},{6,102},{7,103},{8,104... | collective-permute-start | bytes 196616 | tf_op jit(solution)/shard_map/ppermute | solution.py:77
  204.8 2.8 %collective-permute-done.53 = f32[128,128]{1,0:T(8,128)S(1)} collective-permute-done((f32[128,128]{1,0:T(8,128)S(1)}, f32[128,128]{1,0:T(8,128)S(1)}, u32[]{:S(2)}, u32[]{:S(2)}) %collective-permute-start.53) | collective-permute-done | bytes 65568 | tf_op jit(solution)/shard_map/ppermute | solution.py:77
  207.6 4.9 %collective-permute-done.54 = f32[128,128]{1,0:T(8,128)S(1)} collective-permute-done((f32[128,128]{1,0:T(8,128)S(1)}, f32[128,128]{1,0:T(8,128)S(1)}, u32[]{:S(2)}, u32[]{:S(2)}) %collective-permute-start.54) | collective-permute-done | bytes 65568 | tf_op jit(solution)/shard_map/ppermute | solution.py:77
  (136 shorter events, 45.3 us)
Async XLA Ops:
  3.1 71.1 %collective-permute-start.10 = (f32[2048,1024]{1,0:T(8,128)}, f32[2048,1024]{1,0:T(8,128)}, u32[]{:S(2)}, u32[]{:S(2)}) collective-permute-start(f32[2048,1024]{1,0:T(8,128)} %param.9), channel_id=1, source_target_pairs={{0,1},{1,0},{2,3},{3,2},{4,5},{5,4},{6,7},{7,6},{8,9},{9,8},{10,11... | collective-permute-start | bytes 25165832 | tf_op jit(solution)/shard_map/ppermute | solution.py:77
  6.0 14.9 %collective-permute-start.30 = (f32[1,64,768]{2,1,0:T(8,128)S(1)}, f32[1,64,768]{2,1,0:T(8,128)S(1)}, u32[]{:S(2)}, u32[]{:S(2)}) collective-permute-start(f32[1,64,768]{2,1,0:T(8,128)S(1)} %get-tuple-element.160), channel_id=1, source_target_pairs={{0,16},{1,17},{2,18},{3,19},{4,20},{5,21},{6,22},{7,23},{8,24},{9,... | collective-permute-start | bytes 589832 | tf_op jit(solution)/shard_map/ppermute | solution.py:77
  18.3 16.5 %collective-permute-start.4 = (f32[2,64,768]{2,1,0:T(8,128)S(1)}, f32[2,64,768]{2,1,0:T(8,128)S(1)}, u32[]{:S(2)}, u32[]{:S(2)}) collective-permute-start(f32[2,64,768]{2,1,0:T(8,128)S(1)} %pad_maximum_fusion.6), channel_id=1, source_target_pairs={{0,48},{1,49},{2,50},{3,51},{4,52},{5,53},{6,54},{7,55},{8,56},{9,... | collective-permute-start | bytes 1179656 | tf_op jit(solution)/shard_map/ppermute | solution.py:77
  22.2 15.1 %collective-permute-start.35 = (f32[2,64,640]{2,1,0:T(8,128)S(1)}, f32[2,64,640]{2,1,0:T(8,128)S(1)}, u32[]{:S(2)}, u32[]{:S(2)}) collective-permute-start(f32[2,64,640]{2,1,0:T(8,128)S(1)} %pad_maximum_fusion.11), channel_id=1, source_target_pairs={{0,16},{1,17},{2,18},{3,19},{4,20},{5,21},{6,22},{7,23},{8,24},{9,... | collective-permute-start | bytes 983048 | tf_op jit(solution)/shard_map/ppermute | solution.py:77
  30.4 11.3 %collective-permute-start.34 = (f32[2,64,640]{2,1,0:T(8,128)S(1)}, f32[2,64,640]{2,1,0:T(8,128)S(1)}, u32[]{:S(2)}, u32[]{:S(2)}) collective-permute-start(f32[2,64,640]{2,1,0:T(8,128)S(1)} %pad_maximum_fusion.10), channel_id=1, source_target_pairs={{0,64},{1,65},{2,66},{3,67},{4,68},{5,69},{6,70},{7,71},{8,72},{9,... | collective-permute-start | bytes 983048 | tf_op jit(solution)/shard_map/ppermute | solution.py:77
  32.1 13.2 %collective-permute-start.33 = (f32[2,64,768]{2,1,0:T(8,128)S(1)}, f32[2,64,768]{2,1,0:T(8,128)S(1)}, u32[]{:S(2)}, u32[]{:S(2)}) collective-permute-start(f32[2,64,768]{2,1,0:T(8,128)S(1)} %pad_maximum_fusion.7), channel_id=1, source_target_pairs={{0,48},{1,49},{2,50},{3,51},{4,52},{5,53},{6,54},{7,55},{8,56},{9,... | collective-permute-start | bytes 1179656 | tf_op jit(solution)/shard_map/ppermute | solution.py:77
  34.8 15.4 %collective-permute-start.8 = (f32[4,64,640]{2,1,0:T(8,128)S(1)}, f32[4,64,640]{2,1,0:T(8,128)S(1)}, u32[]{:S(2)}, u32[]{:S(2)}) collective-permute-start(f32[4,64,640]{2,1,0:T(8,128)S(1)} %pad_maximum_fusion.2.refs_1_), channel_id=1, source_target_pairs={{0,16},{1,17},{2,18},{3,19},{4,20},{5,21},{6,22},{7,23},{8,24},{9,... | collective-permute-start | bytes 1966088 | tf_op jit(solution)/shard_map/ppermute | solution.py:77
  37.3 22.0 %collective-permute-start.9 = (f32[4,64,640]{2,1,0:T(8,128)S(1)}, f32[4,64,640]{2,1,0:T(8,128)S(1)}, u32[]{:S(2)}, u32[]{:S(2)}) collective-permute-start(f32[4,64,640]{2,1,0:T(8,128)S(1)} %pad_maximum_fusion.3.refs_2_), channel_id=1, source_target_pairs={{0,48},{1,49},{2,50},{3,51},{4,52},{5,53},{6,54},{7,55},{8,56},{9,... | collective-permute-start | bytes 1966088 | tf_op jit(solution)/shard_map/ppermute | solution.py:77
  41.8 22.0 %collective-permute-start.7 = (f32[4,64,768]{2,1,0:T(8,128)S(1)}, f32[4,64,768]{2,1,0:T(8,128)S(1)}, u32[]{:S(2)}, u32[]{:S(2)}) collective-permute-start(f32[4,64,768]{2,1,0:T(8,128)S(1)} %pad_maximum_fusion.refs_0_), channel_id=1, source_target_pairs={{0,64},{1,65},{2,66},{3,67},{4,68},{5,69},{6,70},{7,71},{8,72},{9,... | collective-permute-start | bytes 2359304 | tf_op jit(solution)/shard_map/ppermute | solution.py:77
  45.3 28.9 %collective-permute-start.36 = (f32[4,64,768]{2,1,0:T(8,128)S(1)}, f32[4,64,768]{2,1,0:T(8,128)S(1)}, u32[]{:S(2)}, u32[]{:S(2)}) collective-permute-start(f32[4,64,768]{2,1,0:T(8,128)S(1)} %pad_maximum_fusion.1.refs_0_), channel_id=1, source_target_pairs={{0,64},{1,65},{2,66},{3,67},{4,68},{5,69},{6,70},{7,71},{8,72},{9,... | collective-permute-start | bytes 2359304 | tf_op jit(solution)/shard_map/ppermute | solution.py:77
  50.2 20.6 %collective-permute-start.38 = (f32[4,64,640]{2,1,0:T(8,128)S(1)}, f32[4,64,640]{2,1,0:T(8,128)S(1)}, u32[]{:S(2)}, u32[]{:S(2)}) collective-permute-start(f32[4,64,640]{2,1,0:T(8,128)S(1)} %pad_maximum_fusion.5.refs_2_), channel_id=1, source_target_pairs={{0,48},{1,49},{2,50},{3,51},{4,52},{5,53},{6,54},{7,55},{8,56},{9,... | collective-permute-start | bytes 1966088 | tf_op jit(solution)/shard_map/ppermute | solution.py:77
  59.3 11.6 %collective-permute-start.37 = (f32[4,64,640]{2,1,0:T(8,128)S(1)}, f32[4,64,640]{2,1,0:T(8,128)S(1)}, u32[]{:S(2)}, u32[]{:S(2)}) collective-permute-start(f32[4,64,640]{2,1,0:T(8,128)S(1)} %pad_maximum_fusion.4.refs_1_), channel_id=1, source_target_pairs={{0,16},{1,17},{2,18},{3,19},{4,20},{5,21},{6,22},{7,23},{8,24},{9,... | collective-permute-start | bytes 1966088 | tf_op jit(solution)/shard_map/ppermute | solution.py:77
  78.5 26.9 %collective-permute-start.20 = (f32[2048]{0:T(1024)S(1)}, f32[2048]{0:T(1024)S(1)}, u32[]{:S(2)}, u32[]{:S(2)}) collective-permute-start(f32[2048]{0:T(1024)S(1)} %add.176), channel_id=1, source_target_pairs={{0,4},{1,5},{2,6},{3,7},{4,0},{5,1},{6,2},{7,3},{8,12},{9,13},{10,... | collective-permute-start | bytes 24584 | tf_op jit(solution)/shard_map/ppermute | solution.py:77
  100.9 32.0 %collective-permute-start.11 = (f32[4,64,768]{2,1,0:T(8,128)S(1)}, f32[4,64,768]{2,1,0:T(8,128)S(1)}, u32[]{:S(2)}, u32[]{:S(2)}) collective-permute-start(f32[4,64,768]{2,1,0:T(8,128)S(1)} %get-tuple-element.86), channel_id=1, source_target_pairs={{0,4},{1,5},{2,6},{3,7},{4,0},{5,1},{6,2},{7,3},{8,12},{9,13},{10,... | collective-permute-start | bytes 2359304 | tf_op jit(solution)/shard_map/ppermute | solution.py:77
  101.1 33.8 %collective-permute-start.12 = (f32[4,64,768]{2,1,0:T(8,128)S(1)}, f32[4,64,768]{2,1,0:T(8,128)S(1)}, u32[]{:S(2)}, u32[]{:S(2)}) collective-permute-start(f32[4,64,768]{2,1,0:T(8,128)S(1)} %get-tuple-element.87), channel_id=1, source_target_pairs={{0,12},{1,13},{2,14},{3,15},{4,8},{5,9},{6,10},{7,11},{8,4},{9,5},... | collective-permute-start | bytes 2359304 | tf_op jit(solution)/shard_map/ppermute | solution.py:77
  105.1 27.7 %collective-permute-start.13 = (f32[4,64,512]{2,1,0:T(8,128)S(1)}, f32[4,64,512]{2,1,0:T(8,128)S(1)}, u32[]{:S(2)}, u32[]{:S(2)}) collective-permute-start(f32[4,64,512]{2,1,0:T(8,128)S(1)} %get-tuple-element.88), channel_id=1, source_target_pairs={{0,2},{1,3},{2,0},{3,1},{4,6},{5,7},{6,4},{7,5},{8,10},{9,11},{10,... | collective-permute-start | bytes 1572872 | tf_op jit(solution)/shard_map/ppermute | solution.py:77
  105.4 14.3 %collective-permute-start.21 = (f32[2048]{0:T(1024)S(1)}, f32[2048]{0:T(1024)S(1)}, u32[]{:S(2)}, u32[]{:S(2)}) collective-permute-start(f32[2048]{0:T(1024)S(1)} %add.177), channel_id=1, source_target_pairs={{0,12},{1,13},{2,14},{3,15},{4,8},{5,9},{6,10},{7,11},{8,4},{9,5},... | collective-permute-start | bytes 24584 | tf_op jit(solution)/shard_map/ppermute | solution.py:77
  116.1 31.7 %collective-permute-start.39 = (f32[4,64,768]{2,1,0:T(8,128)S(1)}, f32[4,64,768]{2,1,0:T(8,128)S(1)}, u32[]{:S(2)}, u32[]{:S(2)}) collective-permute-start(f32[4,64,768]{2,1,0:T(8,128)S(1)} %get-tuple-element.119), channel_id=1, source_target_pairs={{0,4},{1,5},{2,6},{3,7},{4,0},{5,1},{6,2},{7,3},{8,12},{9,13},{10,... | collective-permute-start | bytes 2359304 | tf_op jit(solution)/shard_map/ppermute | solution.py:77
  119.8 28.0 %collective-permute-start.40 = (f32[4,64,768]{2,1,0:T(8,128)S(1)}, f32[4,64,768]{2,1,0:T(8,128)S(1)}, u32[]{:S(2)}, u32[]{:S(2)}) collective-permute-start(f32[4,64,768]{2,1,0:T(8,128)S(1)} %get-tuple-element.120), channel_id=1, source_target_pairs={{0,12},{1,13},{2,14},{3,15},{4,8},{5,9},{6,10},{7,11},{8,4},{9,5},... | collective-permute-start | bytes 2359304 | tf_op jit(solution)/shard_map/ppermute | solution.py:77
  132.8 14.9 %collective-permute-start.41 = (f32[4,64,512]{2,1,0:T(8,128)S(1)}, f32[4,64,512]{2,1,0:T(8,128)S(1)}, u32[]{:S(2)}, u32[]{:S(2)}) collective-permute-start(f32[4,64,512]{2,1,0:T(8,128)S(1)} %get-tuple-element.121), channel_id=1, source_target_pairs={{0,2},{1,3},{2,0},{3,1},{4,6},{5,7},{6,4},{7,5},{8,10},{9,11},{10,... | collective-permute-start | bytes 1572872 | tf_op jit(solution)/shard_map/ppermute | solution.py:77
  132.9 35.3 %collective-permute-start.22 = (f32[2048]{0:T(1024)S(1)}, f32[2048]{0:T(1024)S(1)}, u32[]{:S(2)}, u32[]{:S(2)}) collective-permute-start(f32[2048]{0:T(1024)S(1)} %add.178), channel_id=1, source_target_pairs={{0,2},{1,3},{2,0},{3,1},{4,6},{5,7},{6,4},{7,5},{8,10},{9,11},{10,... | collective-permute-start | bytes 24584 | tf_op jit(solution)/shard_map/ppermute | solution.py:77
  135.0 13.0 %collective-permute-start.16 = (f32[2,64,512]{2,1,0:T(8,128)S(1)}, f32[2,64,512]{2,1,0:T(8,128)S(1)}, u32[]{:S(2)}, u32[]{:S(2)}) collective-permute-start(f32[2,64,512]{2,1,0:T(8,128)S(1)} %slice_add_fusion.5), channel_id=1, source_target_pairs={{0,4},{1,5},{2,6},{3,7},{4,0},{5,1},{6,2},{7,3},{8,12},{9,13},{10,... | collective-permute-start | bytes 786440 | tf_op jit(solution)/shard_map/ppermute | solution.py:77
  147.7 11.2 %collective-permute-start.15 = (f32[2,64,768]{2,1,0:T(8,128)S(1)}, f32[2,64,768]{2,1,0:T(8,128)S(1)}, u32[]{:S(2)}, u32[]{:S(2)}) collective-permute-start(f32[2,64,768]{2,1,0:T(8,128)S(1)} %slice_add_fusion.2), channel_id=1, source_target_pairs={{0,2},{1,3},{2,0},{3,1},{4,6},{5,7},{6,4},{7,5},{8,10},{9,11},{10,... | collective-permute-start | bytes 1179656 | tf_op jit(solution)/shard_map/ppermute | solution.py:77
  147.7 11.2 %collective-permute-start.14 = (f32[2,64,768]{2,1,0:T(8,128)S(1)}, f32[2,64,768]{2,1,0:T(8,128)S(1)}, u32[]{:S(2)}, u32[]{:S(2)}) collective-permute-start(f32[2,64,768]{2,1,0:T(8,128)S(1)} %slice_add_fusion.3), channel_id=1, source_target_pairs={{0,12},{1,13},{2,14},{3,15},{4,8},{5,9},{6,10},{7,11},{8,4},{9,5},... | collective-permute-start | bytes 1179656 | tf_op jit(solution)/shard_map/ppermute | solution.py:77
  147.8 14.7 %collective-permute-start.44 = (f32[2,64,512]{2,1,0:T(8,128)S(1)}, f32[2,64,512]{2,1,0:T(8,128)S(1)}, u32[]{:S(2)}, u32[]{:S(2)}) collective-permute-start(f32[2,64,512]{2,1,0:T(8,128)S(1)} %slice_add_fusion.4), channel_id=1, source_target_pairs={{0,4},{1,5},{2,6},{3,7},{4,0},{5,1},{6,2},{7,3},{8,12},{9,13},{10,... | collective-permute-start | bytes 786440 | tf_op jit(solution)/shard_map/ppermute | solution.py:77
  148.0 15.9 %collective-permute-start.43 = (f32[2,64,768]{2,1,0:T(8,128)S(1)}, f32[2,64,768]{2,1,0:T(8,128)S(1)}, u32[]{:S(2)}, u32[]{:S(2)}) collective-permute-start(f32[2,64,768]{2,1,0:T(8,128)S(1)} %slice_add_fusion), channel_id=1, source_target_pairs={{0,2},{1,3},{2,0},{3,1},{4,6},{5,7},{6,4},{7,5},{8,10},{9,11},{10,... | collective-permute-start | bytes 1179656 | tf_op jit(solution)/shard_map/ppermute | solution.py:77
  172.8 17.1 %collective-permute-start.24 = (f32[128,128]{1,0:T(8,128)S(1)}, f32[128,128]{1,0:T(8,128)S(1)}, u32[]{:S(2)}, u32[]{:S(2)}) collective-permute-start(f32[128,128]{1,0:T(8,128)S(1)} %get-tuple-element.102), channel_id=1, source_target_pairs={{0,32},{1,33},{2,34},{3,35},{4,36},{5,37},{6,38},{7,39},{8,40},{9,... | collective-permute-start | bytes 196616 | tf_op jit(solution)/shard_map/ppermute | solution.py:77
  175.1 14.8 %collective-permute-start.25 = (f32[128,128]{1,0:T(8,128)S(1)}, f32[128,128]{1,0:T(8,128)S(1)}, u32[]{:S(2)}, u32[]{:S(2)}) collective-permute-start(f32[128,128]{1,0:T(8,128)S(1)} %get-tuple-element.103), channel_id=1, source_target_pairs={{0,48},{1,49},{2,50},{3,51},{4,52},{5,53},{6,54},{7,55},{8,56},{9,... | collective-permute-start | bytes 196616 | tf_op jit(solution)/shard_map/ppermute | solution.py:77
  176.9 13.1 %collective-permute-start.26 = (f32[128,128]{1,0:T(8,128)S(1)}, f32[128,128]{1,0:T(8,128)S(1)}, u32[]{:S(2)}, u32[]{:S(2)}) collective-permute-start(f32[128,128]{1,0:T(8,128)S(1)} %get-tuple-element.104), channel_id=1, source_target_pairs={{0,64},{1,65},{2,66},{3,67},{4,68},{5,69},{6,70},{7,71},{8,72},{9,... | collective-permute-start | bytes 196616 | tf_op jit(solution)/shard_map/ppermute | solution.py:77
  180.4 13.9 %collective-permute-start.27 = (f32[128,128]{1,0:T(8,128)S(1)}, f32[128,128]{1,0:T(8,128)S(1)}, u32[]{:S(2)}, u32[]{:S(2)}) collective-permute-start(f32[128,128]{1,0:T(8,128)S(1)} %get-tuple-element.105), channel_id=1, source_target_pairs={{0,80},{1,81},{2,82},{3,83},{4,84},{5,85},{6,86},{7,87},{8,88},{9,... | collective-permute-start | bytes 196616 | tf_op jit(solution)/shard_map/ppermute | solution.py:77
  182.8 11.9 %collective-permute-start.28 = (f32[128,128]{1,0:T(8,128)S(1)}, f32[128,128]{1,0:T(8,128)S(1)}, u32[]{:S(2)}, u32[]{:S(2)}) collective-permute-start(f32[128,128]{1,0:T(8,128)S(1)} %get-tuple-element.106), channel_id=1, source_target_pairs={{0,96},{1,97},{2,98},{3,99},{4,100},{5,101},{6,102},{7,103},{8,104... | collective-permute-start | bytes 196616 | tf_op jit(solution)/shard_map/ppermute | solution.py:77
  190.0 14.7 %collective-permute-start.49 = (f32[128,128]{1,0:T(8,128)S(1)}, f32[128,128]{1,0:T(8,128)S(1)}, u32[]{:S(2)}, u32[]{:S(2)}) collective-permute-start(f32[128,128]{1,0:T(8,128)S(1)} %get-tuple-element.135), channel_id=1, source_target_pairs={{0,32},{1,33},{2,34},{3,35},{4,36},{5,37},{6,38},{7,39},{8,40},{9,... | collective-permute-start | bytes 196616 | tf_op jit(solution)/shard_map/ppermute | solution.py:77
  (28 other events, 420.3 us)

commit v3 on v2

--- a/solution.py
+++ b/solution.py
@@ -44,7 +44,6 @@
     perm(lambda yh, x, z, yl, c: (yh, x, 3 - z, yl, c)),
     perm(lambda yh, x, z, yl, c: (yh, x, z, 1 - yl, c)),
 )
-ROW_XOR = [[(i, i ^ (k * 16)) for i in range(128)] for k in range(8)]
 
 
 def gray(v):
@@ -168,8 +167,8 @@
     return res[:3], res[3:]
 
 
-def tail_kernel(row, *refs):
-    pieces, cells, outs, both = refs[:6], refs[6], refs[7:15], refs[15]
+def tail_kernel(*refs):
+    pieces, cells, out, both = refs[:6], refs[6], refs[-2], refs[-1]
     for q in range(3):
         cols = pl.ds(COFF[q], COLS[q])
         mixed = pieces[q][0] + pieces[3 + q][0]
@@ -181,34 +180,40 @@
             both[pl.ds(k * ROWS, ROWS), cols] = h
             both[pl.ds((2 + k) * ROWS, ROWS), cols] = (v - h.astype(jnp.float32)).astype(jnp.bfloat16)
     entity = cells[pl.ds(5, 1), :].astype(jnp.int32)
-    for k in range(8):
-        lines = lax.broadcasted_iota(jnp.int32, (128, 2048), 0) + (row[0] ^ k) * 128
+    before = len(refs) == 10
+    for g in range(8):
+        lines = lax.broadcasted_iota(jnp.int32, (128, 2048), 0) + g * 128
         onehot = jnp.where(lines == entity, 1.0, 0.0).astype(jnp.bfloat16)
         sums = lax.dot_general(
             both[...], onehot, (((1,), (1,)), ((), ())), preferred_element_type=jnp.float32
         )
-        outs[k][...] = sums[: 2 * ROWS] + sums[2 * ROWS :]
-
-
-def tail(row, held, third, cells):
+        sums = sums[: 2 * ROWS] + sums[2 * ROWS :]
+        if before:
+            out[g, pl.ds(0, 2 * ROWS), :] = refs[7][g]
+            out[g, pl.ds(2 * ROWS, 2 * ROWS), :] = sums
+        else:
+            out[g] = sums
+
+
+def tail(held, third, cells, before):
     def at(shape):
-        return pl.BlockSpec(shape, lambda i, r: (0,) * len(shape))
-
+        return pl.BlockSpec(shape, lambda i: (0,) * len(shape))
+
+    rows = 2 * ROWS * (1 + len(before))
     return pl.pallas_call(
         tail_kernel,
-        out_shape=[jax.ShapeDtypeStruct((2 * ROWS, 128), jnp.float32)] * 8,
-        grid_spec=pltpu.PrefetchScalarGridSpec(
-            num_scalar_prefetch=1,
-            grid=(1,),
-            in_specs=[at((1, ROWS, COLS[q])) for q in range(3)] * 2 + [at((6, 2048))],
-            out_specs=[at((2 * ROWS, 128))] * 8,
-            scratch_shapes=[pltpu.VMEM((4 * ROWS, 2048), jnp.bfloat16)],
-        ),
+        out_shape=jax.ShapeDtypeStruct((8, rows, 128), jnp.float32),
+        grid=(1,),
+        in_specs=[at((1, ROWS, COLS[q])) for q in range(3)] * 2
+        + [at((6, 2048))]
+        + [at((8, 2 * ROWS, 128))] * len(before),
+        out_specs=at((8, rows, 128)),
+        scratch_shapes=[pltpu.VMEM((4 * ROWS, 2048), jnp.bfloat16)],
         cost_estimate=pl.CostEstimate(
             flops=2 * 4 * ROWS * 2048 * ENT, bytes_accessed=5 * ROWS * 2048 * 4, transcendentals=ROWS * 2048
         ),
         compiler_params=pltpu.CompilerParams(vmem_limit_bytes=16 * 2**20),
-    )(row.reshape(1), *held, *third, cells)
+    )(*held, *third, cells, *before)
 
 
 def step(normals, factor, cell_entity, scale, volatility, retention, limit):
@@ -257,7 +262,7 @@
             cell_entity.astype(jnp.float32),
         ]
     )
-    results = []
+    sums = ()
     for c in range(CHUNKS):
         sent, parts = mm(0, tbl, (*gathered[c], *last[c]), factors)
         came = lax.optimization_barrier([permute(sent[q], COL_DIMS[q]) for q in range(3)])
@@ -267,12 +272,10 @@
             [permute(kept[q][2:3] + came[q][2:3] + second[q][:1], COL_DIMS[(q + 2) % 3]) for q in range(3)]
         )
         held = [kept[q][3:] + came[q][3:] + second[q][1:] for q in range(3)]
-        sums = tail(row, held, third, cells)
-        total = sums[0]
-        for k in range(1, 8):
-            total = total + permute(sums[k], ROW_XOR[k])
-        results.append(total.reshape(2, ROWS, 128))
-    return jnp.concatenate(results, axis=1)
+        sums = (tail(held, third, cells, sums),)
+    parts = lax.all_to_all(sums[0], "row", split_axis=0, concat_axis=0, tiled=True)
+    total = jnp.sum(parts, axis=0).reshape(CHUNKS, 2, ROWS, 128)
+    return jnp.swapaxes(total, 0, 1).reshape(2, 128, 128)
 
 
 def solution(mesh):

time: 213 us -> 205 us (0.962); the launches traced: 213 us -> 203 us
  starting transfers between devices: 80.1 us -> 49.9 us
  blocking collectives: 0 us -> 19.7 us
    ppermute x55 -> x41, starting transfers between devices: 80.1 us -> 49.9 us  [permute(): return lax.ppermute(x, BOTH, pairs)]
    all_to_all x0 -> x1, blocking collectives: none -> 19.7 us  [step(): lax.all_to_all(sums[0], 'row', split_axis=0, concat_axis=0, tiled=True)]
    ppermute x55 -> x41, waiting for transfers between devices: 74.9 us -> 74.9 us  [permute(): return lax.ppermute(x, BOTH, pairs)]
  transfers between devices with their start and end apart: 55 -> 41, of which waited for: 21 -> 20; matrix products, arithmetic and copies ran while one was open for 3% -> 3% of each run, Pallas kernels for 21% -> 20%
where the time goes in v3:
time: 205 us; the launch traced here: 203 us
  waiting for transfers between devices  74.9 us (37%)
  starting transfers between devices  49.9 us (24%)
  Pallas kernels  45.4 us (22%)
  blocking collectives  19.7 us (10%)
  other arithmetic  7.87 us (4%)
  local copies, waits for them, and re-layouts  4.53 us (2%)
    ppermute x41, waiting for transfers between devices, permute(): return lax.ppermute(x, BOTH, pairs)  74.9 us
    ppermute x41, starting transfers between devices, permute(): return lax.ppermute(x, BOTH, pairs)  49.9 us
    pallas_call x4, Pallas kernels, mm(): pl.pallas_call(functools.partial(mm_kernel, half), out_shape=shapes, grid...  40.8 us
    all_to_all x1, blocking collectives, step(): lax.all_to_all(sums[0], 'row', split_axis=0, concat_axis=0, tiled=True)  19.7 us
    pallas_call x2, Pallas kernels, tail(): pl.pallas_call(tail_kernel, out_shape=jax.ShapeDtypeStruct((8, rows, 128)...  4.66 us
    reduce_sum x1, other arithmetic, step(): far_norms = jnp.sum(far_factor * far_factor, axis=1)  4.26 us
  transfers between devices with their start and end apart: 41, of which 20 were waited for; matrix products, arithmetic and copies ran while one was open for 3% of the time, Pallas kernels for 20%

profile of v3, /device:TPU:0, one launch (start us, length us, event | category | flops | bytes accessed | tf_op | source)
XLA Modules:
  0.0 202.8 jit_solution(4521461532538813777)
XLA Ops:
  7.4 2.9 %collective-permute-start.24 = (f32[1,64,640]{2,1,0:T(8,128)S(1)}, f32[1,64,640]{2,1,0:T(8,128)S(1)}, u32[]{:S(2)}, u32[]{:S(2)}) collective-permute-start(f32[1,64,640]{2,1,0:T(8,128)S(1)} %get-tuple-element.134), channel_id=1, source_target_pairs={{0,48},{1,49},{2,50},{3,51},{4,52},{5,53},{6,54},{7,55},{8,56},{9,... | collective-permute-start | bytes 491528 | tf_op jit(solution)/shard_map/ppermute | solution.py:76
  10.3 3.2 %collective-permute-start.25 = (f32[1,64,640]{2,1,0:T(8,128)S(1)}, f32[1,64,640]{2,1,0:T(8,128)S(1)}, u32[]{:S(2)}, u32[]{:S(2)}) collective-permute-start(f32[1,64,640]{2,1,0:T(8,128)S(1)} %get-tuple-element.131), channel_id=1, source_target_pairs={{0,64},{1,65},{2,66},{3,67},{4,68},{5,69},{6,70},{7,71},{8,72},{9,... | collective-permute-start | bytes 491528 | tf_op jit(solution)/shard_map/ppermute | solution.py:76
  15.0 3.2 %collective-permute-start.3 = (f32[1,64,640]{2,1,0:T(8,128)S(1)}, f32[1,64,640]{2,1,0:T(8,128)S(1)}, u32[]{:S(2)}, u32[]{:S(2)}) collective-permute-start(f32[1,64,640]{2,1,0:T(8,128)S(1)} %get-tuple-element.132), channel_id=1, source_target_pairs={{0,64},{1,65},{2,66},{3,67},{4,68},{5,69},{6,70},{7,71},{8,72},{9,... | collective-permute-start | bytes 491528 | tf_op jit(solution)/shard_map/ppermute | solution.py:76
  18.3 2.5 %collective-permute-start.26 = (f32[2,64,768]{2,1,0:T(8,128)S(1)}, f32[2,64,768]{2,1,0:T(8,128)S(1)}, u32[]{:S(2)}, u32[]{:S(2)}) collective-permute-start(f32[2,64,768]{2,1,0:T(8,128)S(1)} %pad_maximum_fusion.7), channel_id=1, source_target_pairs={{0,48},{1,49},{2,50},{3,51},{4,52},{5,53},{6,54},{7,55},{8,56},{9,... | collective-permute-start | bytes 1179656 | tf_op jit(solution)/shard_map/ppermute | solution.py:76
  23.6 6.8 %collective-permute-done.27 = f32[2,64,640]{2,1,0:T(8,128)S(1)} collective-permute-done((f32[2,64,640]{2,1,0:T(8,128)S(1)}, f32[2,64,640]{2,1,0:T(8,128)S(1)}, u32[]{:S(2)}, u32[]{:S(2)}) %collective-permute-start.27) | collective-permute-done | bytes 327712 | tf_op jit(solution)/shard_map/ppermute | solution.py:76
  32.1 2.7 %collective-permute-start.4 = (f32[2,64,768]{2,1,0:T(8,128)S(1)}, f32[2,64,768]{2,1,0:T(8,128)S(1)}, u32[]{:S(2)}, u32[]{:S(2)}) collective-permute-start(f32[2,64,768]{2,1,0:T(8,128)S(1)} %pad_maximum_fusion.6), channel_id=1, source_target_pairs={{0,48},{1,49},{2,50},{3,51},{4,52},{5,53},{6,54},{7,55},{8,56},{9,... | collective-permute-start | bytes 1179656 | tf_op jit(solution)/shard_map/ppermute | solution.py:76
  34.9 2.3 %collective-permute-done.6 = f32[2,64,640]{2,1,0:T(8,128)S(1)} collective-permute-done((f32[2,64,640]{2,1,0:T(8,128)S(1)}, f32[2,64,640]{2,1,0:T(8,128)S(1)}, u32[]{:S(2)}, u32[]{:S(2)}) %collective-permute-start.6) | collective-permute-done | bytes 327712 | tf_op jit(solution)/shard_map/ppermute | solution.py:76
  37.3 4.4 %collective-permute-start.31 = (f32[4,64,640]{2,1,0:T(8,128)S(1)}, f32[4,64,640]{2,1,0:T(8,128)S(1)}, u32[]{:S(2)}, u32[]{:S(2)}) collective-permute-start(f32[4,64,640]{2,1,0:T(8,128)S(1)} %pad_maximum_fusion.5.refs_2_), channel_id=1, source_target_pairs={{0,48},{1,49},{2,50},{3,51},{4,52},{5,53},{6,54},{7,55},{8,56},{9,... | collective-permute-start | bytes 1966088 | tf_op jit(solution)/shard_map/ppermute | solution.py:76
  42.6 2.6 %collective-permute-done.4 = f32[2,64,768]{2,1,0:T(8,128)S(1)} collective-permute-done((f32[2,64,768]{2,1,0:T(8,128)S(1)}, f32[2,64,768]{2,1,0:T(8,128)S(1)}, u32[]{:S(2)}, u32[]{:S(2)}) %collective-permute-start.4) | collective-permute-done | bytes 393248 | tf_op jit(solution)/shard_map/ppermute | solution.py:76
  45.3 2.6 %collective-permute-start.7 = (f32[4,64,768]{2,1,0:T(8,128)S(1)}, f32[4,64,768]{2,1,0:T(8,128)S(1)}, u32[]{:S(2)}, u32[]{:S(2)}) collective-permute-start(f32[4,64,768]{2,1,0:T(8,128)S(1)} %pad_maximum_fusion.refs_0_), channel_id=1, source_target_pairs={{0,64},{1,65},{2,66},{3,67},{4,68},{5,69},{6,70},{7,71},{8,72},{9,... | collective-permute-start | bytes 2359304 | tf_op jit(solution)/shard_map/ppermute | solution.py:76
  48.0 2.2 %collective-permute-done.30.refs_4_ = f32[4,64,640]{2,1,0:T(8,128)S(1)} collective-permute-done((f32[4,64,640]{2,1,0:T(8,128)S(1)}, f32[4,64,640]{2,1,0:T(8,128)S(1)}, u32[]{:S(2)}, u32[]{:S(2)}) %collective-permute-start.30) | collective-permute-done | bytes 655392 | tf_op jit(solution)/shard_map/ppermute | solution.py:76
  50.2 2.8 %collective-permute-start.9 = (f32[4,64,640]{2,1,0:T(8,128)S(1)}, f32[4,64,640]{2,1,0:T(8,128)S(1)}, u32[]{:S(2)}, u32[]{:S(2)}) collective-permute-start(f32[4,64,640]{2,1,0:T(8,128)S(1)} %pad_maximum_fusion.3.refs_2_), channel_id=1, source_target_pairs={{0,48},{1,49},{2,50},{3,51},{4,52},{5,53},{6,54},{7,55},{8,56},{9,... | collective-permute-start | bytes 1966088 | tf_op jit(solution)/shard_map/ppermute | solution.py:76
  53.0 6.3 %collective-permute-done.31.refs_5_ = f32[4,64,640]{2,1,0:T(8,128)S(1)} collective-permute-done((f32[4,64,640]{2,1,0:T(8,128)S(1)}, f32[4,64,640]{2,1,0:T(8,128)S(1)}, u32[]{:S(2)}, u32[]{:S(2)}) %collective-permute-start.31) | collective-permute-done | bytes 655392 | tf_op jit(solution)/shard_map/ppermute | solution.py:76
  63.8 7.0 %collective-permute-done.9.refs_5_ = f32[4,64,640]{2,1,0:T(8,128)S(1)} collective-permute-done((f32[4,64,640]{2,1,0:T(8,128)S(1)}, f32[4,64,640]{2,1,0:T(8,128)S(1)}, u32[]{:S(2)}, u32[]{:S(2)}) %collective-permute-start.9) | collective-permute-done | bytes 655392 | tf_op jit(solution)/shard_map/ppermute | solution.py:76
  70.9 3.3 %collective-permute-done.7.refs_3_ = f32[4,64,768]{2,1,0:T(8,128)S(1)} collective-permute-done((f32[4,64,768]{2,1,0:T(8,128)S(1)}, f32[4,64,768]{2,1,0:T(8,128)S(1)}, u32[]{:S(2)}, u32[]{:S(2)}) %collective-permute-start.7) | collective-permute-done | bytes 786464 | tf_op jit(solution)/shard_map/ppermute | solution.py:76
  74.2 4.3 %multiply_reduce_fusion = (f32[2048]{0:T(1024)S(1)}, bf16[2048,1024]{1,0:T(8,128)(2,1)S(1)}, bf16[2048,1024]{1,0:T(8,128)(2,1)S(1)}) fusion(f32[2048,1024]{1,0:T(8,128)} %collective-permute-done.10), kind=kLoop, calls=%fused_computation.6 | loop fusion | flops 12580864 | bytes 16785408 | tf_op jit(solution)/shard_map/reduce_sum | solution.py:249
  80.5 10.6 %shard_map.84 = (f32[4,64,768]{2,1,0:T(8,128)S(1)}, f32[4,64,768]{2,1,0:T(8,128)S(1)}, f32[4,64,512]{2,1,0:T(8,128)S(1)}, bf16[2,8,64,2048]{3,2,1,0:T(8,128)(2,1)S(1)}) custom-call(s32[24]{0:T(128)S(1)} %fusion.3.tbl, f32[4,64,768]{2,1,0:T(8,128)S(1)} %pad_maximum_fusion.1.refs_0_, f32[4,64,640]{2,1,0:T(8,128)S(1)} %pad_maximum_fusion.4.refs_1_, ...), custom_call_target="tpu_custom_call" | custom-call | flops 6442450944 | bytes 20971520 | tf_op jit(solution)/shard_map/pallas_call | solution.py:150
  91.1 9.8 %shard_map.85 = (f32[4,64,768]{2,1,0:T(8,128)S(1)}, f32[4,64,768]{2,1,0:T(8,128)S(1)}, f32[4,64,512]{2,1,0:T(8,128)S(1)}) custom-call(s32[24]{0:T(128)S(1)} %fusion.3.tbl, bf16[2,8,64,2048]{3,2,1,0:T(8,128)(2,1)S(1)} %get-tuple-element.93.refs_0_, bf16[2048,1024]{1,0:T(8,128)(2,1)S(1)} %get-tuple-element.114.refs_6_.refs_1_, ...), custom_call_target="tpu_custom_call" | custom-call | flops 6442450944 | bytes 20971520 | tf_op jit(solution)/shard_map/pallas_call | solution.py:150
  101.1 4.0 %collective-permute-start.33 = (f32[4,64,768]{2,1,0:T(8,128)S(1)}, f32[4,64,768]{2,1,0:T(8,128)S(1)}, u32[]{:S(2)}, u32[]{:S(2)}) collective-permute-start(f32[4,64,768]{2,1,0:T(8,128)S(1)} %get-tuple-element.96), channel_id=1, source_target_pairs={{0,12},{1,13},{2,14},{3,15},{4,8},{5,9},{6,10},{7,11},{8,4},{9,5},... | collective-permute-start | bytes 2359304 | tf_op jit(solution)/shard_map/ppermute | solution.py:76
  105.5 10.6 %shard_map.82 = (f32[4,64,768]{2,1,0:T(8,128)S(1)}, f32[4,64,768]{2,1,0:T(8,128)S(1)}, f32[4,64,512]{2,1,0:T(8,128)S(1)}, bf16[2,8,64,2048]{3,2,1,0:T(8,128)(2,1)S(1)}) custom-call(s32[24]{0:T(128)S(1)} %fusion.3.tbl, f32[4,64,768]{2,1,0:T(8,128)S(1)} %pad_maximum_fusion.refs_0_, f32[4,64,640]{2,1,0:T(8,128)S(1)} %pad_maximum_fusion.2.refs_1_, ...), custom_call_target="tpu_custom_call" | custom-call | flops 6442450944 | bytes 20971520 | tf_op jit(solution)/shard_map/pallas_call | solution.py:150
  116.1 3.6 %collective-permute-done.21 = f32[2048]{0:T(1024)S(1)} collective-permute-done((f32[2048]{0:T(1024)S(1)}, f32[2048]{0:T(1024)S(1)}, u32[]{:S(2)}, u32[]{:S(2)}) %collective-permute-start.21) | collective-permute-done | bytes 8224 | tf_op jit(solution)/shard_map/ppermute | solution.py:76
  119.8 3.2 %collective-permute-start.12 = (f32[4,64,768]{2,1,0:T(8,128)S(1)}, f32[4,64,768]{2,1,0:T(8,128)S(1)}, u32[]{:S(2)}, u32[]{:S(2)}) collective-permute-start(f32[4,64,768]{2,1,0:T(8,128)S(1)} %get-tuple-element.71), channel_id=1, source_target_pairs={{0,12},{1,13},{2,14},{3,15},{4,8},{5,9},{6,10},{7,11},{8,4},{9,5},... | collective-permute-start | bytes 2359304 | tf_op jit(solution)/shard_map/ppermute | solution.py:76
  123.0 9.8 %shard_map.83 = (f32[4,64,768]{2,1,0:T(8,128)S(1)}, f32[4,64,768]{2,1,0:T(8,128)S(1)}, f32[4,64,512]{2,1,0:T(8,128)S(1)}) custom-call(s32[24]{0:T(128)S(1)} %fusion.3.tbl, bf16[2,8,64,2048]{3,2,1,0:T(8,128)(2,1)S(1)} %get-tuple-element.68.refs_0_, bf16[2048,1024]{1,0:T(8,128)(2,1)S(1)} %get-tuple-element.114.refs_6_.refs_1_, ...), custom_call_target="tpu_custom_call" | custom-call | flops 6442450944 | bytes 20971520 | tf_op jit(solution)/shard_map/pallas_call | solution.py:150
  135.2 12.5 %collective-permute-done.13 = f32[4,64,512]{2,1,0:T(8,128)S(1)} collective-permute-done((f32[4,64,512]{2,1,0:T(8,128)S(1)}, f32[4,64,512]{2,1,0:T(8,128)S(1)}, u32[]{:S(2)}, u32[]{:S(2)}) %collective-permute-start.13) | collective-permute-done | bytes 524320 | tf_op jit(solution)/shard_map/ppermute | solution.py:76
  150.1 8.8 %collective-permute-done.36 = f32[2,64,768]{2,1,0:T(8,128)S(1)} collective-permute-done((f32[2,64,768]{2,1,0:T(8,128)S(1)}, f32[2,64,768]{2,1,0:T(8,128)S(1)}, u32[]{:S(2)}, u32[]{:S(2)}) %collective-permute-start.36) | collective-permute-done | bytes 393248 | tf_op jit(solution)/shard_map/ppermute | solution.py:76
  159.0 3.3 %collective-permute-start.40 = (f32[1,64,512]{2,1,0:T(8,128)S(1)}, f32[1,64,512]{2,1,0:T(8,128)S(1)}, u32[]{:S(2)}, u32[]{:S(2)}) collective-permute-start(f32[1,64,512]{2,1,0:T(8,128)S(1)} %get-tuple-element.123), channel_id=1, source_target_pairs={{0,12},{1,13},{2,14},{3,15},{4,8},{5,9},{6,10},{7,11},{8,4},{9,5},... | collective-permute-start | bytes 393224 | tf_op jit(solution)/shard_map/ppermute | solution.py:76
  163.9 4.0 %collective-permute-done.14 = f32[2,64,768]{2,1,0:T(8,128)S(1)} collective-permute-done((f32[2,64,768]{2,1,0:T(8,128)S(1)}, f32[2,64,768]{2,1,0:T(8,128)S(1)}, u32[]{:S(2)}, u32[]{:S(2)}) %collective-permute-start.14) | collective-permute-done | bytes 393248 | tf_op jit(solution)/shard_map/ppermute | solution.py:76
  169.6 4.7 %collective-permute-done.19.refs_5_ = f32[1,64,512]{2,1,0:T(8,128)S(1)} collective-permute-done((f32[1,64,512]{2,1,0:T(8,128)S(1)}, f32[1,64,512]{2,1,0:T(8,128)S(1)}, u32[]{:S(2)}, u32[]{:S(2)}) %collective-permute-start.19) | collective-permute-done | bytes 131104 | tf_op jit(solution)/shard_map/ppermute | solution.py:76
  174.3 3.5 %collective-permute-done.17.refs_3_ = f32[1,64,768]{2,1,0:T(8,128)S(1)} collective-permute-done((f32[1,64,768]{2,1,0:T(8,128)S(1)}, f32[1,64,768]{2,1,0:T(8,128)S(1)}, u32[]{:S(2)}, u32[]{:S(2)}) %collective-permute-start.17) | collective-permute-done | bytes 196640 | tf_op jit(solution)/shard_map/ppermute | solution.py:76
  177.7 2.3 %shard_map.86.refs_7_ = f32[8,128,128]{2,1,0:T(8,128)S(1)} custom-call(f32[1,64,768]{2,1,0:T(8,128)S(1)} %get-tuple-element.118.refs_0_, f32[1,64,768]{2,1,0:T(8,128)S(1)} %get-tuple-element.116.refs_1_, f32[1,64,512]{2,1,0:T(8,128)S(1)} %get-tuple-element.124.refs_2_, f32[1,64,768]{2,1,0:T(8,128)S(1)} %collective-permute-done.38.refs_3_, ...), custom_call_target="tpu_custom_call" | custom-call | flops 1073741824 | bytes 2621440 | tf_op jit(solution)/shard_map/pallas_call | solution.py:203
  180.0 2.3 %shard_map.87 = f32[8,256,128]{2,1,0:T(8,128)S(1)} custom-call(f32[1,64,768]{2,1,0:T(8,128)S(1)} %get-tuple-element.122.refs_0_, f32[1,64,768]{2,1,0:T(8,128)S(1)} %get-tuple-element.120.refs_1_, f32[1,64,512]{2,1,0:T(8,128)S(1)} %get-tuple-element.126.refs_2_, f32[1,64,768]{2,1,0:T(8,128)S(1)} %collective-permute-done.17.refs_3_, ...), custom_call_target="tpu_custom_call" | custom-call | flops 1073741824 | bytes 2621440 | tf_op jit(solution)/shard_map/pallas_call | solution.py:203
  182.4 19.7 %all_to_all.5 = f32[8,256,128]{2,1,0:T(8,128)S(1)} all-to-all(f32[8,256,128]{2,1,0:T(8,128)S(1)} %shard_map.87), channel_id=1, replica_groups=mesh['row'=8,'col'=16] {'row'}, dimensions={0} | all-to-all | bytes 2097152 | tf_op jit(solution)/shard_map/all_to_all | solution.py:276
  (108 shorter events, 30.4 us)
Async XLA Ops:
  3.1 71.1 %collective-permute-start.10 = (f32[2048,1024]{1,0:T(8,128)}, f32[2048,1024]{1,0:T(8,128)}, u32[]{:S(2)}, u32[]{:S(2)}) collective-permute-start(f32[2048,1024]{1,0:T(8,128)} %param.9), channel_id=1, source_target_pairs={{0,1},{1,0},{2,3},{3,2},{4,5},{5,4},{6,7},{7,6},{8,9},{9,8},{10,11... | collective-permute-start | bytes 25165832 | tf_op jit(solution)/shard_map/ppermute | solution.py:76
  4.3 9.9 %collective-permute-start.23 = (f32[1,64,768]{2,1,0:T(8,128)S(1)}, f32[1,64,768]{2,1,0:T(8,128)S(1)}, u32[]{:S(2)}, u32[]{:S(2)}) collective-permute-start(f32[1,64,768]{2,1,0:T(8,128)S(1)} %get-tuple-element.127), channel_id=1, source_target_pairs={{0,16},{1,17},{2,18},{3,19},{4,20},{5,21},{6,22},{7,23},{8,24},{9,... | collective-permute-start | bytes 589832 | tf_op jit(solution)/shard_map/ppermute | solution.py:76
  6.0 14.9 %collective-permute-start = (f32[1,64,768]{2,1,0:T(8,128)S(1)}, f32[1,64,768]{2,1,0:T(8,128)S(1)}, u32[]{:S(2)}, u32[]{:S(2)}) collective-permute-start(f32[1,64,768]{2,1,0:T(8,128)S(1)} %get-tuple-element.128), channel_id=1, source_target_pairs={{0,16},{1,17},{2,18},{3,19},{4,20},{5,21},{6,22},{7,23},{8,24},{9,... | collective-permute-start | bytes 589832 | tf_op jit(solution)/shard_map/ppermute | solution.py:76
  18.3 16.5 %collective-permute-start.26 = (f32[2,64,768]{2,1,0:T(8,128)S(1)}, f32[2,64,768]{2,1,0:T(8,128)S(1)}, u32[]{:S(2)}, u32[]{:S(2)}) collective-permute-start(f32[2,64,768]{2,1,0:T(8,128)S(1)} %pad_maximum_fusion.7), channel_id=1, source_target_pairs={{0,48},{1,49},{2,50},{3,51},{4,52},{5,53},{6,54},{7,55},{8,56},{9,... | collective-permute-start | bytes 1179656 | tf_op jit(solution)/shard_map/ppermute | solution.py:76
  20.8 9.6 %collective-permute-start.27 = (f32[2,64,640]{2,1,0:T(8,128)S(1)}, f32[2,64,640]{2,1,0:T(8,128)S(1)}, u32[]{:S(2)}, u32[]{:S(2)}) collective-permute-start(f32[2,64,640]{2,1,0:T(8,128)S(1)} %pad_maximum_fusion.10), channel_id=1, source_target_pairs={{0,64},{1,65},{2,66},{3,67},{4,68},{5,69},{6,70},{7,71},{8,72},{9,... | collective-permute-start | bytes 983048 | tf_op jit(solution)/shard_map/ppermute | solution.py:76
  21.4 10.7 %collective-permute-start.28 = (f32[2,64,640]{2,1,0:T(8,128)S(1)}, f32[2,64,640]{2,1,0:T(8,128)S(1)}, u32[]{:S(2)}, u32[]{:S(2)}) collective-permute-start(f32[2,64,640]{2,1,0:T(8,128)S(1)} %pad_maximum_fusion.11), channel_id=1, source_target_pairs={{0,16},{1,17},{2,18},{3,19},{4,20},{5,21},{6,22},{7,23},{8,24},{9,... | collective-permute-start | bytes 983048 | tf_op jit(solution)/shard_map/ppermute | solution.py:76
  22.2 15.1 %collective-permute-start.6 = (f32[2,64,640]{2,1,0:T(8,128)S(1)}, f32[2,64,640]{2,1,0:T(8,128)S(1)}, u32[]{:S(2)}, u32[]{:S(2)}) collective-permute-start(f32[2,64,640]{2,1,0:T(8,128)S(1)} %pad_maximum_fusion.9), channel_id=1, source_target_pairs={{0,16},{1,17},{2,18},{3,19},{4,20},{5,21},{6,22},{7,23},{8,24},{9,... | collective-permute-start | bytes 983048 | tf_op jit(solution)/shard_map/ppermute | solution.py:76
  30.4 11.3 %collective-permute-start.5 = (f32[2,64,640]{2,1,0:T(8,128)S(1)}, f32[2,64,640]{2,1,0:T(8,128)S(1)}, u32[]{:S(2)}, u32[]{:S(2)}) collective-permute-start(f32[2,64,640]{2,1,0:T(8,128)S(1)} %pad_maximum_fusion.8), channel_id=1, source_target_pairs={{0,64},{1,65},{2,66},{3,67},{4,68},{5,69},{6,70},{7,71},{8,72},{9,... | collective-permute-start | bytes 983048 | tf_op jit(solution)/shard_map/ppermute | solution.py:76
  32.1 13.2 %collective-permute-start.4 = (f32[2,64,768]{2,1,0:T(8,128)S(1)}, f32[2,64,768]{2,1,0:T(8,128)S(1)}, u32[]{:S(2)}, u32[]{:S(2)}) collective-permute-start(f32[2,64,768]{2,1,0:T(8,128)S(1)} %pad_maximum_fusion.6), channel_id=1, source_target_pairs={{0,48},{1,49},{2,50},{3,51},{4,52},{5,53},{6,54},{7,55},{8,56},{9,... | collective-permute-start | bytes 1179656 | tf_op jit(solution)/shard_map/ppermute | solution.py:76
  34.8 15.4 %collective-permute-start.30 = (f32[4,64,640]{2,1,0:T(8,128)S(1)}, f32[4,64,640]{2,1,0:T(8,128)S(1)}, u32[]{:S(2)}, u32[]{:S(2)}) collective-permute-start(f32[4,64,640]{2,1,0:T(8,128)S(1)} %pad_maximum_fusion.4.refs_1_), channel_id=1, source_target_pairs={{0,16},{1,17},{2,18},{3,19},{4,20},{5,21},{6,22},{7,23},{8,24},{9,... | collective-permute-start | bytes 1966088 | tf_op jit(solution)/shard_map/ppermute | solution.py:76
  37.3 22.0 %collective-permute-start.31 = (f32[4,64,640]{2,1,0:T(8,128)S(1)}, f32[4,64,640]{2,1,0:T(8,128)S(1)}, u32[]{:S(2)}, u32[]{:S(2)}) collective-permute-start(f32[4,64,640]{2,1,0:T(8,128)S(1)} %pad_maximum_fusion.5.refs_2_), channel_id=1, source_target_pairs={{0,48},{1,49},{2,50},{3,51},{4,52},{5,53},{6,54},{7,55},{8,56},{9,... | collective-permute-start | bytes 1966088 | tf_op jit(solution)/shard_map/ppermute | solution.py:76
  41.8 22.0 %collective-permute-start.29 = (f32[4,64,768]{2,1,0:T(8,128)S(1)}, f32[4,64,768]{2,1,0:T(8,128)S(1)}, u32[]{:S(2)}, u32[]{:S(2)}) collective-permute-start(f32[4,64,768]{2,1,0:T(8,128)S(1)} %pad_maximum_fusion.1.refs_0_), channel_id=1, source_target_pairs={{0,64},{1,65},{2,66},{3,67},{4,68},{5,69},{6,70},{7,71},{8,72},{9,... | collective-permute-start | bytes 2359304 | tf_op jit(solution)/shard_map/ppermute | solution.py:76
  45.3 28.9 %collective-permute-start.7 = (f32[4,64,768]{2,1,0:T(8,128)S(1)}, f32[4,64,768]{2,1,0:T(8,128)S(1)}, u32[]{:S(2)}, u32[]{:S(2)}) collective-permute-start(f32[4,64,768]{2,1,0:T(8,128)S(1)} %pad_maximum_fusion.refs_0_), channel_id=1, source_target_pairs={{0,64},{1,65},{2,66},{3,67},{4,68},{5,69},{6,70},{7,71},{8,72},{9,... | collective-permute-start | bytes 2359304 | tf_op jit(solution)/shard_map/ppermute | solution.py:76
  50.2 20.6 %collective-permute-start.9 = (f32[4,64,640]{2,1,0:T(8,128)S(1)}, f32[4,64,640]{2,1,0:T(8,128)S(1)}, u32[]{:S(2)}, u32[]{:S(2)}) collective-permute-start(f32[4,64,640]{2,1,0:T(8,128)S(1)} %pad_maximum_fusion.3.refs_2_), channel_id=1, source_target_pairs={{0,48},{1,49},{2,50},{3,51},{4,52},{5,53},{6,54},{7,55},{8,56},{9,... | collective-permute-start | bytes 1966088 | tf_op jit(solution)/shard_map/ppermute | solution.py:76
  59.3 11.6 %collective-permute-start.8 = (f32[4,64,640]{2,1,0:T(8,128)S(1)}, f32[4,64,640]{2,1,0:T(8,128)S(1)}, u32[]{:S(2)}, u32[]{:S(2)}) collective-permute-start(f32[4,64,640]{2,1,0:T(8,128)S(1)} %pad_maximum_fusion.2.refs_1_), channel_id=1, source_target_pairs={{0,16},{1,17},{2,18},{3,19},{4,20},{5,21},{6,22},{7,23},{8,24},{9,... | collective-permute-start | bytes 1966088 | tf_op jit(solution)/shard_map/ppermute | solution.py:76
  78.5 26.9 %collective-permute-start.20 = (f32[2048]{0:T(1024)S(1)}, f32[2048]{0:T(1024)S(1)}, u32[]{:S(2)}, u32[]{:S(2)}) collective-permute-start(f32[2048]{0:T(1024)S(1)} %add.134), channel_id=1, source_target_pairs={{0,4},{1,5},{2,6},{3,7},{4,0},{5,1},{6,2},{7,3},{8,12},{9,13},{10,... | collective-permute-start | bytes 24584 | tf_op jit(solution)/shard_map/ppermute | solution.py:76
  100.9 32.0 %collective-permute-start.32 = (f32[4,64,768]{2,1,0:T(8,128)S(1)}, f32[4,64,768]{2,1,0:T(8,128)S(1)}, u32[]{:S(2)}, u32[]{:S(2)}) collective-permute-start(f32[4,64,768]{2,1,0:T(8,128)S(1)} %get-tuple-element.95), channel_id=1, source_target_pairs={{0,4},{1,5},{2,6},{3,7},{4,0},{5,1},{6,2},{7,3},{8,12},{9,13},{10,... | collective-permute-start | bytes 2359304 | tf_op jit(solution)/shard_map/ppermute | solution.py:76
  101.1 33.8 %collective-permute-start.33 = (f32[4,64,768]{2,1,0:T(8,128)S(1)}, f32[4,64,768]{2,1,0:T(8,128)S(1)}, u32[]{:S(2)}, u32[]{:S(2)}) collective-permute-start(f32[4,64,768]{2,1,0:T(8,128)S(1)} %get-tuple-element.96), channel_id=1, source_target_pairs={{0,12},{1,13},{2,14},{3,15},{4,8},{5,9},{6,10},{7,11},{8,4},{9,5},... | collective-permute-start | bytes 2359304 | tf_op jit(solution)/shard_map/ppermute | solution.py:76
  105.1 27.7 %collective-permute-start.34 = (f32[4,64,512]{2,1,0:T(8,128)S(1)}, f32[4,64,512]{2,1,0:T(8,128)S(1)}, u32[]{:S(2)}, u32[]{:S(2)}) collective-permute-start(f32[4,64,512]{2,1,0:T(8,128)S(1)} %get-tuple-element.97), channel_id=1, source_target_pairs={{0,2},{1,3},{2,0},{3,1},{4,6},{5,7},{6,4},{7,5},{8,10},{9,11},{10,... | collective-permute-start | bytes 1572872 | tf_op jit(solution)/shard_map/ppermute | solution.py:76
  105.4 14.3 %collective-permute-start.21 = (f32[2048]{0:T(1024)S(1)}, f32[2048]{0:T(1024)S(1)}, u32[]{:S(2)}, u32[]{:S(2)}) collective-permute-start(f32[2048]{0:T(1024)S(1)} %add.135), channel_id=1, source_target_pairs={{0,12},{1,13},{2,14},{3,15},{4,8},{5,9},{6,10},{7,11},{8,4},{9,5},... | collective-permute-start | bytes 24584 | tf_op jit(solution)/shard_map/ppermute | solution.py:76
  116.1 31.7 %collective-permute-start.11 = (f32[4,64,768]{2,1,0:T(8,128)S(1)}, f32[4,64,768]{2,1,0:T(8,128)S(1)}, u32[]{:S(2)}, u32[]{:S(2)}) collective-permute-start(f32[4,64,768]{2,1,0:T(8,128)S(1)} %get-tuple-element.70), channel_id=1, source_target_pairs={{0,4},{1,5},{2,6},{3,7},{4,0},{5,1},{6,2},{7,3},{8,12},{9,13},{10,... | collective-permute-start | bytes 2359304 | tf_op jit(solution)/shard_map/ppermute | solution.py:76
  119.8 28.0 %collective-permute-start.12 = (f32[4,64,768]{2,1,0:T(8,128)S(1)}, f32[4,64,768]{2,1,0:T(8,128)S(1)}, u32[]{:S(2)}, u32[]{:S(2)}) collective-permute-start(f32[4,64,768]{2,1,0:T(8,128)S(1)} %get-tuple-element.71), channel_id=1, source_target_pairs={{0,12},{1,13},{2,14},{3,15},{4,8},{5,9},{6,10},{7,11},{8,4},{9,5},... | collective-permute-start | bytes 2359304 | tf_op jit(solution)/shard_map/ppermute | solution.py:76
  132.8 14.9 %collective-permute-start.13 = (f32[4,64,512]{2,1,0:T(8,128)S(1)}, f32[4,64,512]{2,1,0:T(8,128)S(1)}, u32[]{:S(2)}, u32[]{:S(2)}) collective-permute-start(f32[4,64,512]{2,1,0:T(8,128)S(1)} %get-tuple-element.72), channel_id=1, source_target_pairs={{0,2},{1,3},{2,0},{3,1},{4,6},{5,7},{6,4},{7,5},{8,10},{9,11},{10,... | collective-permute-start | bytes 1572872 | tf_op jit(solution)/shard_map/ppermute | solution.py:76
  132.9 35.3 %collective-permute-start.22 = (f32[2048]{0:T(1024)S(1)}, f32[2048]{0:T(1024)S(1)}, u32[]{:S(2)}, u32[]{:S(2)}) collective-permute-start(f32[2048]{0:T(1024)S(1)} %add.136), channel_id=1, source_target_pairs={{0,2},{1,3},{2,0},{3,1},{4,6},{5,7},{6,4},{7,5},{8,10},{9,11},{10,... | collective-permute-start | bytes 24584 | tf_op jit(solution)/shard_map/ppermute | solution.py:76
  135.0 13.0 %collective-permute-start.37 = (f32[2,64,512]{2,1,0:T(8,128)S(1)}, f32[2,64,512]{2,1,0:T(8,128)S(1)}, u32[]{:S(2)}, u32[]{:S(2)}) collective-permute-start(f32[2,64,512]{2,1,0:T(8,128)S(1)} %slice_add_fusion.4), channel_id=1, source_target_pairs={{0,4},{1,5},{2,6},{3,7},{4,0},{5,1},{6,2},{7,3},{8,12},{9,13},{10,... | collective-permute-start | bytes 786440 | tf_op jit(solution)/shard_map/ppermute | solution.py:76
  147.7 11.2 %collective-permute-start.36 = (f32[2,64,768]{2,1,0:T(8,128)S(1)}, f32[2,64,768]{2,1,0:T(8,128)S(1)}, u32[]{:S(2)}, u32[]{:S(2)}) collective-permute-start(f32[2,64,768]{2,1,0:T(8,128)S(1)} %slice_add_fusion), channel_id=1, source_target_pairs={{0,2},{1,3},{2,0},{3,1},{4,6},{5,7},{6,4},{7,5},{8,10},{9,11},{10,... | collective-permute-start | bytes 1179656 | tf_op jit(solution)/shard_map/ppermute | solution.py:76
  147.7 11.2 %collective-permute-start.35 = (f32[2,64,768]{2,1,0:T(8,128)S(1)}, f32[2,64,768]{2,1,0:T(8,128)S(1)}, u32[]{:S(2)}, u32[]{:S(2)}) collective-permute-start(f32[2,64,768]{2,1,0:T(8,128)S(1)} %slice_add_fusion.1), channel_id=1, source_target_pairs={{0,12},{1,13},{2,14},{3,15},{4,8},{5,9},{6,10},{7,11},{8,4},{9,5},... | collective-permute-start | bytes 1179656 | tf_op jit(solution)/shard_map/ppermute | solution.py:76
  147.8 14.7 %collective-permute-start.16 = (f32[2,64,512]{2,1,0:T(8,128)S(1)}, f32[2,64,512]{2,1,0:T(8,128)S(1)}, u32[]{:S(2)}, u32[]{:S(2)}) collective-permute-start(f32[2,64,512]{2,1,0:T(8,128)S(1)} %slice_add_fusion.5), channel_id=1, source_target_pairs={{0,4},{1,5},{2,6},{3,7},{4,0},{5,1},{6,2},{7,3},{8,12},{9,13},{10,... | collective-permute-start | bytes 786440 | tf_op jit(solution)/shard_map/ppermute | solution.py:76
  148.0 15.9 %collective-permute-start.15 = (f32[2,64,768]{2,1,0:T(8,128)S(1)}, f32[2,64,768]{2,1,0:T(8,128)S(1)}, u32[]{:S(2)}, u32[]{:S(2)}) collective-permute-start(f32[2,64,768]{2,1,0:T(8,128)S(1)} %slice_add_fusion.2), channel_id=1, source_target_pairs={{0,2},{1,3},{2,0},{3,1},{4,6},{5,7},{6,4},{7,5},{8,10},{9,11},{10,... | collective-permute-start | bytes 1179656 | tf_op jit(solution)/shard_map/ppermute | solution.py:76
  158.9 9.0 %collective-permute-start.14 = (f32[2,64,768]{2,1,0:T(8,128)S(1)}, f32[2,64,768]{2,1,0:T(8,128)S(1)}, u32[]{:S(2)}, u32[]{:S(2)}) collective-permute-start(f32[2,64,768]{2,1,0:T(8,128)S(1)} %slice_add_fusion.3), channel_id=1, source_target_pairs={{0,12},{1,13},{2,14},{3,15},{4,8},{5,9},{6,10},{7,11},{8,4},{9,5},... | collective-permute-start | bytes 1179656 | tf_op jit(solution)/shard_map/ppermute | solution.py:76
  159.0 10.3 %collective-permute-start.40 = (f32[1,64,512]{2,1,0:T(8,128)S(1)}, f32[1,64,512]{2,1,0:T(8,128)S(1)}, u32[]{:S(2)}, u32[]{:S(2)}) collective-permute-start(f32[1,64,512]{2,1,0:T(8,128)S(1)} %get-tuple-element.123), channel_id=1, source_target_pairs={{0,12},{1,13},{2,14},{3,15},{4,8},{5,9},{6,10},{7,11},{8,4},{9,5},... | collective-permute-start | bytes 393224 | tf_op jit(solution)/shard_map/ppermute | solution.py:76
  169.3 8.4 %collective-permute-start.17 = (f32[1,64,768]{2,1,0:T(8,128)S(1)}, f32[1,64,768]{2,1,0:T(8,128)S(1)}, u32[]{:S(2)}, u32[]{:S(2)}) collective-permute-start(f32[1,64,768]{2,1,0:T(8,128)S(1)} %get-tuple-element.121), channel_id=1, source_target_pairs={{0,2},{1,3},{2,0},{3,1},{4,6},{5,7},{6,4},{7,5},{8,10},{9,11},{10,... | collective-permute-start | bytes 589832 | tf_op jit(solution)/shard_map/ppermute | solution.py:76
  (14 other events, 284.2 us)

commit v4 on v3

--- a/solution.py
+++ b/solution.py
@@ -226,9 +226,10 @@
     factor, given = lax.optimization_barrier((factor, given))
     far_factor = permute(factor, CORE)
     block = jnp.concatenate([kept[:, DEPTH[0] :], given], axis=1)
+    first = [kept[None, c * ROWS : (c + 1) * ROWS, : DEPTH[0]] for c in range(CHUNKS)]
     gathered = [
         [
-            kept[None, c * ROWS : (c + 1) * ROWS, : DEPTH[0]],
+            first[c],
             block[None, c * ROWS : (c + 1) * ROWS, : DEPTH[1]],
             block[None, c * ROWS : (c + 1) * ROWS, DEPTH[1] :],
         ]
@@ -237,7 +238,9 @@
     last = []
     for s in range(3):
         for c in range(CHUNKS):
-            came = lax.optimization_barrier([permute(gathered[c][p], ROW_DIMS[(p + s) % 3]) for p in range(3)])
+            came = lax.optimization_barrier(
+                [permute(gathered[c][p], ROW_DIMS[(p + s) % 3]) for p in range(3)]
+            )
             if s == 2:
                 last.append(came)
                 continue
@@ -267,9 +270,13 @@
         sent, parts = mm(0, tbl, (*gathered[c], *last[c]), factors)
         came = lax.optimization_barrier([permute(sent[q], COL_DIMS[q]) for q in range(3)])
         kept, _ = mm(1, tbl, parts, factors)
-        second = lax.optimization_barrier([permute(kept[q][:2] + came[q][:2], COL_DIMS[(q + 1) % 3]) for q in range(3)])
+        passed = [kept[q][:2] + came[q][:2] for q in range(3)]
+        second = lax.optimization_barrier(
+            [permute(passed[q], COL_DIMS[(q + 1) % 3]) for q in range(3)]
+        )
+        passed = [kept[q][2:3] + came[q][2:3] + second[q][:1] for q in range(3)]
         third = lax.optimization_barrier(
-            [permute(kept[q][2:3] + came[q][2:3] + second[q][:1], COL_DIMS[(q + 2) % 3]) for q in range(3)]
+            [permute(passed[q], COL_DIMS[(q + 2) % 3]) for q in range(3)]
         )
         held = [kept[q][3:] + came[q][3:] + second[q][1:] for q in range(3)]
         sums = (tail(held, third, cells, sums),)

time: 205 us -> 205 us (level)
  no operation moved by 1% of the time
where the time goes in v4:
time: 205 us; the launch traced here: 203 us
  waiting for transfers between devices  74.9 us (37%)
  starting transfers between devices  49.9 us (24%)
  Pallas kernels  45.4 us (22%)
  blocking collectives  19.7 us (10%)
  other arithmetic  7.87 us (4%)
  local copies, waits for them, and re-layouts  4.53 us (2%)
    ppermute x41, waiting for transfers between devices, permute(): return lax.ppermute(x, BOTH, pairs)  74.9 us
    ppermute x41, starting transfers between devices, permute(): return lax.ppermute(x, BOTH, pairs)  49.9 us
    pallas_call x4, Pallas kernels, mm(): pl.pallas_call(functools.partial(mm_kernel, half), out_shape=shapes, grid...  40.8 us
    all_to_all x1, blocking collectives, step(): lax.all_to_all(sums[0], 'row', split_axis=0, concat_axis=0, tiled=True)  19.7 us
    pallas_call x2, Pallas kernels, tail(): pl.pallas_call(tail_kernel, out_shape=jax.ShapeDtypeStruct((8, rows, 128)...  4.66 us
    reduce_sum x1, other arithmetic, step(): far_norms = jnp.sum(far_factor * far_factor, axis=1)  4.26 us
  transfers between devices with their start and end apart: 41, of which 20 were waited for; matrix products, arithmetic and copies ran while one was open for 3% of the time, Pallas kernels for 20%

profile of v4, /device:TPU:0, one launch (start us, length us, event | category | flops | bytes accessed | tf_op | source)
XLA Modules:
  0.0 202.8 jit_solution(4521461532538813777)
XLA Ops:
  7.4 2.9 %collective-permute-start.24 = (f32[1,64,640]{2,1,0:T(8,128)S(1)}, f32[1,64,640]{2,1,0:T(8,128)S(1)}, u32[]{:S(2)}, u32[]{:S(2)}) collective-permute-start(f32[1,64,640]{2,1,0:T(8,128)S(1)} %get-tuple-element.134), channel_id=1, source_target_pairs={{0,48},{1,49},{2,50},{3,51},{4,52},{5,53},{6,54},{7,55},{8,56},{9,... | collective-permute-start | bytes 491528 | tf_op jit(solution)/shard_map/ppermute | solution.py:76
  10.3 3.2 %collective-permute-start.25 = (f32[1,64,640]{2,1,0:T(8,128)S(1)}, f32[1,64,640]{2,1,0:T(8,128)S(1)}, u32[]{:S(2)}, u32[]{:S(2)}) collective-permute-start(f32[1,64,640]{2,1,0:T(8,128)S(1)} %get-tuple-element.131), channel_id=1, source_target_pairs={{0,64},{1,65},{2,66},{3,67},{4,68},{5,69},{6,70},{7,71},{8,72},{9,... | collective-permute-start | bytes 491528 | tf_op jit(solution)/shard_map/ppermute | solution.py:76
  15.0 3.2 %collective-permute-start.3 = (f32[1,64,640]{2,1,0:T(8,128)S(1)}, f32[1,64,640]{2,1,0:T(8,128)S(1)}, u32[]{:S(2)}, u32[]{:S(2)}) collective-permute-start(f32[1,64,640]{2,1,0:T(8,128)S(1)} %get-tuple-element.132), channel_id=1, source_target_pairs={{0,64},{1,65},{2,66},{3,67},{4,68},{5,69},{6,70},{7,71},{8,72},{9,... | collective-permute-start | bytes 491528 | tf_op jit(solution)/shard_map/ppermute | solution.py:76
  18.3 2.5 %collective-permute-start.26 = (f32[2,64,768]{2,1,0:T(8,128)S(1)}, f32[2,64,768]{2,1,0:T(8,128)S(1)}, u32[]{:S(2)}, u32[]{:S(2)}) collective-permute-start(f32[2,64,768]{2,1,0:T(8,128)S(1)} %pad_maximum_fusion.7), channel_id=1, source_target_pairs={{0,48},{1,49},{2,50},{3,51},{4,52},{5,53},{6,54},{7,55},{8,56},{9,... | collective-permute-start | bytes 1179656 | tf_op jit(solution)/shard_map/ppermute | solution.py:76
  23.6 6.8 %collective-permute-done.27 = f32[2,64,640]{2,1,0:T(8,128)S(1)} collective-permute-done((f32[2,64,640]{2,1,0:T(8,128)S(1)}, f32[2,64,640]{2,1,0:T(8,128)S(1)}, u32[]{:S(2)}, u32[]{:S(2)}) %collective-permute-start.27) | collective-permute-done | bytes 327712 | tf_op jit(solution)/shard_map/ppermute | solution.py:76
  32.1 2.7 %collective-permute-start.4 = (f32[2,64,768]{2,1,0:T(8,128)S(1)}, f32[2,64,768]{2,1,0:T(8,128)S(1)}, u32[]{:S(2)}, u32[]{:S(2)}) collective-permute-start(f32[2,64,768]{2,1,0:T(8,128)S(1)} %pad_maximum_fusion.6), channel_id=1, source_target_pairs={{0,48},{1,49},{2,50},{3,51},{4,52},{5,53},{6,54},{7,55},{8,56},{9,... | collective-permute-start | bytes 1179656 | tf_op jit(solution)/shard_map/ppermute | solution.py:76
  34.9 2.3 %collective-permute-done.6 = f32[2,64,640]{2,1,0:T(8,128)S(1)} collective-permute-done((f32[2,64,640]{2,1,0:T(8,128)S(1)}, f32[2,64,640]{2,1,0:T(8,128)S(1)}, u32[]{:S(2)}, u32[]{:S(2)}) %collective-permute-start.6) | collective-permute-done | bytes 327712 | tf_op jit(solution)/shard_map/ppermute | solution.py:76
  37.3 4.4 %collective-permute-start.31 = (f32[4,64,640]{2,1,0:T(8,128)S(1)}, f32[4,64,640]{2,1,0:T(8,128)S(1)}, u32[]{:S(2)}, u32[]{:S(2)}) collective-permute-start(f32[4,64,640]{2,1,0:T(8,128)S(1)} %pad_maximum_fusion.5.refs_2_), channel_id=1, source_target_pairs={{0,48},{1,49},{2,50},{3,51},{4,52},{5,53},{6,54},{7,55},{8,56},{9,... | collective-permute-start | bytes 1966088 | tf_op jit(solution)/shard_map/ppermute | solution.py:76
  42.6 2.6 %collective-permute-done.4 = f32[2,64,768]{2,1,0:T(8,128)S(1)} collective-permute-done((f32[2,64,768]{2,1,0:T(8,128)S(1)}, f32[2,64,768]{2,1,0:T(8,128)S(1)}, u32[]{:S(2)}, u32[]{:S(2)}) %collective-permute-start.4) | collective-permute-done | bytes 393248 | tf_op jit(solution)/shard_map/ppermute | solution.py:76
  45.3 2.6 %collective-permute-start.7 = (f32[4,64,768]{2,1,0:T(8,128)S(1)}, f32[4,64,768]{2,1,0:T(8,128)S(1)}, u32[]{:S(2)}, u32[]{:S(2)}) collective-permute-start(f32[4,64,768]{2,1,0:T(8,128)S(1)} %pad_maximum_fusion.refs_0_), channel_id=1, source_target_pairs={{0,64},{1,65},{2,66},{3,67},{4,68},{5,69},{6,70},{7,71},{8,72},{9,... | collective-permute-start | bytes 2359304 | tf_op jit(solution)/shard_map/ppermute | solution.py:76
  48.0 2.2 %collective-permute-done.30.refs_4_ = f32[4,64,640]{2,1,0:T(8,128)S(1)} collective-permute-done((f32[4,64,640]{2,1,0:T(8,128)S(1)}, f32[4,64,640]{2,1,0:T(8,128)S(1)}, u32[]{:S(2)}, u32[]{:S(2)}) %collective-permute-start.30) | collective-permute-done | bytes 655392 | tf_op jit(solution)/shard_map/ppermute | solution.py:76
  50.2 2.8 %collective-permute-start.9 = (f32[4,64,640]{2,1,0:T(8,128)S(1)}, f32[4,64,640]{2,1,0:T(8,128)S(1)}, u32[]{:S(2)}, u32[]{:S(2)}) collective-permute-start(f32[4,64,640]{2,1,0:T(8,128)S(1)} %pad_maximum_fusion.3.refs_2_), channel_id=1, source_target_pairs={{0,48},{1,49},{2,50},{3,51},{4,52},{5,53},{6,54},{7,55},{8,56},{9,... | collective-permute-start | bytes 1966088 | tf_op jit(solution)/shard_map/ppermute | solution.py:76
  53.0 6.3 %collective-permute-done.31.refs_5_ = f32[4,64,640]{2,1,0:T(8,128)S(1)} collective-permute-done((f32[4,64,640]{2,1,0:T(8,128)S(1)}, f32[4,64,640]{2,1,0:T(8,128)S(1)}, u32[]{:S(2)}, u32[]{:S(2)}) %collective-permute-start.31) | collective-permute-done | bytes 655392 | tf_op jit(solution)/shard_map/ppermute | solution.py:76
  63.8 7.0 %collective-permute-done.9.refs_5_ = f32[4,64,640]{2,1,0:T(8,128)S(1)} collective-permute-done((f32[4,64,640]{2,1,0:T(8,128)S(1)}, f32[4,64,640]{2,1,0:T(8,128)S(1)}, u32[]{:S(2)}, u32[]{:S(2)}) %collective-permute-start.9) | collective-permute-done | bytes 655392 | tf_op jit(solution)/shard_map/ppermute | solution.py:76
  70.9 3.3 %collective-permute-done.7.refs_3_ = f32[4,64,768]{2,1,0:T(8,128)S(1)} collective-permute-done((f32[4,64,768]{2,1,0:T(8,128)S(1)}, f32[4,64,768]{2,1,0:T(8,128)S(1)}, u32[]{:S(2)}, u32[]{:S(2)}) %collective-permute-start.7) | collective-permute-done | bytes 786464 | tf_op jit(solution)/shard_map/ppermute | solution.py:76
  74.2 4.3 %multiply_reduce_fusion = (f32[2048]{0:T(1024)S(1)}, bf16[2048,1024]{1,0:T(8,128)(2,1)S(1)}, bf16[2048,1024]{1,0:T(8,128)(2,1)S(1)}) fusion(f32[2048,1024]{1,0:T(8,128)} %collective-permute-done.10), kind=kLoop, calls=%fused_computation.6 | loop fusion | flops 12580864 | bytes 16785408 | tf_op jit(solution)/shard_map/reduce_sum | solution.py:252
  80.5 10.6 %shard_map.84 = (f32[4,64,768]{2,1,0:T(8,128)S(1)}, f32[4,64,768]{2,1,0:T(8,128)S(1)}, f32[4,64,512]{2,1,0:T(8,128)S(1)}, bf16[2,8,64,2048]{3,2,1,0:T(8,128)(2,1)S(1)}) custom-call(s32[24]{0:T(128)S(1)} %fusion.3.tbl, f32[4,64,768]{2,1,0:T(8,128)S(1)} %pad_maximum_fusion.1.refs_0_, f32[4,64,640]{2,1,0:T(8,128)S(1)} %pad_maximum_fusion.4.refs_1_, ...), custom_call_target="tpu_custom_call" | custom-call | flops 6442450944 | bytes 20971520 | tf_op jit(solution)/shard_map/pallas_call | solution.py:150
  91.1 9.8 %shard_map.85 = (f32[4,64,768]{2,1,0:T(8,128)S(1)}, f32[4,64,768]{2,1,0:T(8,128)S(1)}, f32[4,64,512]{2,1,0:T(8,128)S(1)}) custom-call(s32[24]{0:T(128)S(1)} %fusion.3.tbl, bf16[2,8,64,2048]{3,2,1,0:T(8,128)(2,1)S(1)} %get-tuple-element.93.refs_0_, bf16[2048,1024]{1,0:T(8,128)(2,1)S(1)} %get-tuple-element.114.refs_6_.refs_1_, ...), custom_call_target="tpu_custom_call" | custom-call | flops 6442450944 | bytes 20971520 | tf_op jit(solution)/shard_map/pallas_call | solution.py:150
  101.1 4.0 %collective-permute-start.33 = (f32[4,64,768]{2,1,0:T(8,128)S(1)}, f32[4,64,768]{2,1,0:T(8,128)S(1)}, u32[]{:S(2)}, u32[]{:S(2)}) collective-permute-start(f32[4,64,768]{2,1,0:T(8,128)S(1)} %get-tuple-element.96), channel_id=1, source_target_pairs={{0,12},{1,13},{2,14},{3,15},{4,8},{5,9},{6,10},{7,11},{8,4},{9,5},... | collective-permute-start | bytes 2359304 | tf_op jit(solution)/shard_map/ppermute | solution.py:76
  105.5 10.6 %shard_map.82 = (f32[4,64,768]{2,1,0:T(8,128)S(1)}, f32[4,64,768]{2,1,0:T(8,128)S(1)}, f32[4,64,512]{2,1,0:T(8,128)S(1)}, bf16[2,8,64,2048]{3,2,1,0:T(8,128)(2,1)S(1)}) custom-call(s32[24]{0:T(128)S(1)} %fusion.3.tbl, f32[4,64,768]{2,1,0:T(8,128)S(1)} %pad_maximum_fusion.refs_0_, f32[4,64,640]{2,1,0:T(8,128)S(1)} %pad_maximum_fusion.2.refs_1_, ...), custom_call_target="tpu_custom_call" | custom-call | flops 6442450944 | bytes 20971520 | tf_op jit(solution)/shard_map/pallas_call | solution.py:150
  116.1 3.6 %collective-permute-done.21 = f32[2048]{0:T(1024)S(1)} collective-permute-done((f32[2048]{0:T(1024)S(1)}, f32[2048]{0:T(1024)S(1)}, u32[]{:S(2)}, u32[]{:S(2)}) %collective-permute-start.21) | collective-permute-done | bytes 8224 | tf_op jit(solution)/shard_map/ppermute | solution.py:76
  119.8 3.2 %collective-permute-start.12 = (f32[4,64,768]{2,1,0:T(8,128)S(1)}, f32[4,64,768]{2,1,0:T(8,128)S(1)}, u32[]{:S(2)}, u32[]{:S(2)}) collective-permute-start(f32[4,64,768]{2,1,0:T(8,128)S(1)} %get-tuple-element.71), channel_id=1, source_target_pairs={{0,12},{1,13},{2,14},{3,15},{4,8},{5,9},{6,10},{7,11},{8,4},{9,5},... | collective-permute-start | bytes 2359304 | tf_op jit(solution)/shard_map/ppermute | solution.py:76
  123.0 9.8 %shard_map.83 = (f32[4,64,768]{2,1,0:T(8,128)S(1)}, f32[4,64,768]{2,1,0:T(8,128)S(1)}, f32[4,64,512]{2,1,0:T(8,128)S(1)}) custom-call(s32[24]{0:T(128)S(1)} %fusion.3.tbl, bf16[2,8,64,2048]{3,2,1,0:T(8,128)(2,1)S(1)} %get-tuple-element.68.refs_0_, bf16[2048,1024]{1,0:T(8,128)(2,1)S(1)} %get-tuple-element.114.refs_6_.refs_1_, ...), custom_call_target="tpu_custom_call" | custom-call | flops 6442450944 | bytes 20971520 | tf_op jit(solution)/shard_map/pallas_call | solution.py:150
  135.2 12.5 %collective-permute-done.13 = f32[4,64,512]{2,1,0:T(8,128)S(1)} collective-permute-done((f32[4,64,512]{2,1,0:T(8,128)S(1)}, f32[4,64,512]{2,1,0:T(8,128)S(1)}, u32[]{:S(2)}, u32[]{:S(2)}) %collective-permute-start.13) | collective-permute-done | bytes 524320 | tf_op jit(solution)/shard_map/ppermute | solution.py:76
  150.1 8.8 %collective-permute-done.36 = f32[2,64,768]{2,1,0:T(8,128)S(1)} collective-permute-done((f32[2,64,768]{2,1,0:T(8,128)S(1)}, f32[2,64,768]{2,1,0:T(8,128)S(1)}, u32[]{:S(2)}, u32[]{:S(2)}) %collective-permute-start.36) | collective-permute-done | bytes 393248 | tf_op jit(solution)/shard_map/ppermute | solution.py:76
  159.0 3.3 %collective-permute-start.40 = (f32[1,64,512]{2,1,0:T(8,128)S(1)}, f32[1,64,512]{2,1,0:T(8,128)S(1)}, u32[]{:S(2)}, u32[]{:S(2)}) collective-permute-start(f32[1,64,512]{2,1,0:T(8,128)S(1)} %get-tuple-element.123), channel_id=1, source_target_pairs={{0,12},{1,13},{2,14},{3,15},{4,8},{5,9},{6,10},{7,11},{8,4},{9,5},... | collective-permute-start | bytes 393224 | tf_op jit(solution)/shard_map/ppermute | solution.py:76
  163.9 4.0 %collective-permute-done.14 = f32[2,64,768]{2,1,0:T(8,128)S(1)} collective-permute-done((f32[2,64,768]{2,1,0:T(8,128)S(1)}, f32[2,64,768]{2,1,0:T(8,128)S(1)}, u32[]{:S(2)}, u32[]{:S(2)}) %collective-permute-start.14) | collective-permute-done | bytes 393248 | tf_op jit(solution)/shard_map/ppermute | solution.py:76
  169.6 4.7 %collective-permute-done.19.refs_5_ = f32[1,64,512]{2,1,0:T(8,128)S(1)} collective-permute-done((f32[1,64,512]{2,1,0:T(8,128)S(1)}, f32[1,64,512]{2,1,0:T(8,128)S(1)}, u32[]{:S(2)}, u32[]{:S(2)}) %collective-permute-start.19) | collective-permute-done | bytes 131104 | tf_op jit(solution)/shard_map/ppermute | solution.py:76
  174.3 3.5 %collective-permute-done.17.refs_3_ = f32[1,64,768]{2,1,0:T(8,128)S(1)} collective-permute-done((f32[1,64,768]{2,1,0:T(8,128)S(1)}, f32[1,64,768]{2,1,0:T(8,128)S(1)}, u32[]{:S(2)}, u32[]{:S(2)}) %collective-permute-start.17) | collective-permute-done | bytes 196640 | tf_op jit(solution)/shard_map/ppermute | solution.py:76
  177.7 2.3 %shard_map.86.refs_7_ = f32[8,128,128]{2,1,0:T(8,128)S(1)} custom-call(f32[1,64,768]{2,1,0:T(8,128)S(1)} %get-tuple-element.118.refs_0_, f32[1,64,768]{2,1,0:T(8,128)S(1)} %get-tuple-element.116.refs_1_, f32[1,64,512]{2,1,0:T(8,128)S(1)} %get-tuple-element.124.refs_2_, f32[1,64,768]{2,1,0:T(8,128)S(1)} %collective-permute-done.38.refs_3_, ...), custom_call_target="tpu_custom_call" | custom-call | flops 1073741824 | bytes 2621440 | tf_op jit(solution)/shard_map/pallas_call | solution.py:203
  180.0 2.3 %shard_map.87 = f32[8,256,128]{2,1,0:T(8,128)S(1)} custom-call(f32[1,64,768]{2,1,0:T(8,128)S(1)} %get-tuple-element.122.refs_0_, f32[1,64,768]{2,1,0:T(8,128)S(1)} %get-tuple-element.120.refs_1_, f32[1,64,512]{2,1,0:T(8,128)S(1)} %get-tuple-element.126.refs_2_, f32[1,64,768]{2,1,0:T(8,128)S(1)} %collective-permute-done.17.refs_3_, ...), custom_call_target="tpu_custom_call" | custom-call | flops 1073741824 | bytes 2621440 | tf_op jit(solution)/shard_map/pallas_call | solution.py:203
  182.4 19.7 %all_to_all.5 = f32[8,256,128]{2,1,0:T(8,128)S(1)} all-to-all(f32[8,256,128]{2,1,0:T(8,128)S(1)} %shard_map.87), channel_id=1, replica_groups=mesh['row'=8,'col'=16] {'row'}, dimensions={0} | all-to-all | bytes 2097152 | tf_op jit(solution)/shard_map/all_to_all | solution.py:283
  (108 shorter events, 30.4 us)
Async XLA Ops:
  3.1 71.1 %collective-permute-start.10 = (f32[2048,1024]{1,0:T(8,128)}, f32[2048,1024]{1,0:T(8,128)}, u32[]{:S(2)}, u32[]{:S(2)}) collective-permute-start(f32[2048,1024]{1,0:T(8,128)} %param.9), channel_id=1, source_target_pairs={{0,1},{1,0},{2,3},{3,2},{4,5},{5,4},{6,7},{7,6},{8,9},{9,8},{10,11... | collective-permute-start | bytes 25165832 | tf_op jit(solution)/shard_map/ppermute | solution.py:76
  4.3 9.9 %collective-permute-start.23 = (f32[1,64,768]{2,1,0:T(8,128)S(1)}, f32[1,64,768]{2,1,0:T(8,128)S(1)}, u32[]{:S(2)}, u32[]{:S(2)}) collective-permute-start(f32[1,64,768]{2,1,0:T(8,128)S(1)} %get-tuple-element.127), channel_id=1, source_target_pairs={{0,16},{1,17},{2,18},{3,19},{4,20},{5,21},{6,22},{7,23},{8,24},{9,... | collective-permute-start | bytes 589832 | tf_op jit(solution)/shard_map/ppermute | solution.py:76
  6.0 14.9 %collective-permute-start = (f32[1,64,768]{2,1,0:T(8,128)S(1)}, f32[1,64,768]{2,1,0:T(8,128)S(1)}, u32[]{:S(2)}, u32[]{:S(2)}) collective-permute-start(f32[1,64,768]{2,1,0:T(8,128)S(1)} %get-tuple-element.128), channel_id=1, source_target_pairs={{0,16},{1,17},{2,18},{3,19},{4,20},{5,21},{6,22},{7,23},{8,24},{9,... | collective-permute-start | bytes 589832 | tf_op jit(solution)/shard_map/ppermute | solution.py:76
  18.3 16.5 %collective-permute-start.26 = (f32[2,64,768]{2,1,0:T(8,128)S(1)}, f32[2,64,768]{2,1,0:T(8,128)S(1)}, u32[]{:S(2)}, u32[]{:S(2)}) collective-permute-start(f32[2,64,768]{2,1,0:T(8,128)S(1)} %pad_maximum_fusion.7), channel_id=1, source_target_pairs={{0,48},{1,49},{2,50},{3,51},{4,52},{5,53},{6,54},{7,55},{8,56},{9,... | collective-permute-start | bytes 1179656 | tf_op jit(solution)/shard_map/ppermute | solution.py:76
  20.8 9.6 %collective-permute-start.27 = (f32[2,64,640]{2,1,0:T(8,128)S(1)}, f32[2,64,640]{2,1,0:T(8,128)S(1)}, u32[]{:S(2)}, u32[]{:S(2)}) collective-permute-start(f32[2,64,640]{2,1,0:T(8,128)S(1)} %pad_maximum_fusion.10), channel_id=1, source_target_pairs={{0,64},{1,65},{2,66},{3,67},{4,68},{5,69},{6,70},{7,71},{8,72},{9,... | collective-permute-start | bytes 983048 | tf_op jit(solution)/shard_map/ppermute | solution.py:76
  21.4 10.7 %collective-permute-start.28 = (f32[2,64,640]{2,1,0:T(8,128)S(1)}, f32[2,64,640]{2,1,0:T(8,128)S(1)}, u32[]{:S(2)}, u32[]{:S(2)}) collective-permute-start(f32[2,64,640]{2,1,0:T(8,128)S(1)} %pad_maximum_fusion.11), channel_id=1, source_target_pairs={{0,16},{1,17},{2,18},{3,19},{4,20},{5,21},{6,22},{7,23},{8,24},{9,... | collective-permute-start | bytes 983048 | tf_op jit(solution)/shard_map/ppermute | solution.py:76
  22.2 15.1 %collective-permute-start.6 = (f32[2,64,640]{2,1,0:T(8,128)S(1)}, f32[2,64,640]{2,1,0:T(8,128)S(1)}, u32[]{:S(2)}, u32[]{:S(2)}) collective-permute-start(f32[2,64,640]{2,1,0:T(8,128)S(1)} %pad_maximum_fusion.9), channel_id=1, source_target_pairs={{0,16},{1,17},{2,18},{3,19},{4,20},{5,21},{6,22},{7,23},{8,24},{9,... | collective-permute-start | bytes 983048 | tf_op jit(solution)/shard_map/ppermute | solution.py:76
  30.4 11.3 %collective-permute-start.5 = (f32[2,64,640]{2,1,0:T(8,128)S(1)}, f32[2,64,640]{2,1,0:T(8,128)S(1)}, u32[]{:S(2)}, u32[]{:S(2)}) collective-permute-start(f32[2,64,640]{2,1,0:T(8,128)S(1)} %pad_maximum_fusion.8), channel_id=1, source_target_pairs={{0,64},{1,65},{2,66},{3,67},{4,68},{5,69},{6,70},{7,71},{8,72},{9,... | collective-permute-start | bytes 983048 | tf_op jit(solution)/shard_map/ppermute | solution.py:76
  32.1 13.2 %collective-permute-start.4 = (f32[2,64,768]{2,1,0:T(8,128)S(1)}, f32[2,64,768]{2,1,0:T(8,128)S(1)}, u32[]{:S(2)}, u32[]{:S(2)}) collective-permute-start(f32[2,64,768]{2,1,0:T(8,128)S(1)} %pad_maximum_fusion.6), channel_id=1, source_target_pairs={{0,48},{1,49},{2,50},{3,51},{4,52},{5,53},{6,54},{7,55},{8,56},{9,... | collective-permute-start | bytes 1179656 | tf_op jit(solution)/shard_map/ppermute | solution.py:76
  34.8 15.4 %collective-permute-start.30 = (f32[4,64,640]{2,1,0:T(8,128)S(1)}, f32[4,64,640]{2,1,0:T(8,128)S(1)}, u32[]{:S(2)}, u32[]{:S(2)}) collective-permute-start(f32[4,64,640]{2,1,0:T(8,128)S(1)} %pad_maximum_fusion.4.refs_1_), channel_id=1, source_target_pairs={{0,16},{1,17},{2,18},{3,19},{4,20},{5,21},{6,22},{7,23},{8,24},{9,... | collective-permute-start | bytes 1966088 | tf_op jit(solution)/shard_map/ppermute | solution.py:76
  37.3 22.0 %collective-permute-start.31 = (f32[4,64,640]{2,1,0:T(8,128)S(1)}, f32[4,64,640]{2,1,0:T(8,128)S(1)}, u32[]{:S(2)}, u32[]{:S(2)}) collective-permute-start(f32[4,64,640]{2,1,0:T(8,128)S(1)} %pad_maximum_fusion.5.refs_2_), channel_id=1, source_target_pairs={{0,48},{1,49},{2,50},{3,51},{4,52},{5,53},{6,54},{7,55},{8,56},{9,... | collective-permute-start | bytes 1966088 | tf_op jit(solution)/shard_map/ppermute | solution.py:76
  41.8 22.0 %collective-permute-start.29 = (f32[4,64,768]{2,1,0:T(8,128)S(1)}, f32[4,64,768]{2,1,0:T(8,128)S(1)}, u32[]{:S(2)}, u32[]{:S(2)}) collective-permute-start(f32[4,64,768]{2,1,0:T(8,128)S(1)} %pad_maximum_fusion.1.refs_0_), channel_id=1, source_target_pairs={{0,64},{1,65},{2,66},{3,67},{4,68},{5,69},{6,70},{7,71},{8,72},{9,... | collective-permute-start | bytes 2359304 | tf_op jit(solution)/shard_map/ppermute | solution.py:76
  45.3 28.9 %collective-permute-start.7 = (f32[4,64,768]{2,1,0:T(8,128)S(1)}, f32[4,64,768]{2,1,0:T(8,128)S(1)}, u32[]{:S(2)}, u32[]{:S(2)}) collective-permute-start(f32[4,64,768]{2,1,0:T(8,128)S(1)} %pad_maximum_fusion.refs_0_), channel_id=1, source_target_pairs={{0,64},{1,65},{2,66},{3,67},{4,68},{5,69},{6,70},{7,71},{8,72},{9,... | collective-permute-start | bytes 2359304 | tf_op jit(solution)/shard_map/ppermute | solution.py:76
  50.2 20.6 %collective-permute-start.9 = (f32[4,64,640]{2,1,0:T(8,128)S(1)}, f32[4,64,640]{2,1,0:T(8,128)S(1)}, u32[]{:S(2)}, u32[]{:S(2)}) collective-permute-start(f32[4,64,640]{2,1,0:T(8,128)S(1)} %pad_maximum_fusion.3.refs_2_), channel_id=1, source_target_pairs={{0,48},{1,49},{2,50},{3,51},{4,52},{5,53},{6,54},{7,55},{8,56},{9,... | collective-permute-start | bytes 1966088 | tf_op jit(solution)/shard_map/ppermute | solution.py:76
  59.3 11.6 %collective-permute-start.8 = (f32[4,64,640]{2,1,0:T(8,128)S(1)}, f32[4,64,640]{2,1,0:T(8,128)S(1)}, u32[]{:S(2)}, u32[]{:S(2)}) collective-permute-start(f32[4,64,640]{2,1,0:T(8,128)S(1)} %pad_maximum_fusion.2.refs_1_), channel_id=1, source_target_pairs={{0,16},{1,17},{2,18},{3,19},{4,20},{5,21},{6,22},{7,23},{8,24},{9,... | collective-permute-start | bytes 1966088 | tf_op jit(solution)/shard_map/ppermute | solution.py:76
  78.5 26.9 %collective-permute-start.20 = (f32[2048]{0:T(1024)S(1)}, f32[2048]{0:T(1024)S(1)}, u32[]{:S(2)}, u32[]{:S(2)}) collective-permute-start(f32[2048]{0:T(1024)S(1)} %add.134), channel_id=1, source_target_pairs={{0,4},{1,5},{2,6},{3,7},{4,0},{5,1},{6,2},{7,3},{8,12},{9,13},{10,... | collective-permute-start | bytes 24584 | tf_op jit(solution)/shard_map/ppermute | solution.py:76
  100.9 32.0 %collective-permute-start.32 = (f32[4,64,768]{2,1,0:T(8,128)S(1)}, f32[4,64,768]{2,1,0:T(8,128)S(1)}, u32[]{:S(2)}, u32[]{:S(2)}) collective-permute-start(f32[4,64,768]{2,1,0:T(8,128)S(1)} %get-tuple-element.95), channel_id=1, source_target_pairs={{0,4},{1,5},{2,6},{3,7},{4,0},{5,1},{6,2},{7,3},{8,12},{9,13},{10,... | collective-permute-start | bytes 2359304 | tf_op jit(solution)/shard_map/ppermute | solution.py:76
  101.1 33.8 %collective-permute-start.33 = (f32[4,64,768]{2,1,0:T(8,128)S(1)}, f32[4,64,768]{2,1,0:T(8,128)S(1)}, u32[]{:S(2)}, u32[]{:S(2)}) collective-permute-start(f32[4,64,768]{2,1,0:T(8,128)S(1)} %get-tuple-element.96), channel_id=1, source_target_pairs={{0,12},{1,13},{2,14},{3,15},{4,8},{5,9},{6,10},{7,11},{8,4},{9,5},... | collective-permute-start | bytes 2359304 | tf_op jit(solution)/shard_map/ppermute | solution.py:76
  105.1 27.7 %collective-permute-start.34 = (f32[4,64,512]{2,1,0:T(8,128)S(1)}, f32[4,64,512]{2,1,0:T(8,128)S(1)}, u32[]{:S(2)}, u32[]{:S(2)}) collective-permute-start(f32[4,64,512]{2,1,0:T(8,128)S(1)} %get-tuple-element.97), channel_id=1, source_target_pairs={{0,2},{1,3},{2,0},{3,1},{4,6},{5,7},{6,4},{7,5},{8,10},{9,11},{10,... | collective-permute-start | bytes 1572872 | tf_op jit(solution)/shard_map/ppermute | solution.py:76
  105.4 14.3 %collective-permute-start.21 = (f32[2048]{0:T(1024)S(1)}, f32[2048]{0:T(1024)S(1)}, u32[]{:S(2)}, u32[]{:S(2)}) collective-permute-start(f32[2048]{0:T(1024)S(1)} %add.135), channel_id=1, source_target_pairs={{0,12},{1,13},{2,14},{3,15},{4,8},{5,9},{6,10},{7,11},{8,4},{9,5},... | collective-permute-start | bytes 24584 | tf_op jit(solution)/shard_map/ppermute | solution.py:76
  116.1 31.7 %collective-permute-start.11 = (f32[4,64,768]{2,1,0:T(8,128)S(1)}, f32[4,64,768]{2,1,0:T(8,128)S(1)}, u32[]{:S(2)}, u32[]{:S(2)}) collective-permute-start(f32[4,64,768]{2,1,0:T(8,128)S(1)} %get-tuple-element.70), channel_id=1, source_target_pairs={{0,4},{1,5},{2,6},{3,7},{4,0},{5,1},{6,2},{7,3},{8,12},{9,13},{10,... | collective-permute-start | bytes 2359304 | tf_op jit(solution)/shard_map/ppermute | solution.py:76
  119.8 28.0 %collective-permute-start.12 = (f32[4,64,768]{2,1,0:T(8,128)S(1)}, f32[4,64,768]{2,1,0:T(8,128)S(1)}, u32[]{:S(2)}, u32[]{:S(2)}) collective-permute-start(f32[4,64,768]{2,1,0:T(8,128)S(1)} %get-tuple-element.71), channel_id=1, source_target_pairs={{0,12},{1,13},{2,14},{3,15},{4,8},{5,9},{6,10},{7,11},{8,4},{9,5},... | collective-permute-start | bytes 2359304 | tf_op jit(solution)/shard_map/ppermute | solution.py:76
  132.8 14.9 %collective-permute-start.13 = (f32[4,64,512]{2,1,0:T(8,128)S(1)}, f32[4,64,512]{2,1,0:T(8,128)S(1)}, u32[]{:S(2)}, u32[]{:S(2)}) collective-permute-start(f32[4,64,512]{2,1,0:T(8,128)S(1)} %get-tuple-element.72), channel_id=1, source_target_pairs={{0,2},{1,3},{2,0},{3,1},{4,6},{5,7},{6,4},{7,5},{8,10},{9,11},{10,... | collective-permute-start | bytes 1572872 | tf_op jit(solution)/shard_map/ppermute | solution.py:76
  132.9 35.3 %collective-permute-start.22 = (f32[2048]{0:T(1024)S(1)}, f32[2048]{0:T(1024)S(1)}, u32[]{:S(2)}, u32[]{:S(2)}) collective-permute-start(f32[2048]{0:T(1024)S(1)} %add.136), channel_id=1, source_target_pairs={{0,2},{1,3},{2,0},{3,1},{4,6},{5,7},{6,4},{7,5},{8,10},{9,11},{10,... | collective-permute-start | bytes 24584 | tf_op jit(solution)/shard_map/ppermute | solution.py:76
  135.0 13.0 %collective-permute-start.37 = (f32[2,64,512]{2,1,0:T(8,128)S(1)}, f32[2,64,512]{2,1,0:T(8,128)S(1)}, u32[]{:S(2)}, u32[]{:S(2)}) collective-permute-start(f32[2,64,512]{2,1,0:T(8,128)S(1)} %slice_add_fusion.4), channel_id=1, source_target_pairs={{0,4},{1,5},{2,6},{3,7},{4,0},{5,1},{6,2},{7,3},{8,12},{9,13},{10,... | collective-permute-start | bytes 786440 | tf_op jit(solution)/shard_map/ppermute | solution.py:76
  147.7 11.2 %collective-permute-start.36 = (f32[2,64,768]{2,1,0:T(8,128)S(1)}, f32[2,64,768]{2,1,0:T(8,128)S(1)}, u32[]{:S(2)}, u32[]{:S(2)}) collective-permute-start(f32[2,64,768]{2,1,0:T(8,128)S(1)} %slice_add_fusion), channel_id=1, source_target_pairs={{0,2},{1,3},{2,0},{3,1},{4,6},{5,7},{6,4},{7,5},{8,10},{9,11},{10,... | collective-permute-start | bytes 1179656 | tf_op jit(solution)/shard_map/ppermute | solution.py:76
  147.7 11.2 %collective-permute-start.35 = (f32[2,64,768]{2,1,0:T(8,128)S(1)}, f32[2,64,768]{2,1,0:T(8,128)S(1)}, u32[]{:S(2)}, u32[]{:S(2)}) collective-permute-start(f32[2,64,768]{2,1,0:T(8,128)S(1)} %slice_add_fusion.1), channel_id=1, source_target_pairs={{0,12},{1,13},{2,14},{3,15},{4,8},{5,9},{6,10},{7,11},{8,4},{9,5},... | collective-permute-start | bytes 1179656 | tf_op jit(solution)/shard_map/ppermute | solution.py:76
  147.8 14.7 %collective-permute-start.16 = (f32[2,64,512]{2,1,0:T(8,128)S(1)}, f32[2,64,512]{2,1,0:T(8,128)S(1)}, u32[]{:S(2)}, u32[]{:S(2)}) collective-permute-start(f32[2,64,512]{2,1,0:T(8,128)S(1)} %slice_add_fusion.5), channel_id=1, source_target_pairs={{0,4},{1,5},{2,6},{3,7},{4,0},{5,1},{6,2},{7,3},{8,12},{9,13},{10,... | collective-permute-start | bytes 786440 | tf_op jit(solution)/shard_map/ppermute | solution.py:76
  148.0 15.9 %collective-permute-start.15 = (f32[2,64,768]{2,1,0:T(8,128)S(1)}, f32[2,64,768]{2,1,0:T(8,128)S(1)}, u32[]{:S(2)}, u32[]{:S(2)}) collective-permute-start(f32[2,64,768]{2,1,0:T(8,128)S(1)} %slice_add_fusion.2), channel_id=1, source_target_pairs={{0,2},{1,3},{2,0},{3,1},{4,6},{5,7},{6,4},{7,5},{8,10},{9,11},{10,... | collective-permute-start | bytes 1179656 | tf_op jit(solution)/shard_map/ppermute | solution.py:76
  158.9 9.0 %collective-permute-start.14 = (f32[2,64,768]{2,1,0:T(8,128)S(1)}, f32[2,64,768]{2,1,0:T(8,128)S(1)}, u32[]{:S(2)}, u32[]{:S(2)}) collective-permute-start(f32[2,64,768]{2,1,0:T(8,128)S(1)} %slice_add_fusion.3), channel_id=1, source_target_pairs={{0,12},{1,13},{2,14},{3,15},{4,8},{5,9},{6,10},{7,11},{8,4},{9,5},... | collective-permute-start | bytes 1179656 | tf_op jit(solution)/shard_map/ppermute | solution.py:76
  159.0 10.3 %collective-permute-start.40 = (f32[1,64,512]{2,1,0:T(8,128)S(1)}, f32[1,64,512]{2,1,0:T(8,128)S(1)}, u32[]{:S(2)}, u32[]{:S(2)}) collective-permute-start(f32[1,64,512]{2,1,0:T(8,128)S(1)} %get-tuple-element.123), channel_id=1, source_target_pairs={{0,12},{1,13},{2,14},{3,15},{4,8},{5,9},{6,10},{7,11},{8,4},{9,5},... | collective-permute-start | bytes 393224 | tf_op jit(solution)/shard_map/ppermute | solution.py:76
  169.3 8.4 %collective-permute-start.17 = (f32[1,64,768]{2,1,0:T(8,128)S(1)}, f32[1,64,768]{2,1,0:T(8,128)S(1)}, u32[]{:S(2)}, u32[]{:S(2)}) collective-permute-start(f32[1,64,768]{2,1,0:T(8,128)S(1)} %get-tuple-element.121), channel_id=1, source_target_pairs={{0,2},{1,3},{2,0},{3,1},{4,6},{5,7},{6,4},{7,5},{8,10},{9,11},{10,... | collective-permute-start | bytes 589832 | tf_op jit(solution)/shard_map/ppermute | solution.py:76
  (14 other events, 284.2 us)

commit v5 on v4

--- a/solution.py
+++ b/solution.py
@@ -15,6 +15,7 @@
 DEPTH = (768, 640, 640)
 DOFF = (0, 768, 1408)
 TILE = 256
+LIFT = 256.0
 COLS = (768, 768, 512)
 COFF = (0, 768, 1536)
 BOTH = ("row", "col")
@@ -76,9 +77,17 @@
     return lax.ppermute(x, BOTH, pairs)
 
 
-def split(x):
+def to_f8(x):
+    return jnp.clip(x, -440.0, 440.0).astype(jnp.float8_e4m3fn)
+
+
+def split(x, level):
     high = lax.reduce_precision(x, 8, 7)
-    return high.astype(jnp.bfloat16), (x - high).astype(jnp.bfloat16)
+    return (
+        high.astype(jnp.bfloat16),
+        to_f8(high * level[:, None]),
+        to_f8((x - high) * (level * LIFT)[:, None]),
+    )
 
 
 STARTS = tuple(c // TILE for c in COFF)
@@ -89,12 +98,12 @@
     if half == 0:
         first, last, refs = refs[:3], refs[3:6], refs[6:]
     else:
-        parts, refs = refs[0], refs[1:]
-    (fho, flo, fhp, flp), outs, refs = refs[:4], refs[4:7], refs[7:]
-    m = 4 * ROWS
+        (high, cross), refs = refs[:2], refs[2:]
+    (own16, own8, own_rest, far16, far8, far_rest, level), refs = refs[:7], refs[7:]
+    outs, refs = refs[:3], refs[3:]
     t = pl.program_id(0)
     if half == 0:
-        parts, lhs = refs
+        high, cross, lhs16, lhs8 = refs
 
         @pl.when(t == 0)
         def _():
@@ -104,30 +113,35 @@
                     v = (last if at > 3 else first)[p][at & 3]
                     h = v.astype(jnp.bfloat16)
                     cols = pl.ds(DOFF[p], DEPTH[p])
-                    parts[0, e, :, cols] = h
-                    parts[1, e, :, cols] = (v - h.astype(jnp.float32)).astype(jnp.bfloat16)
+                    high[e, :, cols] = h
+                    cross[0, e, :, cols] = v.astype(jnp.float8_e4m3fn)
+                    rest = (v - h.astype(jnp.float32)) * LIFT
+                    cross[1, e, :, cols] = rest.astype(jnp.float8_e4m3fn)
 
     else:
-        (lhs,) = refs
+        lhs16, lhs8 = refs
     for q in range(3):
 
         @pl.when(t == STARTS[q])
         def _(q=q):
             for i in range(4):
                 e = tbl[q * 8 + half * 4 + i]
+                at = pl.ds(i * ROWS, ROWS)
+                lhs16[at, :] = high[e]
                 for k in range(2):
-                    lhs[pl.ds(k * m + i * ROWS, ROWS), :] = parts[k, e]
+                    lhs8[k, at, :] = cross[k, e]
 
     dot = functools.partial(
         lax.dot_general,
         dimension_numbers=(((1,), (1,)), ((), ())),
         preferred_element_type=jnp.float32,
     )
-    own, far, high = pl.ds(0, 1024), pl.ds(1024, 1024), pl.ds(0, m)
+    own, far = pl.ds(0, 1024), pl.ds(1024, 1024)
     rows = pl.ds(pl.multiple_of(t * TILE, TILE), TILE)
-    acc = dot(lhs[:, own], fho[rows, :]) + dot(lhs[:, far], fhp[rows, :])
-    low = dot(lhs[high, own], flo[rows, :]) + dot(lhs[high, far], flp[rows, :])
-    acc = (acc[:m] + (acc[m:] + low)).reshape(4, ROWS, TILE)
+    acc = dot(lhs16[:, own], own16[rows, :]) + dot(lhs16[:, far], far16[rows, :])
+    low = dot(lhs8[0, :, own], own_rest[rows, :]) + dot(lhs8[0, :, far], far_rest[rows, :])
+    low += dot(lhs8[1, :, own], own8[rows, :]) + dot(lhs8[1, :, far], far8[rows, :])
+    acc = (acc + low * level[...]).reshape(4, ROWS, TILE)
     for q in range(3):
 
         @pl.when((t >= STARTS[q]) & (t < STARTS[q] + SIZES[q]))
@@ -145,20 +159,26 @@
     ]
     shapes = [jax.ShapeDtypeStruct((4, ROWS, COLS[q]), jnp.float32) for q in range(3)]
     if half == 0:
-        outs.append(whole)
-        shapes.append(jax.ShapeDtypeStruct((2, 8, ROWS, 2048), jnp.bfloat16))
+        outs += [whole] * 2
+        shapes += [
+            jax.ShapeDtypeStruct((8, ROWS, 2048), jnp.bfloat16),
+            jax.ShapeDtypeStruct((2, 8, ROWS, 2048), jnp.float8_e4m3fn),
+        ]
     res = pl.pallas_call(
         functools.partial(mm_kernel, half),
         out_shape=shapes,
         grid_spec=pltpu.PrefetchScalarGridSpec(
             num_scalar_prefetch=1,
             grid=(2048 // TILE,),
-            in_specs=[whole] * (len(pieces) + 4),
+            in_specs=[whole] * (len(pieces) + 6) + [pl.BlockSpec((1, TILE), lambda t, tb: (0, t))],
             out_specs=outs,
-            scratch_shapes=[pltpu.VMEM((8 * ROWS, 2048), jnp.bfloat16)],
+            scratch_shapes=[
+                pltpu.VMEM((4 * ROWS, 2048), jnp.bfloat16),
+                pltpu.VMEM((2, 4 * ROWS, 2048), jnp.float8_e4m3fn),
+            ],
         ),
         cost_estimate=pl.CostEstimate(
-            flops=2 * 3 * 4 * ROWS * 2048 * 2048,
+            flops=2 * 2 * 4 * ROWS * 2048 * 2048,
             bytes_accessed=2 * 4 * ROWS * 2048 * 4 + 4 * 2048 * 2048,
             transcendentals=0,
         ),
@@ -246,12 +266,14 @@
                 continue
             gathered[c] = [jnp.concatenate([gathered[c][p], came[p]], axis=0) for p in range(3)]
 
-    fho, flo = split(factor)
     norms = jnp.sum(factor * factor, axis=1)
-    fhp, flp = split(far_factor)
-    far_norms = jnp.sum(far_factor * far_factor, axis=1)
-    factors = (fho, flo, fhp, flp)
-    norms = norms + far_norms
+    norms = norms + permute(norms, CORE)
+    level = 128.0 * lax.rsqrt(jnp.clip(norms, 1e-30, 1e38))
+    level, unlevel, norms = lax.optimization_barrier((level, 1.0 / (level * LIFT), norms))
+    own = split(factor, level)
+    far_factor, far_level, _ = lax.optimization_barrier((far_factor, level, own[0]))
+    far = split(far_factor, far_level)
+    factors = (*own, *far, unlevel[None, :])
     for d in range(3):
         norms = norms + permute(norms, COL_DIMS[d])
 

time: 205 us -> 200 us (0.976)
  other arithmetic: 7.87 us -> 21.2 us
  waiting for transfers between devices: 74.9 us -> 62.1 us
  Pallas kernels: 45.4 us -> 36.8 us
  starting transfers between devices: 49.9 us -> 57.7 us
    convert_element_type x0 -> x2, other arithmetic: none -> 13.5 us  [to_f8(): return jnp.clip(x, -440.0, 440.0).astype(jnp.float8_e4m3fn)]
    ppermute x41 -> x42, waiting for transfers between devices: 74.9 us -> 62.1 us  [permute(): return lax.ppermute(x, BOTH, pairs)]
    pallas_call x4, Pallas kernels: 40.8 us -> 32.1 us  [mm(): pl.pallas_call(functools.partial(mm_kernel, half), out_shape=shapes, grid...]
    ppermute x41 -> x42, starting transfers between devices: 49.9 us -> 57.7 us  [permute(): return lax.ppermute(x, BOTH, pairs)]
    reduce_sum x1 -> x0, other arithmetic: 4.26 us -> none  [step(): far_norms = jnp.sum(far_factor * far_factor, axis=1)]
    reduce_sum x1, other arithmetic: 1.59 us -> 4.15 us  [step(): norms = jnp.sum(factor * factor, axis=1)]
  transfers between devices with their start and end apart: 41 -> 42, of which waited for: 20 -> 15; matrix products, arithmetic and copies ran while one was open for 3% -> 8% of each run, Pallas kernels for 20% -> 12%
where the time goes in v5:
time: 200 us
  waiting for transfers between devices  62.1 us (31%)
  starting transfers between devices  57.7 us (29%)
  Pallas kernels  36.8 us (18%)
  other arithmetic  21.2 us (11%)
  blocking collectives  17.9 us (9%)
  local copies, waits for them, and re-layouts  3.59 us (2%)
    ppermute x42, waiting for transfers between devices, permute(): return lax.ppermute(x, BOTH, pairs)  62.1 us
    ppermute x42, starting transfers between devices, permute(): return lax.ppermute(x, BOTH, pairs)  57.7 us
    pallas_call x4, Pallas kernels, mm(): pl.pallas_call(functools.partial(mm_kernel, half), out_shape=shapes, grid...  32.1 us
    all_to_all x1, blocking collectives, step(): lax.all_to_all(sums[0], 'row', split_axis=0, concat_axis=0, tiled=True)  17.9 us
    convert_element_type x2, other arithmetic, to_f8(): return jnp.clip(x, -440.0, 440.0).astype(jnp.float8_e4m3fn)  13.5 us
    pallas_call x2, Pallas kernels, tail(): pl.pallas_call(tail_kernel, out_shape=jax.ShapeDtypeStruct((8, rows, 128)...  4.66 us
    reduce_sum x1, other arithmetic, step(): norms = jnp.sum(factor * factor, axis=1)  4.15 us
  transfers between devices with their start and end apart: 42, of which 15 were waited for; matrix products, arithmetic and copies ran while one was open for 8% of the time, Pallas kernels for 12%

profile of v5, /device:TPU:0, one launch (start us, length us, event | category | flops | bytes accessed | tf_op | source)
XLA Modules:
  0.0 199.6 jit_solution(7098919720013779958)
XLA Ops:
  9.2 4.1 %multiply_reduce_fusion = f32[2048]{0:T(1024)S(1)} fusion(f32[2048,1024]{1,0:T(8,128)} %param.9), kind=kLoop, calls=%fused_computation.16 | loop fusion | flops 4192256 | bytes 8396800 | tf_op jit(solution)/shard_map/reduce_sum | solution.py:269
  13.5 2.9 %collective-permute-start.2 = (f32[1,64,640]{2,1,0:T(8,128)S(1)}, f32[1,64,640]{2,1,0:T(8,128)S(1)}, u32[]{:S(2)}, u32[]{:S(2)}) collective-permute-start(f32[1,64,640]{2,1,0:T(8,128)S(1)} %get-tuple-element.149), channel_id=1, source_target_pairs={{0,48},{1,49},{2,50},{3,51},{4,52},{5,53},{6,54},{7,55},{8,56},{9,... | collective-permute-start | bytes 491528 | tf_op jit(solution)/shard_map/ppermute | solution.py:77
  16.6 3.3 %collective-permute-start.3 = (f32[1,64,640]{2,1,0:T(8,128)S(1)}, f32[1,64,640]{2,1,0:T(8,128)S(1)}, u32[]{:S(2)}, u32[]{:S(2)}) collective-permute-start(f32[1,64,640]{2,1,0:T(8,128)S(1)} %get-tuple-element.148), channel_id=1, source_target_pairs={{0,64},{1,65},{2,66},{3,67},{4,68},{5,69},{6,70},{7,71},{8,72},{9,... | collective-permute-start | bytes 491528 | tf_op jit(solution)/shard_map/ppermute | solution.py:77
  19.9 2.8 %collective-permute-start.25 = (f32[1,64,640]{2,1,0:T(8,128)S(1)}, f32[1,64,640]{2,1,0:T(8,128)S(1)}, u32[]{:S(2)}, u32[]{:S(2)}) collective-permute-start(f32[1,64,640]{2,1,0:T(8,128)S(1)} %get-tuple-element.150), channel_id=1, source_target_pairs={{0,48},{1,49},{2,50},{3,51},{4,52},{5,53},{6,54},{7,55},{8,56},{9,... | collective-permute-start | bytes 491528 | tf_op jit(solution)/shard_map/ppermute | solution.py:77
  22.8 2.4 %collective-permute-start.26 = (f32[1,64,640]{2,1,0:T(8,128)S(1)}, f32[1,64,640]{2,1,0:T(8,128)S(1)}, u32[]{:S(2)}, u32[]{:S(2)}) collective-permute-start(f32[1,64,640]{2,1,0:T(8,128)S(1)} %get-tuple-element.147), channel_id=1, source_target_pairs={{0,64},{1,65},{2,66},{3,67},{4,68},{5,69},{6,70},{7,71},{8,72},{9,... | collective-permute-start | bytes 491528 | tf_op jit(solution)/shard_map/ppermute | solution.py:77
  25.2 2.8 %collective-permute-start.4 = (f32[2,64,768]{2,1,0:T(8,128)S(1)}, f32[2,64,768]{2,1,0:T(8,128)S(1)}, u32[]{:S(2)}, u32[]{:S(2)}) collective-permute-start(f32[2,64,768]{2,1,0:T(8,128)S(1)} %pad_maximum_fusion.6), channel_id=1, source_target_pairs={{0,48},{1,49},{2,50},{3,51},{4,52},{5,53},{6,54},{7,55},{8,56},{9,... | collective-permute-start | bytes 1179656 | tf_op jit(solution)/shard_map/ppermute | solution.py:77
  28.1 2.5 %collective-permute-start.5 = (f32[2,64,640]{2,1,0:T(8,128)S(1)}, f32[2,64,640]{2,1,0:T(8,128)S(1)}, u32[]{:S(2)}, u32[]{:S(2)}) collective-permute-start(f32[2,64,640]{2,1,0:T(8,128)S(1)} %pad_maximum_fusion.8), channel_id=1, source_target_pairs={{0,64},{1,65},{2,66},{3,67},{4,68},{5,69},{6,70},{7,71},{8,72},{9,... | collective-permute-start | bytes 983048 | tf_op jit(solution)/shard_map/ppermute | solution.py:77
  32.2 8.1 %collective-permute-done.5 = f32[2,64,640]{2,1,0:T(8,128)S(1)} collective-permute-done((f32[2,64,640]{2,1,0:T(8,128)S(1)}, f32[2,64,640]{2,1,0:T(8,128)S(1)}, u32[]{:S(2)}, u32[]{:S(2)}) %collective-permute-start.5) | collective-permute-done | bytes 327712 | tf_op jit(solution)/shard_map/ppermute | solution.py:77
  44.9 2.7 %collective-permute-start.9 = (f32[4,64,640]{2,1,0:T(8,128)S(1)}, f32[4,64,640]{2,1,0:T(8,128)S(1)}, u32[]{:S(2)}, u32[]{:S(2)}) collective-permute-start(f32[4,64,640]{2,1,0:T(8,128)S(1)} %pad_maximum_fusion.3.refs_2_), channel_id=1, source_target_pairs={{0,48},{1,49},{2,50},{3,51},{4,52},{5,53},{6,54},{7,55},{8,56},{9,... | collective-permute-start | bytes 1966088 | tf_op jit(solution)/shard_map/ppermute | solution.py:77
  47.8 5.5 %collective-permute-done.29 = f32[2,64,640]{2,1,0:T(8,128)S(1)} collective-permute-done((f32[2,64,640]{2,1,0:T(8,128)S(1)}, f32[2,64,640]{2,1,0:T(8,128)S(1)}, u32[]{:S(2)}, u32[]{:S(2)}) %collective-permute-start.29) | collective-permute-done | bytes 327712 | tf_op jit(solution)/shard_map/ppermute | solution.py:77
  53.3 2.5 %collective-permute-start.22 = (f32[2048]{0:T(1024)S(1)}, f32[2048]{0:T(1024)S(1)}, u32[]{:S(2)}, u32[]{:S(2)}) collective-permute-start(f32[2048]{0:T(1024)S(1)} %add.135), channel_id=1, source_target_pairs={{0,12},{1,13},{2,14},{3,15},{4,8},{5,9},{6,10},{7,11},{8,4},{9,5},... | collective-permute-start | bytes 24584 | tf_op jit(solution)/shard_map/ppermute | solution.py:77
  55.8 2.4 %collective-permute-start.7 = (f32[4,64,768]{2,1,0:T(8,128)S(1)}, f32[4,64,768]{2,1,0:T(8,128)S(1)}, u32[]{:S(2)}, u32[]{:S(2)}) collective-permute-start(f32[4,64,768]{2,1,0:T(8,128)S(1)} %pad_maximum_fusion.refs_0_), channel_id=1, source_target_pairs={{0,64},{1,65},{2,66},{3,67},{4,68},{5,69},{6,70},{7,71},{8,72},{9,... | collective-permute-start | bytes 2359304 | tf_op jit(solution)/shard_map/ppermute | solution.py:77
  58.4 2.2 %collective-permute-start.30 = (f32[4,64,768]{2,1,0:T(8,128)S(1)}, f32[4,64,768]{2,1,0:T(8,128)S(1)}, u32[]{:S(2)}, u32[]{:S(2)}) collective-permute-start(f32[4,64,768]{2,1,0:T(8,128)S(1)} %pad_maximum_fusion.1.refs_0_), channel_id=1, source_target_pairs={{0,64},{1,65},{2,66},{3,67},{4,68},{5,69},{6,70},{7,71},{8,72},{9,... | collective-permute-start | bytes 2359304 | tf_op jit(solution)/shard_map/ppermute | solution.py:77
  60.6 4.0 %collective-permute-done.8.refs_4_ = f32[4,64,640]{2,1,0:T(8,128)S(1)} collective-permute-done((f32[4,64,640]{2,1,0:T(8,128)S(1)}, f32[4,64,640]{2,1,0:T(8,128)S(1)}, u32[]{:S(2)}, u32[]{:S(2)}) %collective-permute-start.8) | collective-permute-done | bytes 655392 | tf_op jit(solution)/shard_map/ppermute | solution.py:77
  67.4 5.7 %fusion.4 = (f8e4m3fn[2048,1024]{1,0:T(32,128)(4,1)S(1)}, f8e4m3fn[2048,1024]{1,0:T(32,128)(4,1)S(1)}, bf16[2048,1024]{1,0:T(8,128)(2,1)S(1)}) fusion(f32[2048,1024]{1,0:T(8,128)S(1)} %bitcast.30, f32[2048]{0:T(1024)S(1)} %broadcast_multiply_fusion.1, f32[2048]{0:T(1024)S(1)} %fusion.11), kind=kLoop, calls=%fused_computation.10 | loop fusion | flops 18874368 | bytes 16793600 | tf_op jit(solution)/shard_map/convert_element_type | solution.py:81
  73.1 4.1 %collective-permute-done.7.refs_3_ = f32[4,64,768]{2,1,0:T(8,128)S(1)} collective-permute-done((f32[4,64,768]{2,1,0:T(8,128)S(1)}, f32[4,64,768]{2,1,0:T(8,128)S(1)}, u32[]{:S(2)}, u32[]{:S(2)}) %collective-permute-start.7) | collective-permute-done | bytes 786464 | tf_op jit(solution)/shard_map/ppermute | solution.py:77
  78.8 6.9 %collective-permute-done.30.refs_3_ = f32[4,64,768]{2,1,0:T(8,128)S(1)} collective-permute-done((f32[4,64,768]{2,1,0:T(8,128)S(1)}, f32[4,64,768]{2,1,0:T(8,128)S(1)}, u32[]{:S(2)}, u32[]{:S(2)}) %collective-permute-start.30) | collective-permute-done | bytes 786464 | tf_op jit(solution)/shard_map/ppermute | solution.py:77
  85.7 7.9 %fusion.9 = (f8e4m3fn[2048,1024]{1,0:T(32,128)(4,1)S(1)}, f8e4m3fn[2048,1024]{1,0:T(32,128)(4,1)S(1)}, bf16[2048,1024]{1,0:T(8,128)(2,1)S(1)}) fusion(f32[2048,1024]{1,0:T(8,128)} %collective-permute-done.11, f32[2048]{0:T(1024)S(1)} %broadcast_multiply_fusion, f32[2048]{0:T(1024)S(1)} %fusion.11), kind=kLoop, calls=%fused_computation.15 | loop fusion | flops 18874368 | bytes 16793600 | tf_op jit(solution)/shard_map/convert_element_type | solution.py:81
  93.5 8.5 %shard_map.82 = (f32[4,64,768]{2,1,0:T(8,128)S(1)}, f32[4,64,768]{2,1,0:T(8,128)S(1)}, f32[4,64,512]{2,1,0:T(8,128)S(1)}, bf16[8,64,2048]{2,1,0:T(8,128)(2,1)S(1)}, f8e4m3fn[2,8,64,2048]{3,2,1,0:T(32,128)(4,1)S(1)}) custom-call(s32[24]{0:T(128)S(1)} %fusion.12.tbl, f32[4,64,768]{2,1,0:T(8,128)S(1)} %pad_maximum_fusion.refs_0_, ...), custom_call_target="tpu_custom_call" | custom-call | flops 4294967296 | bytes 20971520 | tf_op jit(solution)/shard_map/pallas_call | solution.py:167
  105.2 8.5 %shard_map.84 = (f32[4,64,768]{2,1,0:T(8,128)S(1)}, f32[4,64,768]{2,1,0:T(8,128)S(1)}, f32[4,64,512]{2,1,0:T(8,128)S(1)}, bf16[8,64,2048]{2,1,0:T(8,128)(2,1)S(1)}, f8e4m3fn[2,8,64,2048]{3,2,1,0:T(32,128)(4,1)S(1)}) custom-call(s32[24]{0:T(128)S(1)} %fusion.12.tbl, f32[4,64,768]{2,1,0:T(8,128)S(1)} %pad_maximum_fusion.1.refs_0_, ...), custom_call_target="tpu_custom_call" | custom-call | flops 4294967296 | bytes 20971520 | tf_op jit(solution)/shard_map/pallas_call | solution.py:167
  114.2 2.6 %collective-permute-start.34 = (f32[4,64,768]{2,1,0:T(8,128)S(1)}, f32[4,64,768]{2,1,0:T(8,128)S(1)}, u32[]{:S(2)}, u32[]{:S(2)}) collective-permute-start(f32[4,64,768]{2,1,0:T(8,128)S(1)} %get-tuple-element.110), channel_id=1, source_target_pairs={{0,12},{1,13},{2,14},{3,15},{4,8},{5,9},{6,10},{7,11},{8,4},{9,5},... | collective-permute-start | bytes 2359304 | tf_op jit(solution)/shard_map/ppermute | solution.py:77
  116.9 7.6 %shard_map.83 = (f32[4,64,768]{2,1,0:T(8,128)S(1)}, f32[4,64,768]{2,1,0:T(8,128)S(1)}, f32[4,64,512]{2,1,0:T(8,128)S(1)}) custom-call(s32[24]{0:T(128)S(1)} %fusion.12.tbl, bf16[8,64,2048]{2,1,0:T(8,128)(2,1)S(1)} %get-tuple-element.79.refs_0_, f8e4m3fn[2,8,64,2048]{3,2,1,0:T(32,128)(4,1)S(1)} %get-tuple-element.80.refs_1_, ...), custom_call_target="tpu_custom_call" | custom-call | flops 4294967296 | bytes 20971520 | tf_op jit(solution)/shard_map/pallas_call | solution.py:167
  124.4 7.6 %shard_map.85 = (f32[4,64,768]{2,1,0:T(8,128)S(1)}, f32[4,64,768]{2,1,0:T(8,128)S(1)}, f32[4,64,512]{2,1,0:T(8,128)S(1)}) custom-call(s32[24]{0:T(128)S(1)} %fusion.12.tbl, bf16[8,64,2048]{2,1,0:T(8,128)(2,1)S(1)} %get-tuple-element.106.refs_0_, f8e4m3fn[2,8,64,2048]{3,2,1,0:T(32,128)(4,1)S(1)} %get-tuple-element.107.refs_1_, ...), custom_call_target="tpu_custom_call" | custom-call | flops 4294967296 | bytes 20971520 | tf_op jit(solution)/shard_map/pallas_call | solution.py:167
  135.0 11.6 %collective-permute-done.35 = f32[4,64,512]{2,1,0:T(8,128)S(1)} collective-permute-done((f32[4,64,512]{2,1,0:T(8,128)S(1)}, f32[4,64,512]{2,1,0:T(8,128)S(1)}, u32[]{:S(2)}, u32[]{:S(2)}) %collective-permute-start.35) | collective-permute-done | bytes 524320 | tf_op jit(solution)/shard_map/ppermute | solution.py:77
  146.6 2.4 %collective-permute-start.16 = (f32[2,64,768]{2,1,0:T(8,128)S(1)}, f32[2,64,768]{2,1,0:T(8,128)S(1)}, u32[]{:S(2)}, u32[]{:S(2)}) collective-permute-start(f32[2,64,768]{2,1,0:T(8,128)S(1)} %slice_add_fusion.2), channel_id=1, source_target_pairs={{0,2},{1,3},{2,0},{3,1},{4,6},{5,7},{6,4},{7,5},{8,10},{9,11},{10,... | collective-permute-start | bytes 1179656 | tf_op jit(solution)/shard_map/ppermute | solution.py:77
  150.8 6.0 %collective-permute-done.17 = f32[2,64,512]{2,1,0:T(8,128)S(1)} collective-permute-done((f32[2,64,512]{2,1,0:T(8,128)S(1)}, f32[2,64,512]{2,1,0:T(8,128)S(1)}, u32[]{:S(2)}, u32[]{:S(2)}) %collective-permute-start.17) | collective-permute-done | bytes 262176 | tf_op jit(solution)/shard_map/ppermute | solution.py:77
  159.5 4.0 %collective-permute-done.38 = f32[2,64,512]{2,1,0:T(8,128)S(1)} collective-permute-done((f32[2,64,512]{2,1,0:T(8,128)S(1)}, f32[2,64,512]{2,1,0:T(8,128)S(1)}, u32[]{:S(2)}, u32[]{:S(2)}) %collective-permute-start.38) | collective-permute-done | bytes 262176 | tf_op jit(solution)/shard_map/ppermute | solution.py:77
  168.2 1.9 collective-permute-done.20.refs_5_
  172.1 4.1 %collective-permute-done.41.refs_5_ = f32[1,64,512]{2,1,0:T(8,128)S(1)} collective-permute-done((f32[1,64,512]{2,1,0:T(8,128)S(1)}, f32[1,64,512]{2,1,0:T(8,128)S(1)}, u32[]{:S(2)}, u32[]{:S(2)}) %collective-permute-start.41) | collective-permute-done | bytes 131104 | tf_op jit(solution)/shard_map/ppermute | solution.py:77
  176.3 2.3 %shard_map.86.refs_7_ = f32[8,128,128]{2,1,0:T(8,128)S(1)} custom-call(f32[1,64,768]{2,1,0:T(8,128)S(1)} %get-tuple-element.134.refs_0_, f32[1,64,768]{2,1,0:T(8,128)S(1)} %get-tuple-element.132.refs_1_, f32[1,64,512]{2,1,0:T(8,128)S(1)} %get-tuple-element.140.refs_2_, f32[1,64,768]{2,1,0:T(8,128)S(1)} %collective-permute-done.39.refs_3_, ...), custom_call_target="tpu_custom_call" | custom-call | flops 1073741824 | bytes 2621440 | tf_op jit(solution)/shard_map/pallas_call | solution.py:223
  178.6 2.3 %shard_map.87 = f32[8,256,128]{2,1,0:T(8,128)S(1)} custom-call(f32[1,64,768]{2,1,0:T(8,128)S(1)} %get-tuple-element.138.refs_0_, f32[1,64,768]{2,1,0:T(8,128)S(1)} %get-tuple-element.136.refs_1_, f32[1,64,512]{2,1,0:T(8,128)S(1)} %get-tuple-element.142.refs_2_, f32[1,64,768]{2,1,0:T(8,128)S(1)} %collective-permute-done.18.refs_3_, ...), custom_call_target="tpu_custom_call" | custom-call | flops 1073741824 | bytes 2621440 | tf_op jit(solution)/shard_map/pallas_call | solution.py:223
  181.0 17.9 %all_to_all.5 = f32[8,256,128]{2,1,0:T(8,128)S(1)} all-to-all(f32[8,256,128]{2,1,0:T(8,128)S(1)} %shard_map.87), channel_id=1, replica_groups=mesh['row'=8,'col'=16] {'row'}, dimensions={0} | all-to-all | bytes 2097152 | tf_op jit(solution)/shard_map/all_to_all | solution.py:305
  (114 shorter events, 38.7 us)
Async XLA Ops:
  3.1 82.6 %collective-permute-start.11 = (f32[2048,1024]{1,0:T(8,128)}, f32[2048,1024]{1,0:T(8,128)}, u32[]{:S(2)}, u32[]{:S(2)}) collective-permute-start(f32[2048,1024]{1,0:T(8,128)} %param.9), channel_id=1, source_target_pairs={{0,1},{1,0},{2,3},{3,2},{4,5},{5,4},{6,7},{7,6},{8,9},{9,8},{10,11... | collective-permute-start | bytes 25165832 | tf_op jit(solution)/shard_map/ppermute | solution.py:77
  4.3 15.6 %collective-permute-start = (f32[1,64,768]{2,1,0:T(8,128)S(1)}, f32[1,64,768]{2,1,0:T(8,128)S(1)}, u32[]{:S(2)}, u32[]{:S(2)}) collective-permute-start(f32[1,64,768]{2,1,0:T(8,128)S(1)} %get-tuple-element.144), channel_id=1, source_target_pairs={{0,16},{1,17},{2,18},{3,19},{4,20},{5,21},{6,22},{7,23},{8,24},{9,... | collective-permute-start | bytes 589832 | tf_op jit(solution)/shard_map/ppermute | solution.py:77
  5.9 22.2 %collective-permute-start.24 = (f32[1,64,768]{2,1,0:T(8,128)S(1)}, f32[1,64,768]{2,1,0:T(8,128)S(1)}, u32[]{:S(2)}, u32[]{:S(2)}) collective-permute-start(f32[1,64,768]{2,1,0:T(8,128)S(1)} %get-tuple-element.143), channel_id=1, source_target_pairs={{0,16},{1,17},{2,18},{3,19},{4,20},{5,21},{6,22},{7,23},{8,24},{9,... | collective-permute-start | bytes 589832 | tf_op jit(solution)/shard_map/ppermute | solution.py:77
  13.5 9.2 %collective-permute-start.2 = (f32[1,64,640]{2,1,0:T(8,128)S(1)}, f32[1,64,640]{2,1,0:T(8,128)S(1)}, u32[]{:S(2)}, u32[]{:S(2)}) collective-permute-start(f32[1,64,640]{2,1,0:T(8,128)S(1)} %get-tuple-element.149), channel_id=1, source_target_pairs={{0,48},{1,49},{2,50},{3,51},{4,52},{5,53},{6,54},{7,55},{8,56},{9,... | collective-permute-start | bytes 491528 | tf_op jit(solution)/shard_map/ppermute | solution.py:77
  16.6 8.6 %collective-permute-start.3 = (f32[1,64,640]{2,1,0:T(8,128)S(1)}, f32[1,64,640]{2,1,0:T(8,128)S(1)}, u32[]{:S(2)}, u32[]{:S(2)}) collective-permute-start(f32[1,64,640]{2,1,0:T(8,128)S(1)} %get-tuple-element.148), channel_id=1, source_target_pairs={{0,64},{1,65},{2,66},{3,67},{4,68},{5,69},{6,70},{7,71},{8,72},{9,... | collective-permute-start | bytes 491528 | tf_op jit(solution)/shard_map/ppermute | solution.py:77
  19.9 10.7 %collective-permute-start.25 = (f32[1,64,640]{2,1,0:T(8,128)S(1)}, f32[1,64,640]{2,1,0:T(8,128)S(1)}, u32[]{:S(2)}, u32[]{:S(2)}) collective-permute-start(f32[1,64,640]{2,1,0:T(8,128)S(1)} %get-tuple-element.150), channel_id=1, source_target_pairs={{0,48},{1,49},{2,50},{3,51},{4,52},{5,53},{6,54},{7,55},{8,56},{9,... | collective-permute-start | bytes 491528 | tf_op jit(solution)/shard_map/ppermute | solution.py:77
  25.2 17.5 %collective-permute-start.4 = (f32[2,64,768]{2,1,0:T(8,128)S(1)}, f32[2,64,768]{2,1,0:T(8,128)S(1)}, u32[]{:S(2)}, u32[]{:S(2)}) collective-permute-start(f32[2,64,768]{2,1,0:T(8,128)S(1)} %pad_maximum_fusion.6), channel_id=1, source_target_pairs={{0,48},{1,49},{2,50},{3,51},{4,52},{5,53},{6,54},{7,55},{8,56},{9,... | collective-permute-start | bytes 1179656 | tf_op jit(solution)/shard_map/ppermute | solution.py:77
  28.1 12.2 %collective-permute-start.5 = (f32[2,64,640]{2,1,0:T(8,128)S(1)}, f32[2,64,640]{2,1,0:T(8,128)S(1)}, u32[]{:S(2)}, u32[]{:S(2)}) collective-permute-start(f32[2,64,640]{2,1,0:T(8,128)S(1)} %pad_maximum_fusion.8), channel_id=1, source_target_pairs={{0,64},{1,65},{2,66},{3,67},{4,68},{5,69},{6,70},{7,71},{8,72},{9,... | collective-permute-start | bytes 983048 | tf_op jit(solution)/shard_map/ppermute | solution.py:77
  30.7 11.6 %collective-permute-start.6 = (f32[2,64,640]{2,1,0:T(8,128)S(1)}, f32[2,64,640]{2,1,0:T(8,128)S(1)}, u32[]{:S(2)}, u32[]{:S(2)}) collective-permute-start(f32[2,64,640]{2,1,0:T(8,128)S(1)} %pad_maximum_fusion.9), channel_id=1, source_target_pairs={{0,16},{1,17},{2,18},{3,19},{4,20},{5,21},{6,22},{7,23},{8,24},{9,... | collective-permute-start | bytes 983048 | tf_op jit(solution)/shard_map/ppermute | solution.py:77
  31.3 13.6 %collective-permute-start.28 = (f32[2,64,640]{2,1,0:T(8,128)S(1)}, f32[2,64,640]{2,1,0:T(8,128)S(1)}, u32[]{:S(2)}, u32[]{:S(2)}) collective-permute-start(f32[2,64,640]{2,1,0:T(8,128)S(1)} %pad_maximum_fusion.10), channel_id=1, source_target_pairs={{0,64},{1,65},{2,66},{3,67},{4,68},{5,69},{6,70},{7,71},{8,72},{9,... | collective-permute-start | bytes 983048 | tf_op jit(solution)/shard_map/ppermute | solution.py:77
  42.2 13.6 %collective-permute-start.27 = (f32[2,64,768]{2,1,0:T(8,128)S(1)}, f32[2,64,768]{2,1,0:T(8,128)S(1)}, u32[]{:S(2)}, u32[]{:S(2)}) collective-permute-start(f32[2,64,768]{2,1,0:T(8,128)S(1)} %pad_maximum_fusion.7), channel_id=1, source_target_pairs={{0,48},{1,49},{2,50},{3,51},{4,52},{5,53},{6,54},{7,55},{8,56},{9,... | collective-permute-start | bytes 1179656 | tf_op jit(solution)/shard_map/ppermute | solution.py:77
  42.7 10.6 %collective-permute-start.29 = (f32[2,64,640]{2,1,0:T(8,128)S(1)}, f32[2,64,640]{2,1,0:T(8,128)S(1)}, u32[]{:S(2)}, u32[]{:S(2)}) collective-permute-start(f32[2,64,640]{2,1,0:T(8,128)S(1)} %pad_maximum_fusion.11), channel_id=1, source_target_pairs={{0,16},{1,17},{2,18},{3,19},{4,20},{5,21},{6,22},{7,23},{8,24},{9,... | collective-permute-start | bytes 983048 | tf_op jit(solution)/shard_map/ppermute | solution.py:77
  43.9 20.7 %collective-permute-start.8 = (f32[4,64,640]{2,1,0:T(8,128)S(1)}, f32[4,64,640]{2,1,0:T(8,128)S(1)}, u32[]{:S(2)}, u32[]{:S(2)}) collective-permute-start(f32[4,64,640]{2,1,0:T(8,128)S(1)} %pad_maximum_fusion.2.refs_1_), channel_id=1, source_target_pairs={{0,16},{1,17},{2,18},{3,19},{4,20},{5,21},{6,22},{7,23},{8,24},{9,... | collective-permute-start | bytes 1966088 | tf_op jit(solution)/shard_map/ppermute | solution.py:77
  44.9 20.6 %collective-permute-start.9 = (f32[4,64,640]{2,1,0:T(8,128)S(1)}, f32[4,64,640]{2,1,0:T(8,128)S(1)}, u32[]{:S(2)}, u32[]{:S(2)}) collective-permute-start(f32[4,64,640]{2,1,0:T(8,128)S(1)} %pad_maximum_fusion.3.refs_2_), channel_id=1, source_target_pairs={{0,48},{1,49},{2,50},{3,51},{4,52},{5,53},{6,54},{7,55},{8,56},{9,... | collective-permute-start | bytes 1966088 | tf_op jit(solution)/shard_map/ppermute | solution.py:77
  55.8 21.4 %collective-permute-start.7 = (f32[4,64,768]{2,1,0:T(8,128)S(1)}, f32[4,64,768]{2,1,0:T(8,128)S(1)}, u32[]{:S(2)}, u32[]{:S(2)}) collective-permute-start(f32[4,64,768]{2,1,0:T(8,128)S(1)} %pad_maximum_fusion.refs_0_), channel_id=1, source_target_pairs={{0,64},{1,65},{2,66},{3,67},{4,68},{5,69},{6,70},{7,71},{8,72},{9,... | collective-permute-start | bytes 2359304 | tf_op jit(solution)/shard_map/ppermute | solution.py:77
  58.4 27.2 %collective-permute-start.30 = (f32[4,64,768]{2,1,0:T(8,128)S(1)}, f32[4,64,768]{2,1,0:T(8,128)S(1)}, u32[]{:S(2)}, u32[]{:S(2)}) collective-permute-start(f32[4,64,768]{2,1,0:T(8,128)S(1)} %pad_maximum_fusion.1.refs_0_), channel_id=1, source_target_pairs={{0,64},{1,65},{2,66},{3,67},{4,68},{5,69},{6,70},{7,71},{8,72},{9,... | collective-permute-start | bytes 2359304 | tf_op jit(solution)/shard_map/ppermute | solution.py:77
  64.6 12.6 %collective-permute-start.31 = (f32[4,64,640]{2,1,0:T(8,128)S(1)}, f32[4,64,640]{2,1,0:T(8,128)S(1)}, u32[]{:S(2)}, u32[]{:S(2)}) collective-permute-start(f32[4,64,640]{2,1,0:T(8,128)S(1)} %pad_maximum_fusion.4.refs_1_), channel_id=1, source_target_pairs={{0,16},{1,17},{2,18},{3,19},{4,20},{5,21},{6,22},{7,23},{8,24},{9,... | collective-permute-start | bytes 1966088 | tf_op jit(solution)/shard_map/ppermute | solution.py:77
  65.5 13.2 %collective-permute-start.32 = (f32[4,64,640]{2,1,0:T(8,128)S(1)}, f32[4,64,640]{2,1,0:T(8,128)S(1)}, u32[]{:S(2)}, u32[]{:S(2)}) collective-permute-start(f32[4,64,640]{2,1,0:T(8,128)S(1)} %pad_maximum_fusion.5.refs_2_), channel_id=1, source_target_pairs={{0,48},{1,49},{2,50},{3,51},{4,52},{5,53},{6,54},{7,55},{8,56},{9,... | collective-permute-start | bytes 1966088 | tf_op jit(solution)/shard_map/ppermute | solution.py:77
  102.1 30.6 %collective-permute-start.12 = (f32[4,64,768]{2,1,0:T(8,128)S(1)}, f32[4,64,768]{2,1,0:T(8,128)S(1)}, u32[]{:S(2)}, u32[]{:S(2)}) collective-permute-start(f32[4,64,768]{2,1,0:T(8,128)S(1)} %get-tuple-element.82), channel_id=1, source_target_pairs={{0,4},{1,5},{2,6},{3,7},{4,0},{5,1},{6,2},{7,3},{8,12},{9,13},{10,... | collective-permute-start | bytes 2359304 | tf_op jit(solution)/shard_map/ppermute | solution.py:77
  102.3 31.9 %collective-permute-start.13 = (f32[4,64,768]{2,1,0:T(8,128)S(1)}, f32[4,64,768]{2,1,0:T(8,128)S(1)}, u32[]{:S(2)}, u32[]{:S(2)}) collective-permute-start(f32[4,64,768]{2,1,0:T(8,128)S(1)} %get-tuple-element.83), channel_id=1, source_target_pairs={{0,12},{1,13},{2,14},{3,15},{4,8},{5,9},{6,10},{7,11},{8,4},{9,5},... | collective-permute-start | bytes 2359304 | tf_op jit(solution)/shard_map/ppermute | solution.py:77
  103.8 28.3 %collective-permute-start.14 = (f32[4,64,512]{2,1,0:T(8,128)S(1)}, f32[4,64,512]{2,1,0:T(8,128)S(1)}, u32[]{:S(2)}, u32[]{:S(2)}) collective-permute-start(f32[4,64,512]{2,1,0:T(8,128)S(1)} %get-tuple-element.84), channel_id=1, source_target_pairs={{0,2},{1,3},{2,0},{3,1},{4,6},{5,7},{6,4},{7,5},{8,10},{9,11},{10,... | collective-permute-start | bytes 1572872 | tf_op jit(solution)/shard_map/ppermute | solution.py:77
  113.7 35.3 %collective-permute-start.33 = (f32[4,64,768]{2,1,0:T(8,128)S(1)}, f32[4,64,768]{2,1,0:T(8,128)S(1)}, u32[]{:S(2)}, u32[]{:S(2)}) collective-permute-start(f32[4,64,768]{2,1,0:T(8,128)S(1)} %get-tuple-element.109), channel_id=1, source_target_pairs={{0,4},{1,5},{2,6},{3,7},{4,0},{5,1},{6,2},{7,3},{8,12},{9,13},{10,... | collective-permute-start | bytes 2359304 | tf_op jit(solution)/shard_map/ppermute | solution.py:77
  114.2 34.9 %collective-permute-start.34 = (f32[4,64,768]{2,1,0:T(8,128)S(1)}, f32[4,64,768]{2,1,0:T(8,128)S(1)}, u32[]{:S(2)}, u32[]{:S(2)}) collective-permute-start(f32[4,64,768]{2,1,0:T(8,128)S(1)} %get-tuple-element.110), channel_id=1, source_target_pairs={{0,12},{1,13},{2,14},{3,15},{4,8},{5,9},{6,10},{7,11},{8,4},{9,5},... | collective-permute-start | bytes 2359304 | tf_op jit(solution)/shard_map/ppermute | solution.py:77
  132.1 35.7 %collective-permute-start.23 = (f32[2048]{0:T(1024)S(1)}, f32[2048]{0:T(1024)S(1)}, u32[]{:S(2)}, u32[]{:S(2)}) collective-permute-start(f32[2048]{0:T(1024)S(1)} %add.136), channel_id=1, source_target_pairs={{0,2},{1,3},{2,0},{3,1},{4,6},{5,7},{6,4},{7,5},{8,10},{9,11},{10,... | collective-permute-start | bytes 24584 | tf_op jit(solution)/shard_map/ppermute | solution.py:77
  132.7 13.9 %collective-permute-start.35 = (f32[4,64,512]{2,1,0:T(8,128)S(1)}, f32[4,64,512]{2,1,0:T(8,128)S(1)}, u32[]{:S(2)}, u32[]{:S(2)}) collective-permute-start(f32[4,64,512]{2,1,0:T(8,128)S(1)} %get-tuple-element.111), channel_id=1, source_target_pairs={{0,2},{1,3},{2,0},{3,1},{4,6},{5,7},{6,4},{7,5},{8,10},{9,11},{10,... | collective-permute-start | bytes 1572872 | tf_op jit(solution)/shard_map/ppermute | solution.py:77
  134.2 22.9 %collective-permute-start.15 = (f32[2,64,768]{2,1,0:T(8,128)S(1)}, f32[2,64,768]{2,1,0:T(8,128)S(1)}, u32[]{:S(2)}, u32[]{:S(2)}) collective-permute-start(f32[2,64,768]{2,1,0:T(8,128)S(1)} %slice_add_fusion.3), channel_id=1, source_target_pairs={{0,12},{1,13},{2,14},{3,15},{4,8},{5,9},{6,10},{7,11},{8,4},{9,5},... | collective-permute-start | bytes 1179656 | tf_op jit(solution)/shard_map/ppermute | solution.py:77
  146.6 11.0 %collective-permute-start.16 = (f32[2,64,768]{2,1,0:T(8,128)S(1)}, f32[2,64,768]{2,1,0:T(8,128)S(1)}, u32[]{:S(2)}, u32[]{:S(2)}) collective-permute-start(f32[2,64,768]{2,1,0:T(8,128)S(1)} %slice_add_fusion.2), channel_id=1, source_target_pairs={{0,2},{1,3},{2,0},{3,1},{4,6},{5,7},{6,4},{7,5},{8,10},{9,11},{10,... | collective-permute-start | bytes 1179656 | tf_op jit(solution)/shard_map/ppermute | solution.py:77
  149.2 14.7 %collective-permute-start.36 = (f32[2,64,768]{2,1,0:T(8,128)S(1)}, f32[2,64,768]{2,1,0:T(8,128)S(1)}, u32[]{:S(2)}, u32[]{:S(2)}) collective-permute-start(f32[2,64,768]{2,1,0:T(8,128)S(1)} %slice_add_fusion.1), channel_id=1, source_target_pairs={{0,12},{1,13},{2,14},{3,15},{4,8},{5,9},{6,10},{7,11},{8,4},{9,5},... | collective-permute-start | bytes 1179656 | tf_op jit(solution)/shard_map/ppermute | solution.py:77
  156.8 9.1 %collective-permute-start.37 = (f32[2,64,768]{2,1,0:T(8,128)S(1)}, f32[2,64,768]{2,1,0:T(8,128)S(1)}, u32[]{:S(2)}, u32[]{:S(2)}) collective-permute-start(f32[2,64,768]{2,1,0:T(8,128)S(1)} %slice_add_fusion), channel_id=1, source_target_pairs={{0,2},{1,3},{2,0},{3,1},{4,6},{5,7},{6,4},{7,5},{8,10},{9,11},{10,... | collective-permute-start | bytes 1179656 | tf_op jit(solution)/shard_map/ppermute | solution.py:77
  157.7 14.4 %collective-permute-start.18 = (f32[1,64,768]{2,1,0:T(8,128)S(1)}, f32[1,64,768]{2,1,0:T(8,128)S(1)}, u32[]{:S(2)}, u32[]{:S(2)}) collective-permute-start(f32[1,64,768]{2,1,0:T(8,128)S(1)} %get-tuple-element.137), channel_id=1, source_target_pairs={{0,2},{1,3},{2,0},{3,1},{4,6},{5,7},{6,4},{7,5},{8,10},{9,11},{10,... | collective-permute-start | bytes 589832 | tf_op jit(solution)/shard_map/ppermute | solution.py:77
  163.5 8.6 %collective-permute-start.19 = (f32[1,64,768]{2,1,0:T(8,128)S(1)}, f32[1,64,768]{2,1,0:T(8,128)S(1)}, u32[]{:S(2)}, u32[]{:S(2)}) collective-permute-start(f32[1,64,768]{2,1,0:T(8,128)S(1)} %get-tuple-element.135), channel_id=1, source_target_pairs={{0,4},{1,5},{2,6},{3,7},{4,0},{5,1},{6,2},{7,3},{8,12},{9,13},{10,... | collective-permute-start | bytes 589832 | tf_op jit(solution)/shard_map/ppermute | solution.py:77
  166.1 10.2 %collective-permute-start.39 = (f32[1,64,768]{2,1,0:T(8,128)S(1)}, f32[1,64,768]{2,1,0:T(8,128)S(1)}, u32[]{:S(2)}, u32[]{:S(2)}) collective-permute-start(f32[1,64,768]{2,1,0:T(8,128)S(1)} %get-tuple-element.133), channel_id=1, source_target_pairs={{0,2},{1,3},{2,0},{3,1},{4,6},{5,7},{6,4},{7,5},{8,10},{9,11},{10,... | collective-permute-start | bytes 589832 | tf_op jit(solution)/shard_map/ppermute | solution.py:77
  (15 other events, 245.1 us)

commit v6 on v5

--- a/solution.py
+++ b/solution.py
@@ -77,17 +77,38 @@
     return lax.ppermute(x, BOTH, pairs)
 
 
-def to_f8(x):
-    return jnp.clip(x, -440.0, 440.0).astype(jnp.float8_e4m3fn)
-
-
-def split(x, level):
-    high = lax.reduce_precision(x, 8, 7)
-    return (
-        high.astype(jnp.bfloat16),
-        to_f8(high * level[:, None]),
-        to_f8((x - high) * (level * LIFT)[:, None]),
-    )
+def split_kernel(x, high, near, rest, norms, unlevel):
+    v = x[...]
+    h = v.astype(jnp.bfloat16)
+    high[...] = h
+    total = jnp.sum(v * v, axis=1, keepdims=True)
+    fits = total < 3e38
+    level = jnp.where(fits, 128.0 * lax.rsqrt(jnp.maximum(total, 1e-30)), 0.0)
+    near[...] = (v * level).astype(jnp.float8_e4m3fn)
+    rest[...] = ((v - h.astype(jnp.float32)) * (level * LIFT)).astype(jnp.float8_e4m3fn)
+    back = jnp.where(fits, 1.0 / (jnp.where(fits, level, 1.0) * LIFT), 0.0)
+    norms[...] = jnp.transpose(jnp.broadcast_to(total, (TILE, 128)))[:1]
+    unlevel[...] = jnp.transpose(jnp.broadcast_to(back, (TILE, 128)))[:1]
+
+
+def split(x):
+    block = pl.BlockSpec((TILE, 1024), lambda t: (t, 0))
+    line = pl.BlockSpec((1, TILE), lambda t: (0, t))
+    return pl.pallas_call(
+        split_kernel,
+        out_shape=[
+            jax.ShapeDtypeStruct((2048, 1024), jnp.bfloat16),
+            jax.ShapeDtypeStruct((2048, 1024), jnp.float8_e4m3fn),
+            jax.ShapeDtypeStruct((2048, 1024), jnp.float8_e4m3fn),
+            jax.ShapeDtypeStruct((1, 2048), jnp.float32),
+            jax.ShapeDtypeStruct((1, 2048), jnp.float32),
+        ],
+        grid=(2048 // TILE,),
+        in_specs=[block],
+        out_specs=[block] * 3 + [line] * 2,
+        cost_estimate=pl.CostEstimate(flops=8 * 2**21, bytes_accessed=16 * 2**20, transcendentals=2048),
+        compiler_params=pltpu.CompilerParams(vmem_limit_bytes=8 * 2**20),
+    )(pltpu.with_memory_space_constraint(x, pltpu.HBM))
 
 
 STARTS = tuple(c // TILE for c in COFF)
@@ -99,7 +120,7 @@
         first, last, refs = refs[:3], refs[3:6], refs[6:]
     else:
         (high, cross), refs = refs[:2], refs[2:]
-    (own16, own8, own_rest, far16, far8, far_rest, level), refs = refs[:7], refs[7:]
+    (own16, own8, own_rest, own_level, far16, far8, far_rest, far_level), refs = refs[:8], refs[8:]
     outs, refs = refs[:3], refs[3:]
     t = pl.program_id(0)
     if half == 0:
@@ -139,9 +160,10 @@
     own, far = pl.ds(0, 1024), pl.ds(1024, 1024)
     rows = pl.ds(pl.multiple_of(t * TILE, TILE), TILE)
     acc = dot(lhs16[:, own], own16[rows, :]) + dot(lhs16[:, far], far16[rows, :])
-    low = dot(lhs8[0, :, own], own_rest[rows, :]) + dot(lhs8[0, :, far], far_rest[rows, :])
-    low += dot(lhs8[1, :, own], own8[rows, :]) + dot(lhs8[1, :, far], far8[rows, :])
-    acc = (acc + low * level[...]).reshape(4, ROWS, TILE)
+    low = dot(lhs8[0, :, own], own_rest[rows, :]) + dot(lhs8[1, :, own], own8[rows, :])
+    acc += low * own_level[...]
+    low = dot(lhs8[0, :, far], far_rest[rows, :]) + dot(lhs8[1, :, far], far8[rows, :])
+    acc = (acc + low * far_level[...]).reshape(4, ROWS, TILE)
     for q in range(3):
 
         @pl.when((t >= STARTS[q]) & (t < STARTS[q] + SIZES[q]))
@@ -170,7 +192,7 @@
         grid_spec=pltpu.PrefetchScalarGridSpec(
             num_scalar_prefetch=1,
             grid=(2048 // TILE,),
-            in_specs=[whole] * (len(pieces) + 6) + [pl.BlockSpec((1, TILE), lambda t, tb: (0, t))],
+            in_specs=[whole] * len(pieces) + ([whole] * 3 + [pl.BlockSpec((1, TILE), lambda t, tb: (0, t))]) * 2,
             out_specs=outs,
             scratch_shapes=[
                 pltpu.VMEM((4 * ROWS, 2048), jnp.bfloat16),
@@ -258,22 +280,16 @@
     last = []
     for s in range(3):
         for c in range(CHUNKS):
-            came = lax.optimization_barrier(
-                [permute(gathered[c][p], ROW_DIMS[(p + s) % 3]) for p in range(3)]
-            )
+            came = lax.optimization_barrier([permute(gathered[c][p], ROW_DIMS[(p + s) % 3]) for p in range(3)])
             if s == 2:
                 last.append(came)
                 continue
             gathered[c] = [jnp.concatenate([gathered[c][p], came[p]], axis=0) for p in range(3)]
 
-    norms = jnp.sum(factor * factor, axis=1)
-    norms = norms + permute(norms, CORE)
-    level = 128.0 * lax.rsqrt(jnp.clip(norms, 1e-30, 1e38))
-    level, unlevel, norms = lax.optimization_barrier((level, 1.0 / (level * LIFT), norms))
-    own = split(factor, level)
-    far_factor, far_level, _ = lax.optimization_barrier((far_factor, level, own[0]))
-    far = split(far_factor, far_level)
-    factors = (*own, *far, unlevel[None, :])
+    *own, own_norms, own_level = split(factor)
+    *far, far_norms, far_level = split(far_factor)
+    factors = (*own, own_level, *far, far_level)
+    norms = (own_norms + far_norms).reshape(2048)
     for d in range(3):
         norms = norms + permute(norms, COL_DIMS[d])
 
@@ -293,13 +309,9 @@
         came = lax.optimization_barrier([permute(sent[q], COL_DIMS[q]) for q in range(3)])
         kept, _ = mm(1, tbl, parts, factors)
         passed = [kept[q][:2] + came[q][:2] for q in range(3)]
-        second = lax.optimization_barrier(
-            [permute(passed[q], COL_DIMS[(q + 1) % 3]) for q in range(3)]
-        )
+        second = lax.optimization_barrier([permute(passed[q], COL_DIMS[(q + 1) % 3]) for q in range(3)])
         passed = [kept[q][2:3] + came[q][2:3] + second[q][:1] for q in range(3)]
-        third = lax.optimization_barrier(
-            [permute(passed[q], COL_DIMS[(q + 2) % 3]) for q in range(3)]
-        )
+        third = lax.optimization_barrier([permute(passed[q], COL_DIMS[(q + 2) % 3]) for q in range(3)])
         held = [kept[q][3:] + came[q][3:] + second[q][1:] for q in range(3)]
         sums = (tail(held, third, cells, sums),)
     parts = lax.all_to_all(sums[0], "row", split_axis=0, concat_axis=0, tiled=True)

time: 200 us -> 204 us (1.020)
  Pallas kernels: 36.8 us -> 54.5 us
  other arithmetic: 21.2 us -> 4.1 us
  local copies, waits for them, and re-layouts: 3.59 us -> 6.24 us
    pallas_call x0 -> x2, Pallas kernels: none -> 14.6 us  [split(): pl.pallas_call(split_kernel, out_shape=[jax.ShapeDtypeStruct((2048, 1024)...]
    convert_element_type x2 -> x0, other arithmetic: 13.5 us -> none  [to_f8(): return jnp.clip(x, -440.0, 440.0).astype(jnp.float8_e4m3fn)]
    reduce_sum x1 -> x0, other arithmetic: 4.15 us -> none  [step(): norms = jnp.sum(factor * factor, axis=1)]
    pallas_call x4, Pallas kernels: 32.1 us -> 35.2 us  [mm(): pl.pallas_call(functools.partial(mm_kernel, half), out_shape=shapes, grid...]
    ppermute x42 -> x41, waiting for transfers between devices: 62.1 us -> 61.3 us  [permute(): return lax.ppermute(x, BOTH, pairs)]
    ppermute x42 -> x41, starting transfers between devices: 57.7 us -> 58.3 us  [permute(): return lax.ppermute(x, BOTH, pairs)]
  transfers between devices with their start and end apart: 42 -> 41, of which waited for: 15 -> 17; matrix products, arithmetic and copies ran while one was open for 8% -> 3% of each run, Pallas kernels for 12% -> 16%
where the time goes in v6:
time: 204 us; the launch traced here: 203 us
  waiting for transfers between devices  61.3 us (30%)
  starting transfers between devices  58.3 us (29%)
  Pallas kernels  54.5 us (27%)
  blocking collectives  18.5 us (9%)
  local copies, waits for them, and re-layouts  6.24 us (3%)
  other arithmetic  4.1 us (2%)
    ppermute x41, waiting for transfers between devices, permute(): return lax.ppermute(x, BOTH, pairs)  61.3 us
    ppermute x41, starting transfers between devices, permute(): return lax.ppermute(x, BOTH, pairs)  58.3 us
    pallas_call x4, Pallas kernels, mm(): pl.pallas_call(functools.partial(mm_kernel, half), out_shape=shapes, grid...  35.2 us
    all_to_all x1, blocking collectives, step(): lax.all_to_all(sums[0], 'row', split_axis=0, concat_axis=0, tiled=True)  18.5 us
    pallas_call x2, Pallas kernels, split(): pl.pallas_call(split_kernel, out_shape=[jax.ShapeDtypeStruct((2048, 1024)...  14.6 us
    pallas_call x2, Pallas kernels, tail(): pl.pallas_call(tail_kernel, out_shape=jax.ShapeDtypeStruct((8, rows, 128)...  4.67 us
  transfers between devices with their start and end apart: 41, of which 17 were waited for; matrix products, arithmetic and copies ran while one was open for 3% of the time, Pallas kernels for 16%

profile of v6, /device:TPU:0, one launch (start us, length us, event | category | flops | bytes accessed | tf_op | source)
XLA Modules:
  0.0 203.4 jit_solution(7312848840141139128)
XLA Ops:
  6.9 2.2 %collective-permute-start.24 = (f32[1,64,640]{2,1,0:T(8,128)S(1)}, f32[1,64,640]{2,1,0:T(8,128)S(1)}, u32[]{:S(2)}, u32[]{:S(2)}) collective-permute-start(f32[1,64,640]{2,1,0:T(8,128)S(1)} %get-tuple-element.152), channel_id=1, source_target_pairs={{0,48},{1,49},{2,50},{3,51},{4,52},{5,53},{6,54},{7,55},{8,56},{9,... | collective-permute-start | bytes 491528 | tf_op jit(solution)/shard_map/ppermute | solution.py:77
  9.1 3.2 %collective-permute-start.25 = (f32[1,64,640]{2,1,0:T(8,128)S(1)}, f32[1,64,640]{2,1,0:T(8,128)S(1)}, u32[]{:S(2)}, u32[]{:S(2)}) collective-permute-start(f32[1,64,640]{2,1,0:T(8,128)S(1)} %get-tuple-element.149), channel_id=1, source_target_pairs={{0,64},{1,65},{2,66},{3,67},{4,68},{5,69},{6,70},{7,71},{8,72},{9,... | collective-permute-start | bytes 491528 | tf_op jit(solution)/shard_map/ppermute | solution.py:77
  14.4 3.8 %collective-permute-start.3 = (f32[1,64,640]{2,1,0:T(8,128)S(1)}, f32[1,64,640]{2,1,0:T(8,128)S(1)}, u32[]{:S(2)}, u32[]{:S(2)}) collective-permute-start(f32[1,64,640]{2,1,0:T(8,128)S(1)} %get-tuple-element.150), channel_id=1, source_target_pairs={{0,64},{1,65},{2,66},{3,67},{4,68},{5,69},{6,70},{7,71},{8,72},{9,... | collective-permute-start | bytes 491528 | tf_op jit(solution)/shard_map/ppermute | solution.py:77
  23.3 6.4 %collective-permute-done.27 = f32[2,64,640]{2,1,0:T(8,128)S(1)} collective-permute-done((f32[2,64,640]{2,1,0:T(8,128)S(1)}, f32[2,64,640]{2,1,0:T(8,128)S(1)}, u32[]{:S(2)}, u32[]{:S(2)}) %collective-permute-start.27) | collective-permute-done | bytes 327712 | tf_op jit(solution)/shard_map/ppermute | solution.py:77
  29.7 2.3 %collective-permute-start.5 = (f32[2,64,640]{2,1,0:T(8,128)S(1)}, f32[2,64,640]{2,1,0:T(8,128)S(1)}, u32[]{:S(2)}, u32[]{:S(2)}) collective-permute-start(f32[2,64,640]{2,1,0:T(8,128)S(1)} %pad_maximum_fusion.8), channel_id=1, source_target_pairs={{0,64},{1,65},{2,66},{3,67},{4,68},{5,69},{6,70},{7,71},{8,72},{9,... | collective-permute-start | bytes 983048 | tf_op jit(solution)/shard_map/ppermute | solution.py:77
  34.0 4.2 %collective-permute-done.6 = f32[2,64,640]{2,1,0:T(8,128)S(1)} collective-permute-done((f32[2,64,640]{2,1,0:T(8,128)S(1)}, f32[2,64,640]{2,1,0:T(8,128)S(1)}, u32[]{:S(2)}, u32[]{:S(2)}) %collective-permute-start.6) | collective-permute-done | bytes 327712 | tf_op jit(solution)/shard_map/ppermute | solution.py:77
  40.2 2.6 %collective-permute-start.29 = (f32[4,64,768]{2,1,0:T(8,128)S(1)}, f32[4,64,768]{2,1,0:T(8,128)}, u32[]{:S(2)}, u32[]{:S(2)}) collective-permute-start(f32[4,64,768]{2,1,0:T(8,128)S(1)} %pad_maximum_fusion.1.refs_0_), channel_id=1, source_target_pairs={{0,64},{1,65},{2,66},{3,67},{4,68},{5,69},{6,70},{7,71},{8,72},{9,... | collective-permute-start | bytes 2359304 | tf_op jit(solution)/shard_map/ppermute | solution.py:77
  42.8 2.4 %collective-permute-done.4 = f32[2,64,768]{2,1,0:T(8,128)S(1)} collective-permute-done((f32[2,64,768]{2,1,0:T(8,128)S(1)}, f32[2,64,768]{2,1,0:T(8,128)S(1)}, u32[]{:S(2)}, u32[]{:S(2)}) %collective-permute-start.4) | collective-permute-done | bytes 393248 | tf_op jit(solution)/shard_map/ppermute | solution.py:77
  47.6 2.6 %collective-permute-done.30.refs_4_ = f32[4,64,640]{2,1,0:T(8,128)S(1)} collective-permute-done((f32[4,64,640]{2,1,0:T(8,128)S(1)}, f32[4,64,640]{2,1,0:T(8,128)S(1)}, u32[]{:S(2)}, u32[]{:S(2)}) %collective-permute-start.30) | collective-permute-done | bytes 655392 | tf_op jit(solution)/shard_map/ppermute | solution.py:77
  51.1 2.1 %collective-permute-start.9 = (f32[4,64,640]{2,1,0:T(8,128)S(1)}, f32[4,64,640]{2,1,0:T(8,128)}, u32[]{:S(2)}, u32[]{:S(2)}) collective-permute-start(f32[4,64,640]{2,1,0:T(8,128)S(1)} %pad_maximum_fusion.3.refs_2_), channel_id=1, source_target_pairs={{0,48},{1,49},{2,50},{3,51},{4,52},{5,53},{6,54},{7,55},{8,56},{9,... | collective-permute-start | bytes 1966088 | tf_op jit(solution)/shard_map/ppermute | solution.py:77
  53.2 6.1 %collective-permute-done.31.refs_5_ = f32[4,64,640]{2,1,0:T(8,128)S(1)} collective-permute-done((f32[4,64,640]{2,1,0:T(8,128)S(1)}, f32[4,64,640]{2,1,0:T(8,128)S(1)}, u32[]{:S(2)}, u32[]{:S(2)}) %collective-permute-start.31) | collective-permute-done | bytes 655392 | tf_op jit(solution)/shard_map/ppermute | solution.py:77
  62.8 7.3 %shard_map.82 = (bf16[2048,1024]{1,0:T(8,128)(2,1)S(1)}, f8e4m3fn[2048,1024]{1,0:T(32,128)(4,1)S(1)}, f8e4m3fn[2048,1024]{1,0:T(32,128)(4,1)S(1)}, f32[1,2048]{1,0:T(1,128)S(1)}, f32[1,2048]{1,0:T(1,128)S(1)}) custom-call(f32[2048,1024]{1,0:T(8,128)} %x), custom_call_target="tpu_custom_call" | custom-call | flops 16777216 | bytes 16777216 | tf_op jit(solution)/shard_map/pallas_call | solution.py:97
  72.7 2.2 %collective-permute-done.7.refs_3_ = f32[4,64,768]{2,1,0:T(8,128)} collective-permute-done((f32[4,64,768]{2,1,0:T(8,128)S(1)}, f32[4,64,768]{2,1,0:T(8,128)}, u32[]{:S(2)}, u32[]{:S(2)}) %collective-permute-start.7) | collective-permute-done | bytes 786464 | tf_op jit(solution)/shard_map/ppermute | solution.py:77
  74.8 7.3 %shard_map.83 = (bf16[2048,1024]{1,0:T(8,128)(2,1)S(1)}, f8e4m3fn[2048,1024]{1,0:T(32,128)(4,1)S(1)}, f8e4m3fn[2048,1024]{1,0:T(32,128)(4,1)S(1)}, f32[1,2048]{1,0:T(1,128)S(1)}, f32[1,2048]{1,0:T(1,128)S(1)}) custom-call(f32[2048,1024]{1,0:T(8,128)} %collective-permute-done.10.x), custom_call_target="tpu_custom_call" | custom-call | flops 16777216 | bytes 16777216 | tf_op jit(solution)/shard_map/pallas_call | solution.py:97
  82.2 9.7 %shard_map.86 = (f32[4,64,768]{2,1,0:T(8,128)S(1)}, f32[4,64,768]{2,1,0:T(8,128)S(1)}, f32[4,64,512]{2,1,0:T(8,128)S(1)}, bf16[8,64,2048]{2,1,0:T(8,128)(2,1)S(1)}, f8e4m3fn[2,8,64,2048]{3,2,1,0:T(32,128)(4,1)S(1)}) custom-call(s32[24]{0:T(128)S(1)} %fusion.1.tbl, f32[4,64,768]{2,1,0:T(8,128)S(1)} %pad_maximum_fusion.1.refs_0_, ...), custom_call_target="tpu_custom_call" | custom-call | flops 4294967296 | bytes 20971520 | tf_op jit(solution)/shard_map/pallas_call | solution.py:189
  93.9 2.5 %collective-permute-start.33 = (f32[4,64,768]{2,1,0:T(8,128)S(1)}, f32[4,64,768]{2,1,0:T(8,128)S(1)}, u32[]{:S(2)}, u32[]{:S(2)}) collective-permute-start(f32[4,64,768]{2,1,0:T(8,128)S(1)} %get-tuple-element.120), channel_id=1, source_target_pairs={{0,12},{1,13},{2,14},{3,15},{4,8},{5,9},{6,10},{7,11},{8,4},{9,5},... | collective-permute-start | bytes 2359304 | tf_op jit(solution)/shard_map/ppermute | solution.py:77
  98.2 10.3 %shard_map.84 = (f32[4,64,768]{2,1,0:T(8,128)S(1)}, f32[4,64,768]{2,1,0:T(8,128)S(1)}, f32[4,64,512]{2,1,0:T(8,128)S(1)}, bf16[8,64,2048]{2,1,0:T(8,128)(2,1)S(1)}, f8e4m3fn[2,8,64,2048]{3,2,1,0:T(32,128)(4,1)S(1)}) custom-call(s32[24]{0:T(128)S(1)} %fusion.1.tbl, f32[4,64,768]{2,1,0:T(8,128)S(1)} %pad_maximum_fusion.refs_0_, ...), custom_call_target="tpu_custom_call" | custom-call | flops 4294967296 | bytes 20971520 | tf_op jit(solution)/shard_map/pallas_call | solution.py:189
  109.6 6.7 %collective-permute-start.21 = (f32[2048]{0:T(1024)S(1)}, f32[2048]{0:T(1024)S(1)}, u32[]{:S(2)}, u32[]{:S(2)}) collective-permute-start(f32[2048]{0:T(1024)S(1)} %add.135), channel_id=1, source_target_pairs={{0,12},{1,13},{2,14},{3,15},{4,8},{5,9},{6,10},{7,11},{8,4},{9,5},... | collective-permute-start | bytes 24584 | tf_op jit(solution)/shard_map/ppermute | solution.py:77
  116.3 7.6 %shard_map.87 = (f32[4,64,768]{2,1,0:T(8,128)S(1)}, f32[4,64,768]{2,1,0:T(8,128)S(1)}, f32[4,64,512]{2,1,0:T(8,128)S(1)}) custom-call(s32[24]{0:T(128)S(1)} %fusion.1.tbl, bf16[8,64,2048]{2,1,0:T(8,128)(2,1)S(1)} %get-tuple-element.116.refs_0_, f8e4m3fn[2,8,64,2048]{3,2,1,0:T(32,128)(4,1)S(1)} %get-tuple-element.117.refs_1_, ...), custom_call_target="tpu_custom_call" | custom-call | flops 4294967296 | bytes 20971520 | tf_op jit(solution)/shard_map/pallas_call | solution.py:189
  124.0 7.6 %shard_map.85 = (f32[4,64,768]{2,1,0:T(8,128)S(1)}, f32[4,64,768]{2,1,0:T(8,128)S(1)}, f32[4,64,512]{2,1,0:T(8,128)S(1)}) custom-call(s32[24]{0:T(128)S(1)} %fusion.1.tbl, bf16[8,64,2048]{2,1,0:T(8,128)(2,1)S(1)} %get-tuple-element.88.refs_0_, f8e4m3fn[2,8,64,2048]{3,2,1,0:T(32,128)(4,1)S(1)} %get-tuple-element.89.refs_1_, ...), custom_call_target="tpu_custom_call" | custom-call | flops 4294967296 | bytes 20971520 | tf_op jit(solution)/shard_map/pallas_call | solution.py:189
  134.0 12.5 %collective-permute-done.13 = f32[4,64,512]{2,1,0:T(8,128)S(1)} collective-permute-done((f32[4,64,512]{2,1,0:T(8,128)S(1)}, f32[4,64,512]{2,1,0:T(8,128)S(1)}, u32[]{:S(2)}, u32[]{:S(2)}) %collective-permute-start.13) | collective-permute-done | bytes 524320 | tf_op jit(solution)/shard_map/ppermute | solution.py:77
  146.6 3.2 %collective-permute-start.35 = (f32[2,64,768]{2,1,0:T(8,128)S(1)}, f32[2,64,768]{2,1,0:T(8,128)S(1)}, u32[]{:S(2)}, u32[]{:S(2)}) collective-permute-start(f32[2,64,768]{2,1,0:T(8,128)S(1)} %slice_add_fusion.1), channel_id=1, source_target_pairs={{0,12},{1,13},{2,14},{3,15},{4,8},{5,9},{6,10},{7,11},{8,4},{9,5},... | collective-permute-start | bytes 1179656 | tf_op jit(solution)/shard_map/ppermute | solution.py:77
  151.8 6.0 %collective-permute-done.36 = f32[2,64,768]{2,1,0:T(8,128)S(1)} collective-permute-done((f32[2,64,768]{2,1,0:T(8,128)S(1)}, f32[2,64,768]{2,1,0:T(8,128)S(1)}, u32[]{:S(2)}, u32[]{:S(2)}) %collective-permute-start.36) | collective-permute-done | bytes 393248 | tf_op jit(solution)/shard_map/ppermute | solution.py:77
  157.9 2.5 %collective-permute-start.14 = (f32[2,64,768]{2,1,0:T(8,128)S(1)}, f32[2,64,768]{2,1,0:T(8,128)S(1)}, u32[]{:S(2)}, u32[]{:S(2)}) collective-permute-start(f32[2,64,768]{2,1,0:T(8,128)S(1)} %slice_add_fusion.3), channel_id=1, source_target_pairs={{0,12},{1,13},{2,14},{3,15},{4,8},{5,9},{6,10},{7,11},{8,4},{9,5},... | collective-permute-start | bytes 1179656 | tf_op jit(solution)/shard_map/ppermute | solution.py:77
  162.8 4.1 %collective-permute-done.14 = f32[2,64,768]{2,1,0:T(8,128)S(1)} collective-permute-done((f32[2,64,768]{2,1,0:T(8,128)S(1)}, f32[2,64,768]{2,1,0:T(8,128)S(1)}, u32[]{:S(2)}, u32[]{:S(2)}) %collective-permute-start.14) | collective-permute-done | bytes 393248 | tf_op jit(solution)/shard_map/ppermute | solution.py:77
  166.9 2.6 %collective-permute-start.19 = (f32[1,64,512]{2,1,0:T(8,128)S(1)}, f32[1,64,512]{2,1,0:T(8,128)S(1)}, u32[]{:S(2)}, u32[]{:S(2)}) collective-permute-start(f32[1,64,512]{2,1,0:T(8,128)S(1)} %get-tuple-element.143), channel_id=1, source_target_pairs={{0,12},{1,13},{2,14},{3,15},{4,8},{5,9},{6,10},{7,11},{8,4},{9,5},... | collective-permute-start | bytes 393224 | tf_op jit(solution)/shard_map/ppermute | solution.py:77
  170.7 2.4 %collective-permute-done.19.refs_5_ = f32[1,64,512]{2,1,0:T(8,128)S(1)} collective-permute-done((f32[1,64,512]{2,1,0:T(8,128)S(1)}, f32[1,64,512]{2,1,0:T(8,128)S(1)}, u32[]{:S(2)}, u32[]{:S(2)}) %collective-permute-start.19) | collective-permute-done | bytes 131104 | tf_op jit(solution)/shard_map/ppermute | solution.py:77
  173.2 2.2 %collective-permute-done.18.refs_4_ = f32[1,64,768]{2,1,0:T(8,128)S(1)} collective-permute-done((f32[1,64,768]{2,1,0:T(8,128)S(1)}, f32[1,64,768]{2,1,0:T(8,128)S(1)}, u32[]{:S(2)}, u32[]{:S(2)}) %collective-permute-start.18) | collective-permute-done | bytes 196640 | tf_op jit(solution)/shard_map/ppermute | solution.py:77
  175.4 4.1 %collective-permute-done.17.refs_3_ = f32[1,64,768]{2,1,0:T(8,128)S(1)} collective-permute-done((f32[1,64,768]{2,1,0:T(8,128)S(1)}, f32[1,64,768]{2,1,0:T(8,128)S(1)}, u32[]{:S(2)}, u32[]{:S(2)}) %collective-permute-start.17) | collective-permute-done | bytes 196640 | tf_op jit(solution)/shard_map/ppermute | solution.py:77
  179.5 2.3 %shard_map.88.refs_7_ = f32[8,128,128]{2,1,0:T(8,128)S(1)} custom-call(f32[1,64,768]{2,1,0:T(8,128)S(1)} %get-tuple-element.136.refs_0_, f32[1,64,768]{2,1,0:T(8,128)S(1)} %get-tuple-element.134.refs_1_, f32[1,64,512]{2,1,0:T(8,128)S(1)} %get-tuple-element.142.refs_2_, f32[1,64,768]{2,1,0:T(8,128)S(1)} %collective-permute-done.38.refs_3_, ...), custom_call_target="tpu_custom_call" | custom-call | flops 1073741824 | bytes 2621440 | tf_op jit(solution)/shard_map/pallas_call | solution.py:245
  181.8 2.3 %shard_map.89 = f32[8,256,128]{2,1,0:T(8,128)S(1)} custom-call(f32[1,64,768]{2,1,0:T(8,128)S(1)} %get-tuple-element.140.refs_0_, f32[1,64,768]{2,1,0:T(8,128)S(1)} %get-tuple-element.138.refs_1_, f32[1,64,512]{2,1,0:T(8,128)S(1)} %get-tuple-element.144.refs_2_, f32[1,64,768]{2,1,0:T(8,128)S(1)} %collective-permute-done.17.refs_3_, ...), custom_call_target="tpu_custom_call" | custom-call | flops 1073741824 | bytes 2621440 | tf_op jit(solution)/shard_map/pallas_call | solution.py:245
  184.2 18.5 %all_to_all.5 = f32[8,256,128]{2,1,0:T(8,128)S(1)} all-to-all(f32[8,256,128]{2,1,0:T(8,128)S(1)} %shard_map.89), channel_id=1, replica_groups=mesh['row'=8,'col'=16] {'row'}, dimensions={0} | all-to-all | bytes 2097152 | tf_op jit(solution)/shard_map/all_to_all | solution.py:317
  (114 shorter events, 41.1 us)
Async XLA Ops:
  3.1 71.8 %collective-permute-start.10 = (f32[2048,1024]{1,0:T(8,128)}, f32[2048,1024]{1,0:T(8,128)}, u32[]{:S(2)}, u32[]{:S(2)}) collective-permute-start(f32[2048,1024]{1,0:T(8,128)} %x), channel_id=1, source_target_pairs={{0,1},{1,0},{2,3},{3,2},{4,5},{5,4},{6,7},{7,6},{8,9},{9,8},{10,11... | collective-permute-start | bytes 25165832 | tf_op jit(solution)/shard_map/ppermute | solution.py:77
  9.1 9.1 %collective-permute-start.25 = (f32[1,64,640]{2,1,0:T(8,128)S(1)}, f32[1,64,640]{2,1,0:T(8,128)S(1)}, u32[]{:S(2)}, u32[]{:S(2)}) collective-permute-start(f32[1,64,640]{2,1,0:T(8,128)S(1)} %get-tuple-element.149), channel_id=1, source_target_pairs={{0,64},{1,65},{2,66},{3,67},{4,68},{5,69},{6,70},{7,71},{8,72},{9,... | collective-permute-start | bytes 491528 | tf_op jit(solution)/shard_map/ppermute | solution.py:77
  18.2 15.5 %collective-permute-start.26 = (f32[2,64,768]{2,1,0:T(8,128)S(1)}, f32[2,64,768]{2,1,0:T(8,128)S(1)}, u32[]{:S(2)}, u32[]{:S(2)}) collective-permute-start(f32[2,64,768]{2,1,0:T(8,128)S(1)} %pad_maximum_fusion.7), channel_id=1, source_target_pairs={{0,48},{1,49},{2,50},{3,51},{4,52},{5,53},{6,54},{7,55},{8,56},{9,... | collective-permute-start | bytes 1179656 | tf_op jit(solution)/shard_map/ppermute | solution.py:77
  19.9 9.9 %collective-permute-start.27 = (f32[2,64,640]{2,1,0:T(8,128)S(1)}, f32[2,64,640]{2,1,0:T(8,128)S(1)}, u32[]{:S(2)}, u32[]{:S(2)}) collective-permute-start(f32[2,64,640]{2,1,0:T(8,128)S(1)} %pad_maximum_fusion.10), channel_id=1, source_target_pairs={{0,64},{1,65},{2,66},{3,67},{4,68},{5,69},{6,70},{7,71},{8,72},{9,... | collective-permute-start | bytes 983048 | tf_op jit(solution)/shard_map/ppermute | solution.py:77
  21.1 10.9 %collective-permute-start.28 = (f32[2,64,640]{2,1,0:T(8,128)S(1)}, f32[2,64,640]{2,1,0:T(8,128)S(1)}, u32[]{:S(2)}, u32[]{:S(2)}) collective-permute-start(f32[2,64,640]{2,1,0:T(8,128)S(1)} %pad_maximum_fusion.11), channel_id=1, source_target_pairs={{0,16},{1,17},{2,18},{3,19},{4,20},{5,21},{6,22},{7,23},{8,24},{9,... | collective-permute-start | bytes 983048 | tf_op jit(solution)/shard_map/ppermute | solution.py:77
  22.2 16.0 %collective-permute-start.6 = (f32[2,64,640]{2,1,0:T(8,128)S(1)}, f32[2,64,640]{2,1,0:T(8,128)S(1)}, u32[]{:S(2)}, u32[]{:S(2)}) collective-permute-start(f32[2,64,640]{2,1,0:T(8,128)S(1)} %pad_maximum_fusion.9), channel_id=1, source_target_pairs={{0,16},{1,17},{2,18},{3,19},{4,20},{5,21},{6,22},{7,23},{8,24},{9,... | collective-permute-start | bytes 983048 | tf_op jit(solution)/shard_map/ppermute | solution.py:77
  29.7 10.4 %collective-permute-start.5 = (f32[2,64,640]{2,1,0:T(8,128)S(1)}, f32[2,64,640]{2,1,0:T(8,128)S(1)}, u32[]{:S(2)}, u32[]{:S(2)}) collective-permute-start(f32[2,64,640]{2,1,0:T(8,128)S(1)} %pad_maximum_fusion.8), channel_id=1, source_target_pairs={{0,64},{1,65},{2,66},{3,67},{4,68},{5,69},{6,70},{7,71},{8,72},{9,... | collective-permute-start | bytes 983048 | tf_op jit(solution)/shard_map/ppermute | solution.py:77
  32.0 13.2 %collective-permute-start.4 = (f32[2,64,768]{2,1,0:T(8,128)S(1)}, f32[2,64,768]{2,1,0:T(8,128)S(1)}, u32[]{:S(2)}, u32[]{:S(2)}) collective-permute-start(f32[2,64,768]{2,1,0:T(8,128)S(1)} %pad_maximum_fusion.6), channel_id=1, source_target_pairs={{0,48},{1,49},{2,50},{3,51},{4,52},{5,53},{6,54},{7,55},{8,56},{9,... | collective-permute-start | bytes 1179656 | tf_op jit(solution)/shard_map/ppermute | solution.py:77
  33.8 16.4 %collective-permute-start.30 = (f32[4,64,640]{2,1,0:T(8,128)S(1)}, f32[4,64,640]{2,1,0:T(8,128)S(1)}, u32[]{:S(2)}, u32[]{:S(2)}) collective-permute-start(f32[4,64,640]{2,1,0:T(8,128)S(1)} %pad_maximum_fusion.4.refs_1_), channel_id=1, source_target_pairs={{0,16},{1,17},{2,18},{3,19},{4,20},{5,21},{6,22},{7,23},{8,24},{9,... | collective-permute-start | bytes 1966088 | tf_op jit(solution)/shard_map/ppermute | solution.py:77
  38.2 21.1 %collective-permute-start.31 = (f32[4,64,640]{2,1,0:T(8,128)S(1)}, f32[4,64,640]{2,1,0:T(8,128)S(1)}, u32[]{:S(2)}, u32[]{:S(2)}) collective-permute-start(f32[4,64,640]{2,1,0:T(8,128)S(1)} %pad_maximum_fusion.5.refs_2_), channel_id=1, source_target_pairs={{0,48},{1,49},{2,50},{3,51},{4,52},{5,53},{6,54},{7,55},{8,56},{9,... | collective-permute-start | bytes 1966088 | tf_op jit(solution)/shard_map/ppermute | solution.py:77
  40.2 30.0 %collective-permute-start.29 = (f32[4,64,768]{2,1,0:T(8,128)S(1)}, f32[4,64,768]{2,1,0:T(8,128)}, u32[]{:S(2)}, u32[]{:S(2)}) collective-permute-start(f32[4,64,768]{2,1,0:T(8,128)S(1)} %pad_maximum_fusion.1.refs_0_), channel_id=1, source_target_pairs={{0,64},{1,65},{2,66},{3,67},{4,68},{5,69},{6,70},{7,71},{8,72},{9,... | collective-permute-start | bytes 2359304 | tf_op jit(solution)/shard_map/ppermute | solution.py:77
  45.3 29.6 %collective-permute-start.7 = (f32[4,64,768]{2,1,0:T(8,128)S(1)}, f32[4,64,768]{2,1,0:T(8,128)}, u32[]{:S(2)}, u32[]{:S(2)}) collective-permute-start(f32[4,64,768]{2,1,0:T(8,128)S(1)} %pad_maximum_fusion.refs_0_), channel_id=1, source_target_pairs={{0,64},{1,65},{2,66},{3,67},{4,68},{5,69},{6,70},{7,71},{8,72},{9,... | collective-permute-start | bytes 2359304 | tf_op jit(solution)/shard_map/ppermute | solution.py:77
  51.1 20.0 %collective-permute-start.9 = (f32[4,64,640]{2,1,0:T(8,128)S(1)}, f32[4,64,640]{2,1,0:T(8,128)}, u32[]{:S(2)}, u32[]{:S(2)}) collective-permute-start(f32[4,64,640]{2,1,0:T(8,128)S(1)} %pad_maximum_fusion.3.refs_2_), channel_id=1, source_target_pairs={{0,48},{1,49},{2,50},{3,51},{4,52},{5,53},{6,54},{7,55},{8,56},{9,... | collective-permute-start | bytes 1966088 | tf_op jit(solution)/shard_map/ppermute | solution.py:77
  60.1 12.6 %collective-permute-start.8 = (f32[4,64,640]{2,1,0:T(8,128)}, f32[4,64,640]{2,1,0:T(8,128)}, u32[]{:S(2)}, u32[]{:S(2)}) collective-permute-start(f32[4,64,640]{2,1,0:T(8,128)} %pad_maximum_fusion.2.refs_1_), channel_id=1, source_target_pairs={{0,16},{1,17},{2,18},{3,19},{4,20},{5,21},{6,22},{7,23},{8,24},{9,... | collective-permute-start | bytes 1966088 | tf_op jit(solution)/shard_map/ppermute | solution.py:77
  91.9 39.9 %collective-permute-start.32 = (f32[4,64,768]{2,1,0:T(8,128)S(1)}, f32[4,64,768]{2,1,0:T(8,128)S(1)}, u32[]{:S(2)}, u32[]{:S(2)}) collective-permute-start(f32[4,64,768]{2,1,0:T(8,128)S(1)} %get-tuple-element.119), channel_id=1, source_target_pairs={{0,4},{1,5},{2,6},{3,7},{4,0},{5,1},{6,2},{7,3},{8,12},{9,13},{10,... | collective-permute-start | bytes 2359304 | tf_op jit(solution)/shard_map/ppermute | solution.py:77
  93.9 39.9 %collective-permute-start.33 = (f32[4,64,768]{2,1,0:T(8,128)S(1)}, f32[4,64,768]{2,1,0:T(8,128)S(1)}, u32[]{:S(2)}, u32[]{:S(2)}) collective-permute-start(f32[4,64,768]{2,1,0:T(8,128)S(1)} %get-tuple-element.120), channel_id=1, source_target_pairs={{0,12},{1,13},{2,14},{3,15},{4,8},{5,9},{6,10},{7,11},{8,4},{9,5},... | collective-permute-start | bytes 2359304 | tf_op jit(solution)/shard_map/ppermute | solution.py:77
  96.4 35.2 %collective-permute-start.34 = (f32[4,64,512]{2,1,0:T(8,128)S(1)}, f32[4,64,512]{2,1,0:T(8,128)S(1)}, u32[]{:S(2)}, u32[]{:S(2)}) collective-permute-start(f32[4,64,512]{2,1,0:T(8,128)S(1)} %get-tuple-element.121), channel_id=1, source_target_pairs={{0,2},{1,3},{2,0},{3,1},{4,6},{5,7},{6,4},{7,5},{8,10},{9,11},{10,... | collective-permute-start | bytes 1572872 | tf_op jit(solution)/shard_map/ppermute | solution.py:77
  96.9 12.7 %collective-permute-start.20 = (f32[2048]{0:T(1024)S(1)}, f32[2048]{0:T(1024)S(1)}, u32[]{:S(2)}, u32[]{:S(2)}) collective-permute-start(f32[2048]{0:T(1024)S(1)} %bitcast.30), channel_id=1, source_target_pairs={{0,4},{1,5},{2,6},{3,7},{4,0},{5,1},{6,2},{7,3},{8,12},{9,13},{10,... | collective-permute-start | bytes 24584 | tf_op jit(solution)/shard_map/ppermute | solution.py:77
  108.6 38.0 %collective-permute-start.11 = (f32[4,64,768]{2,1,0:T(8,128)S(1)}, f32[4,64,768]{2,1,0:T(8,128)S(1)}, u32[]{:S(2)}, u32[]{:S(2)}) collective-permute-start(f32[4,64,768]{2,1,0:T(8,128)S(1)} %get-tuple-element.91), channel_id=1, source_target_pairs={{0,4},{1,5},{2,6},{3,7},{4,0},{5,1},{6,2},{7,3},{8,12},{9,13},{10,... | collective-permute-start | bytes 2359304 | tf_op jit(solution)/shard_map/ppermute | solution.py:77
  109.6 14.3 %collective-permute-start.21 = (f32[2048]{0:T(1024)S(1)}, f32[2048]{0:T(1024)S(1)}, u32[]{:S(2)}, u32[]{:S(2)}) collective-permute-start(f32[2048]{0:T(1024)S(1)} %add.135), channel_id=1, source_target_pairs={{0,12},{1,13},{2,14},{3,15},{4,8},{5,9},{6,10},{7,11},{8,4},{9,5},... | collective-permute-start | bytes 24584 | tf_op jit(solution)/shard_map/ppermute | solution.py:77
  123.9 25.8 %collective-permute-start.12 = (f32[4,64,768]{2,1,0:T(8,128)S(1)}, f32[4,64,768]{2,1,0:T(8,128)S(1)}, u32[]{:S(2)}, u32[]{:S(2)}) collective-permute-start(f32[4,64,768]{2,1,0:T(8,128)S(1)} %get-tuple-element.92), channel_id=1, source_target_pairs={{0,12},{1,13},{2,14},{3,15},{4,8},{5,9},{6,10},{7,11},{8,4},{9,5},... | collective-permute-start | bytes 2359304 | tf_op jit(solution)/shard_map/ppermute | solution.py:77
  131.7 14.9 %collective-permute-start.13 = (f32[4,64,512]{2,1,0:T(8,128)S(1)}, f32[4,64,512]{2,1,0:T(8,128)S(1)}, u32[]{:S(2)}, u32[]{:S(2)}) collective-permute-start(f32[4,64,512]{2,1,0:T(8,128)S(1)} %get-tuple-element.93), channel_id=1, source_target_pairs={{0,2},{1,3},{2,0},{3,1},{4,6},{5,7},{6,4},{7,5},{8,10},{9,11},{10,... | collective-permute-start | bytes 1572872 | tf_op jit(solution)/shard_map/ppermute | solution.py:77
  131.8 37.9 %collective-permute-start.22 = (f32[2048]{0:T(1024)S(1)}, f32[2048]{0:T(1024)S(1)}, u32[]{:S(2)}, u32[]{:S(2)}) collective-permute-start(f32[2048]{0:T(1024)S(1)} %add.136), channel_id=1, source_target_pairs={{0,2},{1,3},{2,0},{3,1},{4,6},{5,7},{6,4},{7,5},{8,10},{9,11},{10,... | collective-permute-start | bytes 24584 | tf_op jit(solution)/shard_map/ppermute | solution.py:77
  133.8 16.2 %collective-permute-start.37 = (f32[2,64,512]{2,1,0:T(8,128)S(1)}, f32[2,64,512]{2,1,0:T(8,128)S(1)}, u32[]{:S(2)}, u32[]{:S(2)}) collective-permute-start(f32[2,64,512]{2,1,0:T(8,128)S(1)} %slice_add_fusion.4), channel_id=1, source_target_pairs={{0,4},{1,5},{2,6},{3,7},{4,0},{5,1},{6,2},{7,3},{8,12},{9,13},{10,... | collective-permute-start | bytes 786440 | tf_op jit(solution)/shard_map/ppermute | solution.py:77
  146.5 11.3 %collective-permute-start.36 = (f32[2,64,768]{2,1,0:T(8,128)S(1)}, f32[2,64,768]{2,1,0:T(8,128)S(1)}, u32[]{:S(2)}, u32[]{:S(2)}) collective-permute-start(f32[2,64,768]{2,1,0:T(8,128)S(1)} %slice_add_fusion), channel_id=1, source_target_pairs={{0,2},{1,3},{2,0},{3,1},{4,6},{5,7},{6,4},{7,5},{8,10},{9,11},{10,... | collective-permute-start | bytes 1179656 | tf_op jit(solution)/shard_map/ppermute | solution.py:77
  146.6 13.8 %collective-permute-start.35 = (f32[2,64,768]{2,1,0:T(8,128)S(1)}, f32[2,64,768]{2,1,0:T(8,128)S(1)}, u32[]{:S(2)}, u32[]{:S(2)}) collective-permute-start(f32[2,64,768]{2,1,0:T(8,128)S(1)} %slice_add_fusion.1), channel_id=1, source_target_pairs={{0,12},{1,13},{2,14},{3,15},{4,8},{5,9},{6,10},{7,11},{8,4},{9,5},... | collective-permute-start | bytes 1179656 | tf_op jit(solution)/shard_map/ppermute | solution.py:77
  149.8 11.6 %collective-permute-start.16 = (f32[2,64,512]{2,1,0:T(8,128)S(1)}, f32[2,64,512]{2,1,0:T(8,128)S(1)}, u32[]{:S(2)}, u32[]{:S(2)}) collective-permute-start(f32[2,64,512]{2,1,0:T(8,128)S(1)} %slice_add_fusion.5), channel_id=1, source_target_pairs={{0,4},{1,5},{2,6},{3,7},{4,0},{5,1},{6,2},{7,3},{8,12},{9,13},{10,... | collective-permute-start | bytes 786440 | tf_op jit(solution)/shard_map/ppermute | solution.py:77
  150.0 12.0 %collective-permute-start.15 = (f32[2,64,768]{2,1,0:T(8,128)S(1)}, f32[2,64,768]{2,1,0:T(8,128)S(1)}, u32[]{:S(2)}, u32[]{:S(2)}) collective-permute-start(f32[2,64,768]{2,1,0:T(8,128)S(1)} %slice_add_fusion.2), channel_id=1, source_target_pairs={{0,2},{1,3},{2,0},{3,1},{4,6},{5,7},{6,4},{7,5},{8,10},{9,11},{10,... | collective-permute-start | bytes 1179656 | tf_op jit(solution)/shard_map/ppermute | solution.py:77
  157.9 9.0 %collective-permute-start.14 = (f32[2,64,768]{2,1,0:T(8,128)S(1)}, f32[2,64,768]{2,1,0:T(8,128)S(1)}, u32[]{:S(2)}, u32[]{:S(2)}) collective-permute-start(f32[2,64,768]{2,1,0:T(8,128)S(1)} %slice_add_fusion.3), channel_id=1, source_target_pairs={{0,12},{1,13},{2,14},{3,15},{4,8},{5,9},{6,10},{7,11},{8,4},{9,5},... | collective-permute-start | bytes 1179656 | tf_op jit(solution)/shard_map/ppermute | solution.py:77
  160.4 9.3 %collective-permute-start.40 = (f32[1,64,512]{2,1,0:T(8,128)S(1)}, f32[1,64,512]{2,1,0:T(8,128)S(1)}, u32[]{:S(2)}, u32[]{:S(2)}) collective-permute-start(f32[1,64,512]{2,1,0:T(8,128)S(1)} %get-tuple-element.141), channel_id=1, source_target_pairs={{0,12},{1,13},{2,14},{3,15},{4,8},{5,9},{6,10},{7,11},{8,4},{9,5},... | collective-permute-start | bytes 393224 | tf_op jit(solution)/shard_map/ppermute | solution.py:77
  161.4 9.3 %collective-permute-start.39 = (f32[1,64,768]{2,1,0:T(8,128)S(1)}, f32[1,64,768]{2,1,0:T(8,128)S(1)}, u32[]{:S(2)}, u32[]{:S(2)}) collective-permute-start(f32[1,64,768]{2,1,0:T(8,128)S(1)} %get-tuple-element.133), channel_id=1, source_target_pairs={{0,4},{1,5},{2,6},{3,7},{4,0},{5,1},{6,2},{7,3},{8,12},{9,13},{10,... | collective-permute-start | bytes 589832 | tf_op jit(solution)/shard_map/ppermute | solution.py:77
  169.7 9.7 %collective-permute-start.17 = (f32[1,64,768]{2,1,0:T(8,128)S(1)}, f32[1,64,768]{2,1,0:T(8,128)S(1)}, u32[]{:S(2)}, u32[]{:S(2)}) collective-permute-start(f32[1,64,768]{2,1,0:T(8,128)S(1)} %get-tuple-element.139), channel_id=1, source_target_pairs={{0,2},{1,3},{2,0},{3,1},{4,6},{5,7},{6,4},{7,5},{8,10},{9,11},{10,... | collective-permute-start | bytes 589832 | tf_op jit(solution)/shard_map/ppermute | solution.py:77
  (17 other events, 133.8 us)

commit v7 on v5

--- a/solution.py
+++ b/solution.py
@@ -77,16 +77,12 @@
     return lax.ppermute(x, BOTH, pairs)
 
 
-def to_f8(x):
-    return jnp.clip(x, -440.0, 440.0).astype(jnp.float8_e4m3fn)
-
-
 def split(x, level):
     high = lax.reduce_precision(x, 8, 7)
     return (
         high.astype(jnp.bfloat16),
-        to_f8(high * level[:, None]),
-        to_f8((x - high) * (level * LIFT)[:, None]),
+        (high * level[:, None]).astype(jnp.float8_e4m3fn),
+        ((x - high) * (level * LIFT)[:, None]).astype(jnp.float8_e4m3fn),
     )
 
 
@@ -268,8 +264,10 @@
 
     norms = jnp.sum(factor * factor, axis=1)
     norms = norms + permute(norms, CORE)
-    level = 128.0 * lax.rsqrt(jnp.clip(norms, 1e-30, 1e38))
-    level, unlevel, norms = lax.optimization_barrier((level, 1.0 / (level * LIFT), norms))
+    fits = norms < 3e38
+    level = 128.0 * lax.rsqrt(jnp.where(fits, jnp.maximum(norms, 1e-30), 1.0))
+    unlevel = jnp.where(fits, 1.0 / (level * LIFT), 0.0)
+    level, unlevel, norms = lax.optimization_barrier((jnp.where(fits, level, 0.0), unlevel, norms))
     own = split(factor, level)
     far_factor, far_level, _ = lax.optimization_barrier((far_factor, level, own[0]))
     far = split(far_factor, far_level)

time: 200 us -> 200 us (level)
  transfers between devices with their start and end apart: 42 -> 42, of which waited for: 15 -> 15; matrix products, arithmetic and copies ran while one was open for 8% -> 7% of each run, Pallas kernels for 12% -> 12%
where the time goes in v7:
time: 200 us; the launch traced here: 199 us
  waiting for transfers between devices  62.5 us (31%)
  starting transfers between devices  57.7 us (29%)
  Pallas kernels  36.8 us (18%)
  other arithmetic  20.6 us (10%)
  blocking collectives  17.9 us (9%)
  local copies, waits for them, and re-layouts  3.59 us (2%)
    ppermute x42, waiting for transfers between devices, permute(): return lax.ppermute(x, BOTH, pairs)  62.5 us
    ppermute x42, starting transfers between devices, permute(): return lax.ppermute(x, BOTH, pairs)  57.7 us
    pallas_call x4, Pallas kernels, mm(): pl.pallas_call(functools.partial(mm_kernel, half), out_shape=shapes, grid...  32.1 us
    all_to_all x1, blocking collectives, step(): lax.all_to_all(sums[0], 'row', split_axis=0, concat_axis=0, tiled=True)  17.9 us
    convert_element_type x2, other arithmetic, split(): ((x - high) * (level * LIFT)[:, None]).astype(jnp.float8_e4m3fn)  12.9 us
    pallas_call x2, Pallas kernels, tail(): pl.pallas_call(tail_kernel, out_shape=jax.ShapeDtypeStruct((8, rows, 128)...  4.67 us
    reduce_sum x1, other arithmetic, step(): norms = jnp.sum(factor * factor, axis=1)  4.15 us
  transfers between devices with their start and end apart: 42, of which 15 were waited for; matrix products, arithmetic and copies ran while one was open for 7% of the time, Pallas kernels for 12%

profile of v7, /device:TPU:0, one launch (start us, length us, event | category | flops | bytes accessed | tf_op | source)
XLA Modules:
  0.0 199.4 jit_solution(17879026235481233603)
XLA Ops:
  9.2 4.1 %multiply_reduce_fusion = f32[2048]{0:T(1024)S(1)} fusion(f32[2048,1024]{1,0:T(8,128)} %param.9), kind=kLoop, calls=%fused_computation.12 | loop fusion | flops 4192256 | bytes 8396800 | tf_op jit(solution)/shard_map/reduce_sum | solution.py:265
  13.5 2.9 %collective-permute-start.2 = (f32[1,64,640]{2,1,0:T(8,128)S(1)}, f32[1,64,640]{2,1,0:T(8,128)S(1)}, u32[]{:S(2)}, u32[]{:S(2)}) collective-permute-start(f32[1,64,640]{2,1,0:T(8,128)S(1)} %get-tuple-element.149), channel_id=1, source_target_pairs={{0,48},{1,49},{2,50},{3,51},{4,52},{5,53},{6,54},{7,55},{8,56},{9,... | collective-permute-start | bytes 491528 | tf_op jit(solution)/shard_map/ppermute | solution.py:77
  16.6 3.3 %collective-permute-start.3 = (f32[1,64,640]{2,1,0:T(8,128)S(1)}, f32[1,64,640]{2,1,0:T(8,128)S(1)}, u32[]{:S(2)}, u32[]{:S(2)}) collective-permute-start(f32[1,64,640]{2,1,0:T(8,128)S(1)} %get-tuple-element.148), channel_id=1, source_target_pairs={{0,64},{1,65},{2,66},{3,67},{4,68},{5,69},{6,70},{7,71},{8,72},{9,... | collective-permute-start | bytes 491528 | tf_op jit(solution)/shard_map/ppermute | solution.py:77
  19.9 2.8 %collective-permute-start.25 = (f32[1,64,640]{2,1,0:T(8,128)S(1)}, f32[1,64,640]{2,1,0:T(8,128)S(1)}, u32[]{:S(2)}, u32[]{:S(2)}) collective-permute-start(f32[1,64,640]{2,1,0:T(8,128)S(1)} %get-tuple-element.150), channel_id=1, source_target_pairs={{0,48},{1,49},{2,50},{3,51},{4,52},{5,53},{6,54},{7,55},{8,56},{9,... | collective-permute-start | bytes 491528 | tf_op jit(solution)/shard_map/ppermute | solution.py:77
  22.8 2.4 %collective-permute-start.26 = (f32[1,64,640]{2,1,0:T(8,128)S(1)}, f32[1,64,640]{2,1,0:T(8,128)S(1)}, u32[]{:S(2)}, u32[]{:S(2)}) collective-permute-start(f32[1,64,640]{2,1,0:T(8,128)S(1)} %get-tuple-element.147), channel_id=1, source_target_pairs={{0,64},{1,65},{2,66},{3,67},{4,68},{5,69},{6,70},{7,71},{8,72},{9,... | collective-permute-start | bytes 491528 | tf_op jit(solution)/shard_map/ppermute | solution.py:77
  25.2 2.8 %collective-permute-start.4 = (f32[2,64,768]{2,1,0:T(8,128)S(1)}, f32[2,64,768]{2,1,0:T(8,128)S(1)}, u32[]{:S(2)}, u32[]{:S(2)}) collective-permute-start(f32[2,64,768]{2,1,0:T(8,128)S(1)} %pad_maximum_fusion.6), channel_id=1, source_target_pairs={{0,48},{1,49},{2,50},{3,51},{4,52},{5,53},{6,54},{7,55},{8,56},{9,... | collective-permute-start | bytes 1179656 | tf_op jit(solution)/shard_map/ppermute | solution.py:77
  28.1 2.5 %collective-permute-start.5 = (f32[2,64,640]{2,1,0:T(8,128)S(1)}, f32[2,64,640]{2,1,0:T(8,128)S(1)}, u32[]{:S(2)}, u32[]{:S(2)}) collective-permute-start(f32[2,64,640]{2,1,0:T(8,128)S(1)} %pad_maximum_fusion.8), channel_id=1, source_target_pairs={{0,64},{1,65},{2,66},{3,67},{4,68},{5,69},{6,70},{7,71},{8,72},{9,... | collective-permute-start | bytes 983048 | tf_op jit(solution)/shard_map/ppermute | solution.py:77
  32.2 8.1 %collective-permute-done.5 = f32[2,64,640]{2,1,0:T(8,128)S(1)} collective-permute-done((f32[2,64,640]{2,1,0:T(8,128)S(1)}, f32[2,64,640]{2,1,0:T(8,128)S(1)}, u32[]{:S(2)}, u32[]{:S(2)}) %collective-permute-start.5) | collective-permute-done | bytes 327712 | tf_op jit(solution)/shard_map/ppermute | solution.py:77
  44.9 2.7 %collective-permute-start.9 = (f32[4,64,640]{2,1,0:T(8,128)S(1)}, f32[4,64,640]{2,1,0:T(8,128)S(1)}, u32[]{:S(2)}, u32[]{:S(2)}) collective-permute-start(f32[4,64,640]{2,1,0:T(8,128)S(1)} %pad_maximum_fusion.3.refs_2_), channel_id=1, source_target_pairs={{0,48},{1,49},{2,50},{3,51},{4,52},{5,53},{6,54},{7,55},{8,56},{9,... | collective-permute-start | bytes 1966088 | tf_op jit(solution)/shard_map/ppermute | solution.py:77
  47.8 5.5 %collective-permute-done.29 = f32[2,64,640]{2,1,0:T(8,128)S(1)} collective-permute-done((f32[2,64,640]{2,1,0:T(8,128)S(1)}, f32[2,64,640]{2,1,0:T(8,128)S(1)}, u32[]{:S(2)}, u32[]{:S(2)}) %collective-permute-start.29) | collective-permute-done | bytes 327712 | tf_op jit(solution)/shard_map/ppermute | solution.py:77
  53.3 2.5 %collective-permute-start.22 = (f32[2048]{0:T(1024)S(1)}, f32[2048]{0:T(1024)S(1)}, u32[]{:S(2)}, u32[]{:S(2)}) collective-permute-start(f32[2048]{0:T(1024)S(1)} %add.135), channel_id=1, source_target_pairs={{0,12},{1,13},{2,14},{3,15},{4,8},{5,9},{6,10},{7,11},{8,4},{9,5},... | collective-permute-start | bytes 24584 | tf_op jit(solution)/shard_map/ppermute | solution.py:77
  55.8 2.4 %collective-permute-start.7 = (f32[4,64,768]{2,1,0:T(8,128)S(1)}, f32[4,64,768]{2,1,0:T(8,128)S(1)}, u32[]{:S(2)}, u32[]{:S(2)}) collective-permute-start(f32[4,64,768]{2,1,0:T(8,128)S(1)} %pad_maximum_fusion.refs_0_), channel_id=1, source_target_pairs={{0,64},{1,65},{2,66},{3,67},{4,68},{5,69},{6,70},{7,71},{8,72},{9,... | collective-permute-start | bytes 2359304 | tf_op jit(solution)/shard_map/ppermute | solution.py:77
  58.4 2.2 %collective-permute-start.30 = (f32[4,64,768]{2,1,0:T(8,128)S(1)}, f32[4,64,768]{2,1,0:T(8,128)S(1)}, u32[]{:S(2)}, u32[]{:S(2)}) collective-permute-start(f32[4,64,768]{2,1,0:T(8,128)S(1)} %pad_maximum_fusion.1.refs_0_), channel_id=1, source_target_pairs={{0,64},{1,65},{2,66},{3,67},{4,68},{5,69},{6,70},{7,71},{8,72},{9,... | collective-permute-start | bytes 2359304 | tf_op jit(solution)/shard_map/ppermute | solution.py:77
  60.6 4.0 %collective-permute-done.8.refs_4_ = f32[4,64,640]{2,1,0:T(8,128)S(1)} collective-permute-done((f32[4,64,640]{2,1,0:T(8,128)S(1)}, f32[4,64,640]{2,1,0:T(8,128)S(1)}, u32[]{:S(2)}, u32[]{:S(2)}) %collective-permute-start.8) | collective-permute-done | bytes 655392 | tf_op jit(solution)/shard_map/ppermute | solution.py:77
  67.4 5.3 %fusion.2 = (f8e4m3fn[2048,1024]{1,0:T(32,128)(4,1)S(1)}, f8e4m3fn[2048,1024]{1,0:T(32,128)(4,1)S(1)}, bf16[2048,1024]{1,0:T(8,128)(2,1)S(1)}) fusion(f32[2048,1024]{1,0:T(8,128)S(1)} %bitcast.30, f32[2048]{0:T(1024)S(1)} %broadcast_multiply_fusion.1, f32[2048]{0:T(1024)S(1)} %multiply_select_fusion), kind=kLoop, calls=%fused_computation.8 | loop fusion | flops 14680064 | bytes 16793600 | tf_op jit(solution)/shard_map/convert_element_type | solution.py:85
  72.7 4.5 %collective-permute-done.7.refs_3_ = f32[4,64,768]{2,1,0:T(8,128)S(1)} collective-permute-done((f32[4,64,768]{2,1,0:T(8,128)S(1)}, f32[4,64,768]{2,1,0:T(8,128)S(1)}, u32[]{:S(2)}, u32[]{:S(2)}) %collective-permute-start.7) | collective-permute-done | bytes 786464 | tf_op jit(solution)/shard_map/ppermute | solution.py:77
  78.8 6.9 %collective-permute-done.30.refs_3_ = f32[4,64,768]{2,1,0:T(8,128)S(1)} collective-permute-done((f32[4,64,768]{2,1,0:T(8,128)S(1)}, f32[4,64,768]{2,1,0:T(8,128)S(1)}, u32[]{:S(2)}, u32[]{:S(2)}) %collective-permute-start.30) | collective-permute-done | bytes 786464 | tf_op jit(solution)/shard_map/ppermute | solution.py:77
  85.7 7.6 %fusion.5 = (f8e4m3fn[2048,1024]{1,0:T(32,128)(4,1)S(1)}, f8e4m3fn[2048,1024]{1,0:T(32,128)(4,1)S(1)}, bf16[2048,1024]{1,0:T(8,128)(2,1)S(1)}) fusion(f32[2048,1024]{1,0:T(8,128)} %collective-permute-done.11, f32[2048]{0:T(1024)S(1)} %broadcast_multiply_fusion, f32[2048]{0:T(1024)S(1)} %multiply_select_fusion), kind=kLoop, calls=%fused_computation.11 | loop fusion | flops 14680064 | bytes 16793600 | tf_op jit(solution)/shard_map/convert_element_type | solution.py:85
  93.3 8.5 %shard_map.82 = (f32[4,64,768]{2,1,0:T(8,128)S(1)}, f32[4,64,768]{2,1,0:T(8,128)S(1)}, f32[4,64,512]{2,1,0:T(8,128)S(1)}, bf16[8,64,2048]{2,1,0:T(8,128)(2,1)S(1)}, f8e4m3fn[2,8,64,2048]{3,2,1,0:T(32,128)(4,1)S(1)}) custom-call(s32[24]{0:T(128)S(1)} %fusion.7.tbl, f32[4,64,768]{2,1,0:T(8,128)S(1)} %pad_maximum_fusion.refs_0_, ...), custom_call_target="tpu_custom_call" | custom-call | flops 4294967296 | bytes 20971520 | tf_op jit(solution)/shard_map/pallas_call | solution.py:163
  105.0 8.5 %shard_map.84 = (f32[4,64,768]{2,1,0:T(8,128)S(1)}, f32[4,64,768]{2,1,0:T(8,128)S(1)}, f32[4,64,512]{2,1,0:T(8,128)S(1)}, bf16[8,64,2048]{2,1,0:T(8,128)(2,1)S(1)}, f8e4m3fn[2,8,64,2048]{3,2,1,0:T(32,128)(4,1)S(1)}) custom-call(s32[24]{0:T(128)S(1)} %fusion.7.tbl, f32[4,64,768]{2,1,0:T(8,128)S(1)} %pad_maximum_fusion.1.refs_0_, ...), custom_call_target="tpu_custom_call" | custom-call | flops 4294967296 | bytes 20971520 | tf_op jit(solution)/shard_map/pallas_call | solution.py:163
  114.0 2.6 %collective-permute-start.34 = (f32[4,64,768]{2,1,0:T(8,128)S(1)}, f32[4,64,768]{2,1,0:T(8,128)S(1)}, u32[]{:S(2)}, u32[]{:S(2)}) collective-permute-start(f32[4,64,768]{2,1,0:T(8,128)S(1)} %get-tuple-element.110), channel_id=1, source_target_pairs={{0,12},{1,13},{2,14},{3,15},{4,8},{5,9},{6,10},{7,11},{8,4},{9,5},... | collective-permute-start | bytes 2359304 | tf_op jit(solution)/shard_map/ppermute | solution.py:77
  116.6 7.6 %shard_map.83 = (f32[4,64,768]{2,1,0:T(8,128)S(1)}, f32[4,64,768]{2,1,0:T(8,128)S(1)}, f32[4,64,512]{2,1,0:T(8,128)S(1)}) custom-call(s32[24]{0:T(128)S(1)} %fusion.7.tbl, bf16[8,64,2048]{2,1,0:T(8,128)(2,1)S(1)} %get-tuple-element.79.refs_0_, f8e4m3fn[2,8,64,2048]{3,2,1,0:T(32,128)(4,1)S(1)} %get-tuple-element.80.refs_1_, ...), custom_call_target="tpu_custom_call" | custom-call | flops 4294967296 | bytes 20971520 | tf_op jit(solution)/shard_map/pallas_call | solution.py:163
  124.2 7.6 %shard_map.85 = (f32[4,64,768]{2,1,0:T(8,128)S(1)}, f32[4,64,768]{2,1,0:T(8,128)S(1)}, f32[4,64,512]{2,1,0:T(8,128)S(1)}) custom-call(s32[24]{0:T(128)S(1)} %fusion.7.tbl, bf16[8,64,2048]{2,1,0:T(8,128)(2,1)S(1)} %get-tuple-element.106.refs_0_, f8e4m3fn[2,8,64,2048]{3,2,1,0:T(32,128)(4,1)S(1)} %get-tuple-element.107.refs_1_, ...), custom_call_target="tpu_custom_call" | custom-call | flops 4294967296 | bytes 20971520 | tf_op jit(solution)/shard_map/pallas_call | solution.py:163
  134.8 11.6 %collective-permute-done.35 = f32[4,64,512]{2,1,0:T(8,128)S(1)} collective-permute-done((f32[4,64,512]{2,1,0:T(8,128)S(1)}, f32[4,64,512]{2,1,0:T(8,128)S(1)}, u32[]{:S(2)}, u32[]{:S(2)}) %collective-permute-start.35) | collective-permute-done | bytes 524320 | tf_op jit(solution)/shard_map/ppermute | solution.py:77
  146.4 2.4 %collective-permute-start.16 = (f32[2,64,768]{2,1,0:T(8,128)S(1)}, f32[2,64,768]{2,1,0:T(8,128)S(1)}, u32[]{:S(2)}, u32[]{:S(2)}) collective-permute-start(f32[2,64,768]{2,1,0:T(8,128)S(1)} %slice_add_fusion.2), channel_id=1, source_target_pairs={{0,2},{1,3},{2,0},{3,1},{4,6},{5,7},{6,4},{7,5},{8,10},{9,11},{10,... | collective-permute-start | bytes 1179656 | tf_op jit(solution)/shard_map/ppermute | solution.py:77
  150.5 6.0 %collective-permute-done.17 = f32[2,64,512]{2,1,0:T(8,128)S(1)} collective-permute-done((f32[2,64,512]{2,1,0:T(8,128)S(1)}, f32[2,64,512]{2,1,0:T(8,128)S(1)}, u32[]{:S(2)}, u32[]{:S(2)}) %collective-permute-start.17) | collective-permute-done | bytes 262176 | tf_op jit(solution)/shard_map/ppermute | solution.py:77
  159.3 4.0 %collective-permute-done.38 = f32[2,64,512]{2,1,0:T(8,128)S(1)} collective-permute-done((f32[2,64,512]{2,1,0:T(8,128)S(1)}, f32[2,64,512]{2,1,0:T(8,128)S(1)}, u32[]{:S(2)}, u32[]{:S(2)}) %collective-permute-start.38) | collective-permute-done | bytes 262176 | tf_op jit(solution)/shard_map/ppermute | solution.py:77
  167.9 1.9 collective-permute-done.20.refs_5_
  171.9 4.1 %collective-permute-done.41.refs_5_ = f32[1,64,512]{2,1,0:T(8,128)S(1)} collective-permute-done((f32[1,64,512]{2,1,0:T(8,128)S(1)}, f32[1,64,512]{2,1,0:T(8,128)S(1)}, u32[]{:S(2)}, u32[]{:S(2)}) %collective-permute-start.41) | collective-permute-done | bytes 131104 | tf_op jit(solution)/shard_map/ppermute | solution.py:77
  176.1 2.3 %shard_map.86.refs_7_ = f32[8,128,128]{2,1,0:T(8,128)S(1)} custom-call(f32[1,64,768]{2,1,0:T(8,128)S(1)} %get-tuple-element.134.refs_0_, f32[1,64,768]{2,1,0:T(8,128)S(1)} %get-tuple-element.132.refs_1_, f32[1,64,512]{2,1,0:T(8,128)S(1)} %get-tuple-element.140.refs_2_, f32[1,64,768]{2,1,0:T(8,128)S(1)} %collective-permute-done.39.refs_3_, ...), custom_call_target="tpu_custom_call" | custom-call | flops 1073741824 | bytes 2621440 | tf_op jit(solution)/shard_map/pallas_call | solution.py:219
  178.4 2.3 %shard_map.87 = f32[8,256,128]{2,1,0:T(8,128)S(1)} custom-call(f32[1,64,768]{2,1,0:T(8,128)S(1)} %get-tuple-element.138.refs_0_, f32[1,64,768]{2,1,0:T(8,128)S(1)} %get-tuple-element.136.refs_1_, f32[1,64,512]{2,1,0:T(8,128)S(1)} %get-tuple-element.142.refs_2_, f32[1,64,768]{2,1,0:T(8,128)S(1)} %collective-permute-done.18.refs_3_, ...), custom_call_target="tpu_custom_call" | custom-call | flops 1073741824 | bytes 2621440 | tf_op jit(solution)/shard_map/pallas_call | solution.py:219
  180.7 17.9 %all_to_all.5 = f32[8,256,128]{2,1,0:T(8,128)S(1)} all-to-all(f32[8,256,128]{2,1,0:T(8,128)S(1)} %shard_map.87), channel_id=1, replica_groups=mesh['row'=8,'col'=16] {'row'}, dimensions={0} | all-to-all | bytes 2097152 | tf_op jit(solution)/shard_map/all_to_all | solution.py:303
  (114 shorter events, 38.7 us)
Async XLA Ops:
  3.1 82.6 %collective-permute-start.11 = (f32[2048,1024]{1,0:T(8,128)}, f32[2048,1024]{1,0:T(8,128)}, u32[]{:S(2)}, u32[]{:S(2)}) collective-permute-start(f32[2048,1024]{1,0:T(8,128)} %param.9), channel_id=1, source_target_pairs={{0,1},{1,0},{2,3},{3,2},{4,5},{5,4},{6,7},{7,6},{8,9},{9,8},{10,11... | collective-permute-start | bytes 25165832 | tf_op jit(solution)/shard_map/ppermute | solution.py:77
  4.3 15.7 %collective-permute-start = (f32[1,64,768]{2,1,0:T(8,128)S(1)}, f32[1,64,768]{2,1,0:T(8,128)S(1)}, u32[]{:S(2)}, u32[]{:S(2)}) collective-permute-start(f32[1,64,768]{2,1,0:T(8,128)S(1)} %get-tuple-element.144), channel_id=1, source_target_pairs={{0,16},{1,17},{2,18},{3,19},{4,20},{5,21},{6,22},{7,23},{8,24},{9,... | collective-permute-start | bytes 589832 | tf_op jit(solution)/shard_map/ppermute | solution.py:77
  5.9 22.2 %collective-permute-start.24 = (f32[1,64,768]{2,1,0:T(8,128)S(1)}, f32[1,64,768]{2,1,0:T(8,128)S(1)}, u32[]{:S(2)}, u32[]{:S(2)}) collective-permute-start(f32[1,64,768]{2,1,0:T(8,128)S(1)} %get-tuple-element.143), channel_id=1, source_target_pairs={{0,16},{1,17},{2,18},{3,19},{4,20},{5,21},{6,22},{7,23},{8,24},{9,... | collective-permute-start | bytes 589832 | tf_op jit(solution)/shard_map/ppermute | solution.py:77
  13.5 9.3 %collective-permute-start.2 = (f32[1,64,640]{2,1,0:T(8,128)S(1)}, f32[1,64,640]{2,1,0:T(8,128)S(1)}, u32[]{:S(2)}, u32[]{:S(2)}) collective-permute-start(f32[1,64,640]{2,1,0:T(8,128)S(1)} %get-tuple-element.149), channel_id=1, source_target_pairs={{0,48},{1,49},{2,50},{3,51},{4,52},{5,53},{6,54},{7,55},{8,56},{9,... | collective-permute-start | bytes 491528 | tf_op jit(solution)/shard_map/ppermute | solution.py:77
  16.6 8.6 %collective-permute-start.3 = (f32[1,64,640]{2,1,0:T(8,128)S(1)}, f32[1,64,640]{2,1,0:T(8,128)S(1)}, u32[]{:S(2)}, u32[]{:S(2)}) collective-permute-start(f32[1,64,640]{2,1,0:T(8,128)S(1)} %get-tuple-element.148), channel_id=1, source_target_pairs={{0,64},{1,65},{2,66},{3,67},{4,68},{5,69},{6,70},{7,71},{8,72},{9,... | collective-permute-start | bytes 491528 | tf_op jit(solution)/shard_map/ppermute | solution.py:77
  19.9 10.7 %collective-permute-start.25 = (f32[1,64,640]{2,1,0:T(8,128)S(1)}, f32[1,64,640]{2,1,0:T(8,128)S(1)}, u32[]{:S(2)}, u32[]{:S(2)}) collective-permute-start(f32[1,64,640]{2,1,0:T(8,128)S(1)} %get-tuple-element.150), channel_id=1, source_target_pairs={{0,48},{1,49},{2,50},{3,51},{4,52},{5,53},{6,54},{7,55},{8,56},{9,... | collective-permute-start | bytes 491528 | tf_op jit(solution)/shard_map/ppermute | solution.py:77
  25.2 17.5 %collective-permute-start.4 = (f32[2,64,768]{2,1,0:T(8,128)S(1)}, f32[2,64,768]{2,1,0:T(8,128)S(1)}, u32[]{:S(2)}, u32[]{:S(2)}) collective-permute-start(f32[2,64,768]{2,1,0:T(8,128)S(1)} %pad_maximum_fusion.6), channel_id=1, source_target_pairs={{0,48},{1,49},{2,50},{3,51},{4,52},{5,53},{6,54},{7,55},{8,56},{9,... | collective-permute-start | bytes 1179656 | tf_op jit(solution)/shard_map/ppermute | solution.py:77
  28.1 12.2 %collective-permute-start.5 = (f32[2,64,640]{2,1,0:T(8,128)S(1)}, f32[2,64,640]{2,1,0:T(8,128)S(1)}, u32[]{:S(2)}, u32[]{:S(2)}) collective-permute-start(f32[2,64,640]{2,1,0:T(8,128)S(1)} %pad_maximum_fusion.8), channel_id=1, source_target_pairs={{0,64},{1,65},{2,66},{3,67},{4,68},{5,69},{6,70},{7,71},{8,72},{9,... | collective-permute-start | bytes 983048 | tf_op jit(solution)/shard_map/ppermute | solution.py:77
  30.7 11.6 %collective-permute-start.6 = (f32[2,64,640]{2,1,0:T(8,128)S(1)}, f32[2,64,640]{2,1,0:T(8,128)S(1)}, u32[]{:S(2)}, u32[]{:S(2)}) collective-permute-start(f32[2,64,640]{2,1,0:T(8,128)S(1)} %pad_maximum_fusion.9), channel_id=1, source_target_pairs={{0,16},{1,17},{2,18},{3,19},{4,20},{5,21},{6,22},{7,23},{8,24},{9,... | collective-permute-start | bytes 983048 | tf_op jit(solution)/shard_map/ppermute | solution.py:77
  31.3 13.6 %collective-permute-start.28 = (f32[2,64,640]{2,1,0:T(8,128)S(1)}, f32[2,64,640]{2,1,0:T(8,128)S(1)}, u32[]{:S(2)}, u32[]{:S(2)}) collective-permute-start(f32[2,64,640]{2,1,0:T(8,128)S(1)} %pad_maximum_fusion.10), channel_id=1, source_target_pairs={{0,64},{1,65},{2,66},{3,67},{4,68},{5,69},{6,70},{7,71},{8,72},{9,... | collective-permute-start | bytes 983048 | tf_op jit(solution)/shard_map/ppermute | solution.py:77
  42.2 13.6 %collective-permute-start.27 = (f32[2,64,768]{2,1,0:T(8,128)S(1)}, f32[2,64,768]{2,1,0:T(8,128)S(1)}, u32[]{:S(2)}, u32[]{:S(2)}) collective-permute-start(f32[2,64,768]{2,1,0:T(8,128)S(1)} %pad_maximum_fusion.7), channel_id=1, source_target_pairs={{0,48},{1,49},{2,50},{3,51},{4,52},{5,53},{6,54},{7,55},{8,56},{9,... | collective-permute-start | bytes 1179656 | tf_op jit(solution)/shard_map/ppermute | solution.py:77
  42.7 10.6 %collective-permute-start.29 = (f32[2,64,640]{2,1,0:T(8,128)S(1)}, f32[2,64,640]{2,1,0:T(8,128)S(1)}, u32[]{:S(2)}, u32[]{:S(2)}) collective-permute-start(f32[2,64,640]{2,1,0:T(8,128)S(1)} %pad_maximum_fusion.11), channel_id=1, source_target_pairs={{0,16},{1,17},{2,18},{3,19},{4,20},{5,21},{6,22},{7,23},{8,24},{9,... | collective-permute-start | bytes 983048 | tf_op jit(solution)/shard_map/ppermute | solution.py:77
  43.9 20.7 %collective-permute-start.8 = (f32[4,64,640]{2,1,0:T(8,128)S(1)}, f32[4,64,640]{2,1,0:T(8,128)S(1)}, u32[]{:S(2)}, u32[]{:S(2)}) collective-permute-start(f32[4,64,640]{2,1,0:T(8,128)S(1)} %pad_maximum_fusion.2.refs_1_), channel_id=1, source_target_pairs={{0,16},{1,17},{2,18},{3,19},{4,20},{5,21},{6,22},{7,23},{8,24},{9,... | collective-permute-start | bytes 1966088 | tf_op jit(solution)/shard_map/ppermute | solution.py:77
  44.9 20.6 %collective-permute-start.9 = (f32[4,64,640]{2,1,0:T(8,128)S(1)}, f32[4,64,640]{2,1,0:T(8,128)S(1)}, u32[]{:S(2)}, u32[]{:S(2)}) collective-permute-start(f32[4,64,640]{2,1,0:T(8,128)S(1)} %pad_maximum_fusion.3.refs_2_), channel_id=1, source_target_pairs={{0,48},{1,49},{2,50},{3,51},{4,52},{5,53},{6,54},{7,55},{8,56},{9,... | collective-permute-start | bytes 1966088 | tf_op jit(solution)/shard_map/ppermute | solution.py:77
  55.8 21.4 %collective-permute-start.7 = (f32[4,64,768]{2,1,0:T(8,128)S(1)}, f32[4,64,768]{2,1,0:T(8,128)S(1)}, u32[]{:S(2)}, u32[]{:S(2)}) collective-permute-start(f32[4,64,768]{2,1,0:T(8,128)S(1)} %pad_maximum_fusion.refs_0_), channel_id=1, source_target_pairs={{0,64},{1,65},{2,66},{3,67},{4,68},{5,69},{6,70},{7,71},{8,72},{9,... | collective-permute-start | bytes 2359304 | tf_op jit(solution)/shard_map/ppermute | solution.py:77
  58.4 27.2 %collective-permute-start.30 = (f32[4,64,768]{2,1,0:T(8,128)S(1)}, f32[4,64,768]{2,1,0:T(8,128)S(1)}, u32[]{:S(2)}, u32[]{:S(2)}) collective-permute-start(f32[4,64,768]{2,1,0:T(8,128)S(1)} %pad_maximum_fusion.1.refs_0_), channel_id=1, source_target_pairs={{0,64},{1,65},{2,66},{3,67},{4,68},{5,69},{6,70},{7,71},{8,72},{9,... | collective-permute-start | bytes 2359304 | tf_op jit(solution)/shard_map/ppermute | solution.py:77
  64.6 12.6 %collective-permute-start.31 = (f32[4,64,640]{2,1,0:T(8,128)S(1)}, f32[4,64,640]{2,1,0:T(8,128)S(1)}, u32[]{:S(2)}, u32[]{:S(2)}) collective-permute-start(f32[4,64,640]{2,1,0:T(8,128)S(1)} %pad_maximum_fusion.4.refs_1_), channel_id=1, source_target_pairs={{0,16},{1,17},{2,18},{3,19},{4,20},{5,21},{6,22},{7,23},{8,24},{9,... | collective-permute-start | bytes 1966088 | tf_op jit(solution)/shard_map/ppermute | solution.py:77
  65.5 13.2 %collective-permute-start.32 = (f32[4,64,640]{2,1,0:T(8,128)S(1)}, f32[4,64,640]{2,1,0:T(8,128)S(1)}, u32[]{:S(2)}, u32[]{:S(2)}) collective-permute-start(f32[4,64,640]{2,1,0:T(8,128)S(1)} %pad_maximum_fusion.5.refs_2_), channel_id=1, source_target_pairs={{0,48},{1,49},{2,50},{3,51},{4,52},{5,53},{6,54},{7,55},{8,56},{9,... | collective-permute-start | bytes 1966088 | tf_op jit(solution)/shard_map/ppermute | solution.py:77
  101.8 30.6 %collective-permute-start.12 = (f32[4,64,768]{2,1,0:T(8,128)S(1)}, f32[4,64,768]{2,1,0:T(8,128)S(1)}, u32[]{:S(2)}, u32[]{:S(2)}) collective-permute-start(f32[4,64,768]{2,1,0:T(8,128)S(1)} %get-tuple-element.82), channel_id=1, source_target_pairs={{0,4},{1,5},{2,6},{3,7},{4,0},{5,1},{6,2},{7,3},{8,12},{9,13},{10,... | collective-permute-start | bytes 2359304 | tf_op jit(solution)/shard_map/ppermute | solution.py:77
  102.1 31.9 %collective-permute-start.13 = (f32[4,64,768]{2,1,0:T(8,128)S(1)}, f32[4,64,768]{2,1,0:T(8,128)S(1)}, u32[]{:S(2)}, u32[]{:S(2)}) collective-permute-start(f32[4,64,768]{2,1,0:T(8,128)S(1)} %get-tuple-element.83), channel_id=1, source_target_pairs={{0,12},{1,13},{2,14},{3,15},{4,8},{5,9},{6,10},{7,11},{8,4},{9,5},... | collective-permute-start | bytes 2359304 | tf_op jit(solution)/shard_map/ppermute | solution.py:77
  103.5 28.3 %collective-permute-start.14 = (f32[4,64,512]{2,1,0:T(8,128)S(1)}, f32[4,64,512]{2,1,0:T(8,128)S(1)}, u32[]{:S(2)}, u32[]{:S(2)}) collective-permute-start(f32[4,64,512]{2,1,0:T(8,128)S(1)} %get-tuple-element.84), channel_id=1, source_target_pairs={{0,2},{1,3},{2,0},{3,1},{4,6},{5,7},{6,4},{7,5},{8,10},{9,11},{10,... | collective-permute-start | bytes 1572872 | tf_op jit(solution)/shard_map/ppermute | solution.py:77
  113.5 35.3 %collective-permute-start.33 = (f32[4,64,768]{2,1,0:T(8,128)S(1)}, f32[4,64,768]{2,1,0:T(8,128)S(1)}, u32[]{:S(2)}, u32[]{:S(2)}) collective-permute-start(f32[4,64,768]{2,1,0:T(8,128)S(1)} %get-tuple-element.109), channel_id=1, source_target_pairs={{0,4},{1,5},{2,6},{3,7},{4,0},{5,1},{6,2},{7,3},{8,12},{9,13},{10,... | collective-permute-start | bytes 2359304 | tf_op jit(solution)/shard_map/ppermute | solution.py:77
  114.0 34.9 %collective-permute-start.34 = (f32[4,64,768]{2,1,0:T(8,128)S(1)}, f32[4,64,768]{2,1,0:T(8,128)S(1)}, u32[]{:S(2)}, u32[]{:S(2)}) collective-permute-start(f32[4,64,768]{2,1,0:T(8,128)S(1)} %get-tuple-element.110), channel_id=1, source_target_pairs={{0,12},{1,13},{2,14},{3,15},{4,8},{5,9},{6,10},{7,11},{8,4},{9,5},... | collective-permute-start | bytes 2359304 | tf_op jit(solution)/shard_map/ppermute | solution.py:77
  131.8 35.7 %collective-permute-start.23 = (f32[2048]{0:T(1024)S(1)}, f32[2048]{0:T(1024)S(1)}, u32[]{:S(2)}, u32[]{:S(2)}) collective-permute-start(f32[2048]{0:T(1024)S(1)} %add.136), channel_id=1, source_target_pairs={{0,2},{1,3},{2,0},{3,1},{4,6},{5,7},{6,4},{7,5},{8,10},{9,11},{10,... | collective-permute-start | bytes 24584 | tf_op jit(solution)/shard_map/ppermute | solution.py:77
  132.4 13.9 %collective-permute-start.35 = (f32[4,64,512]{2,1,0:T(8,128)S(1)}, f32[4,64,512]{2,1,0:T(8,128)S(1)}, u32[]{:S(2)}, u32[]{:S(2)}) collective-permute-start(f32[4,64,512]{2,1,0:T(8,128)S(1)} %get-tuple-element.111), channel_id=1, source_target_pairs={{0,2},{1,3},{2,0},{3,1},{4,6},{5,7},{6,4},{7,5},{8,10},{9,11},{10,... | collective-permute-start | bytes 1572872 | tf_op jit(solution)/shard_map/ppermute | solution.py:77
  134.0 23.0 %collective-permute-start.15 = (f32[2,64,768]{2,1,0:T(8,128)S(1)}, f32[2,64,768]{2,1,0:T(8,128)S(1)}, u32[]{:S(2)}, u32[]{:S(2)}) collective-permute-start(f32[2,64,768]{2,1,0:T(8,128)S(1)} %slice_add_fusion.3), channel_id=1, source_target_pairs={{0,12},{1,13},{2,14},{3,15},{4,8},{5,9},{6,10},{7,11},{8,4},{9,5},... | collective-permute-start | bytes 1179656 | tf_op jit(solution)/shard_map/ppermute | solution.py:77
  146.4 11.0 %collective-permute-start.16 = (f32[2,64,768]{2,1,0:T(8,128)S(1)}, f32[2,64,768]{2,1,0:T(8,128)S(1)}, u32[]{:S(2)}, u32[]{:S(2)}) collective-permute-start(f32[2,64,768]{2,1,0:T(8,128)S(1)} %slice_add_fusion.2), channel_id=1, source_target_pairs={{0,2},{1,3},{2,0},{3,1},{4,6},{5,7},{6,4},{7,5},{8,10},{9,11},{10,... | collective-permute-start | bytes 1179656 | tf_op jit(solution)/shard_map/ppermute | solution.py:77
  149.0 14.7 %collective-permute-start.36 = (f32[2,64,768]{2,1,0:T(8,128)S(1)}, f32[2,64,768]{2,1,0:T(8,128)S(1)}, u32[]{:S(2)}, u32[]{:S(2)}) collective-permute-start(f32[2,64,768]{2,1,0:T(8,128)S(1)} %slice_add_fusion.1), channel_id=1, source_target_pairs={{0,12},{1,13},{2,14},{3,15},{4,8},{5,9},{6,10},{7,11},{8,4},{9,5},... | collective-permute-start | bytes 1179656 | tf_op jit(solution)/shard_map/ppermute | solution.py:77
  156.6 9.1 %collective-permute-start.37 = (f32[2,64,768]{2,1,0:T(8,128)S(1)}, f32[2,64,768]{2,1,0:T(8,128)S(1)}, u32[]{:S(2)}, u32[]{:S(2)}) collective-permute-start(f32[2,64,768]{2,1,0:T(8,128)S(1)} %slice_add_fusion), channel_id=1, source_target_pairs={{0,2},{1,3},{2,0},{3,1},{4,6},{5,7},{6,4},{7,5},{8,10},{9,11},{10,... | collective-permute-start | bytes 1179656 | tf_op jit(solution)/shard_map/ppermute | solution.py:77
  157.5 14.4 %collective-permute-start.18 = (f32[1,64,768]{2,1,0:T(8,128)S(1)}, f32[1,64,768]{2,1,0:T(8,128)S(1)}, u32[]{:S(2)}, u32[]{:S(2)}) collective-permute-start(f32[1,64,768]{2,1,0:T(8,128)S(1)} %get-tuple-element.137), channel_id=1, source_target_pairs={{0,2},{1,3},{2,0},{3,1},{4,6},{5,7},{6,4},{7,5},{8,10},{9,11},{10,... | collective-permute-start | bytes 589832 | tf_op jit(solution)/shard_map/ppermute | solution.py:77
  163.3 8.6 %collective-permute-start.19 = (f32[1,64,768]{2,1,0:T(8,128)S(1)}, f32[1,64,768]{2,1,0:T(8,128)S(1)}, u32[]{:S(2)}, u32[]{:S(2)}) collective-permute-start(f32[1,64,768]{2,1,0:T(8,128)S(1)} %get-tuple-element.135), channel_id=1, source_target_pairs={{0,4},{1,5},{2,6},{3,7},{4,0},{5,1},{6,2},{7,3},{8,12},{9,13},{10,... | collective-permute-start | bytes 589832 | tf_op jit(solution)/shard_map/ppermute | solution.py:77
  165.8 10.2 %collective-permute-start.39 = (f32[1,64,768]{2,1,0:T(8,128)S(1)}, f32[1,64,768]{2,1,0:T(8,128)S(1)}, u32[]{:S(2)}, u32[]{:S(2)}) collective-permute-start(f32[1,64,768]{2,1,0:T(8,128)S(1)} %get-tuple-element.133), channel_id=1, source_target_pairs={{0,2},{1,3},{2,0},{3,1},{4,6},{5,7},{6,4},{7,5},{8,10},{9,11},{10,... | collective-permute-start | bytes 589832 | tf_op jit(solution)/shard_map/ppermute | solution.py:77
  (15 other events, 245.1 us)

commit v8 on v7

--- a/solution.py
+++ b/solution.py
@@ -90,15 +90,16 @@
 SIZES = tuple(c // TILE for c in COLS)
 
 
-def mm_kernel(half, tbl, *refs):
-    if half == 0:
+def mm_kernel(half, qs, tbl, *refs):
+    fresh = half == 0 and qs[0] == 0
+    if fresh:
         first, last, refs = refs[:3], refs[3:6], refs[6:]
     else:
         (high, cross), refs = refs[:2], refs[2:]
     (own16, own8, own_rest, far16, far8, far_rest, level), refs = refs[:7], refs[7:]
-    outs, refs = refs[:3], refs[3:]
-    t = pl.program_id(0)
-    if half == 0:
+    outs, refs = refs[: len(qs)], refs[len(qs) :]
+    t = pl.program_id(0) + STARTS[qs[0]]
+    if fresh:
         high, cross, lhs16, lhs8 = refs
 
         @pl.when(t == 0)
@@ -116,7 +117,7 @@
 
     else:
         lhs16, lhs8 = refs
-    for q in range(3):
+    for q in qs:
 
         @pl.when(t == STARTS[q])
         def _(q=q):
@@ -138,35 +139,37 @@
     low = dot(lhs8[0, :, own], own_rest[rows, :]) + dot(lhs8[0, :, far], far_rest[rows, :])
     low += dot(lhs8[1, :, own], own8[rows, :]) + dot(lhs8[1, :, far], far8[rows, :])
     acc = (acc + low * level[...]).reshape(4, ROWS, TILE)
-    for q in range(3):
+    for k, q in enumerate(qs):
 
         @pl.when((t >= STARTS[q]) & (t < STARTS[q] + SIZES[q]))
-        def _(q=q):
-            outs[q][...] = acc
-
-
-def mm(half, tbl, pieces, factors):
+        def _(k=k):
+            outs[k][...] = acc
+
+
+def mm(half, qs, tbl, pieces, factors):
+    start = STARTS[qs[0]]
     whole = pl.BlockSpec(memory_space=pltpu.VMEM)
     outs = [
         pl.BlockSpec(
-            (4, ROWS, TILE), lambda t, tb, q=q: (0, 0, jnp.clip(t - STARTS[q], 0, SIZES[q] - 1))
+            (4, ROWS, TILE), lambda t, tb, q=q: (0, 0, jnp.clip(t + start - STARTS[q], 0, SIZES[q] - 1))
         )
-        for q in range(3)
+        for q in qs
     ]
-    shapes = [jax.ShapeDtypeStruct((4, ROWS, COLS[q]), jnp.float32) for q in range(3)]
-    if half == 0:
+    shapes = [jax.ShapeDtypeStruct((4, ROWS, COLS[q]), jnp.float32) for q in qs]
+    tiles = sum(SIZES[q] for q in qs)
+    if half == 0 and qs[0] == 0:
         outs += [whole] * 2
         shapes += [
             jax.ShapeDtypeStruct((8, ROWS, 2048), jnp.bfloat16),
             jax.ShapeDtypeStruct((2, 8, ROWS, 2048), jnp.float8_e4m3fn),
         ]
     res = pl.pallas_call(
-        functools.partial(mm_kernel, half),
+        functools.partial(mm_kernel, half, qs),
         out_shape=shapes,
         grid_spec=pltpu.PrefetchScalarGridSpec(
             num_scalar_prefetch=1,
-            grid=(2048 // TILE,),
-            in_specs=[whole] * (len(pieces) + 6) + [pl.BlockSpec((1, TILE), lambda t, tb: (0, t))],
+            grid=(tiles,),
+            in_specs=[whole] * (len(pieces) + 6) + [pl.BlockSpec((1, TILE), lambda t, tb: (0, t + start))],
             out_specs=outs,
             scratch_shapes=[
                 pltpu.VMEM((4 * ROWS, 2048), jnp.bfloat16),
@@ -174,13 +177,13 @@
             ],
         ),
         cost_estimate=pl.CostEstimate(
-            flops=2 * 2 * 4 * ROWS * 2048 * 2048,
-            bytes_accessed=2 * 4 * ROWS * 2048 * 4 + 4 * 2048 * 2048,
+            flops=2 * 2 * 4 * ROWS * 2048 * tiles * TILE,
+            bytes_accessed=4 * ROWS * 2048 * 4 + tiles * TILE * (4 * 2048 + 16 * ROWS),
             transcendentals=0,
         ),
         compiler_params=pltpu.CompilerParams(vmem_limit_bytes=8 * 2**20),
     )(tbl, *pieces, *factors)
-    return res[:3], res[3:]
+    return res[: len(qs)], res[len(qs) :]
 
 
 def tail_kernel(*refs):
@@ -254,9 +257,7 @@
     last = []
     for s in range(3):
         for c in range(CHUNKS):
-            came = lax.optimization_barrier(
-                [permute(gathered[c][p], ROW_DIMS[(p + s) % 3]) for p in range(3)]
-            )
+            came = lax.optimization_barrier([permute(gathered[c][p], ROW_DIMS[(p + s) % 3]) for p in range(3)])
             if s == 2:
                 last.append(came)
                 continue
@@ -287,17 +288,14 @@
     )
     sums = ()
     for c in range(CHUNKS):
-        sent, parts = mm(0, tbl, (*gathered[c], *last[c]), factors)
+        sent, parts = mm(0, (0,), tbl, (*gathered[c], *last[c]), factors)
+        sent = [*sent, *mm(0, (1, 2), tbl, parts, factors)[0]]
         came = lax.optimization_barrier([permute(sent[q], COL_DIMS[q]) for q in range(3)])
-        kept, _ = mm(1, tbl, parts, factors)
+        kept, _ = mm(1, (0, 1, 2), tbl, parts, factors)
         passed = [kept[q][:2] + came[q][:2] for q in range(3)]
-        second = lax.optimization_barrier(
-            [permute(passed[q], COL_DIMS[(q + 1) % 3]) for q in range(3)]
-        )
+        second = lax.optimization_barrier([permute(passed[q], COL_DIMS[(q + 1) % 3]) for q in range(3)])
         passed = [kept[q][2:3] + came[q][2:3] + second[q][:1] for q in range(3)]
-        third = lax.optimization_barrier(
-            [permute(passed[q], COL_DIMS[(q + 2) % 3]) for q in range(3)]
-        )
+        third = lax.optimization_barrier([permute(passed[q], COL_DIMS[(q + 2) % 3]) for q in range(3)])
         held = [kept[q][3:] + came[q][3:] + second[q][1:] for q in range(3)]
         sums = (tail(held, third, cells, sums),)
     parts = lax.all_to_all(sums[0], "row", split_axis=0, concat_axis=0, tiled=True)

time: 200 us -> 198 us (0.990)
  waiting for transfers between devices: 62.5 us -> 58.1 us
  starting transfers between devices: 57.7 us -> 60.1 us
    ppermute x42, waiting for transfers between devices: 62.5 us -> 58.1 us  [permute(): return lax.ppermute(x, BOTH, pairs)]
    ppermute x42, starting transfers between devices: 57.7 us -> 60.1 us  [permute(): return lax.ppermute(x, BOTH, pairs)]
    pallas_call x4 -> x6, Pallas kernels: 32.1 us -> 32.7 us  [mm(): pl.pallas_call(functools.partial(mm_kernel, half, qs), out_shape=shapes,...]
  transfers between devices with their start and end apart: 42 -> 42, of which waited for: 15 -> 15; matrix products, arithmetic and copies ran while one was open for 7% -> 7% of each run, Pallas kernels for 12% -> 8%
where the time goes in v8:
time: 198 us; the launch traced here: 197 us
  starting transfers between devices  60.1 us (30%)
  waiting for transfers between devices  58.1 us (29%)
  Pallas kernels  37.4 us (19%)
  other arithmetic  20.6 us (10%)
  blocking collectives  17.2 us (9%)
  local copies, waits for them, and re-layouts  3.59 us (2%)
    ppermute x42, starting transfers between devices, permute(): return lax.ppermute(x, BOTH, pairs)  60.1 us
    ppermute x42, waiting for transfers between devices, permute(): return lax.ppermute(x, BOTH, pairs)  58.1 us
    pallas_call x6, Pallas kernels, mm(): pl.pallas_call(functools.partial(mm_kernel, half, qs), out_shape=shapes,...  32.7 us
    all_to_all x1, blocking collectives, step(): lax.all_to_all(sums[0], 'row', split_axis=0, concat_axis=0, tiled=True)  17.2 us
    convert_element_type x2, other arithmetic, split(): ((x - high) * (level * LIFT)[:, None]).astype(jnp.float8_e4m3fn)  12.9 us
    pallas_call x2, Pallas kernels, tail(): pl.pallas_call(tail_kernel, out_shape=jax.ShapeDtypeStruct((8, rows, 128)...  4.67 us
    reduce_sum x1, other arithmetic, step(): norms = jnp.sum(factor * factor, axis=1)  4.15 us
  transfers between devices with their start and end apart: 42, of which 15 were waited for; matrix products, arithmetic and copies ran while one was open for 7% of the time, Pallas kernels for 8%

profile of v8, /device:TPU:0, one launch (start us, length us, event | category | flops | bytes accessed | tf_op | source)
XLA Modules:
  0.0 197.3 jit_solution(5036890419743854536)
XLA Ops:
  9.2 4.1 %multiply_reduce_fusion = f32[2048]{0:T(1024)S(1)} fusion(f32[2048,1024]{1,0:T(8,128)} %param.9), kind=kLoop, calls=%fused_computation.12 | loop fusion | flops 4192256 | bytes 8396800 | tf_op jit(solution)/shard_map/reduce_sum | solution.py:266
  13.5 2.9 %collective-permute-start.2 = (f32[1,64,640]{2,1,0:T(8,128)S(1)}, f32[1,64,640]{2,1,0:T(8,128)S(1)}, u32[]{:S(2)}, u32[]{:S(2)}) collective-permute-start(f32[1,64,640]{2,1,0:T(8,128)S(1)} %get-tuple-element.149), channel_id=1, source_target_pairs={{0,48},{1,49},{2,50},{3,51},{4,52},{5,53},{6,54},{7,55},{8,56},{9,... | collective-permute-start | bytes 491528 | tf_op jit(solution)/shard_map/ppermute | solution.py:77
  16.6 3.3 %collective-permute-start.3 = (f32[1,64,640]{2,1,0:T(8,128)S(1)}, f32[1,64,640]{2,1,0:T(8,128)S(1)}, u32[]{:S(2)}, u32[]{:S(2)}) collective-permute-start(f32[1,64,640]{2,1,0:T(8,128)S(1)} %get-tuple-element.148), channel_id=1, source_target_pairs={{0,64},{1,65},{2,66},{3,67},{4,68},{5,69},{6,70},{7,71},{8,72},{9,... | collective-permute-start | bytes 491528 | tf_op jit(solution)/shard_map/ppermute | solution.py:77
  19.9 2.8 %collective-permute-start.25 = (f32[1,64,640]{2,1,0:T(8,128)S(1)}, f32[1,64,640]{2,1,0:T(8,128)S(1)}, u32[]{:S(2)}, u32[]{:S(2)}) collective-permute-start(f32[1,64,640]{2,1,0:T(8,128)S(1)} %get-tuple-element.150), channel_id=1, source_target_pairs={{0,48},{1,49},{2,50},{3,51},{4,52},{5,53},{6,54},{7,55},{8,56},{9,... | collective-permute-start | bytes 491528 | tf_op jit(solution)/shard_map/ppermute | solution.py:77
  22.8 2.4 %collective-permute-start.26 = (f32[1,64,640]{2,1,0:T(8,128)S(1)}, f32[1,64,640]{2,1,0:T(8,128)S(1)}, u32[]{:S(2)}, u32[]{:S(2)}) collective-permute-start(f32[1,64,640]{2,1,0:T(8,128)S(1)} %get-tuple-element.147), channel_id=1, source_target_pairs={{0,64},{1,65},{2,66},{3,67},{4,68},{5,69},{6,70},{7,71},{8,72},{9,... | collective-permute-start | bytes 491528 | tf_op jit(solution)/shard_map/ppermute | solution.py:77
  25.2 2.8 %collective-permute-start.4 = (f32[2,64,768]{2,1,0:T(8,128)S(1)}, f32[2,64,768]{2,1,0:T(8,128)S(1)}, u32[]{:S(2)}, u32[]{:S(2)}) collective-permute-start(f32[2,64,768]{2,1,0:T(8,128)S(1)} %pad_maximum_fusion.6), channel_id=1, source_target_pairs={{0,48},{1,49},{2,50},{3,51},{4,52},{5,53},{6,54},{7,55},{8,56},{9,... | collective-permute-start | bytes 1179656 | tf_op jit(solution)/shard_map/ppermute | solution.py:77
  28.1 2.5 %collective-permute-start.5 = (f32[2,64,640]{2,1,0:T(8,128)S(1)}, f32[2,64,640]{2,1,0:T(8,128)S(1)}, u32[]{:S(2)}, u32[]{:S(2)}) collective-permute-start(f32[2,64,640]{2,1,0:T(8,128)S(1)} %pad_maximum_fusion.8), channel_id=1, source_target_pairs={{0,64},{1,65},{2,66},{3,67},{4,68},{5,69},{6,70},{7,71},{8,72},{9,... | collective-permute-start | bytes 983048 | tf_op jit(solution)/shard_map/ppermute | solution.py:77
  32.2 8.1 %collective-permute-done.5 = f32[2,64,640]{2,1,0:T(8,128)S(1)} collective-permute-done((f32[2,64,640]{2,1,0:T(8,128)S(1)}, f32[2,64,640]{2,1,0:T(8,128)S(1)}, u32[]{:S(2)}, u32[]{:S(2)}) %collective-permute-start.5) | collective-permute-done | bytes 327712 | tf_op jit(solution)/shard_map/ppermute | solution.py:77
  44.9 2.7 %collective-permute-start.9 = (f32[4,64,640]{2,1,0:T(8,128)S(1)}, f32[4,64,640]{2,1,0:T(8,128)S(1)}, u32[]{:S(2)}, u32[]{:S(2)}) collective-permute-start(f32[4,64,640]{2,1,0:T(8,128)S(1)} %pad_maximum_fusion.3.refs_2_), channel_id=1, source_target_pairs={{0,48},{1,49},{2,50},{3,51},{4,52},{5,53},{6,54},{7,55},{8,56},{9,... | collective-permute-start | bytes 1966088 | tf_op jit(solution)/shard_map/ppermute | solution.py:77
  47.8 5.5 %collective-permute-done.29 = f32[2,64,640]{2,1,0:T(8,128)S(1)} collective-permute-done((f32[2,64,640]{2,1,0:T(8,128)S(1)}, f32[2,64,640]{2,1,0:T(8,128)S(1)}, u32[]{:S(2)}, u32[]{:S(2)}) %collective-permute-start.29) | collective-permute-done | bytes 327712 | tf_op jit(solution)/shard_map/ppermute | solution.py:77
  53.3 2.5 %collective-permute-start.22 = (f32[2048]{0:T(1024)S(1)}, f32[2048]{0:T(1024)S(1)}, u32[]{:S(2)}, u32[]{:S(2)}) collective-permute-start(f32[2048]{0:T(1024)S(1)} %add.135), channel_id=1, source_target_pairs={{0,12},{1,13},{2,14},{3,15},{4,8},{5,9},{6,10},{7,11},{8,4},{9,5},... | collective-permute-start | bytes 24584 | tf_op jit(solution)/shard_map/ppermute | solution.py:77
  55.8 2.4 %collective-permute-start.7 = (f32[4,64,768]{2,1,0:T(8,128)S(1)}, f32[4,64,768]{2,1,0:T(8,128)S(1)}, u32[]{:S(2)}, u32[]{:S(2)}) collective-permute-start(f32[4,64,768]{2,1,0:T(8,128)S(1)} %pad_maximum_fusion.refs_0_), channel_id=1, source_target_pairs={{0,64},{1,65},{2,66},{3,67},{4,68},{5,69},{6,70},{7,71},{8,72},{9,... | collective-permute-start | bytes 2359304 | tf_op jit(solution)/shard_map/ppermute | solution.py:77
  60.6 4.0 %collective-permute-done.8.refs_4_ = f32[4,64,640]{2,1,0:T(8,128)S(1)} collective-permute-done((f32[4,64,640]{2,1,0:T(8,128)S(1)}, f32[4,64,640]{2,1,0:T(8,128)S(1)}, u32[]{:S(2)}, u32[]{:S(2)}) %collective-permute-start.8) | collective-permute-done | bytes 655392 | tf_op jit(solution)/shard_map/ppermute | solution.py:77
  67.4 5.3 %fusion.2 = (f8e4m3fn[2048,1024]{1,0:T(32,128)(4,1)S(1)}, f8e4m3fn[2048,1024]{1,0:T(32,128)(4,1)S(1)}, bf16[2048,1024]{1,0:T(8,128)(2,1)S(1)}) fusion(f32[2048,1024]{1,0:T(8,128)S(1)} %bitcast.32, f32[2048]{0:T(1024)S(1)} %broadcast_multiply_fusion.1, f32[2048]{0:T(1024)S(1)} %multiply_select_fusion), kind=kLoop, calls=%fused_computation.8 | loop fusion | flops 14680064 | bytes 16793600 | tf_op jit(solution)/shard_map/convert_element_type | solution.py:85
  72.7 4.5 %collective-permute-done.7.refs_3_ = f32[4,64,768]{2,1,0:T(8,128)S(1)} collective-permute-done((f32[4,64,768]{2,1,0:T(8,128)S(1)}, f32[4,64,768]{2,1,0:T(8,128)S(1)}, u32[]{:S(2)}, u32[]{:S(2)}) %collective-permute-start.7) | collective-permute-done | bytes 786464 | tf_op jit(solution)/shard_map/ppermute | solution.py:77
  78.8 6.9 %collective-permute-done.30.refs_3_ = f32[4,64,768]{2,1,0:T(8,128)S(1)} collective-permute-done((f32[4,64,768]{2,1,0:T(8,128)S(1)}, f32[4,64,768]{2,1,0:T(8,128)S(1)}, u32[]{:S(2)}, u32[]{:S(2)}) %collective-permute-start.30) | collective-permute-done | bytes 786464 | tf_op jit(solution)/shard_map/ppermute | solution.py:77
  85.7 7.6 %fusion.5 = (f8e4m3fn[2048,1024]{1,0:T(32,128)(4,1)S(1)}, f8e4m3fn[2048,1024]{1,0:T(32,128)(4,1)S(1)}, bf16[2048,1024]{1,0:T(8,128)(2,1)S(1)}) fusion(f32[2048,1024]{1,0:T(8,128)} %collective-permute-done.11, f32[2048]{0:T(1024)S(1)} %broadcast_multiply_fusion, f32[2048]{0:T(1024)S(1)} %multiply_select_fusion), kind=kLoop, calls=%fused_computation.11 | loop fusion | flops 14680064 | bytes 16793600 | tf_op jit(solution)/shard_map/convert_element_type | solution.py:85
  93.3 4.0 %shard_map.82 = (f32[4,64,768]{2,1,0:T(8,128)S(1)}, bf16[8,64,2048]{2,1,0:T(8,128)(2,1)S(1)}, f8e4m3fn[2,8,64,2048]{3,2,1,0:T(32,128)(4,1)S(1)}) custom-call(s32[24]{0:T(128)S(1)} %fusion.7.tbl, f32[4,64,768]{2,1,0:T(8,128)S(1)} %pad_maximum_fusion.refs_0_, f32[4,64,640]{2,1,0:T(8,128)S(1)} %pad_maximum_fusion.2.refs_1_, ...), custom_call_target="tpu_custom_call" | custom-call | flops 1610612736 | bytes 9175040 | tf_op jit(solution)/shard_map/pallas_call | solution.py:166
  97.3 4.8 %shard_map.84 = (f32[4,64,768]{2,1,0:T(8,128)S(1)}, f32[4,64,512]{2,1,0:T(8,128)S(1)}) custom-call(s32[24]{0:T(128)S(1)} %fusion.7.tbl, bf16[8,64,2048]{2,1,0:T(8,128)(2,1)S(1)} %get-tuple-element.79.refs_0_, f8e4m3fn[2,8,64,2048]{3,2,1,0:T(32,128)(4,1)S(1)} %get-tuple-element.80.refs_1_, bf16[2048,1024]{1,0:T(8,128)(2,1)S(1)} %get-tuple-element.130.refs_6_.refs_2_, ...), custom_call_target="tpu_custom_call" | custom-call | flops 2684354560 | bytes 13893632 | tf_op jit(solution)/shard_map/pallas_call | solution.py:166
  102.1 7.6 %shard_map.83 = (f32[4,64,768]{2,1,0:T(8,128)S(1)}, f32[4,64,768]{2,1,0:T(8,128)S(1)}, f32[4,64,512]{2,1,0:T(8,128)S(1)}) custom-call(s32[24]{0:T(128)S(1)} %fusion.7.tbl, bf16[8,64,2048]{2,1,0:T(8,128)(2,1)S(1)} %get-tuple-element.79.refs_0_, f8e4m3fn[2,8,64,2048]{3,2,1,0:T(32,128)(4,1)S(1)} %get-tuple-element.80.refs_1_, ...), custom_call_target="tpu_custom_call" | custom-call | flops 4294967296 | bytes 20971520 | tf_op jit(solution)/shard_map/pallas_call | solution.py:166
  112.8 4.0 %shard_map.85 = (f32[4,64,768]{2,1,0:T(8,128)S(1)}, bf16[8,64,2048]{2,1,0:T(8,128)(2,1)S(1)}, f8e4m3fn[2,8,64,2048]{3,2,1,0:T(32,128)(4,1)S(1)}) custom-call(s32[24]{0:T(128)S(1)} %fusion.7.tbl, f32[4,64,768]{2,1,0:T(8,128)S(1)} %pad_maximum_fusion.1.refs_0_, f32[4,64,640]{2,1,0:T(8,128)S(1)} %pad_maximum_fusion.4.refs_1_, ...), custom_call_target="tpu_custom_call" | custom-call | flops 1610612736 | bytes 9175040 | tf_op jit(solution)/shard_map/pallas_call | solution.py:166
  117.6 4.8 %shard_map.87 = (f32[4,64,768]{2,1,0:T(8,128)S(1)}, f32[4,64,512]{2,1,0:T(8,128)S(1)}) custom-call(s32[24]{0:T(128)S(1)} %fusion.7.tbl, bf16[8,64,2048]{2,1,0:T(8,128)(2,1)S(1)} %get-tuple-element.106.refs_0_, f8e4m3fn[2,8,64,2048]{3,2,1,0:T(32,128)(4,1)S(1)} %get-tuple-element.107.refs_1_, bf16[2048,1024]{1,0:T(8,128)(2,1)S(1)} %get-tuple-element.130.refs_6_.refs_2_, ...), custom_call_target="tpu_custom_call" | custom-call | flops 2684354560 | bytes 13893632 | tf_op jit(solution)/shard_map/pallas_call | solution.py:166
  122.4 2.7 %collective-permute-start.34 = (f32[4,64,768]{2,1,0:T(8,128)S(1)}, f32[4,64,768]{2,1,0:T(8,128)S(1)}, u32[]{:S(2)}, u32[]{:S(2)}) collective-permute-start(f32[4,64,768]{2,1,0:T(8,128)S(1)} %get-tuple-element.110), channel_id=1, source_target_pairs={{0,12},{1,13},{2,14},{3,15},{4,8},{5,9},{6,10},{7,11},{8,4},{9,5},... | collective-permute-start | bytes 2359304 | tf_op jit(solution)/shard_map/ppermute | solution.py:77
  125.1 7.6 %shard_map.86 = (f32[4,64,768]{2,1,0:T(8,128)S(1)}, f32[4,64,768]{2,1,0:T(8,128)S(1)}, f32[4,64,512]{2,1,0:T(8,128)S(1)}) custom-call(s32[24]{0:T(128)S(1)} %fusion.7.tbl, bf16[8,64,2048]{2,1,0:T(8,128)(2,1)S(1)} %get-tuple-element.106.refs_0_, f8e4m3fn[2,8,64,2048]{3,2,1,0:T(32,128)(4,1)S(1)} %get-tuple-element.107.refs_1_, ...), custom_call_target="tpu_custom_call" | custom-call | flops 4294967296 | bytes 20971520 | tf_op jit(solution)/shard_map/pallas_call | solution.py:166
  135.7 9.9 %collective-permute-done.35 = f32[4,64,512]{2,1,0:T(8,128)S(1)} collective-permute-done((f32[4,64,512]{2,1,0:T(8,128)S(1)}, f32[4,64,512]{2,1,0:T(8,128)S(1)}, u32[]{:S(2)}, u32[]{:S(2)}) %collective-permute-start.35) | collective-permute-done | bytes 524320 | tf_op jit(solution)/shard_map/ppermute | solution.py:77
  150.0 5.6 %collective-permute-done.17 = f32[2,64,512]{2,1,0:T(8,128)S(1)} collective-permute-done((f32[2,64,512]{2,1,0:T(8,128)S(1)}, f32[2,64,512]{2,1,0:T(8,128)S(1)}, u32[]{:S(2)}, u32[]{:S(2)}) %collective-permute-start.17) | collective-permute-done | bytes 262176 | tf_op jit(solution)/shard_map/ppermute | solution.py:77
  158.4 3.8 %collective-permute-done.38 = f32[2,64,512]{2,1,0:T(8,128)S(1)} collective-permute-done((f32[2,64,512]{2,1,0:T(8,128)S(1)}, f32[2,64,512]{2,1,0:T(8,128)S(1)}, u32[]{:S(2)}, u32[]{:S(2)}) %collective-permute-start.38) | collective-permute-done | bytes 262176 | tf_op jit(solution)/shard_map/ppermute | solution.py:77
  162.4 2.7 %collective-permute-start.20 = (f32[1,64,512]{2,1,0:T(8,128)S(1)}, f32[1,64,512]{2,1,0:T(8,128)S(1)}, u32[]{:S(2)}, u32[]{:S(2)}) collective-permute-start(f32[1,64,512]{2,1,0:T(8,128)S(1)} %get-tuple-element.141), channel_id=1, source_target_pairs={{0,12},{1,13},{2,14},{3,15},{4,8},{5,9},{6,10},{7,11},{8,4},{9,5},... | collective-permute-start | bytes 393224 | tf_op jit(solution)/shard_map/ppermute | solution.py:77
  168.6 2.7 %collective-permute-start.41 = (f32[1,64,512]{2,1,0:T(8,128)S(1)}, f32[1,64,512]{2,1,0:T(8,128)S(1)}, u32[]{:S(2)}, u32[]{:S(2)}) collective-permute-start(f32[1,64,512]{2,1,0:T(8,128)S(1)} %get-tuple-element.139), channel_id=1, source_target_pairs={{0,12},{1,13},{2,14},{3,15},{4,8},{5,9},{6,10},{7,11},{8,4},{9,5},... | collective-permute-start | bytes 393224 | tf_op jit(solution)/shard_map/ppermute | solution.py:77
  171.4 3.4 %collective-permute-done.41.refs_5_ = f32[1,64,512]{2,1,0:T(8,128)S(1)} collective-permute-done((f32[1,64,512]{2,1,0:T(8,128)S(1)}, f32[1,64,512]{2,1,0:T(8,128)S(1)}, u32[]{:S(2)}, u32[]{:S(2)}) %collective-permute-start.41) | collective-permute-done | bytes 131104 | tf_op jit(solution)/shard_map/ppermute | solution.py:77
  174.8 2.3 %shard_map.88.refs_7_ = f32[8,128,128]{2,1,0:T(8,128)S(1)} custom-call(f32[1,64,768]{2,1,0:T(8,128)S(1)} %get-tuple-element.134.refs_0_, f32[1,64,768]{2,1,0:T(8,128)S(1)} %get-tuple-element.132.refs_1_, f32[1,64,512]{2,1,0:T(8,128)S(1)} %get-tuple-element.140.refs_2_, f32[1,64,768]{2,1,0:T(8,128)S(1)} %collective-permute-done.39.refs_3_, ...), custom_call_target="tpu_custom_call" | custom-call | flops 1073741824 | bytes 2621440 | tf_op jit(solution)/shard_map/pallas_call | solution.py:222
  179.4 17.2 %all_to_all.5 = f32[8,256,128]{2,1,0:T(8,128)S(1)} all-to-all(f32[8,256,128]{2,1,0:T(8,128)S(1)} %shard_map.89), channel_id=1, replica_groups=mesh['row'=8,'col'=16] {'row'}, dimensions={0} | all-to-all | bytes 2097152 | tf_op jit(solution)/shard_map/all_to_all | solution.py:301
  (116 shorter events, 43.3 us)
Async XLA Ops:
  3.1 82.6 %collective-permute-start.11 = (f32[2048,1024]{1,0:T(8,128)}, f32[2048,1024]{1,0:T(8,128)}, u32[]{:S(2)}, u32[]{:S(2)}) collective-permute-start(f32[2048,1024]{1,0:T(8,128)} %param.9), channel_id=1, source_target_pairs={{0,1},{1,0},{2,3},{3,2},{4,5},{5,4},{6,7},{7,6},{8,9},{9,8},{10,11... | collective-permute-start | bytes 25165832 | tf_op jit(solution)/shard_map/ppermute | solution.py:77
  4.3 15.7 %collective-permute-start = (f32[1,64,768]{2,1,0:T(8,128)S(1)}, f32[1,64,768]{2,1,0:T(8,128)S(1)}, u32[]{:S(2)}, u32[]{:S(2)}) collective-permute-start(f32[1,64,768]{2,1,0:T(8,128)S(1)} %get-tuple-element.144), channel_id=1, source_target_pairs={{0,16},{1,17},{2,18},{3,19},{4,20},{5,21},{6,22},{7,23},{8,24},{9,... | collective-permute-start | bytes 589832 | tf_op jit(solution)/shard_map/ppermute | solution.py:77
  5.9 22.2 %collective-permute-start.24 = (f32[1,64,768]{2,1,0:T(8,128)S(1)}, f32[1,64,768]{2,1,0:T(8,128)S(1)}, u32[]{:S(2)}, u32[]{:S(2)}) collective-permute-start(f32[1,64,768]{2,1,0:T(8,128)S(1)} %get-tuple-element.143), channel_id=1, source_target_pairs={{0,16},{1,17},{2,18},{3,19},{4,20},{5,21},{6,22},{7,23},{8,24},{9,... | collective-permute-start | bytes 589832 | tf_op jit(solution)/shard_map/ppermute | solution.py:77
  13.5 9.3 %collective-permute-start.2 = (f32[1,64,640]{2,1,0:T(8,128)S(1)}, f32[1,64,640]{2,1,0:T(8,128)S(1)}, u32[]{:S(2)}, u32[]{:S(2)}) collective-permute-start(f32[1,64,640]{2,1,0:T(8,128)S(1)} %get-tuple-element.149), channel_id=1, source_target_pairs={{0,48},{1,49},{2,50},{3,51},{4,52},{5,53},{6,54},{7,55},{8,56},{9,... | collective-permute-start | bytes 491528 | tf_op jit(solution)/shard_map/ppermute | solution.py:77
  16.6 8.6 %collective-permute-start.3 = (f32[1,64,640]{2,1,0:T(8,128)S(1)}, f32[1,64,640]{2,1,0:T(8,128)S(1)}, u32[]{:S(2)}, u32[]{:S(2)}) collective-permute-start(f32[1,64,640]{2,1,0:T(8,128)S(1)} %get-tuple-element.148), channel_id=1, source_target_pairs={{0,64},{1,65},{2,66},{3,67},{4,68},{5,69},{6,70},{7,71},{8,72},{9,... | collective-permute-start | bytes 491528 | tf_op jit(solution)/shard_map/ppermute | solution.py:77
  19.9 10.7 %collective-permute-start.25 = (f32[1,64,640]{2,1,0:T(8,128)S(1)}, f32[1,64,640]{2,1,0:T(8,128)S(1)}, u32[]{:S(2)}, u32[]{:S(2)}) collective-permute-start(f32[1,64,640]{2,1,0:T(8,128)S(1)} %get-tuple-element.150), channel_id=1, source_target_pairs={{0,48},{1,49},{2,50},{3,51},{4,52},{5,53},{6,54},{7,55},{8,56},{9,... | collective-permute-start | bytes 491528 | tf_op jit(solution)/shard_map/ppermute | solution.py:77
  25.2 17.5 %collective-permute-start.4 = (f32[2,64,768]{2,1,0:T(8,128)S(1)}, f32[2,64,768]{2,1,0:T(8,128)S(1)}, u32[]{:S(2)}, u32[]{:S(2)}) collective-permute-start(f32[2,64,768]{2,1,0:T(8,128)S(1)} %pad_maximum_fusion.6), channel_id=1, source_target_pairs={{0,48},{1,49},{2,50},{3,51},{4,52},{5,53},{6,54},{7,55},{8,56},{9,... | collective-permute-start | bytes 1179656 | tf_op jit(solution)/shard_map/ppermute | solution.py:77
  28.1 12.2 %collective-permute-start.5 = (f32[2,64,640]{2,1,0:T(8,128)S(1)}, f32[2,64,640]{2,1,0:T(8,128)S(1)}, u32[]{:S(2)}, u32[]{:S(2)}) collective-permute-start(f32[2,64,640]{2,1,0:T(8,128)S(1)} %pad_maximum_fusion.8), channel_id=1, source_target_pairs={{0,64},{1,65},{2,66},{3,67},{4,68},{5,69},{6,70},{7,71},{8,72},{9,... | collective-permute-start | bytes 983048 | tf_op jit(solution)/shard_map/ppermute | solution.py:77
  30.7 11.6 %collective-permute-start.6 = (f32[2,64,640]{2,1,0:T(8,128)S(1)}, f32[2,64,640]{2,1,0:T(8,128)S(1)}, u32[]{:S(2)}, u32[]{:S(2)}) collective-permute-start(f32[2,64,640]{2,1,0:T(8,128)S(1)} %pad_maximum_fusion.9), channel_id=1, source_target_pairs={{0,16},{1,17},{2,18},{3,19},{4,20},{5,21},{6,22},{7,23},{8,24},{9,... | collective-permute-start | bytes 983048 | tf_op jit(solution)/shard_map/ppermute | solution.py:77
  31.3 13.6 %collective-permute-start.28 = (f32[2,64,640]{2,1,0:T(8,128)S(1)}, f32[2,64,640]{2,1,0:T(8,128)S(1)}, u32[]{:S(2)}, u32[]{:S(2)}) collective-permute-start(f32[2,64,640]{2,1,0:T(8,128)S(1)} %pad_maximum_fusion.10), channel_id=1, source_target_pairs={{0,64},{1,65},{2,66},{3,67},{4,68},{5,69},{6,70},{7,71},{8,72},{9,... | collective-permute-start | bytes 983048 | tf_op jit(solution)/shard_map/ppermute | solution.py:77
  42.2 13.6 %collective-permute-start.27 = (f32[2,64,768]{2,1,0:T(8,128)S(1)}, f32[2,64,768]{2,1,0:T(8,128)S(1)}, u32[]{:S(2)}, u32[]{:S(2)}) collective-permute-start(f32[2,64,768]{2,1,0:T(8,128)S(1)} %pad_maximum_fusion.7), channel_id=1, source_target_pairs={{0,48},{1,49},{2,50},{3,51},{4,52},{5,53},{6,54},{7,55},{8,56},{9,... | collective-permute-start | bytes 1179656 | tf_op jit(solution)/shard_map/ppermute | solution.py:77
  42.7 10.6 %collective-permute-start.29 = (f32[2,64,640]{2,1,0:T(8,128)S(1)}, f32[2,64,640]{2,1,0:T(8,128)S(1)}, u32[]{:S(2)}, u32[]{:S(2)}) collective-permute-start(f32[2,64,640]{2,1,0:T(8,128)S(1)} %pad_maximum_fusion.11), channel_id=1, source_target_pairs={{0,16},{1,17},{2,18},{3,19},{4,20},{5,21},{6,22},{7,23},{8,24},{9,... | collective-permute-start | bytes 983048 | tf_op jit(solution)/shard_map/ppermute | solution.py:77
  43.9 20.7 %collective-permute-start.8 = (f32[4,64,640]{2,1,0:T(8,128)S(1)}, f32[4,64,640]{2,1,0:T(8,128)S(1)}, u32[]{:S(2)}, u32[]{:S(2)}) collective-permute-start(f32[4,64,640]{2,1,0:T(8,128)S(1)} %pad_maximum_fusion.2.refs_1_), channel_id=1, source_target_pairs={{0,16},{1,17},{2,18},{3,19},{4,20},{5,21},{6,22},{7,23},{8,24},{9,... | collective-permute-start | bytes 1966088 | tf_op jit(solution)/shard_map/ppermute | solution.py:77
  44.9 20.6 %collective-permute-start.9 = (f32[4,64,640]{2,1,0:T(8,128)S(1)}, f32[4,64,640]{2,1,0:T(8,128)S(1)}, u32[]{:S(2)}, u32[]{:S(2)}) collective-permute-start(f32[4,64,640]{2,1,0:T(8,128)S(1)} %pad_maximum_fusion.3.refs_2_), channel_id=1, source_target_pairs={{0,48},{1,49},{2,50},{3,51},{4,52},{5,53},{6,54},{7,55},{8,56},{9,... | collective-permute-start | bytes 1966088 | tf_op jit(solution)/shard_map/ppermute | solution.py:77
  55.8 21.4 %collective-permute-start.7 = (f32[4,64,768]{2,1,0:T(8,128)S(1)}, f32[4,64,768]{2,1,0:T(8,128)S(1)}, u32[]{:S(2)}, u32[]{:S(2)}) collective-permute-start(f32[4,64,768]{2,1,0:T(8,128)S(1)} %pad_maximum_fusion.refs_0_), channel_id=1, source_target_pairs={{0,64},{1,65},{2,66},{3,67},{4,68},{5,69},{6,70},{7,71},{8,72},{9,... | collective-permute-start | bytes 2359304 | tf_op jit(solution)/shard_map/ppermute | solution.py:77
  58.4 27.2 %collective-permute-start.30 = (f32[4,64,768]{2,1,0:T(8,128)S(1)}, f32[4,64,768]{2,1,0:T(8,128)S(1)}, u32[]{:S(2)}, u32[]{:S(2)}) collective-permute-start(f32[4,64,768]{2,1,0:T(8,128)S(1)} %pad_maximum_fusion.1.refs_0_), channel_id=1, source_target_pairs={{0,64},{1,65},{2,66},{3,67},{4,68},{5,69},{6,70},{7,71},{8,72},{9,... | collective-permute-start | bytes 2359304 | tf_op jit(solution)/shard_map/ppermute | solution.py:77
  64.6 12.6 %collective-permute-start.31 = (f32[4,64,640]{2,1,0:T(8,128)S(1)}, f32[4,64,640]{2,1,0:T(8,128)S(1)}, u32[]{:S(2)}, u32[]{:S(2)}) collective-permute-start(f32[4,64,640]{2,1,0:T(8,128)S(1)} %pad_maximum_fusion.4.refs_1_), channel_id=1, source_target_pairs={{0,16},{1,17},{2,18},{3,19},{4,20},{5,21},{6,22},{7,23},{8,24},{9,... | collective-permute-start | bytes 1966088 | tf_op jit(solution)/shard_map/ppermute | solution.py:77
  65.5 13.2 %collective-permute-start.32 = (f32[4,64,640]{2,1,0:T(8,128)S(1)}, f32[4,64,640]{2,1,0:T(8,128)S(1)}, u32[]{:S(2)}, u32[]{:S(2)}) collective-permute-start(f32[4,64,640]{2,1,0:T(8,128)S(1)} %pad_maximum_fusion.5.refs_2_), channel_id=1, source_target_pairs={{0,48},{1,49},{2,50},{3,51},{4,52},{5,53},{6,54},{7,55},{8,56},{9,... | collective-permute-start | bytes 1966088 | tf_op jit(solution)/shard_map/ppermute | solution.py:77
  109.7 23.6 %collective-permute-start.12 = (f32[4,64,768]{2,1,0:T(8,128)S(1)}, f32[4,64,768]{2,1,0:T(8,128)S(1)}, u32[]{:S(2)}, u32[]{:S(2)}) collective-permute-start(f32[4,64,768]{2,1,0:T(8,128)S(1)} %get-tuple-element.82), channel_id=1, source_target_pairs={{0,4},{1,5},{2,6},{3,7},{4,0},{5,1},{6,2},{7,3},{8,12},{9,13},{10,... | collective-permute-start | bytes 2359304 | tf_op jit(solution)/shard_map/ppermute | solution.py:77
  110.0 24.9 %collective-permute-start.13 = (f32[4,64,768]{2,1,0:T(8,128)S(1)}, f32[4,64,768]{2,1,0:T(8,128)S(1)}, u32[]{:S(2)}, u32[]{:S(2)}) collective-permute-start(f32[4,64,768]{2,1,0:T(8,128)S(1)} %get-tuple-element.83), channel_id=1, source_target_pairs={{0,12},{1,13},{2,14},{3,15},{4,8},{5,9},{6,10},{7,11},{8,4},{9,5},... | collective-permute-start | bytes 2359304 | tf_op jit(solution)/shard_map/ppermute | solution.py:77
  111.4 21.3 %collective-permute-start.14 = (f32[4,64,512]{2,1,0:T(8,128)S(1)}, f32[4,64,512]{2,1,0:T(8,128)S(1)}, u32[]{:S(2)}, u32[]{:S(2)}) collective-permute-start(f32[4,64,512]{2,1,0:T(8,128)S(1)} %get-tuple-element.84), channel_id=1, source_target_pairs={{0,2},{1,3},{2,0},{3,1},{4,6},{5,7},{6,4},{7,5},{8,10},{9,11},{10,... | collective-permute-start | bytes 1572872 | tf_op jit(solution)/shard_map/ppermute | solution.py:77
  116.8 30.6 %collective-permute-start.33 = (f32[4,64,768]{2,1,0:T(8,128)S(1)}, f32[4,64,768]{2,1,0:T(8,128)S(1)}, u32[]{:S(2)}, u32[]{:S(2)}) collective-permute-start(f32[4,64,768]{2,1,0:T(8,128)S(1)} %get-tuple-element.109), channel_id=1, source_target_pairs={{0,4},{1,5},{2,6},{3,7},{4,0},{5,1},{6,2},{7,3},{8,12},{9,13},{10,... | collective-permute-start | bytes 2359304 | tf_op jit(solution)/shard_map/ppermute | solution.py:77
  122.4 25.3 %collective-permute-start.34 = (f32[4,64,768]{2,1,0:T(8,128)S(1)}, f32[4,64,768]{2,1,0:T(8,128)S(1)}, u32[]{:S(2)}, u32[]{:S(2)}) collective-permute-start(f32[4,64,768]{2,1,0:T(8,128)S(1)} %get-tuple-element.110), channel_id=1, source_target_pairs={{0,12},{1,13},{2,14},{3,15},{4,8},{5,9},{6,10},{7,11},{8,4},{9,5},... | collective-permute-start | bytes 2359304 | tf_op jit(solution)/shard_map/ppermute | solution.py:77
  132.7 34.0 %collective-permute-start.23 = (f32[2048]{0:T(1024)S(1)}, f32[2048]{0:T(1024)S(1)}, u32[]{:S(2)}, u32[]{:S(2)}) collective-permute-start(f32[2048]{0:T(1024)S(1)} %add.136), channel_id=1, source_target_pairs={{0,2},{1,3},{2,0},{3,1},{4,6},{5,7},{6,4},{7,5},{8,10},{9,11},{10,... | collective-permute-start | bytes 24584 | tf_op jit(solution)/shard_map/ppermute | solution.py:77
  133.3 12.3 %collective-permute-start.35 = (f32[4,64,512]{2,1,0:T(8,128)S(1)}, f32[4,64,512]{2,1,0:T(8,128)S(1)}, u32[]{:S(2)}, u32[]{:S(2)}) collective-permute-start(f32[4,64,512]{2,1,0:T(8,128)S(1)} %get-tuple-element.111), channel_id=1, source_target_pairs={{0,2},{1,3},{2,0},{3,1},{4,6},{5,7},{6,4},{7,5},{8,10},{9,11},{10,... | collective-permute-start | bytes 1572872 | tf_op jit(solution)/shard_map/ppermute | solution.py:77
  134.9 20.9 %collective-permute-start.15 = (f32[2,64,768]{2,1,0:T(8,128)S(1)}, f32[2,64,768]{2,1,0:T(8,128)S(1)}, u32[]{:S(2)}, u32[]{:S(2)}) collective-permute-start(f32[2,64,768]{2,1,0:T(8,128)S(1)} %slice_add_fusion.3), channel_id=1, source_target_pairs={{0,12},{1,13},{2,14},{3,15},{4,8},{5,9},{6,10},{7,11},{8,4},{9,5},... | collective-permute-start | bytes 1179656 | tf_op jit(solution)/shard_map/ppermute | solution.py:77
  145.6 10.4 %collective-permute-start.16 = (f32[2,64,768]{2,1,0:T(8,128)S(1)}, f32[2,64,768]{2,1,0:T(8,128)S(1)}, u32[]{:S(2)}, u32[]{:S(2)}) collective-permute-start(f32[2,64,768]{2,1,0:T(8,128)S(1)} %slice_add_fusion.2), channel_id=1, source_target_pairs={{0,2},{1,3},{2,0},{3,1},{4,6},{5,7},{6,4},{7,5},{8,10},{9,11},{10,... | collective-permute-start | bytes 1179656 | tf_op jit(solution)/shard_map/ppermute | solution.py:77
  147.8 14.6 %collective-permute-start.36 = (f32[2,64,768]{2,1,0:T(8,128)S(1)}, f32[2,64,768]{2,1,0:T(8,128)S(1)}, u32[]{:S(2)}, u32[]{:S(2)}) collective-permute-start(f32[2,64,768]{2,1,0:T(8,128)S(1)} %slice_add_fusion.1), channel_id=1, source_target_pairs={{0,12},{1,13},{2,14},{3,15},{4,8},{5,9},{6,10},{7,11},{8,4},{9,5},... | collective-permute-start | bytes 1179656 | tf_op jit(solution)/shard_map/ppermute | solution.py:77
  155.5 9.5 %collective-permute-start.37 = (f32[2,64,768]{2,1,0:T(8,128)S(1)}, f32[2,64,768]{2,1,0:T(8,128)S(1)}, u32[]{:S(2)}, u32[]{:S(2)}) collective-permute-start(f32[2,64,768]{2,1,0:T(8,128)S(1)} %slice_add_fusion), channel_id=1, source_target_pairs={{0,2},{1,3},{2,0},{3,1},{4,6},{5,7},{6,4},{7,5},{8,10},{9,11},{10,... | collective-permute-start | bytes 1179656 | tf_op jit(solution)/shard_map/ppermute | solution.py:77
  156.2 15.2 %collective-permute-start.18 = (f32[1,64,768]{2,1,0:T(8,128)S(1)}, f32[1,64,768]{2,1,0:T(8,128)S(1)}, u32[]{:S(2)}, u32[]{:S(2)}) collective-permute-start(f32[1,64,768]{2,1,0:T(8,128)S(1)} %get-tuple-element.137), channel_id=1, source_target_pairs={{0,2},{1,3},{2,0},{3,1},{4,6},{5,7},{6,4},{7,5},{8,10},{9,11},{10,... | collective-permute-start | bytes 589832 | tf_op jit(solution)/shard_map/ppermute | solution.py:77
  162.2 9.2 %collective-permute-start.19 = (f32[1,64,768]{2,1,0:T(8,128)S(1)}, f32[1,64,768]{2,1,0:T(8,128)S(1)}, u32[]{:S(2)}, u32[]{:S(2)}) collective-permute-start(f32[1,64,768]{2,1,0:T(8,128)S(1)} %get-tuple-element.135), channel_id=1, source_target_pairs={{0,4},{1,5},{2,6},{3,7},{4,0},{5,1},{6,2},{7,3},{8,12},{9,13},{10,... | collective-permute-start | bytes 589832 | tf_op jit(solution)/shard_map/ppermute | solution.py:77
  165.3 9.5 %collective-permute-start.39 = (f32[1,64,768]{2,1,0:T(8,128)S(1)}, f32[1,64,768]{2,1,0:T(8,128)S(1)}, u32[]{:S(2)}, u32[]{:S(2)}) collective-permute-start(f32[1,64,768]{2,1,0:T(8,128)S(1)} %get-tuple-element.133), channel_id=1, source_target_pairs={{0,2},{1,3},{2,0},{3,1},{4,6},{5,7},{6,4},{7,5},{8,10},{9,11},{10,... | collective-permute-start | bytes 589832 | tf_op jit(solution)/shard_map/ppermute | solution.py:77
  (15 other events, 242.0 us)
